TPU v7x, 32 devices: a whole 2x2x4 slice. The times are simulated.
32 devices in a mesh: seq: 8 (over z, x), tensor: 4 (over y, core).
Axes of the slice: x: 2, y: 2, z: 4, core: 2. Of those that a mesh axis runs over, the one named last changes fastest.
Arguments:
- inputs: bfloat16 [2, 2048, 2048], P(None, 'seq'), may hold values from -6 to 6
- segment: int32 [2, 2048], P(None, 'seq'), may hold values from 0 to 2, as said below
- position: int32 [2, 2048], P(None, 'seq'), may hold values from 0 to 1535, as said below
- w_query: float32 [2048, 2048], P('seq', 'tensor'), may hold values from -0.125 to 0.125
- w_keyval: float32 [2048, 256], P(('seq', 'tensor')), may hold values from -0.125 to 0.125
- w_out: float32 [2048, 2048], P('tensor', 'seq'), may hold values from -3 to 3
- w_fc: float32 [2048, 8192], P('seq', 'tensor'), may hold values from -0.125 to 0.125
- w_proj: float32 [8192, 2048], P('tensor', 'seq'), may hold values from -0.0625 to 0.0625
- vectors: float32 [7, 2048], P(None, ('seq', 'tensor'))
- fc_bias: float32 [8192], P(('seq', 'tensor')), may hold values from -1.5 to 1.5
- value_bias: float32 [128], replicated, may hold values from -0.1 to 0.1
- grad_out: bfloat16 [2, 2048, 2048], P(None, 'seq'), may hold values from -6 to 6
Outputs:
- output: bfloat16 [2, 2048, 2048], P(None, 'seq')
- grad_input: bfloat16 [2, 2048, 2048], P(None, 'seq')
- grad_w_query: float32 [2048, 2048], P('seq', 'tensor')
- grad_w_keyval: float32 [2048, 256], P(('seq', 'tensor'))
- grad_w_out: float32 [2048, 2048], P('tensor', 'seq')
- grad_w_fc: float32 [2048, 8192], P('seq', 'tensor')
- grad_w_proj: float32 [8192, 2048], P('tensor', 'seq')
- grad_vectors: float32 [7, 2048], P(None, ('seq', 'tensor'))
- grad_fc_bias: float32 [8192], P(('seq', 'tensor'))
- grad_value_bias: float32 [128], replicated
- grad_shift_two: float32 [2048], P(('seq', 'tensor'))
Inputs may be any that keep to these rules, and one draw needn't show every extreme that they name: The rows of a micro-batch form blocks of 256 rows in an arbitrary order; each block holds 256 consecutive positions of one sequence. Segment 0 is the prompt of 1024 tokens with positions 0 to 1023; each segment of 1 to 2 is a continuation of 512 tokens with positions 1024 to 1535. `position`: positions of each sequence are distinct and as stated under segment.
All inputs are finite; a program needn't handle non-finite values.
Results may differ from a plain program's by a relative error of at most 0.02.
Values may be sent and summed in bfloat16 or wider, within the bound.
A program may use at most 192 MiB of HBM per device.

v0:
```python
from functools import partial

import jax
import jax.numpy as jnp
from jax import lax
from jax.sharding import PartitionSpec as P

UNIT = 256


EPS = 1e-05
NEG = -1e30


def layer_norm(values, gain_vec, shift_vec):
    average = jnp.mean(values, axis=-1, keepdims=True)
    centred = values - average
    spread = jnp.mean(centred * centred, axis=-1, keepdims=True)
    return centred * lax.rsqrt(spread + EPS) * gain_vec + shift_vec


def product(left, right):
    return jnp.dot(left, right, preferred_element_type=jnp.float32)


def product_left(left, right):
    return lax.dot_general(
        left, right, (((0,), (0,)), ((), ())), preferred_element_type=jnp.float32
    )


def product_right(left, right):
    return lax.dot_general(
        left, right, (((1,), (1,)), ((), ())), preferred_element_type=jnp.float32
    )


def visible_mask(seg_query, pos_query, seg_keys, pos_keys):
    same = (seg_keys[None, :] == 0) | (seg_keys[None, :] == seg_query[:, None])
    return same & (pos_keys[None, :] <= pos_query[:, None])


def attention_parts(queries, keyval, seg_query, pos_query, seg_keys, pos_keys):
    row_count = queries.shape[0]
    head_dim = keyval.shape[1] // 2
    head_count = queries.shape[1] // head_dim
    scale = float(head_dim) ** (-0.5)
    query_heads = queries.reshape(row_count, head_count, head_dim)
    total_keys = keyval.shape[0]
    block_rows = UNIT
    num_blocks = total_keys // block_rows

    def block_mask(index):
        start = index * block_rows
        seg_block = lax.dynamic_slice_in_dim(seg_keys, start, block_rows, 0)
        pos_block = lax.dynamic_slice_in_dim(pos_keys, start, block_rows, 0)
        return visible_mask(seg_query, pos_query, seg_block, pos_block)

    def block_live(index):
        return jnp.any(block_mask(index))

    def block_scores(index):
        key_block = lax.dynamic_slice_in_dim(keyval, index * block_rows, block_rows, 0)
        visible = block_mask(index)
        scores = (
            jnp.einsum(
                "rhd,kd->hrk",
                query_heads,
                key_block[:, :head_dim],
                preferred_element_type=jnp.float32,
            )
            * scale
        )
        return (key_block, visible, jnp.where(visible[None], scores, NEG))

    return dict(
        row_count=row_count,
        head_dim=head_dim,
        head_count=head_count,
        scale=scale,
        query_heads=query_heads,
        block_rows=block_rows,
        num_blocks=num_blocks,
        block_live=block_live,
        block_scores=block_scores,
    )


def attend_forward(parts):
    row_count, head_dim, head_count = (parts["row_count"], parts["head_dim"], parts["head_count"])
    block_live, block_scores = (parts["block_live"], parts["block_scores"])

    def stats_step(index, carry):

        def stats_update(state):
            top_now, total_now = state
            key_block, visible, scores = block_scores(index)
            top_next = jnp.maximum(top_now, jnp.max(scores, axis=-1))
            terms = jnp.where(visible[None], jnp.exp(scores - top_next[:, :, None]), 0.0)
            return (top_next, total_now * jnp.exp(top_now - top_next) + jnp.sum(terms, axis=-1))

        return lax.cond(block_live(index), stats_update, lambda state: state, carry)

    start_state = (
        jnp.full((head_count, row_count), NEG, jnp.float32),
        jnp.zeros((head_count, row_count), jnp.float32),
    )
    top_final, total_final = lax.fori_loop(0, parts["num_blocks"], stats_step, start_state)
    log_total = top_final + jnp.log(total_final)

    def output_step(index, carry):

        def output_update(acc):
            key_block, visible, scores = block_scores(index)
            probs_full = jnp.where(visible[None], jnp.exp(scores - log_total[:, :, None]), 0.0)
            return acc + jnp.einsum(
                "hrk,kd->rhd",
                probs_full.astype(jnp.bfloat16),
                key_block[:, head_dim:],
                preferred_element_type=jnp.float32,
            )

        return lax.cond(block_live(index), output_update, lambda acc: acc, carry)

    mixed_acc = lax.fori_loop(
        0,
        parts["num_blocks"],
        output_step,
        jnp.zeros((row_count, head_count, head_dim), jnp.float32),
    )
    return (mixed_acc.reshape(row_count, head_count * head_dim), log_total)


def attend_backward(parts, log_total, grad_mixed):
    row_count, head_dim, head_count = (parts["row_count"], parts["head_dim"], parts["head_count"])
    block_live, block_scores, scale = (parts["block_live"], parts["block_scores"], parts["scale"])
    block_rows, query_heads = (parts["block_rows"], parts["query_heads"])
    grad_heads = grad_mixed.reshape(row_count, head_count, head_dim)

    def block_probs(index):
        key_block, visible, scores = block_scores(index)
        probs_full = jnp.where(visible[None], jnp.exp(scores - log_total[:, :, None]), 0.0)
        grad_probs = jnp.einsum(
            "rhd,kd->hrk", grad_heads, key_block[:, head_dim:], preferred_element_type=jnp.float32
        )
        return (key_block, probs_full, grad_probs)

    def delta_step(index, carry):

        def delta_update(acc):
            key_block, probs_full, grad_probs = block_probs(index)
            return acc + jnp.sum(probs_full * grad_probs, axis=-1)

        return lax.cond(block_live(index), delta_update, lambda acc: acc, carry)

    delta = lax.fori_loop(
        0, parts["num_blocks"], delta_step, jnp.zeros((head_count, row_count), jnp.float32)
    )

    def grad_step(carry, index):

        def grad_update(acc):
            key_block, probs_full, grad_probs = block_probs(index)
            grad_scores = (probs_full * (grad_probs - delta[:, :, None])).astype(jnp.bfloat16)
            acc_next = acc + jnp.einsum(
                "hrk,kd->rhd",
                grad_scores,
                key_block[:, :head_dim],
                preferred_element_type=jnp.float32,
            )
            grad_keys = (
                jnp.einsum(
                    "hrk,rhd->kd", grad_scores, query_heads, preferred_element_type=jnp.float32
                )
                * scale
            )
            grad_values = jnp.einsum(
                "hrk,rhd->kd",
                probs_full.astype(jnp.bfloat16),
                grad_heads,
                preferred_element_type=jnp.float32,
            )
            return (acc_next, jnp.concatenate([grad_keys, grad_values], axis=1))

        def skip_block(acc):
            return (acc, jnp.zeros((block_rows, 2 * head_dim), jnp.float32))

        return lax.cond(block_live(index), grad_update, skip_block, carry)

    grad_query_acc, key_blocks = lax.scan(
        grad_step,
        jnp.zeros((row_count, head_count, head_dim), jnp.float32),
        jnp.arange(parts["num_blocks"]),
    )
    grad_queries = (grad_query_acc * scale).reshape(row_count, head_count * head_dim)
    return (grad_queries, key_blocks.reshape(parts["num_blocks"] * block_rows, 2 * head_dim))


def fetch_weights(w_query, w_keyval, w_out, w_fc, w_proj, vectors, fc_bias):
    larger = (
        lax.all_gather(w_query.astype(jnp.bfloat16), "seq", axis=0, tiled=True),
        lax.all_gather(w_out.astype(jnp.bfloat16), "seq", axis=1, tiled=True),
        lax.all_gather(w_fc.astype(jnp.bfloat16), "seq", axis=0, tiled=True),
        lax.all_gather(w_proj.astype(jnp.bfloat16), "seq", axis=1, tiled=True),
    )
    smaller = (
        lax.all_gather(w_keyval.astype(jnp.bfloat16), ("seq", "tensor"), axis=0, tiled=True),
        lax.all_gather(vectors.astype(jnp.bfloat16), ("seq", "tensor"), axis=1, tiled=True),
        lax.all_gather(fc_bias.astype(jnp.bfloat16), ("seq", "tensor"), axis=0, tiled=True),
    )
    return tuple(larger) + tuple(smaller)


def local(
    inputs,
    segment,
    position,
    w_query,
    w_keyval,
    w_out,
    w_fc,
    w_proj,
    vectors,
    fc_bias,
    value_bias,
    grad_out,
):
    tensor_index = lax.axis_index("tensor")
    seq_size = lax.axis_size("seq")
    tensor_size = lax.axis_size("tensor")
    leading = tensor_index == 0
    seg_all, pos_all = (
        lax.all_gather(segment, "seq", axis=1, tiled=True),
        lax.all_gather(position, "seq", axis=1, tiled=True),
    )
    group_width = w_query.shape[1]
    hidden_width = w_fc.shape[1]
    head_dim = value_bias.shape[0]
    full_width = w_query.shape[0] * seq_size
    full_hidden = fc_bias.shape[0] * seq_size * tensor_size
    bias_value = value_bias.astype(jnp.bfloat16).astype(jnp.float32)
    kv_bias = jnp.concatenate([jnp.zeros((head_dim,), jnp.float32), bias_value])
    fetch_args = (w_query, w_keyval, w_out, w_fc, w_proj, vectors, fc_bias)
    acc_query = jnp.zeros((full_width, group_width), jnp.float32)
    acc_out = jnp.zeros((group_width, full_width), jnp.float32)
    acc_fc = jnp.zeros((full_width, hidden_width), jnp.float32)
    acc_proj = jnp.zeros((hidden_width, full_width), jnp.float32)
    acc_keyval = jnp.zeros((full_width, 2 * head_dim), jnp.float32)
    acc_vectors = jnp.zeros((7, full_width), jnp.float32)
    acc_fcbias = jnp.zeros((full_hidden,), jnp.float32)
    acc_vbias = jnp.zeros((head_dim,), jnp.float32)
    results = []
    input_grads = []
    for batch_index in range(inputs.shape[0]):
        loaded = fetch_weights(*fetch_args)
        query_mat, out_mat, fc_mat, proj_mat, keyval_mat, vec_rows, fc_row = loaded
        vec_float = vec_rows.astype(jnp.float32)
        gain_one, shift_one, query_bias_all, out_bias, gain_two, shift_two, proj_bias = [
            vec_float[row_index] for row_index in range(7)
        ]
        query_bias = lax.dynamic_slice_in_dim(
            query_bias_all, tensor_index * group_width, group_width, 0
        )
        fc_local = lax.dynamic_slice_in_dim(
            fc_row.astype(jnp.float32), tensor_index * hidden_width, hidden_width, 0
        )
        residual_in = inputs[batch_index].astype(jnp.float32)
        normed = layer_norm(residual_in, gain_one, shift_one).astype(jnp.bfloat16)
        queries = (product(normed, query_mat) + query_bias).astype(jnp.bfloat16)
        keyval_local = (product(normed, keyval_mat) + kv_bias).astype(jnp.bfloat16)
        keyval_all = lax.all_gather(keyval_local, "seq", axis=0, tiled=True)
        parts = attention_parts(
            queries,
            keyval_all,
            segment[batch_index],
            position[batch_index],
            seg_all[batch_index],
            pos_all[batch_index],
        )
        mixed_float, log_total = attend_forward(parts)
        mixed_heads = mixed_float.astype(jnp.bfloat16)
        attn_total = lax.psum(product(mixed_heads, out_mat).astype(jnp.bfloat16), "tensor").astype(
            jnp.float32
        )
        middle = residual_in + attn_total + out_bias
        normed_two = layer_norm(middle, gain_two, shift_two).astype(jnp.bfloat16)
        hidden = product(normed_two, fc_mat) + fc_local
        active = jax.nn.gelu(hidden, approximate=True).astype(jnp.bfloat16)
        ff_total = lax.psum(product(active, proj_mat).astype(jnp.bfloat16), "tensor").astype(
            jnp.float32
        )
        results.append((middle + ff_total + proj_bias).astype(jnp.bfloat16))
        loaded = fetch_weights(*fetch_args)
        query_mat, out_mat, fc_mat, proj_mat, keyval_mat, vec_rows, fc_row = loaded
        grad_final = grad_out[batch_index]
        grad_final_f = grad_final.astype(jnp.float32)
        acc_proj = acc_proj + product_left(active, grad_final)
        grad_active = product_right(grad_final, proj_mat)
        gelu_value, gelu_pull = jax.vjp(partial(jax.nn.gelu, approximate=True), hidden)
        grad_hidden = gelu_pull(grad_active)[0].astype(jnp.bfloat16)
        fcbias_local = jnp.sum(grad_hidden.astype(jnp.float32), axis=0)
        acc_fc = acc_fc + product_left(normed_two, grad_hidden)
        grad_normed_two = product_right(grad_hidden, fc_mat)
        norm_value, second_pull = jax.vjp(layer_norm, middle, gain_two, shift_two)
        grad_middle_part, grad_gain_two, grad_shift_two = second_pull(grad_normed_two)
        grad_middle = grad_final_f + lax.psum(
            grad_middle_part.astype(jnp.bfloat16), "tensor"
        ).astype(jnp.float32)
        grad_middle_low = grad_middle.astype(jnp.bfloat16)
        acc_out = acc_out + product_left(mixed_heads, grad_middle_low)
        grad_mixed = product_right(grad_middle_low, out_mat).astype(jnp.bfloat16)
        grad_queries, grad_keyval_all = attend_backward(parts, log_total, grad_mixed)
        grad_keyval = lax.psum_scatter(
            grad_keyval_all.astype(jnp.bfloat16), "seq", scatter_dimension=0, tiled=True
        )
        grad_queries_low = grad_queries.astype(jnp.bfloat16)
        acc_query = acc_query + product_left(normed, grad_queries_low)
        acc_keyval = acc_keyval + product_left(normed, grad_keyval)
        acc_vbias = acc_vbias + jnp.sum(grad_keyval[:, head_dim:].astype(jnp.float32), axis=0)
        grad_normed = product_right(grad_queries_low, query_mat) + product_right(
            grad_keyval, keyval_mat
        )
        first_value, first_pull = jax.vjp(layer_norm, residual_in, gain_one, shift_one)
        grad_in_part, grad_gain_one, grad_shift_one = first_pull(grad_normed)
        input_grads.append(
            (
                grad_middle
                + lax.psum(grad_in_part.astype(jnp.bfloat16), "tensor").astype(jnp.float32)
            ).astype(jnp.bfloat16)
        )
        qbias_full = lax.dynamic_update_slice_in_dim(
            jnp.zeros((full_width,), jnp.float32),
            jnp.sum(grad_queries_low.astype(jnp.float32), axis=0),
            tensor_index * group_width,
            0,
        )
        obias_grad = jnp.where(leading, jnp.sum(grad_middle, axis=0), 0.0)
        pbias_grad = jnp.where(leading, jnp.sum(grad_final_f, axis=0), 0.0)
        acc_vectors = acc_vectors + jnp.stack(
            [
                grad_gain_one,
                grad_shift_one,
                qbias_full,
                obias_grad,
                grad_gain_two,
                grad_shift_two,
                pbias_grad,
            ]
        )
        acc_fcbias = acc_fcbias + lax.dynamic_update_slice_in_dim(
            jnp.zeros((full_hidden,), jnp.float32), fcbias_local, tensor_index * hidden_width, 0
        )
    larger_grads = (
        lax.psum_scatter(
            acc_query.astype(jnp.bfloat16), "seq", scatter_dimension=0, tiled=True
        ).astype(jnp.float32),
        lax.psum_scatter(
            acc_out.astype(jnp.bfloat16), "seq", scatter_dimension=1, tiled=True
        ).astype(jnp.float32),
        lax.psum_scatter(
            acc_fc.astype(jnp.bfloat16), "seq", scatter_dimension=0, tiled=True
        ).astype(jnp.float32),
        lax.psum_scatter(
            acc_proj.astype(jnp.bfloat16), "seq", scatter_dimension=1, tiled=True
        ).astype(jnp.float32),
    )
    smaller_grads = (
        lax.psum_scatter(acc_keyval, ("seq", "tensor"), scatter_dimension=0, tiled=True),
        lax.psum_scatter(acc_vectors, ("seq", "tensor"), scatter_dimension=1, tiled=True),
        lax.psum_scatter(acc_fcbias, ("seq", "tensor"), scatter_dimension=0, tiled=True),
    )
    vbias_total = lax.psum(acc_vbias, ("seq", "tensor"))
    return (
        jnp.stack(results),
        jnp.stack(input_grads),
        larger_grads[0],
        smaller_grads[0],
        larger_grads[1],
        larger_grads[2],
        larger_grads[3],
        smaller_grads[1],
        smaller_grads[2],
        vbias_total,
        smaller_grads[1][5],
    )


def solution(mesh):
    in_specs = (
        P(None, "seq", None),
        P(None, "seq"),
        P(None, "seq"),
        P("seq", "tensor"),
        P(("seq", "tensor"), None),
        P("tensor", "seq"),
        P("seq", "tensor"),
        P("tensor", "seq"),
        P(None, ("seq", "tensor")),
        P(("seq", "tensor")),
        P(),
        P(None, "seq", None),
    )
    out_specs = (
        P(None, "seq", None),
        P(None, "seq", None),
        P("seq", "tensor"),
        P(("seq", "tensor"), None),
        P("tensor", "seq"),
        P("seq", "tensor"),
        P("tensor", "seq"),
        P(None, ("seq", "tensor")),
        P(("seq", "tensor")),
        P(),
        P(("seq", "tensor")),
    )
    return jax.shard_map(local, mesh=mesh, in_specs=in_specs, out_specs=out_specs, check_vma=False)
```

profile of v0, /device:TPU:0, one launch (start us, length us, event | category | flops | bytes accessed | tf_op | source)
XLA Modules:
  0.0 1981.2 jit_solution(15178087917641814251)
XLA Ops:
  12.1 43.4 %all-gather = bf16[32,64,7]{1,2,0:T(8,128)(2,1)S(1)} all-gather(bf16[1,64,7]{1,2,0:T(8,128)(2,1)S(1)} %convert_bitcast_fusion.2), channel_id=1, replica_groups=mesh['seq'=8,'tensor'=4] {'seq','tensor'}, dimensions={0}, use_global_device_ids=true | all-gather | bytes 29568 | tf_op jit(solution)/shard_map/all_gather | solution.py:208
  58.7 9.2 all-gather.10.cloned.1.call-done
  71.3 26.2 %all_gather.22 = s32[2,2048]{1,0:T(2,128)S(1)} all-gather(s32[2,256]{1,0:T(2,128)S(1)} %copy-done.87), channel_id=1, replica_groups=mesh['seq'=8,'tensor'=4] {'seq'}, dimensions={1}, use_global_device_ids=true | all-gather | bytes 18432 | tf_op jit(solution)/shard_map/all_gather | solution.py:233
  97.5 26.5 %all_gather.23 = s32[2,2048]{1,0:T(2,128)S(1)} all-gather(s32[2,256]{1,0:T(2,128)S(1)} %copy-done.88), channel_id=1, replica_groups=mesh['seq'=8,'tensor'=4] {'seq'}, dimensions={1}, use_global_device_ids=true | all-gather | bytes 18432 | tf_op jit(solution)/shard_map/all_gather | solution.py:234
  127.6 32.8 %all-gather.12.cloned.1.call-done = bf16[2048,256]{1,0:T(8,128)(2,1)} async-done(((bf16[256,256]{1,0:T(8,128)(2,1)}), bf16[2048,256]{1,0:T(8,128)(2,1)}) %all-gather.12.cloned.1.call-update) | async-done | bytes 1048592 | tf_op jit(solution)/shard_map/all_gather | solution.py:271
  160.5 26.9 %while.124 = (s32[]{:T(128)}, f32[4,256]{1,0:T(4,128)S(1)}, f32[4,256]{1,0:T(4,128)S(1)}, s32[2048]{0:T(1024)}, s32[1,256]{1,0:T(1,128)S(1)}, /*index=5*/s32[204...) while((s32[]{:T(128)}, f32[4,256]{1,0:T(4,128)S(1)}, ...), condition=%wide.region_8.9_spmd, body=%wide.region_2.8_spmd.sunk | while | flops 69274120 | bytes 2692459 | solution.py:108
  187.5 27.0 %while.125 = (s32[]{:T(128)}, f32[256,4,128]{0,2,1:T(8,128)S(1)}, s32[2048]{0:T(1024)}, s32[1,256]{1,0:T(1,128)S(1)}, s32[2048]{0:T(1024)}, /*index=5*/s32[1,256...) while((s32[]{:T(128)}, f32[256,4,128]{0,2,1:T(8,128)S(1)}, ...), condition=%wide.region_13.14_spmd, body=%wide.region_9.13_spmd.sunk | while | flops 136249856 | bytes 1596243 | solution.py:125
  218.1 65.1 %all-reduce.10.cloned.1.call-done = bf16[256,2048]{1,0:T(8,128)(2,1)} async-done(((bf16[256,2048]{1,0:T(8,128)(2,1)}), bf16[256,2048]{1,0:T(8,128)(2,1)}) %all-reduce.10.cloned.1.call-update) | async-done | bytes 1048592 | tf_op jit(solution)/shard_map/psum | solution.py:282
  288.9 38.4 %all-gather.22.cloned.1.call-done = bf16[2048,256]{1,0:T(8,128)(2,1)} async-done(((bf16[256,256]{1,0:T(8,128)(2,1)}), bf16[2048,256]{1,0:T(8,128)(2,1)}) %all-gather.22.cloned.1.call-update) | async-done | bytes 1048592 | tf_op jit(solution)/shard_map/all_gather | solution.py:271
  327.3 36.2 %while.126 = (s32[]{:T(128)}, f32[4,256]{1,0:T(4,128)S(1)}, f32[4,256]{1,0:T(4,128)S(1)}, s32[2048]{0:T(1024)}, s32[1,256]{1,0:T(1,128)S(1)}, /*index=5*/s32[204...) while((s32[]{:T(128)}, f32[4,256]{1,0:T(4,128)S(1)}, ...), condition=%wide.region_26.27_spmd, body=%wide.region_20.26_spmd.sunk | while | flops 69274120 | bytes 2692459 | solution.py:108
  364.1 36.4 %while.127 = (s32[]{:T(128)}, f32[256,4,128]{0,2,1:T(8,128)S(1)}, s32[2048]{0:T(1024)}, s32[1,256]{1,0:T(1,128)S(1)}, s32[2048]{0:T(1024)}, /*index=5*/s32[1,256...) while((s32[]{:T(128)}, f32[256,4,128]{0,2,1:T(8,128)S(1)}, ...), condition=%wide.region_31.0_spmd, body=%wide.region_27.31_spmd.sunk | while | flops 136249856 | bytes 1596243 | solution.py:125
  410.4 47.4 %all-gather.1 = bf16[32,1,256]{2,1,0:T(2,128)(2,1)S(1)} all-gather(bf16[1,1,256]{2,1,0:T(2,128)(2,1)S(1)} %reshape.972), channel_id=1, replica_groups=mesh['seq'=8,'tensor'=4] {'seq','tensor'}, dimensions={0}, use_global_device_ids=true | all-gather | bytes 16896 | tf_op jit(solution)/shard_map/all_gather | solution.py:209
  460.8 117.9 %all-gather.18.cloned.1.call-done = bf16[2048,2048]{1,0:T(8,128)(2,1)} async-done(((bf16[256,2048]{1,0:T(8,128)(2,1)}), bf16[2048,2048]{1,0:T(8,128)(2,1)}) %all-gather.18.cloned.1.call-update) | async-done | bytes 8388624 | tf_op jit(solution)/shard_map/all_gather | solution.py:203
  578.8 7.6 convolution_add_fusion.3
  590.2 114.3 %all-gather.20.cloned.1.call-done = bf16[2048,2048]{1,0:T(8,128)(2,1)} async-done(((bf16[2048,256]{1,0:T(8,128)(2,1)}), bf16[2048,2048]{1,0:T(8,128)(2,1)}) %all-gather.20.cloned.1.call-update) | async-done | bytes 8388624 | tf_op jit(solution)/shard_map/all_gather | solution.py:204
  704.5 8.5 convert_reduce_fusion.4
  717.5 6.2 fusion.211
  723.7 6.5 multiply_reduce_fusion.3
  739.1 47.0 %all-reduce.16.cloned.1.call-done = (bf16[256,2048]{1,0:T(8,128)(2,1)}, bf16[256,2048]{1,0:T(8,128)(2,1)}) async-done(((bf16[256,2048]{1,0:T(8,128)(2,1)}, bf16[256,2048]{1,0:T(8,128)(2,1)}), (bf16[256,2048]{1,0:T(8,128)(2,1)}, bf16[256,2048]{1,0:T(8,128)(2,1)})) %all-reduce.16.cloned.1.call-update) | async-done | bytes 2097168 | tf_op jit(solution)/shard_map/psum | solution.py:306
  797.9 27.1 %while.128 = (s32[]{:T(128)}, f32[4,256]{1,0:T(4,128)S(1)}, s32[2048]{0:T(1024)}, s32[1,256]{1,0:T(1,128)S(1)}, s32[2048]{0:T(1024)}, /*index=5*/s32[1,256]{1,0:...) while((s32[]{:T(128)}, f32[4,256]{1,0:T(4,128)S(1)}, ...), condition=%wide.region_44.45_spmd, body=%wide.region_39.44_spmd.sunk | while | flops 136380928 | bytes 3970443 | solution.py:156
  825.6 44.8 %while.130 = (s32[]{:T(128)}, f32[4,256]{1,0:T(4,128)}, s32[2048]{0:T(1024)}, s32[1,256]{1,0:T(1,128)S(1)}, s32[2048]{0:T(1024)}, /*index=5*/s32[1,256]{1,0:T(1,...) while((s32[]{:T(128)}, f32[4,256]{1,0:T(4,128)}, ...), condition=%wide.region_62.63_spmd, body=%wide.region_57.0_spmd.sunk | while | flops 136380928 | bytes 3970443 | solution.py:156
  828.4 5.6 conditional.22
  839.6 5.6 conditional.22
  848.0 5.6 conditional.22
  864.9 5.6 conditional.22
  872.9 86.3 %while.131 = (s32[]{:T(128)}, f32[256,4,128]{0,2,1:T(8,128)}, bf16[8,256,256]{2,1,0:T(8,128)(2,1)}, s32[8]{0:T(128)}, s32[2048]{0:T(1024)}, /*index=5*/s32[1,256...) while((s32[]{:T(128)}, f32[256,4,128]{0,2,1:T(8,128)}, ...), condition=%wide.region_67.68_spmd, body=%wide.region_63.67_spmd.sunk | while | flops 338690560 | bytes 14902839 | solution.py:190
  877.7 7.2 conditional.23
  899.3 7.2 conditional.23
  913.6 7.2 conditional.23
  949.6 7.2 conditional.23
  961.6 64.9 %while.129 = (s32[]{:T(128)}, f32[256,4,128]{0,2,1:T(8,128)}, bf16[8,256,256]{2,1,0:T(8,128)(2,1)}, s32[8]{0:T(128)}, s32[2048]{0:T(1024)}, /*index=5*/s32[1,256...) while((s32[]{:T(128)}, f32[256,4,128]{0,2,1:T(8,128)}, ...), condition=%wide.region_49.50_spmd, body=%wide.region_45.0_spmd.sunk | while | flops 338690560 | bytes 13854235 | solution.py:190
  966.5 7.2 conditional.21
  1026.8 7.7 convolution_convert_fusion.2
  1034.5 7.0 convolution_convert_fusion.3
  1042.5 22.2 %reduce-scatter.13.cloned.1.call-done = bf16[256,256]{1,0:T(8,128)(2,1)} async-done(((bf16[2048,256]{1,0:T(8,128)(2,1)}), bf16[256,256]{1,0:T(8,128)(2,1)}) %reduce-scatter.13.cloned.1.call-update) | async-done | bytes 131088 | tf_op jit(solution)/shard_map/reduce_scatter | solution.py:313
  1067.7 93.0 %reduce-scatter.11.cloned.1.call-done = bf16[256,256]{1,0:T(8,128)(2,1)} async-done(((bf16[2048,256]{1,0:T(8,128)(2,1)}), bf16[256,256]{1,0:T(8,128)(2,1)}) %reduce-scatter.11.cloned.1.call-update) | async-done | bytes 131088 | tf_op jit(solution)/shard_map/reduce_scatter | solution.py:313
  1182.4 9.6 fusion.187
  1192.1 63.8 %all-reduce.14.cloned.1.call-done = (bf16[256,2048]{1,0:T(8,128)(2,1)}, bf16[256,2048]{1,0:T(8,128)(2,1)}, bf16[256,2048]{1,0:T(8,128)(2,1)}, bf16[256,2048]{1,0:T(8,128)(2,1)}) async-done(((bf16[256,2048]{1,0:T(8,128)(2,1)}, bf16[256,2048]{1,0:T(8,128)(2,1)}, bf16[256,2048]{1,0:T(8,128)(2,1)}, bf16[256,2048]{1,0:T(8,128)(2,1)}), (bf16[256,2048]{1,0:T(8,128)(2,1)}, bf16[256,2048]{1,0:T(8,128)(2,1)}, ...) | async-done | bytes 4194320 | tf_op jit(solution)/shard_map/psum | solution.py:289
  1255.9 5.7 convert_reduce_fusion.2
  1263.4 12.7 add_convert_fusion.1
  1276.3 10.4 fusion.158
  1286.8 9.5 add_convert_fusion
  1301.1 40.5 %all-reduce.2 = (f32[8192]{0:T(1024)S(1)}, f32[128]{0:T(128)}) all-reduce(f32[8192]{0:T(1024)S(1)} %add_dynamic-update-slice_fusion, f32[128]{0:T(128)S(1)} %add.569), channel_id=10, replica_groups=mesh['seq'=8,'tensor'=4] {'seq','tensor'}, use_global_device_ids=true, to_apply=%region_94.95.clone | all-reduce | flops 8320 | bytes 66560
  1351.1 48.3 %reduce-scatter.15.cloned.1.call-done = bf16[256,512]{1,0:T(8,128)(2,1)} async-done(((bf16[2048,512]{1,0:T(8,128)(2,1)}), bf16[256,512]{1,0:T(8,128)(2,1)}) %reduce-scatter.15.cloned.1.call-update) | async-done | bytes 262160 | tf_op jit(solution)/shard_map/reduce_scatter | solution.py:354
  1401.2 135.9 %reduce-scatter.25.cloned.1.call-done = f32[64,7]{1,0:T(8,128)} async-done(((f32[2048,7]{1,0:T(8,128)}), f32[64,7]{1,0:T(8,128)}) %reduce-scatter.25.cloned.1.call-update) | async-done | bytes 1808
  1538.5 145.5 %reduce-scatter.21.cloned.1.call-done = bf16[256,2048]{1,0:T(8,128)(2,1)} async-done(((bf16[2048,2048]{1,0:T(8,128)(2,1)}), bf16[256,2048]{1,0:T(8,128)(2,1)}) %reduce-scatter.21.cloned.1.call-update) | async-done | bytes 1048592 | tf_op jit(solution)/shard_map/reduce_scatter | solution.py:360
  1686.8 147.7 %reduce-scatter.23.cloned.1.call-done = bf16[2048,256]{1,0:T(8,128)(2,1)} async-done(((bf16[2048,2048]{1,0:T(8,128)(2,1)}), bf16[2048,256]{1,0:T(8,128)(2,1)}) %reduce-scatter.23.cloned.1.call-update) | async-done | bytes 1048592 | tf_op jit(solution)/shard_map/reduce_scatter | solution.py:363
  1837.2 137.3 %reduce-scatter.17.cloned.1.call-done = f32[64,256]{1,0:T(8,128)} async-done(((f32[2048,256]{1,0:T(8,128)}), f32[64,256]{1,0:T(8,128)}) %reduce-scatter.17.cloned.1.call-update) | async-done | bytes 65552 | tf_op jit(solution)/shard_map/reduce_scatter | solution.py:368
  (856 shorter events, 451.1 us)
Async XLA Ops:
  7.2 50.4 %copy-start = (bf16[2,256,2048]{2,1,0:T(8,128)(2,1)S(1)}, bf16[2,256,2048]{2,1,0:T(8,128)(2,1)}, u32[]{:S(2)}) copy-start(bf16[2,256,2048]{2,1,0:T(8,128)(2,1)} %param.44) | copy-start | bytes 6291460
  7.2 60.7 %all-gather.10.cloned.1.call-start = ((), (), s32[]{:S(2)}) async-start(), calls=%async_computation.8 | async-start | bytes 1081344 | tf_op jit(solution)/shard_map/all_gather | solution.py:207
  8.9 116.3 %all-gather.14.cloned.1.call-start = ((), (), s32[]{:S(2)}) async-start(), calls=%async_computation.10 | async-start | bytes 2359296 | tf_op jit(solution)/shard_map/all_gather | solution.py:201
  10.7 149.8 %all-gather.12.cloned.1.call-start = ((), (), s32[]{:S(2)}) async-start(), calls=%async_computation.9 | async-start | bytes 1179648 | tf_op jit(solution)/shard_map/all_gather | solution.py:271
  57.5 67.6 %copy-start.70 = (f32[256]{0:T(256)}, f32[256]{0:T(256)S(1)}, u32[]{:S(2)}) copy-start(f32[256]{0:T(256)S(1)} %broadcast_multiply_fusion.3) | copy-start | bytes 3076
  58.0 9.9 copy-start.83
  58.0 67.2 %copy-start.73 = (f32[256]{0:T(256)}, f32[256]{0:T(256)S(1)}, u32[]{:S(2)}) copy-start(f32[256]{0:T(256)S(1)} %fusion.181) | copy-start | bytes 3076
  58.6 227.8 %copy-start.49 = (f32[1,2048]{1,0:T(1,128)}, f32[1,2048]{1,0:T(1,128)S(1)}, u32[]{:S(2)}) copy-start(f32[1,2048]{1,0:T(1,128)S(1)} %get-tuple-element.2077) | copy-start | bytes 24580
  58.6 227.8 %copy-start.52 = (f32[1,2048]{1,0:T(1,128)}, f32[1,2048]{1,0:T(1,128)S(1)}, u32[]{:S(2)}) copy-start(f32[1,2048]{1,0:T(1,128)S(1)} %get-tuple-element.2076) | copy-start | bytes 24580
  58.6 527.8 %copy-start.56 = (f32[1,2048]{1,0:T(1,128)}, f32[1,2048]{1,0:T(1,128)S(1)}, u32[]{:S(2)}) copy-start(f32[1,2048]{1,0:T(1,128)S(1)} %get-tuple-element.2072) | copy-start | bytes 24580
  58.6 674.7 %copy-start.44 = (f32[1,2048]{1,0:T(1,128)}, f32[1,2048]{1,0:T(1,128)S(1)}, u32[]{:S(2)}) copy-start(f32[1,2048]{1,0:T(1,128)S(1)} %get-tuple-element.2074) | copy-start | bytes 24580
  58.7 674.6 %copy-start.54 = (f32[1,2048]{1,0:T(1,128)}, f32[1,2048]{1,0:T(1,128)S(1)}, u32[]{:S(2)}) copy-start(f32[1,2048]{1,0:T(1,128)S(1)} %get-tuple-element.2073) | copy-start | bytes 24580
  67.9 29.6 %copy-start.88 = (s32[2,256]{1,0:T(2,128)S(1)}, s32[2,256]{1,0:T(2,128)}, u32[]{:S(2)}) copy-start(s32[2,256]{1,0:T(2,128)} %param.46) | copy-start | bytes 6148
  70.4 144.1 %all-gather.16.cloned.1.call-start = ((), (), s32[]{:S(2)}) async-start(), calls=%async_computation.11 | async-start | bytes 2359296 | tf_op jit(solution)/shard_map/all_gather | solution.py:202
  71.3 211.9 %all-reduce.10.cloned.1.call-start = ((), (), s32[]{:S(2)}) async-start(), calls=%async_computation.12 | async-start | bytes 2097152 | tf_op jit(solution)/shard_map/psum | solution.py:282
  218.0 67.2 %copy-start.23 = (bf16[2048,256]{1,0:T(8,128)(2,1)S(1)}, bf16[2048,256]{1,0:T(8,128)(2,1)}, u32[]{:S(2)}) copy-start(bf16[2048,256]{1,0:T(8,128)(2,1)} %all-gather.10.cloned.1.call-done) | copy-start | bytes 3145732
  218.0 109.3 %all-gather.22.cloned.1.call-start = ((), (), s32[]{:S(2)}) async-start(), calls=%async_computation.15 | async-start | bytes 1179648 | tf_op jit(solution)/shard_map/all_gather | solution.py:271
  218.1 68.4 %copy-start.63 = (f32[256]{0:T(256)}, f32[256]{0:T(256)S(1)}, u32[]{:S(2)}) copy-start(f32[256]{0:T(256)S(1)} %broadcast_multiply_fusion.1) | copy-start | bytes 3076
  286.4 171.5 %all-reduce.12.cloned.1.call-start = ((), (), s32[]{:S(2)}) async-start(), calls=%async_computation.16 | async-start | bytes 2097152 | tf_op jit(solution)/shard_map/psum | solution.py:282
  288.9 38.5 %copy-start.39 = (bf16[256,512]{1,0:T(8,128)(2,1)}, bf16[256,512]{1,0:T(8,128)(2,1)S(1)}, u32[]{:S(2)}) copy-start(bf16[256,512]{1,0:T(8,128)(2,1)S(1)} %fusion.141) | copy-start | bytes 786436
  404.7 174.1 %all-gather.18.cloned.1.call-start = ((), (), s32[]{:S(2)}) async-start(), calls=%async_computation.13 | async-start | bytes 9437184 | tf_op jit(solution)/shard_map/all_gather | solution.py:203
  407.5 50.5 %copy-start.1 = (bf16[256,2048]{1,0:T(8,128)(2,1)S(1)}, bf16[256,2048]{1,0:T(8,128)(2,1)}, u32[]{:S(2)}) copy-start(bf16[256,2048]{1,0:T(8,128)(2,1)} %all-reduce.10.cloned.1.call-done) | copy-start | bytes 3145732
  407.5 297.0 %all-gather.20.cloned.1.call-start = ((), (), s32[]{:S(2)}) async-start(), calls=%async_computation.14 | async-start | bytes 9437184 | tf_op jit(solution)/shard_map/all_gather | solution.py:204
  410.3 375.8 %all-reduce.16.cloned.1.call-start = ((), (), s32[]{:S(2)}) async-start(), calls=%async_computation.26 | async-start | bytes 4194304 | tf_op jit(solution)/shard_map/psum | solution.py:306
  457.9 275.4 %copy-start.58 = (f32[256]{0:T(256)}, f32[256]{0:T(256)S(1)}, u32[]{:S(2)}) copy-start(f32[256]{0:T(256)S(1)} %broadcast_multiply_fusion.2) | copy-start | bytes 3076
  460.2 273.1 %copy-start.66 = (f32[256]{0:T(256)}, f32[256]{0:T(256)S(1)}, u32[]{:S(2)}) copy-start(f32[256]{0:T(256)S(1)} %broadcast_multiply_fusion) | copy-start | bytes 3076
  460.2 273.1 %copy-start.68 = (f32[256]{0:T(256)}, f32[256]{0:T(256)S(1)}, u32[]{:S(2)}) copy-start(f32[256]{0:T(256)S(1)} %fusion.182) | copy-start | bytes 3076
  460.8 272.5 %copy-start.79 = (f32[256]{0:T(256)}, f32[256]{0:T(256)S(1)}, u32[]{:S(2)}) copy-start(f32[256]{0:T(256)S(1)} %fusion.184) | copy-start | bytes 3076
  578.8 7.7 copy-start.95
  704.5 8.5 copy-start.11
  704.5 8.5 copy-start.35
  704.5 8.5 copy-start.94
  736.4 328.3 %reduce-scatter.13.cloned.1.call-start = ((), (), s32[]{:S(2)}) async-start(), calls=%async_computation.18 | async-start | bytes 1179648 | tf_op jit(solution)/shard_map/reduce_scatter | solution.py:313
  959.2 201.6 %reduce-scatter.11.cloned.1.call-start = ((), (), s32[]{:S(2)}) async-start(), calls=%async_computation.17 | async-start | bytes 1179648 | tf_op jit(solution)/shard_map/reduce_scatter | solution.py:313
  1026.5 229.4 %all-reduce.14.cloned.1.call-start = ((), (), s32[]{:S(2)}) async-start(), calls=%async_computation.25 | async-start | bytes 8388608 | tf_op jit(solution)/shard_map/psum | solution.py:289
  1026.8 7.7 copy-start.36
  1034.5 7.2 copy-start.10
  1041.7 121.0 %copy-start.29 = (bf16[256,4,128]{0,2,1:T(8,128)(2,1)}, bf16[256,4,128]{0,2,1:T(8,128)(2,1)S(1)}, u32[]{:S(2)}) copy-start(bf16[256,4,128]{0,2,1:T(8,128)(2,1)S(1)} %get-tuple-element.2052) | copy-start | bytes 786436
  1171.3 178.1 %reduce-scatter.19.cloned.1.call-start = ((), (), s32[]{:S(2)}) async-start(), calls=%async_computation.21 | async-start | bytes 2359296 | tf_op jit(solution)/shard_map/reduce_scatter | solution.py:357
  1176.8 222.6 %reduce-scatter.15.cloned.1.call-start = ((), (), s32[]{:S(2)}) async-start(), calls=%async_computation.19 | async-start | bytes 2359296 | tf_op jit(solution)/shard_map/reduce_scatter | solution.py:354
  1181.7 355.5 %reduce-scatter.25.cloned.1.call-start = ((), (), s32[]{:S(2)}) async-start(), calls=%async_computation.24 | async-start | bytes 1081344
  1263.3 420.7 %reduce-scatter.21.cloned.1.call-start = ((), (), s32[]{:S(2)}) async-start(), calls=%async_computation.22 | async-start | bytes 9437184 | tf_op jit(solution)/shard_map/reduce_scatter | solution.py:360
  1276.1 558.4 %reduce-scatter.23.cloned.1.call-start = ((), (), s32[]{:S(2)}) async-start(), calls=%async_computation.23 | async-start | bytes 9437184 | tf_op jit(solution)/shard_map/reduce_scatter | solution.py:363
  1276.3 10.5 copy-start.13
  1276.3 10.4 copy-start.34
  1296.3 678.2 %reduce-scatter.17.cloned.1.call-start = ((), (), s32[]{:S(2)}) async-start(), calls=%async_computation.20 | async-start | bytes 2162688 | tf_op jit(solution)/shard_map/reduce_scatter | solution.py:368
  1300.1 42.2 %copy-start.62 = (f32[1,2048]{1,0:T(1,128)S(1)}, f32[1,2048]{1,0:T(1,128)}, u32[]{:S(2)}) copy-start(f32[1,2048]{1,0:T(1,128)} %get-tuple-element.2071) | copy-start | bytes 24580
  1538.0 299.2 %copy-start.93 = (f32[7,64]{1,0:T(8,128)}, f32[7,64]{1,0:T(8,128)S(1)}, u32[]{:S(2)}) copy-start(f32[7,64]{1,0:T(8,128)S(1)} %copy.188) | copy-start | bytes 5380
  (97 other events, 197.8 us)
Sparse Core Ops, SparseCore 0:
  11.4 56.3 all-gather.9
  70.6 48.2 all-gather.13
  121.6 38.8 all-gather.11
  162.9 49.3 all-gather.15
  218.1 65.0 all-reduce.9
  286.5 40.7 all-gather.21
  404.8 46.2 all-reduce.11
  453.8 124.9 all-gather.17
  581.4 123.0 all-gather.19
  736.5 49.5 all-reduce.15
  959.3 105.3 reduce-scatter.12
  1067.9 92.8 reduce-scatter.10
  1171.4 84.4 all-reduce.13
  1259.3 69.3 reduce-scatter.18
  1332.0 67.3 reduce-scatter.14
  1401.5 135.5 reduce-scatter.24
  1540.6 143.3 reduce-scatter.20
  1687.5 146.9 reduce-scatter.22
  1837.3 137.1 reduce-scatter.16
where the time goes:
time: 2000 us; the launch traced here: 1980 us
  waiting for transfers between devices  1220 us (61%)
  blocking collectives  184 us (9%)
  matrix products  183 us (9%)
  other arithmetic  173 us (9%)
  local copies, waits for them, and re-layouts  147 us (7%)
  loops' own time  57.4 us (3%)
    reduce_scatter x1, waiting for transfers between devices, local(): lax.psum_scatter(acc_proj.astype(jnp.bfloat16), 'seq', scatter_dimension=...  148 us
    reduce_scatter x1, waiting for transfers between devices, local(): lax.psum_scatter(acc_fc.astype(jnp.bfloat16), 'seq', scatter_dimension=0,...  146 us
    reduce_scatter x1, waiting for transfers between devices, local(): lax.psum_scatter(acc_keyval, ('seq', 'tensor'), scatter_dimension=0, tile...  137 us
    unnamed x20, waiting for transfers between devices  136 us
    all_gather x1, waiting for transfers between devices, fetch_weights(): lax.all_gather(w_fc.astype(jnp.bfloat16), 'seq', axis=0, tiled=True)  118 us
    reduce_scatter x2, waiting for transfers between devices, local(): lax.psum_scatter(grad_keyval_all.astype(jnp.bfloat16), 'seq', scatter_dim...  115 us
    all_gather x1, waiting for transfers between devices, fetch_weights(): lax.all_gather(w_proj.astype(jnp.bfloat16), 'seq', axis=1, tiled=True)  114 us
    all_gather x2, waiting for transfers between devices, local(): keyval_all = lax.all_gather(keyval_local, 'seq', axis=0, tiled=True)  71.2 us
  transfers between devices with their start and end apart: 19, of which 15 were waited for; matrix products, arithmetic and copies ran while one was open for 12% of the time, Pallas kernels for 0%

commit v1 on v0

v1 whole, which is shorter than its diff:
```python
from functools import partial

import jax
import jax.numpy as jnp
from jax import lax
from jax.experimental import pallas as pl
from jax.experimental.pallas import tpu as pltpu
from jax.sharding import PartitionSpec as P

EPS = 1e-05
NEG = -1e30
LOW = jnp.bfloat16
F32 = jnp.float32


def bits_of(count):
    return count.bit_length() - 1


def swap(value, axis, bit):
    count = lax.axis_size(axis)
    return lax.ppermute(value, axis, [(i, i ^ (1 << bit)) for i in range(count)])


def after(value, *others):
    return lax.optimization_barrier((value,) + others)[0]


def dot(left, right):
    return jnp.dot(left, right, preferred_element_type=F32)


def dot_tn(left, right):
    return lax.dot_general(left, right, (((0,), (0,)), ((), ())), preferred_element_type=F32)


def dot_nt(left, right):
    return lax.dot_general(left, right, (((1,), (1,)), ((), ())), preferred_element_type=F32)


def offsets_in_order(count):
    width = bits_of(count)
    return [int(format(p, "0%db" % width)[::-1], 2) if width else 0 for p in range(count)]


def gather_blocks(own):
    count = lax.axis_size("seq")
    blocks = {0: own}
    for bit in reversed(range(bits_of(count))):
        for r in list(blocks):
            blocks[r | (1 << bit)] = swap(blocks[r], "seq", bit)
    return blocks


def scatter_blocks(blocks):
    count = lax.axis_size("seq")
    blocks = dict(blocks)
    for bit in range(bits_of(count)):
        for r in sorted(blocks):
            if r & (1 << bit):
                arrived = swap(blocks.pop(r).astype(LOW), "seq", bit)
                blocks[r ^ (1 << bit)] = blocks[r ^ (1 << bit)] + arrived.astype(F32)
    return blocks[0]


def tensor_gather(own, axis):
    count = lax.axis_size("tensor")
    out = jnp.expand_dims(own, axis)
    for bit in reversed(range(bits_of(count))):
        out_other = swap(out, "tensor", bit)
        mine = (lax.axis_index("tensor") >> bit) & 1
        low_part = jnp.where(mine == 0, out, out_other)
        high_part = jnp.where(mine == 0, out_other, out)
        size = out.shape[axis]
        shape = out.shape
        low_part = jnp.expand_dims(low_part, axis)
        high_part = jnp.expand_dims(high_part, axis)
        out = jnp.concatenate([low_part, high_part], axis=axis)
        out = jnp.swapaxes(out, axis, axis + 1) if size > 1 else out
        out = out.reshape(shape[:axis] + (2 * size,) + shape[axis + 1 :])
    return out


def tensor_scatter(parts, axis):
    count = lax.axis_size("tensor")
    index = lax.axis_index("tensor")
    for bit in range(bits_of(count)):
        shape = parts.shape
        split = parts.reshape(shape[:axis] + (shape[axis] // 2, 2) + shape[axis + 1 :])
        mine = (index >> bit) & 1
        keep = lax.dynamic_index_in_dim(split, mine, axis + 1, keepdims=False)
        give = lax.dynamic_index_in_dim(split, 1 - mine, axis + 1, keepdims=False)
        parts = keep.astype(F32) + swap(give.astype(LOW), "tensor", bit).astype(F32)
    return lax.squeeze(parts, (axis,))


def visible(meta_q, meta_k):
    seg_q, pos_q = meta_q[:, 0:1], meta_q[:, 1:2]
    seg_k, pos_k = meta_k[0:1, :], meta_k[1:2, :]
    return ((seg_k == 0) | (seg_k == seg_q)) & (pos_k <= pos_q)


def forward_kernel(live_ref, q_ref, kv_ref, mq_ref, mk_ref, o_ref, lse_ref, top, total, acc):
    batch = pl.program_id(0)
    hd = kv_ref.shape[-1] // 2
    heads = q_ref.shape[-1] // hd
    blocks = kv_ref.shape[1]
    scale = float(hd) ** (-0.5)
    top[...] = jnp.full_like(top, NEG)
    total[...] = jnp.zeros_like(total)
    acc[...] = jnp.zeros_like(acc)

    def step(index, carry):
        @pl.when(live_ref[batch, index] > 0)
        def _():
            mask = visible(mq_ref[0], mk_ref[0, index])
            keys = kv_ref[0, index, :, :hd]
            values = kv_ref[0, index, :, hd:]
            for head in range(heads):
                cols = slice(head * hd, (head + 1) * hd)
                scores = jnp.where(mask, dot_nt(q_ref[0, :, cols], keys) * scale, NEG)
                before = top[head]
                now = jnp.maximum(before, jnp.max(scores, axis=-1, keepdims=True))
                shrink = jnp.exp(before - now)
                probs = jnp.exp(scores - now)
                total[head] = total[head] * shrink + jnp.sum(probs, axis=-1, keepdims=True)
                acc[:, cols] = acc[:, cols] * shrink + dot(probs.astype(LOW), values)
                top[head] = now

        return carry

    lax.fori_loop(0, blocks, step, 0)
    for head in range(heads):
        cols = slice(head * hd, (head + 1) * hd)
        o_ref[0, :, cols] = (acc[:, cols] / total[head]).astype(LOW)
        lse_ref[0, head] = top[head] + jnp.log(total[head])


def attend_forward(queries, keyval, meta_q, meta_k, live):
    batches, rows, width = queries.shape
    _, blocks, keys, two = keyval.shape
    hd = two // 2
    heads = width // hd
    flops = 4 * batches * rows * width * blocks * keys
    return pl.pallas_call(
        forward_kernel,
        grid_spec=pltpu.PrefetchScalarGridSpec(
            num_scalar_prefetch=1,
            grid=(batches,),
            in_specs=[
                pl.BlockSpec((1, rows, width), lambda b, live: (b, 0, 0)),
                pl.BlockSpec((1, blocks, keys, two), lambda b, live: (b, 0, 0, 0)),
                pl.BlockSpec((1, rows, 128), lambda b, live: (b, 0, 0)),
                pl.BlockSpec((1, blocks, 8, keys), lambda b, live: (b, 0, 0, 0)),
            ],
            out_specs=[
                pl.BlockSpec((1, rows, width), lambda b, live: (b, 0, 0)),
                pl.BlockSpec((1, heads, rows, 1), lambda b, live: (b, 0, 0, 0)),
            ],
            scratch_shapes=[
                pltpu.VMEM((heads, rows, 1), F32),
                pltpu.VMEM((heads, rows, 1), F32),
                pltpu.VMEM((rows, width), F32),
            ],
        ),
        out_shape=[
            jax.ShapeDtypeStruct((batches, rows, width), LOW),
            jax.ShapeDtypeStruct((batches, heads, rows, 1), F32),
        ],
        name="attend_forward",
        cost_estimate=pl.CostEstimate(
            flops=flops, transcendentals=0, bytes_accessed=2 * keyval.size
        ),
    )(live, queries, keyval, meta_q, meta_k)


def backward_kernel(
    live_ref, q_ref, kv_ref, mq_ref, mk_ref, o_ref, lse_ref, do_ref, dq_ref, dkv_ref, delta, acc
):
    batch = pl.program_id(0)
    hd = kv_ref.shape[-1] // 2
    heads = q_ref.shape[-1] // hd
    blocks = kv_ref.shape[1]
    scale = float(hd) ** (-0.5)
    acc[...] = jnp.zeros_like(acc)
    for head in range(heads):
        cols = slice(head * hd, (head + 1) * hd)
        delta[head] = jnp.sum(
            do_ref[0, :, cols].astype(F32) * o_ref[0, :, cols].astype(F32), axis=-1, keepdims=True
        )

    def step(index, carry):
        @pl.when(live_ref[batch, index] > 0)
        def _():
            mask = visible(mq_ref[0], mk_ref[0, index])
            keys = kv_ref[0, index, :, :hd]
            values = kv_ref[0, index, :, hd:]
            grad_k = jnp.zeros((keys.shape[0], hd), F32)
            grad_v = jnp.zeros((keys.shape[0], hd), F32)
            for head in range(heads):
                cols = slice(head * hd, (head + 1) * hd)
                query = q_ref[0, :, cols]
                grad_o = do_ref[0, :, cols]
                scores = dot_nt(query, keys) * scale
                probs = jnp.where(mask, jnp.exp(scores - lse_ref[0, head]), 0.0)
                grad_p = dot_nt(grad_o, values)
                grad_s = (probs * (grad_p - delta[head])).astype(LOW)
                acc[:, cols] += dot(grad_s, keys)
                grad_k = grad_k + dot_tn(grad_s, query)
                grad_v = grad_v + dot_tn(probs.astype(LOW), grad_o)
            dkv_ref[0, index, :, :hd] = (grad_k * scale).astype(LOW)
            dkv_ref[0, index, :, hd:] = grad_v.astype(LOW)

        @pl.when(live_ref[batch, index] == 0)
        def _():
            dkv_ref[0, index] = jnp.zeros(dkv_ref.shape[2:], LOW)

        return carry

    lax.fori_loop(0, blocks, step, 0)
    dq_ref[0] = (acc[...] * scale).astype(LOW)


def attend_backward(queries, keyval, meta_q, meta_k, live, mixed, lse, grad_mixed):
    batches, rows, width = queries.shape
    _, blocks, keys, two = keyval.shape
    hd = two // 2
    heads = width // hd
    flops = 10 * batches * rows * width * blocks * keys
    row_spec = pl.BlockSpec((1, rows, width), lambda b, live: (b, 0, 0))
    kv_spec = pl.BlockSpec((1, blocks, keys, two), lambda b, live: (b, 0, 0, 0))
    return pl.pallas_call(
        backward_kernel,
        grid_spec=pltpu.PrefetchScalarGridSpec(
            num_scalar_prefetch=1,
            grid=(batches,),
            in_specs=[
                row_spec,
                kv_spec,
                pl.BlockSpec((1, rows, 128), lambda b, live: (b, 0, 0)),
                pl.BlockSpec((1, blocks, 8, keys), lambda b, live: (b, 0, 0, 0)),
                row_spec,
                pl.BlockSpec((1, heads, rows, 1), lambda b, live: (b, 0, 0, 0)),
                row_spec,
            ],
            out_specs=[row_spec, kv_spec],
            scratch_shapes=[
                pltpu.VMEM((heads, rows, 1), F32),
                pltpu.VMEM((rows, width), F32),
            ],
        ),
        out_shape=[
            jax.ShapeDtypeStruct((batches, rows, width), LOW),
            jax.ShapeDtypeStruct((batches, blocks, keys, two), LOW),
        ],
        name="attend_backward",
        cost_estimate=pl.CostEstimate(
            flops=flops, transcendentals=0, bytes_accessed=4 * keyval.size
        ),
    )(live, queries, keyval, meta_q, meta_k, mixed, lse, grad_mixed)


def norm_parts(values):
    average = jnp.mean(values, axis=-1, keepdims=True)
    centred = values - average
    spread = jnp.mean(centred * centred, axis=-1, keepdims=True)
    return centred, lax.rsqrt(spread + EPS)


def norm_back(values, gain, grad):
    centred, inverse = norm_parts(values)
    unit = centred * inverse
    scaled = grad * gain
    inner = (
        scaled
        - jnp.mean(scaled, axis=-1, keepdims=True)
        - unit * jnp.mean(scaled * unit, axis=-1, keepdims=True)
    )
    return inverse * inner, grad * unit


def gelu_pair(values):
    const = 0.7978845608028654
    square = values * values
    inner = jnp.tanh(const * (values + 0.044715 * (values * square)))
    half = 0.5 * (1.0 + inner)
    slope = half + 0.5 * values * (1.0 - inner * inner) * const * (1.0 + 3 * 0.044715 * square)
    return values * half, slope


def local(
    inputs,
    segment,
    position,
    w_query,
    w_keyval,
    w_out,
    w_fc,
    w_proj,
    vectors,
    fc_bias,
    value_bias,
    grad_out,
):
    seq_size, tensor_size = lax.axis_size("seq"), lax.axis_size("tensor")
    seq_index, tensor_index = lax.axis_index("seq"), lax.axis_index("tensor")
    batches, rows, full_width = inputs.shape
    width_block = w_query.shape[0]
    group_width = w_query.shape[1]
    hidden_width = w_fc.shape[1]
    hd = value_bias.shape[0]
    quarter = rows // tensor_size
    order = offsets_in_order(seq_size)
    shard = vectors.shape[1]
    bias_shard = fc_bias.shape[0]

    def to_order(array):
        starts = [jnp.bitwise_xor(seq_index, r) * width_block for r in order]
        last = array.ndim - 1
        return jnp.concatenate(
            [lax.dynamic_slice_in_dim(array, start, width_block, last) for start in starts], last
        )

    def from_order(array):
        place = {r: p for p, r in enumerate(order)}
        table = jnp.array([place[r] for r in range(seq_size)], jnp.int32)
        last = array.ndim - 1
        return jnp.concatenate(
            [
                lax.dynamic_slice_in_dim(
                    array, table[jnp.bitwise_xor(seq_index, b)] * width_block, width_block, last
                )
                for b in range(seq_size)
            ],
            last,
        )

    pieces = [
        vectors.reshape(-1).astype(LOW),
        fc_bias.astype(LOW),
        segment.reshape(-1).astype(LOW),
        (position // 128).reshape(-1).astype(LOW),
        (position % 128).reshape(-1).astype(LOW),
    ]
    sizes = [piece.shape[0] for piece in pieces]
    packed = jnp.concatenate(pieces)
    pad = -packed.shape[0] % 1024
    packed = jnp.pad(packed, (0, pad)).reshape(-1, 128)
    small = lax.all_gather(packed, ("seq", "tensor"), axis=0, tiled=False)
    small = small.reshape(seq_size, tensor_size, -1).astype(F32)
    cuts = [0]
    for size in sizes:
        cuts.append(cuts[-1] + size)
    vec_all = small[:, :, cuts[0] : cuts[1]].reshape(seq_size * tensor_size, 7, shard)
    vec_all = jnp.swapaxes(vec_all, 0, 1).reshape(7, full_width)
    fc_all = small[:, :, cuts[1] : cuts[2]].reshape(-1)
    seg_all = small[:, 0, cuts[2] : cuts[3]].reshape(seq_size, batches, rows)
    pos_all = 128.0 * small[:, 0, cuts[3] : cuts[4]] + small[:, 0, cuts[4] : cuts[5]]
    pos_all = pos_all.reshape(seq_size, batches, rows)
    offset_ids = jnp.bitwise_xor(seq_index, jnp.array(order, jnp.int32))
    seg_keys = jnp.swapaxes(seg_all[offset_ids], 0, 1).astype(jnp.int32)
    pos_keys = jnp.swapaxes(pos_all[offset_ids], 0, 1).astype(jnp.int32)
    meta_k = jnp.pad(jnp.stack([seg_keys, pos_keys], axis=2), ((0, 0), (0, 0), (0, 6), (0, 0)))
    meta_q = jnp.pad(jnp.stack([segment, position], axis=2), ((0, 0), (0, 0), (0, 126)))
    seg_lo, seg_hi = jnp.min(seg_keys, axis=2), jnp.max(seg_keys, axis=2)
    own_lo = jnp.min(segment, axis=1, keepdims=True)
    own_hi = jnp.max(segment, axis=1, keepdims=True)
    live = (
        ((seg_lo == 0) | ((seg_lo <= own_hi) & (own_lo <= seg_hi)))
        & (jnp.min(pos_keys, axis=2) <= jnp.max(position, axis=1, keepdims=True))
    ).astype(jnp.int32)

    vec_rows = to_order(vec_all)
    gain_one, shift_one, _, out_bias, gain_two, shift_two, proj_bias = [
        vec_rows[i] for i in range(7)
    ]
    query_bias = lax.dynamic_slice_in_dim(vec_all[2], tensor_index * group_width, group_width, 0)
    fc_local = lax.dynamic_slice_in_dim(fc_all, tensor_index * hidden_width, hidden_width, 0)
    bias_value = value_bias.astype(LOW).astype(F32)
    kv_bias = jnp.concatenate([jnp.zeros((hd,), F32), bias_value])

    kv_rows = tensor_gather(w_keyval.astype(LOW), 0).reshape(width_block, 2 * hd)
    first_own = jnp.concatenate([w_query.astype(LOW), kv_rows], axis=1)
    first_blocks = gather_blocks(first_own)
    first_mat = jnp.concatenate([first_blocks[r] for r in order], axis=0)
    out_blocks = gather_blocks(after(w_out.T.astype(LOW), first_blocks[seq_size - 1]))
    out_t = jnp.concatenate([out_blocks[r] for r in order], axis=0)
    fc_blocks = gather_blocks(after(w_fc.astype(LOW), out_blocks[seq_size // 2 - 1]))
    fc_mat = jnp.concatenate([fc_blocks[r] for r in order], axis=0)
    proj_blocks = gather_blocks(after(w_proj.T.astype(LOW), fc_blocks[seq_size // 2 - 1]))
    proj_t = jnp.concatenate([proj_blocks[r] for r in order], axis=0)

    hidden_in = to_order(inputs)
    residual = hidden_in.astype(F32)
    centred, inverse = norm_parts(residual)
    normed = (centred * inverse * gain_one + shift_one).astype(LOW).reshape(-1, full_width)
    first_out = dot(normed, first_mat)
    queries = (first_out[:, :group_width] + query_bias).astype(LOW)
    queries = queries.reshape(batches, rows, group_width)
    keyval = (first_out[:, group_width:] + kv_bias).astype(LOW).reshape(batches, rows, 2 * hd)
    kv_blocks = gather_blocks(keyval)
    kv_all = jnp.stack([kv_blocks[r] for r in order], axis=1)
    mixed, lse = attend_forward(queries, kv_all, meta_q, meta_k, live)
    mixed_rows = mixed.reshape(-1, group_width)

    def quarters(array):
        return array.reshape(batches, tensor_size, quarter, array.shape[-1])

    def my_quarter(array):
        split = quarters(array)
        return lax.dynamic_index_in_dim(split, tensor_index, 1, keepdims=False)

    attn_part = quarters(dot_nt(mixed_rows, out_t))
    attn_sum = tensor_scatter(attn_part, 1)
    middle = my_quarter(hidden_in).astype(F32) + attn_sum + out_bias
    centred, inverse = norm_parts(middle)
    normed_q = (centred * inverse * gain_two + shift_two).astype(LOW)
    normed_two = tensor_gather(normed_q, 1).reshape(-1, full_width)
    hidden = dot(normed_two, fc_mat) + fc_local
    active_f, slope = gelu_pair(hidden)
    active = active_f.astype(LOW)

    grad_rows = to_order(grad_out)
    grad_flat = grad_rows.reshape(-1, full_width)
    grad_hidden = (slope * dot(grad_flat, proj_t)).astype(LOW)
    fcbias_local = jnp.sum(grad_hidden.astype(F32), axis=0)
    grad_normed_two = quarters(dot_nt(grad_hidden, fc_mat))
    back_sum = tensor_scatter(grad_normed_two, 1)
    grad_q = my_quarter(grad_rows).astype(F32)
    norm_part, gain_part = norm_back(middle, gain_two, back_sum)
    grad_middle = grad_q + norm_part
    grad_gain_two = jnp.sum(gain_part, axis=(0, 1))
    grad_shift_two = jnp.sum(back_sum, axis=(0, 1))
    grad_out_bias = jnp.sum(grad_middle, axis=(0, 1))
    grad_proj_bias = jnp.sum(grad_q, axis=(0, 1))
    grad_middle_low = tensor_gather(grad_middle.astype(LOW), 1).reshape(-1, full_width)

    def grads_by_block(left, right):
        return {
            r: dot_tn(left[:, p * width_block : (p + 1) * width_block], right)
            for p, r in enumerate(order)
        }

    proj_sum = scatter_blocks(grads_by_block(grad_flat, active))
    fc_sum = scatter_blocks(grads_by_block(normed_two, grad_hidden))

    ff_sum = tensor_scatter(quarters(dot_nt(active, proj_t)), 1)
    result_q = (middle + ff_sum + proj_bias).astype(LOW)
    result = from_order(tensor_gather(result_q, 1).reshape(batches, rows, full_width))

    grad_mixed = dot(grad_middle_low, out_t).astype(LOW).reshape(batches, rows, group_width)
    out_sum = scatter_blocks(grads_by_block(grad_middle_low, mixed_rows))
    grad_queries, grad_kv_all = attend_backward(
        queries, kv_all, meta_q, meta_k, live, mixed, lse, grad_mixed
    )
    grad_keyval = scatter_blocks({r: grad_kv_all[:, p].astype(F32) for p, r in enumerate(order)})
    grad_keyval = grad_keyval.astype(LOW).reshape(-1, 2 * hd)
    grad_queries = grad_queries.reshape(-1, group_width)
    grad_first = jnp.concatenate([grad_queries, grad_keyval], axis=1)
    first_sum = scatter_blocks(grads_by_block(normed, grad_first))
    grad_normed = quarters(dot_nt(grad_first, first_mat))
    in_sum = tensor_scatter(grad_normed, 1)
    residual_q = my_quarter(hidden_in).astype(F32)
    norm_part, gain_part = norm_back(residual_q, gain_one, in_sum)
    grad_in_q = (grad_middle + norm_part).astype(LOW)
    input_grad = from_order(tensor_gather(grad_in_q, 1).reshape(batches, rows, full_width))
    grad_gain_one = jnp.sum(gain_part, axis=(0, 1))
    grad_shift_one = jnp.sum(in_sum, axis=(0, 1))
    qbias_local = jnp.sum(grad_queries.astype(F32), axis=0)
    vbias_local = jnp.sum(grad_keyval[:, hd:].astype(F32), axis=0)

    qbias_full = lax.dynamic_update_slice_in_dim(
        jnp.zeros((full_width,), F32), qbias_local, tensor_index * group_width, 0
    )
    full_hidden = bias_shard * seq_size * tensor_size
    fcbias_full = lax.dynamic_update_slice_in_dim(
        jnp.zeros((full_hidden,), F32), fcbias_local, tensor_index * hidden_width, 0
    )
    grads_rel = jnp.stack(
        [
            grad_gain_one,
            grad_shift_one,
            to_order(qbias_full),
            grad_out_bias,
            grad_gain_two,
            grad_shift_two,
            grad_proj_bias,
        ]
    )
    chunk = full_hidden // seq_size
    small_rows = {}
    for p, r in enumerate(order):
        part = lax.dynamic_slice_in_dim(
            fcbias_full, jnp.bitwise_xor(seq_index, r) * chunk, chunk, 0
        )
        vec_part = grads_rel[:, p * width_block : (p + 1) * width_block].reshape(-1)
        row = jnp.concatenate([vec_part, part, vbias_local])
        small_rows[r] = jnp.pad(row, (0, -row.shape[0] % 1024)).reshape(-1, 128)
    for bit in range(bits_of(seq_size)):
        for r in sorted(small_rows):
            if r & (1 << bit):
                got = swap(small_rows.pop(r), "seq", bit)
                small_rows[r ^ (1 << bit)] = small_rows[r ^ (1 << bit)] + got
    small_sum = small_rows[0]
    for bit in range(bits_of(tensor_size)):
        small_sum = small_sum + swap(small_sum, "tensor", bit)
    small_sum = small_sum.reshape(-1)
    vec_cut = 7 * width_block
    vec_grad = lax.dynamic_slice_in_dim(
        small_sum[:vec_cut].reshape(7, width_block), tensor_index * shard, shard, 1
    )
    fcbias_grad = lax.dynamic_slice_in_dim(
        small_sum[vec_cut : vec_cut + chunk], tensor_index * bias_shard, bias_shard, 0
    )
    vbias_grad = small_sum[vec_cut + chunk : vec_cut + chunk + hd]

    query_grad = first_sum[:, :group_width]
    kv_part = first_sum[:, group_width:].reshape(tensor_size, -1, 2 * hd)
    keyval_grad = tensor_scatter(kv_part, 0)
    return (
        result,
        input_grad,
        query_grad,
        keyval_grad,
        out_sum.T,
        fc_sum,
        proj_sum.T,
        vec_grad,
        fcbias_grad,
        vbias_grad,
        vec_grad[5],
    )


def solution(mesh):
    in_specs = (
        P(None, "seq", None),
        P(None, "seq"),
        P(None, "seq"),
        P("seq", "tensor"),
        P(("seq", "tensor"), None),
        P("tensor", "seq"),
        P("seq", "tensor"),
        P("tensor", "seq"),
        P(None, ("seq", "tensor")),
        P(("seq", "tensor")),
        P(),
        P(None, "seq", None),
    )
    out_specs = (
        P(None, "seq", None),
        P(None, "seq", None),
        P("seq", "tensor"),
        P(("seq", "tensor"), None),
        P("tensor", "seq"),
        P("seq", "tensor"),
        P("tensor", "seq"),
        P(None, ("seq", "tensor")),
        P(("seq", "tensor")),
        P(),
        P(("seq", "tensor")),
    )
    return jax.shard_map(local, mesh=mesh, in_specs=in_specs, out_specs=out_specs, check_vma=False)
```

time: 2000 us -> 881 us (0.44)
  waiting for transfers between devices: 1220 us -> 437 us
  blocking collectives: 184 us -> 41.3 us
  starting transfers between devices: 1.58 us -> 130 us
  other arithmetic: 173 us -> 53.5 us
  matrix products: 183 us -> 90.2 us
  local copies, waits for them, and re-layouts: 147 us -> 82 us
  loops' own time: 57.4 us -> 0 us
  Pallas kernels: 0 us -> 32.8 us
    reduce_scatter x7 -> x0, waiting for transfers between devices: 594 us -> none  [the longest x1 148 us: local(): lax.psum_scatter(acc_proj.astype(jnp.bfloat16), 'seq', scatter_dimension=...]
    ppermute x0 -> x99, waiting for transfers between devices: none -> 437 us  [swap(): return lax.ppermute(value, axis, [(i, i ^ 1 << bit) for i in range(count)])]
    all_gather x7 -> x0, waiting for transfers between devices: 313 us -> none  [the longest x1 118 us: fetch_weights(): lax.all_gather(w_fc.astype(jnp.bfloat16), 'seq', axis=0, tiled=True)]
    psum x4 -> x0, waiting for transfers between devices: 176 us -> none  [the longest x2 65.2 us: local(): lax.psum(product(mixed_heads, out_mat).astype(jnp.bfloat16), 'tensor')]
    unnamed x20 -> x0, waiting for transfers between devices: 136 us -> none
    ppermute x0 -> x99, starting transfers between devices: none -> 130 us  [swap(): return lax.ppermute(value, axis, [(i, i ^ 1 << bit) for i in range(count)])]
    all_gather x4 -> x1, blocking collectives: 143 us -> 41.3 us  [local(): small = lax.all_gather(packed, ('seq', 'tensor'), axis=0, tiled=False)]
    dot_general x75 -> x40, matrix products: 183 us -> 90.2 us  [the longest x32 45.7 us: dot_tn(): lax.dot_general(left, right, (((0,), (0,)), ((), ())), preferred_element_...]
  transfers between devices with their start and end apart: 19 -> 99, of which waited for: 15 -> 44; matrix products, arithmetic and copies ran while one was open for 12% -> 23% of each run, Pallas kernels for 0% -> 4%
where the time goes in v1:
time: 881 us; the launch traced here: 875 us
  waiting for transfers between devices  437 us (50%)
  starting transfers between devices  130 us (15%)
  matrix products  90.2 us (10%)
  local copies, waits for them, and re-layouts  82 us (9%)
  other arithmetic  53.5 us (6%)
  blocking collectives  41.3 us (5%)
  Pallas kernels  32.8 us (4%)
    ppermute x99, waiting for transfers between devices, swap(): return lax.ppermute(value, axis, [(i, i ^ 1 << bit) for i in range(count)])  437 us
    ppermute x99, starting transfers between devices, swap(): return lax.ppermute(value, axis, [(i, i ^ 1 << bit) for i in range(count)])  130 us
    unnamed x250, local copies, waits for them, and re-layouts  59.2 us
    dot_general x32, matrix products, dot_tn(): lax.dot_general(left, right, (((0,), (0,)), ((), ())), preferred_element_...  45.7 us
    all_gather x1, blocking collectives, local(): small = lax.all_gather(packed, ('seq', 'tensor'), axis=0, tiled=False)  41.3 us
    dot_general x4, matrix products, dot(): return jnp.dot(left, right, preferred_element_type=F32)  27.9 us
    pallas_call x1, Pallas kernels, attend_forward(): pl.pallas_call(forward_kernel, grid_spec=pltpu.PrefetchScalarGridSpec(num...  18.2 us
  transfers between devices with their start and end apart: 99, of which 44 were waited for; matrix products, arithmetic and copies ran while one was open for 23% of the time, Pallas kernels for 4%

profile of v1, /device:TPU:0, one launch (start us, length us, event | category | flops | bytes accessed | tf_op | source)
XLA Modules:
  0.0 875.0 jit_solution(16532302054905274980)
XLA Ops:
  8.1 41.3 %all_gather.3 = bf16[32,24,128]{2,1,0:T(8,128)(2,1)S(1)} all-gather(bf16[1,24,128]{2,1,0:T(8,128)(2,1)S(1)} %pad_bitcast_fusion.4), channel_id=1, replica_groups=mesh['seq'=8,'tensor'=4] {'seq','tensor'}, dimensions={0}, use_global_device_ids=true | all-gather | bytes 202752 | tf_op jit(solution)/shard_map/all_gather | solution.py:349
  71.2 3.8 add_convert_fusion
  81.9 15.1 %collective-permute-done.2 = bf16[256,768]{1,0:T(8,128)(2,1)S(1)} collective-permute-done((bf16[256,768]{1,0:T(8,128)(2,1)}, bf16[256,768]{1,0:T(8,128)(2,1)S(1)}, u32[]{:S(2)}, u32[]{:S(2)}) %collective-permute-start.2) | collective-permute-done | bytes 393248 | tf_op jit(solution)/shard_map/ppermute | solution.py:22
  105.6 4.5 collective-permute-done.4
  113.7 4.0 collective-permute-done.6
  118.6 7.6 collective-permute-done.7
  127.0 6.6 collective-permute-done.8
  134.4 3.7 fusion.142
  145.9 7.2 collective-permute-done.9
  154.3 5.0 collective-permute-done.10
  159.4 5.6 collective-permute-done.17
  170.7 3.4 collective-permute-done.13
  180.1 10.9 %collective-permute-done.20 = bf16[256,512]{1,0:T(8,128)(2,1)S(1)} collective-permute-done((bf16[256,512]{1,0:T(8,128)(2,1)S(1)}, bf16[256,512]{1,0:T(8,128)(2,1)S(1)}, u32[]{:S(2)}, u32[]{:S(2)}) %collective-permute-start.20) | collective-permute-done | bytes 262176 | tf_op jit(solution)/shard_map/ppermute | solution.py:22
  196.3 18.2 %attend_forward.1 = (bf16[2,256,512]{2,1,0:T(8,128)(2,1)}, f32[2,4,256,1]{3,2,1,0:T(8,128)}) custom-call(s32[2,8]{1,0:T(2,128)} %and_convert_fusion.live_ref, bf16[2,256,512]{2,1,0:T(8,128)(2,1)} %bitcast.488, bf16[2,8,256,256]{3,2,1,0:T(8,128)(2,1)} %copy-done.51, s32[2,256,128]{2,1,0:T(8,128)} %pad.40.mq_ref, s32[2,8,8,256]{3,2,1,0:T(8,128)} %pad.41.mk_ref), custom_call_target="tpu_custom_call" | custom-call | flops 2147483648 | bytes 2097152 | tf_op jit(solution)/shard_map/attend_forward/pallas_call | solution.py:145
  237.5 11.0 %collective-permute-start.30 = (bf16[256,2048]{1,0:T(8,128)(2,1)}, bf16[256,2048]{1,0:T(8,128)(2,1)S(1)}, u32[]{:S(2)}, u32[]{:S(2)}) collective-permute-start(bf16[256,2048]{1,0:T(8,128)(2,1)} %convert_element_type.506), channel_id=1, source_target_pairs={{0,4},{4,0},{8,12},{12,8},{16,20},{20,16},{24,28},{28,24},{1,5},{5... | collective-permute-start | bytes 3145736 | tf_op jit(solution)/shard_map/ppermute | solution.py:22
  248.5 25.9 %collective-permute-done.27 = bf16[256,2048]{1,0:T(8,128)(2,1)} collective-permute-done((bf16[256,2048]{1,0:T(8,128)(2,1)}, bf16[256,2048]{1,0:T(8,128)(2,1)}, u32[]{:S(2)}, u32[]{:S(2)}) %collective-permute-start.27) | collective-permute-done | bytes 1048608 | tf_op jit(solution)/shard_map/ppermute | solution.py:22
  274.3 10.9 %collective-permute-start.31 = (bf16[256,2048]{1,0:T(8,128)(2,1)}, bf16[256,2048]{1,0:T(8,128)(2,1)S(1)}, u32[]{:S(2)}, u32[]{:S(2)}) collective-permute-start(bf16[256,2048]{1,0:T(8,128)(2,1)} %collective-permute-done.27), channel_id=1, source_target_pairs={{0,4},{4,0},{8,12},{12,8},{16,20},{20,16},{24,28},{28,24},{1,5},{5... | collective-permute-start | bytes 3145736 | tf_op jit(solution)/shard_map/ppermute | solution.py:22
  290.8 38.9 %collective-permute-done.32 = bf16[256,2048]{1,0:T(8,128)(2,1)S(1)} collective-permute-done((bf16[256,2048]{1,0:T(8,128)(2,1)}, bf16[256,2048]{1,0:T(8,128)(2,1)S(1)}, u32[]{:S(2)}, u32[]{:S(2)}) %collective-permute-start.32) | collective-permute-done | bytes 1048608 | tf_op jit(solution)/shard_map/ppermute | solution.py:22
  334.9 41.3 %collective-permute-done.34 = bf16[256,2048]{0,1:T(8,128)(2,1)S(1)} collective-permute-done((bf16[256,2048]{0,1:T(8,128)(2,1)S(1)}, bf16[256,2048]{0,1:T(8,128)(2,1)S(1)}, u32[]{:S(2)}, u32[]{:S(2)}) %collective-permute-start.34) | collective-permute-done | bytes 1048608 | tf_op jit(solution)/shard_map/ppermute | solution.py:22
  382.2 7.3 multiply_convert_fusion
  406.3 18.7 %collective-permute-done.39 = bf16[256,2048]{0,1:T(8,128)(2,1)S(1)} collective-permute-done((bf16[256,2048]{0,1:T(8,128)(2,1)S(1)}, bf16[256,2048]{0,1:T(8,128)(2,1)S(1)}, u32[]{:S(2)}, u32[]{:S(2)}) %collective-permute-start.39) | collective-permute-done | bytes 1048608 | tf_op jit(solution)/shard_map/ppermute | solution.py:22
  426.5 20.9 %collective-permute-done.87 = bf16[256,2048]{1,0:T(8,128)(2,1)S(1)} collective-permute-done((bf16[256,2048]{1,0:T(8,128)(2,1)S(1)}, bf16[256,2048]{1,0:T(8,128)(2,1)S(1)}, u32[]{:S(2)}, u32[]{:S(2)}) %collective-permute-start.87) | collective-permute-done | bytes 1048608 | tf_op jit(solution)/shard_map/ppermute | solution.py:22
  452.1 40.3 %collective-permute-done.84 = bf16[256,2048]{1,0:T(8,128)(2,1)S(1)} collective-permute-done((bf16[256,2048]{1,0:T(8,128)(2,1)S(1)}, bf16[256,2048]{1,0:T(8,128)(2,1)S(1)}, u32[]{:S(2)}, u32[]{:S(2)}) %collective-permute-start.84) | collective-permute-done | bytes 1048608 | tf_op jit(solution)/shard_map/ppermute | solution.py:22
  496.2 18.7 %collective-permute-done.40 = bf16[256,2048]{0,1:T(8,128)(2,1)S(1)} collective-permute-done((bf16[256,2048]{0,1:T(8,128)(2,1)S(1)}, bf16[256,2048]{0,1:T(8,128)(2,1)S(1)}, u32[]{:S(2)}, u32[]{:S(2)}) %collective-permute-start.40) | collective-permute-done | bytes 1048608 | tf_op jit(solution)/shard_map/ppermute | solution.py:22
  515.0 4.6 fusion.143
  519.6 12.5 %convert_reduce_fusion.1 = (f32[2048]{0:T(1024)}, bf16[512,2048]{1,0:T(8,128)(2,1)S(1)}) fusion(bf16[512,2048]{1,0:T(8,128)(2,1)} %bitcast.83, bf16[2048,2048]{0,1:T(8,128)(2,1)} %copy-done.38, f32[512,2048]{1,0:T(8,128)} %get-tuple-element.184, f32[2048]{0:T(1024)} %copy-done.66), kind=kOutput, calls=%fused_computation.17 | convolution fusion | flops 4316985344 | bytes 16793600 | tf_op jit(solution)/shard_map/dot_general | solution.py:30
  532.1 7.2 fusion.144
  559.3 17.4 %collective-permute-done.80 = bf16[256,2048]{1,0:T(8,128)(2,1)S(1)} collective-permute-done((bf16[256,2048]{1,0:T(8,128)(2,1)S(1)}, bf16[256,2048]{1,0:T(8,128)(2,1)S(1)}, u32[]{:S(2)}, u32[]{:S(2)}) %collective-permute-start.80) | collective-permute-done | bytes 1048608 | tf_op jit(solution)/shard_map/ppermute | solution.py:22
  579.9 19.3 %collective-permute-done.77 = bf16[256,2048]{1,0:T(8,128)(2,1)S(1)} collective-permute-done((bf16[256,2048]{1,0:T(8,128)(2,1)S(1)}, bf16[256,2048]{1,0:T(8,128)(2,1)S(1)}, u32[]{:S(2)}, u32[]{:S(2)}) %collective-permute-start.77) | collective-permute-done | bytes 1048608 | tf_op jit(solution)/shard_map/ppermute | solution.py:22
  611.3 6.2 collective-permute-done.46
  621.5 4.3 collective-permute-done.42
  635.4 14.6 %collective-permute-done.47 = bf16[2,1,64,2048]{3,2,0,1:T(8,128)(2,1)S(1)} collective-permute-done((bf16[2,1,64,2048]{3,2,0,1:T(8,128)(2,1)S(1)}, bf16[2,1,64,2048]{3,2,0,1:T(8,128)(2,1)S(1)}, u32[]{:S(2)}, u32[]{:S(2)}) %collective-permute-start.47) | collective-permute-done | bytes 524320 | tf_op jit(solution)/shard_map/ppermute | solution.py:22
  652.8 14.6 %collective-permute-done.78 = bf16[256,2048]{1,0:T(8,128)(2,1)S(1)} collective-permute-done((bf16[256,2048]{1,0:T(8,128)(2,1)}, bf16[256,2048]{1,0:T(8,128)(2,1)S(1)}, u32[]{:S(2)}, u32[]{:S(2)}) %collective-permute-start.78) | collective-permute-done | bytes 1048608 | tf_op jit(solution)/shard_map/ppermute | solution.py:22
  667.4 11.3 %collective-permute-done.82 = bf16[256,2048]{1,0:T(8,128)(2,1)S(1)} collective-permute-done((bf16[256,2048]{1,0:T(8,128)(2,1)S(1)}, bf16[256,2048]{1,0:T(8,128)(2,1)S(1)}, u32[]{:S(2)}, u32[]{:S(2)}) %collective-permute-start.82) | collective-permute-done | bytes 1048608 | tf_op jit(solution)/shard_map/ppermute | solution.py:22
  682.4 4.4 convolution_convert_fusion.8
  686.9 14.7 %attend_backward.1 = (bf16[2,256,512]{2,1,0:T(8,128)(2,1)}, bf16[2,8,256,256]{3,2,1,0:T(8,128)(2,1)}) custom-call(s32[2,8]{1,0:T(2,128)} %and_convert_fusion.live_ref, bf16[2,256,512]{2,1,0:T(8,128)(2,1)} %bitcast.489, bf16[2,8,256,256]{3,2,1,0:T(8,128)(2,1)} %copy-done.51, s32[2,256,128]{2,1,0:T(8,128)} %pad.40.mq_ref, s32[2,8,8,256]{3,2,1,0:T(8,128)} %pad.41.mk_ref, ...), custom_call_target="tpu_custom_call" | custom-call | flops 5368709120 | bytes 4194304 | tf_op jit(solution)/shard_map/attend_backward/pallas_call | solution.py:232
  714.8 7.9 collective-permute-start.50
  739.1 8.1 collective-permute-done.73
  748.5 5.9 collective-permute-done.70
  765.3 3.7 collective-permute-done.55
  778.2 7.3 collective-permute-done.64
  785.9 3.4 collective-permute-start.65
  789.7 12.2 %collective-permute-done.61 = bf16[256,768]{1,0:T(8,128)(2,1)S(1)} collective-permute-done((bf16[256,768]{1,0:T(8,128)(2,1)S(1)}, bf16[256,768]{1,0:T(8,128)(2,1)S(1)}, u32[]{:S(2)}, u32[]{:S(2)}) %collective-permute-start.61) | collective-permute-done | bytes 393248 | tf_op jit(solution)/shard_map/ppermute | solution.py:22
  804.0 3.6 collective-permute-start.62
  813.5 10.0 %collective-permute-done.62 = bf16[256,768]{1,0:T(8,128)(2,1)S(1)} collective-permute-done((bf16[256,768]{1,0:T(8,128)(2,1)S(1)}, bf16[256,768]{1,0:T(8,128)(2,1)S(1)}, u32[]{:S(2)}, u32[]{:S(2)}) %collective-permute-start.62) | collective-permute-done | bytes 393248 | tf_op jit(solution)/shard_map/ppermute | solution.py:22
  823.5 3.8 collective-permute-done.66
  833.0 4.5 collective-permute-start.58
  854.9 4.2 collective-permute-done.71
  (615 shorter events, 290.4 us)
Async XLA Ops:
  2.1 75.6 %collective-permute-start = (bf16[1,64,256]{2,1,0:T(8,128)(2,1)}, bf16[1,64,256]{2,1,0:T(8,128)(2,1)}, u32[]{:S(2)}, u32[]{:S(2)}) collective-permute-start(bf16[1,64,256]{2,1,0:T(8,128)(2,1)} %convert_bitcast_fusion.4), channel_id=1, source_target_pairs={{0,2},{1,3},{2,0},{3,1},{4,6},{5,7},{6,4},{7,5},{8,10},{9,11},{10,... | collective-permute-start | bytes 98312 | tf_op jit(solution)/shard_map/ppermute | solution.py:22
  102.6 23.5 %collective-permute-start.7 = (bf16[256,768]{1,0:T(8,128)(2,1)}, bf16[256,768]{1,0:T(8,128)(2,1)S(1)}, u32[]{:S(2)}, u32[]{:S(2)}) collective-permute-start(bf16[256,768]{1,0:T(8,128)(2,1)} %collective-permute-done.3), channel_id=1, source_target_pairs={{0,4},{4,0},{8,12},{12,8},{16,20},{20,16},{24,28},{28,24},{1,5},{5... | collective-permute-start | bytes 1179656 | tf_op jit(solution)/shard_map/ppermute | solution.py:22
  110.1 23.5 %collective-permute-start.8 = (bf16[256,768]{1,0:T(8,128)(2,1)}, bf16[256,768]{1,0:T(8,128)(2,1)S(1)}, u32[]{:S(2)}, u32[]{:S(2)}) collective-permute-start(bf16[256,768]{1,0:T(8,128)(2,1)} %collective-permute-done.4), channel_id=1, source_target_pairs={{0,4},{4,0},{8,12},{12,8},{16,20},{20,16},{24,28},{28,24},{1,5},{5... | collective-permute-start | bytes 1179656 | tf_op jit(solution)/shard_map/ppermute | solution.py:22
  140.2 30.0 %collective-permute-start.12 = (bf16[2,256,256]{2,1,0:T(8,128)(2,1)S(1)}, bf16[2,256,256]{2,1,0:T(8,128)(2,1)S(1)}, u32[]{:S(2)}, u32[]{:S(2)}) collective-permute-start(bf16[2,256,256]{2,1,0:T(8,128)(2,1)S(1)} %bitcast.464), channel_id=1, source_target_pairs={{0,4},{4,0},{8,12},{12,8},{16,20},{20,16},{24,28},{28,24},{1,5},{5... | collective-permute-start | bytes 786440 | tf_op jit(solution)/shard_map/ppermute | solution.py:22
  153.2 24.9 %collective-permute-start.19 = (bf16[256,512]{1,0:T(8,128)(2,1)S(1)}, bf16[256,512]{1,0:T(8,128)(2,1)S(1)}, u32[]{:S(2)}, u32[]{:S(2)}) collective-permute-start(bf16[256,512]{1,0:T(8,128)(2,1)S(1)} %bitcast.460), channel_id=1, source_target_pairs={{0,4},{4,0},{8,12},{12,8},{16,20},{20,16},{24,28},{28,24},{1,5},{5... | collective-permute-start | bytes 786440 | tf_op jit(solution)/shard_map/ppermute | solution.py:22
  166.7 25.0 %collective-permute-start.21 = (bf16[256,512]{1,0:T(8,128)(2,1)S(1)}, bf16[256,512]{1,0:T(8,128)(2,1)S(1)}, u32[]{:S(2)}, u32[]{:S(2)}) collective-permute-start(bf16[256,512]{1,0:T(8,128)(2,1)S(1)} %collective-permute-done.17), channel_id=1, source_target_pairs={{0,4},{4,0},{8,12},{12,8},{16,20},{20,16},{24,28},{28,24},{1,5},{5... | collective-permute-start | bytes 786440 | tf_op jit(solution)/shard_map/ppermute | solution.py:22
  168.8 23.7 %collective-permute-start.14 = (bf16[2,256,256]{2,1,0:T(8,128)(2,1)S(1)}, bf16[2,256,256]{2,1,0:T(8,128)(2,1)S(1)}, u32[]{:S(2)}, u32[]{:S(2)}) collective-permute-start(bf16[2,256,256]{2,1,0:T(8,128)(2,1)S(1)} %collective-permute-done.10), channel_id=1, source_target_pairs={{0,4},{4,0},{8,12},{12,8},{16,20},{20,16},{24,28},{28,24},{1,5},{5... | collective-permute-start | bytes 786440 | tf_op jit(solution)/shard_map/ppermute | solution.py:22
  178.0 36.5 %collective-permute-start.22 = (bf16[256,512]{1,0:T(8,128)(2,1)S(1)}, bf16[256,512]{1,0:T(8,128)(2,1)S(1)}, u32[]{:S(2)}, u32[]{:S(2)}) collective-permute-start(bf16[256,512]{1,0:T(8,128)(2,1)S(1)} %collective-permute-done.18), channel_id=1, source_target_pairs={{0,4},{4,0},{8,12},{12,8},{16,20},{20,16},{24,28},{28,24},{1,5},{5... | collective-permute-start | bytes 786440 | tf_op jit(solution)/shard_map/ppermute | solution.py:22
  226.2 59.1 %collective-permute-start.28 = (bf16[256,2048]{1,0:T(8,128)(2,1)}, bf16[256,2048]{1,0:T(8,128)(2,1)}, u32[]{:S(2)}, u32[]{:S(2)}) collective-permute-start(bf16[256,2048]{1,0:T(8,128)(2,1)} %convert_element_type.506), channel_id=1, source_target_pairs={{0,8},{4,12},{8,0},{12,4},{16,24},{20,28},{24,16},{28,20},{1,9},{5... | collective-permute-start | bytes 3145736 | tf_op jit(solution)/shard_map/ppermute | solution.py:22
  226.3 48.1 %collective-permute-start.27 = (bf16[256,2048]{1,0:T(8,128)(2,1)}, bf16[256,2048]{1,0:T(8,128)(2,1)}, u32[]{:S(2)}, u32[]{:S(2)}) collective-permute-start(bf16[256,2048]{1,0:T(8,128)(2,1)} %convert_element_type.506), channel_id=1, source_target_pairs={{0,16},{4,20},{8,24},{12,28},{16,0},{20,4},{24,8},{28,12},{1,17},{... | collective-permute-start | bytes 3145736 | tf_op jit(solution)/shard_map/ppermute | solution.py:22
  236.1 51.9 %collective-permute-start.24 = (bf16[2,1,64,2048]{3,2,1,0:T(8,128)(2,1)S(1)}, bf16[2,1,64,2048]{3,2,1,0:T(8,128)(2,1)S(1)}, u32[]{:S(2)}, u32[]{:S(2)}) collective-permute-start(bf16[2,1,64,2048]{3,2,1,0:T(8,128)(2,1)S(1)} %dynamic-slice_convert_fusion.4), channel_id=1, source_target_pairs={{0,2},{1,3},{2,0},{3,1},{4,6},{5,7},{6,4},{7,5},{8,10},{9,11},{10,... | collective-permute-start | bytes 1572872 | tf_op jit(solution)/shard_map/ppermute | solution.py:22
  237.5 94.8 %collective-permute-start.30 = (bf16[256,2048]{1,0:T(8,128)(2,1)}, bf16[256,2048]{1,0:T(8,128)(2,1)S(1)}, u32[]{:S(2)}, u32[]{:S(2)}) collective-permute-start(bf16[256,2048]{1,0:T(8,128)(2,1)} %convert_element_type.506), channel_id=1, source_target_pairs={{0,4},{4,0},{8,12},{12,8},{16,20},{20,16},{24,28},{28,24},{1,5},{5... | collective-permute-start | bytes 3145736 | tf_op jit(solution)/shard_map/ppermute | solution.py:22
  274.3 56.1 %collective-permute-start.29 = (bf16[256,2048]{1,0:T(8,128)(2,1)}, bf16[256,2048]{1,0:T(8,128)(2,1)S(1)}, u32[]{:S(2)}, u32[]{:S(2)}) collective-permute-start(bf16[256,2048]{1,0:T(8,128)(2,1)} %collective-permute-done.27), channel_id=1, source_target_pairs={{0,8},{4,12},{8,0},{12,4},{16,24},{20,28},{24,16},{28,20},{1,9},{5... | collective-permute-start | bytes 3145736 | tf_op jit(solution)/shard_map/ppermute | solution.py:22
  274.3 60.3 %collective-permute-start.31 = (bf16[256,2048]{1,0:T(8,128)(2,1)}, bf16[256,2048]{1,0:T(8,128)(2,1)S(1)}, u32[]{:S(2)}, u32[]{:S(2)}) collective-permute-start(bf16[256,2048]{1,0:T(8,128)(2,1)} %collective-permute-done.27), channel_id=1, source_target_pairs={{0,4},{4,0},{8,12},{12,8},{16,20},{20,16},{24,28},{28,24},{1,5},{5... | collective-permute-start | bytes 3145736 | tf_op jit(solution)/shard_map/ppermute | solution.py:22
  285.3 44.5 %collective-permute-start.32 = (bf16[256,2048]{1,0:T(8,128)(2,1)}, bf16[256,2048]{1,0:T(8,128)(2,1)S(1)}, u32[]{:S(2)}, u32[]{:S(2)}) collective-permute-start(bf16[256,2048]{1,0:T(8,128)(2,1)} %collective-permute-done.28), channel_id=1, source_target_pairs={{0,4},{4,0},{8,12},{12,8},{16,20},{20,16},{24,28},{28,24},{1,5},{5... | collective-permute-start | bytes 3145736 | tf_op jit(solution)/shard_map/ppermute | solution.py:22
  290.2 43.9 %collective-permute-start.25 = (bf16[2,1,64,2048]{3,2,0,1:T(8,128)(2,1)S(1)}, bf16[2,1,64,2048]{3,2,0,1:T(8,128)(2,1)S(1)}, u32[]{:S(2)}, u32[]{:S(2)}) collective-permute-start(bf16[2,1,64,2048]{3,2,0,1:T(8,128)(2,1)S(1)} %get-tuple-element.85), channel_id=1, source_target_pairs={{0,2},{1,3},{2,0},{3,1},{4,6},{5,7},{6,4},{7,5},{8,10},{9,11},{10,... | collective-permute-start | bytes 1572872 | tf_op jit(solution)/shard_map/ppermute | solution.py:22
  329.9 46.3 %collective-permute-start.34 = (bf16[256,2048]{0,1:T(8,128)(2,1)S(1)}, bf16[256,2048]{0,1:T(8,128)(2,1)S(1)}, u32[]{:S(2)}, u32[]{:S(2)}) collective-permute-start(bf16[256,2048]{0,1:T(8,128)(2,1)S(1)} %convert_bitcast_fusion.2), channel_id=1, source_target_pairs={{0,16},{4,20},{8,24},{12,28},{16,0},{20,4},{24,8},{28,12},{1,17},{... | collective-permute-start | bytes 3145736 | tf_op jit(solution)/shard_map/ppermute | solution.py:22
  330.4 46.0 %collective-permute-start.35 = (bf16[256,2048]{0,1:T(8,128)(2,1)S(1)}, bf16[256,2048]{0,1:T(8,128)(2,1)S(1)}, u32[]{:S(2)}, u32[]{:S(2)}) collective-permute-start(bf16[256,2048]{0,1:T(8,128)(2,1)S(1)} %convert_bitcast_fusion.2), channel_id=1, source_target_pairs={{0,8},{4,12},{8,0},{12,4},{16,24},{20,28},{24,16},{28,20},{1,9},{5... | collective-permute-start | bytes 3145736 | tf_op jit(solution)/shard_map/ppermute | solution.py:22
  332.2 71.6 %collective-permute-start.37 = (bf16[256,2048]{0,1:T(8,128)(2,1)S(1)}, bf16[256,2048]{0,1:T(8,128)(2,1)S(1)}, u32[]{:S(2)}, u32[]{:S(2)}) collective-permute-start(bf16[256,2048]{0,1:T(8,128)(2,1)S(1)} %convert_bitcast_fusion.2), channel_id=1, source_target_pairs={{0,4},{4,0},{8,12},{12,8},{16,20},{20,16},{24,28},{28,24},{1,5},{5... | collective-permute-start | bytes 3145736 | tf_op jit(solution)/shard_map/ppermute | solution.py:22
  334.1 44.0 %collective-permute-start.33 = (bf16[256,2048]{1,0:T(8,128)(2,1)S(1)}, bf16[256,2048]{1,0:T(8,128)(2,1)S(1)}, u32[]{:S(2)}, u32[]{:S(2)}) collective-permute-start(bf16[256,2048]{1,0:T(8,128)(2,1)S(1)} %collective-permute-done.29), channel_id=1, source_target_pairs={{0,4},{4,0},{8,12},{12,8},{16,20},{20,16},{24,28},{28,24},{1,5},{5... | collective-permute-start | bytes 3145736 | tf_op jit(solution)/shard_map/ppermute | solution.py:22
  334.7 44.2 %collective-permute-start.26 = (bf16[2,2,64,2048]{3,2,0,1:T(8,128)(2,1)S(1)}, bf16[2,2,64,2048]{3,2,0,1:T(8,128)(2,1)S(1)}, u32[]{:S(2)}, u32[]{:S(2)}) collective-permute-start(bf16[2,2,64,2048]{3,2,0,1:T(8,128)(2,1)S(1)} %maximum_bitcast_fusion.4), channel_id=1, source_target_pairs={{0,1},{1,0},{2,3},{3,2},{4,5},{5,4},{6,7},{7,6},{8,9},{9,8},{10,11... | collective-permute-start | bytes 3145736 | tf_op jit(solution)/shard_map/ppermute | solution.py:22
  376.2 26.8 %collective-permute-start.36 = (bf16[256,2048]{0,1:T(8,128)(2,1)S(1)}, bf16[256,2048]{0,1:T(8,128)(2,1)S(1)}, u32[]{:S(2)}, u32[]{:S(2)}) collective-permute-start(bf16[256,2048]{0,1:T(8,128)(2,1)S(1)} %collective-permute-done.34), channel_id=1, source_target_pairs={{0,8},{4,12},{8,0},{12,4},{16,24},{20,28},{24,16},{28,20},{1,9},{5... | collective-permute-start | bytes 3145736 | tf_op jit(solution)/shard_map/ppermute | solution.py:22
  376.4 29.1 %collective-permute-start.38 = (bf16[256,2048]{0,1:T(8,128)(2,1)S(1)}, bf16[256,2048]{0,1:T(8,128)(2,1)S(1)}, u32[]{:S(2)}, u32[]{:S(2)}) collective-permute-start(bf16[256,2048]{0,1:T(8,128)(2,1)S(1)} %collective-permute-done.34), channel_id=1, source_target_pairs={{0,4},{4,0},{8,12},{12,8},{16,20},{20,16},{24,28},{28,24},{1,5},{5... | collective-permute-start | bytes 3145736 | tf_op jit(solution)/shard_map/ppermute | solution.py:22
  378.1 46.9 %collective-permute-start.39 = (bf16[256,2048]{0,1:T(8,128)(2,1)S(1)}, bf16[256,2048]{0,1:T(8,128)(2,1)S(1)}, u32[]{:S(2)}, u32[]{:S(2)}) collective-permute-start(bf16[256,2048]{0,1:T(8,128)(2,1)S(1)} %collective-permute-done.35), channel_id=1, source_target_pairs={{0,4},{4,0},{8,12},{12,8},{16,20},{20,16},{24,28},{28,24},{1,5},{5... | collective-permute-start | bytes 3145736 | tf_op jit(solution)/shard_map/ppermute | solution.py:22
  394.6 52.9 %collective-permute-start.87 = (bf16[256,2048]{1,0:T(8,128)(2,1)S(1)}, bf16[256,2048]{1,0:T(8,128)(2,1)S(1)}, u32[]{:S(2)}, u32[]{:S(2)}) collective-permute-start(bf16[256,2048]{1,0:T(8,128)(2,1)S(1)} %convolution_convert_fusion), channel_id=1, source_target_pairs={{0,4},{4,0},{8,12},{12,8},{16,20},{20,16},{24,28},{28,24},{1,5},{5... | collective-permute-start | bytes 3145736 | tf_op jit(solution)/shard_map/ppermute | solution.py:22
  403.1 147.1 %collective-permute-start.86 = (bf16[256,2048]{1,0:T(8,128)(2,1)}, bf16[256,2048]{1,0:T(8,128)(2,1)}, u32[]{:S(2)}, u32[]{:S(2)}) collective-permute-start(bf16[256,2048]{1,0:T(8,128)(2,1)} %convolution_convert_fusion.1), channel_id=1, source_target_pairs={{0,4},{4,0},{8,12},{12,8},{16,20},{20,16},{24,28},{28,24},{1,5},{5... | collective-permute-start | bytes 3145736 | tf_op jit(solution)/shard_map/ppermute | solution.py:22
  403.8 88.6 %collective-permute-start.84 = (bf16[256,2048]{1,0:T(8,128)(2,1)S(1)}, bf16[256,2048]{1,0:T(8,128)(2,1)S(1)}, u32[]{:S(2)}, u32[]{:S(2)}) collective-permute-start(bf16[256,2048]{1,0:T(8,128)(2,1)S(1)} %convolution_convert_fusion.2), channel_id=1, source_target_pairs={{0,4},{4,0},{8,12},{12,8},{16,20},{20,16},{24,28},{28,24},{1,5},{5... | collective-permute-start | bytes 3145736 | tf_op jit(solution)/shard_map/ppermute | solution.py:22
  405.5 109.4 %collective-permute-start.40 = (bf16[256,2048]{0,1:T(8,128)(2,1)S(1)}, bf16[256,2048]{0,1:T(8,128)(2,1)S(1)}, u32[]{:S(2)}, u32[]{:S(2)}) collective-permute-start(bf16[256,2048]{0,1:T(8,128)(2,1)S(1)} %collective-permute-done.36), channel_id=1, source_target_pairs={{0,4},{4,0},{8,12},{12,8},{16,20},{20,16},{24,28},{28,24},{1,5},{5... | collective-permute-start | bytes 3145736 | tf_op jit(solution)/shard_map/ppermute | solution.py:22
  425.0 177.4 %collective-permute-start.83 = (bf16[256,2048]{1,0:T(8,128)(2,1)}, bf16[256,2048]{1,0:T(8,128)(2,1)S(1)}, u32[]{:S(2)}, u32[]{:S(2)}) collective-permute-start(bf16[256,2048]{1,0:T(8,128)(2,1)} %convolution_convert_fusion.3), channel_id=1, source_target_pairs={{0,4},{4,0},{8,12},{12,8},{16,20},{20,16},{24,28},{28,24},{1,5},{5... | collective-permute-start | bytes 3145736 | tf_op jit(solution)/shard_map/ppermute | solution.py:22
  450.1 100.6 %collective-permute-start.88 = (bf16[256,2048]{1,0:T(8,128)(2,1)}, bf16[256,2048]{1,0:T(8,128)(2,1)}, u32[]{:S(2)}, u32[]{:S(2)}) collective-permute-start(bf16[256,2048]{1,0:T(8,128)(2,1)} %add_convert_fusion.2), channel_id=1, source_target_pairs={{0,8},{4,12},{8,0},{12,4},{16,24},{20,28},{24,16},{28,20},{1,9},{5... | collective-permute-start | bytes 3145736 | tf_op jit(solution)/shard_map/ppermute | solution.py:22
  494.1 108.3 %collective-permute-start.85 = (bf16[256,2048]{1,0:T(8,128)(2,1)S(1)}, bf16[256,2048]{1,0:T(8,128)(2,1)S(1)}, u32[]{:S(2)}, u32[]{:S(2)}) collective-permute-start(bf16[256,2048]{1,0:T(8,128)(2,1)S(1)} %add_convert_fusion.3), channel_id=1, source_target_pairs={{0,8},{4,12},{8,0},{12,4},{16,24},{20,28},{24,16},{28,20},{1,9},{5... | collective-permute-start | bytes 3145736 | tf_op jit(solution)/shard_map/ppermute | solution.py:22
  550.7 26.0 %collective-permute-start.80 = (bf16[256,2048]{1,0:T(8,128)(2,1)S(1)}, bf16[256,2048]{1,0:T(8,128)(2,1)S(1)}, u32[]{:S(2)}, u32[]{:S(2)}) collective-permute-start(bf16[256,2048]{1,0:T(8,128)(2,1)S(1)} %convolution_convert_fusion.4), channel_id=1, source_target_pairs={{0,4},{4,0},{8,12},{12,8},{16,20},{20,16},{24,28},{28,24},{1,5},{5... | collective-permute-start | bytes 3145736 | tf_op jit(solution)/shard_map/ppermute | solution.py:22
  554.2 45.0 %collective-permute-start.77 = (bf16[256,2048]{1,0:T(8,128)(2,1)S(1)}, bf16[256,2048]{1,0:T(8,128)(2,1)S(1)}, u32[]{:S(2)}, u32[]{:S(2)}) collective-permute-start(bf16[256,2048]{1,0:T(8,128)(2,1)S(1)} %convolution_convert_fusion.6), channel_id=1, source_target_pairs={{0,4},{4,0},{8,12},{12,8},{16,20},{20,16},{24,28},{28,24},{1,5},{5... | collective-permute-start | bytes 3145736 | tf_op jit(solution)/shard_map/ppermute | solution.py:22
  555.2 49.2 %collective-permute-start.89 = (bf16[256,2048]{1,0:T(8,128)(2,1)S(1)}, bf16[256,2048]{1,0:T(8,128)(2,1)S(1)}, u32[]{:S(2)}, u32[]{:S(2)}) collective-permute-start(bf16[256,2048]{1,0:T(8,128)(2,1)S(1)} %add_convert_fusion.1), channel_id=1, source_target_pairs={{0,16},{4,20},{8,24},{12,28},{16,0},{20,4},{24,8},{28,12},{1,17},{... | collective-permute-start | bytes 3145736 | tf_op jit(solution)/shard_map/ppermute | solution.py:22
  576.7 53.1 %collective-permute-start.79 = (bf16[256,2048]{1,0:T(8,128)(2,1)}, bf16[256,2048]{1,0:T(8,128)(2,1)}, u32[]{:S(2)}, u32[]{:S(2)}) collective-permute-start(bf16[256,2048]{1,0:T(8,128)(2,1)} %convolution_convert_fusion.5), channel_id=1, source_target_pairs={{0,4},{4,0},{8,12},{12,8},{16,20},{20,16},{24,28},{28,24},{1,5},{5... | collective-permute-start | bytes 3145736 | tf_op jit(solution)/shard_map/ppermute | solution.py:22
  599.2 53.6 %collective-permute-start.76 = (bf16[256,2048]{1,0:T(8,128)(2,1)}, bf16[256,2048]{1,0:T(8,128)(2,1)}, u32[]{:S(2)}, u32[]{:S(2)}) collective-permute-start(bf16[256,2048]{1,0:T(8,128)(2,1)} %convolution_convert_fusion.7), channel_id=1, source_target_pairs={{0,4},{4,0},{8,12},{12,8},{16,20},{20,16},{24,28},{28,24},{1,5},{5... | collective-permute-start | bytes 3145736 | tf_op jit(solution)/shard_map/ppermute | solution.py:22
  604.4 27.0 %collective-permute-start.81 = (bf16[256,2048]{1,0:T(8,128)(2,1)}, bf16[256,2048]{1,0:T(8,128)(2,1)}, u32[]{:S(2)}, u32[]{:S(2)}) collective-permute-start(bf16[256,2048]{1,0:T(8,128)(2,1)} %add_convert_fusion.5), channel_id=1, source_target_pairs={{0,8},{4,12},{8,0},{12,4},{16,24},{20,28},{24,16},{28,20},{1,9},{5... | collective-permute-start | bytes 3145736 | tf_op jit(solution)/shard_map/ppermute | solution.py:22
  617.5 49.9 %collective-permute-start.78 = (bf16[256,2048]{1,0:T(8,128)(2,1)}, bf16[256,2048]{1,0:T(8,128)(2,1)S(1)}, u32[]{:S(2)}, u32[]{:S(2)}) collective-permute-start(bf16[256,2048]{1,0:T(8,128)(2,1)} %add_convert_fusion.6), channel_id=1, source_target_pairs={{0,8},{4,12},{8,0},{12,4},{16,24},{20,28},{24,16},{28,20},{1,9},{5... | collective-permute-start | bytes 3145736 | tf_op jit(solution)/shard_map/ppermute | solution.py:22
  633.5 45.2 %collective-permute-start.82 = (bf16[256,2048]{1,0:T(8,128)(2,1)S(1)}, bf16[256,2048]{1,0:T(8,128)(2,1)S(1)}, u32[]{:S(2)}, u32[]{:S(2)}) collective-permute-start(bf16[256,2048]{1,0:T(8,128)(2,1)S(1)} %add_convert_fusion.4), channel_id=1, source_target_pairs={{0,16},{4,20},{8,24},{12,28},{16,0},{20,4},{24,8},{28,12},{1,17},{... | collective-permute-start | bytes 3145736 | tf_op jit(solution)/shard_map/ppermute | solution.py:22
  650.2 31.6 %collective-permute-start.48 = (bf16[2,2,64,2048]{3,2,0,1:T(8,128)(2,1)S(1)}, bf16[2,2,64,2048]{3,2,0,1:T(8,128)(2,1)S(1)}, u32[]{:S(2)}, u32[]{:S(2)}) collective-permute-start(bf16[2,2,64,2048]{3,2,0,1:T(8,128)(2,1)S(1)} %maximum_bitcast_fusion.6), channel_id=1, source_target_pairs={{0,1},{1,0},{2,3},{3,2},{4,5},{5,4},{6,7},{7,6},{8,9},{9,8},{10,11... | collective-permute-start | bytes 3145736 | tf_op jit(solution)/shard_map/ppermute | solution.py:22
  652.3 59.4 %collective-permute-start.44 = (bf16[2,2,64,2048]{3,2,0,1:T(8,128)(2,1)}, bf16[2,2,64,2048]{3,2,0,1:T(8,128)(2,1)}, u32[]{:S(2)}, u32[]{:S(2)}) collective-permute-start(bf16[2,2,64,2048]{3,2,0,1:T(8,128)(2,1)} %maximum_bitcast_fusion.5), channel_id=1, source_target_pairs={{0,1},{1,0},{2,3},{3,2},{4,5},{5,4},{6,7},{7,6},{8,9},{9,8},{10,11... | collective-permute-start | bytes 3145736 | tf_op jit(solution)/shard_map/ppermute | solution.py:22
  722.7 32.7 %collective-permute-start.52 = (bf16[2,256,256]{2,1,0:T(8,128)(2,1)}, bf16[2,256,256]{2,1,0:T(8,128)(2,1)}, u32[]{:S(2)}, u32[]{:S(2)}) collective-permute-start(bf16[2,256,256]{2,1,0:T(8,128)(2,1)} %get-tuple-element.111), channel_id=1, source_target_pairs={{0,4},{4,0},{8,12},{12,8},{16,20},{20,16},{24,28},{28,24},{1,5},{5... | collective-permute-start | bytes 786440 | tf_op jit(solution)/shard_map/ppermute | solution.py:22
  724.7 39.0 %collective-permute-start.49 = (bf16[2,256,256]{2,1,0:T(8,128)(2,1)}, bf16[2,256,256]{2,1,0:T(8,128)(2,1)S(1)}, u32[]{:S(2)}, u32[]{:S(2)}) collective-permute-start(bf16[2,256,256]{2,1,0:T(8,128)(2,1)} %get-tuple-element.110), channel_id=1, source_target_pairs={{0,4},{4,0},{8,12},{12,8},{16,20},{20,16},{24,28},{28,24},{1,5},{5... | collective-permute-start | bytes 786440 | tf_op jit(solution)/shard_map/ppermute | solution.py:22
  734.9 25.6 %collective-permute-start.72 = (bf16[256,512]{1,0:T(8,128)(2,1)S(1)}, bf16[256,512]{1,0:T(8,128)(2,1)S(1)}, u32[]{:S(2)}, u32[]{:S(2)}) collective-permute-start(bf16[256,512]{1,0:T(8,128)(2,1)S(1)} %copy-done.76), channel_id=1, source_target_pairs={{0,4},{4,0},{8,12},{12,8},{16,20},{20,16},{24,28},{28,24},{1,5},{5... | collective-permute-start | bytes 786440 | tf_op jit(solution)/shard_map/ppermute | solution.py:22
  755.4 99.0 %collective-permute-start.69 = (bf16[256,512]{1,0:T(8,128)(2,1)}, bf16[256,512]{1,0:T(8,128)(2,1)}, u32[]{:S(2)}, u32[]{:S(2)}) collective-permute-start(bf16[256,512]{1,0:T(8,128)(2,1)} %convolution_convert_fusion.16), channel_id=1, source_target_pairs={{0,4},{4,0},{8,12},{12,8},{16,20},{20,16},{24,28},{28,24},{1,5},{5... | collective-permute-start | bytes 786440 | tf_op jit(solution)/shard_map/ppermute | solution.py:22
  773.4 36.4 %collective-permute-start.56 = (bf16[2,2,64,2048]{3,2,0,1:T(8,128)(2,1)S(1)}, bf16[2,2,64,2048]{3,2,0,1:T(8,128)(2,1)S(1)}, u32[]{:S(2)}, u32[]{:S(2)}) collective-permute-start(bf16[2,2,64,2048]{3,2,0,1:T(8,128)(2,1)S(1)} %fusion.35), channel_id=1, source_target_pairs={{0,1},{1,0},{2,3},{3,2},{4,5},{5,4},{6,7},{7,6},{8,9},{9,8},{10,11... | collective-permute-start | bytes 3145736 | tf_op jit(solution)/shard_map/ppermute | solution.py:22
  776.1 27.9 %collective-permute-start.63 = (bf16[256,768]{1,0:T(8,128)(2,1)S(1)}, bf16[256,768]{1,0:T(8,128)(2,1)S(1)}, u32[]{:S(2)}, u32[]{:S(2)}) collective-permute-start(bf16[256,768]{1,0:T(8,128)(2,1)S(1)} %convolution_convert_fusion.10), channel_id=1, source_target_pairs={{0,4},{4,0},{8,12},{12,8},{16,20},{20,16},{24,28},{28,24},{1,5},{5... | collective-permute-start | bytes 1179656 | tf_op jit(solution)/shard_map/ppermute | solution.py:22
  776.4 25.5 %collective-permute-start.61 = (bf16[256,768]{1,0:T(8,128)(2,1)S(1)}, bf16[256,768]{1,0:T(8,128)(2,1)S(1)}, u32[]{:S(2)}, u32[]{:S(2)}) collective-permute-start(bf16[256,768]{1,0:T(8,128)(2,1)S(1)} %convolution_convert_fusion.11), channel_id=1, source_target_pairs={{0,4},{4,0},{8,12},{12,8},{16,20},{20,16},{24,28},{28,24},{1,5},{5... | collective-permute-start | bytes 1179656 | tf_op jit(solution)/shard_map/ppermute | solution.py:22
  (130 other events, 1645.8 us)

commit v2 on v1

--- a/solution.py
+++ b/solution.py
@@ -38,18 +38,287 @@
     return lax.dot_general(left, right, (((1,), (1,)), ((), ())), preferred_element_type=F32)
 
 
-def offsets_in_order(count):
-    width = bits_of(count)
-    return [int(format(p, "0%db" % width)[::-1], 2) if width else 0 for p in range(count)]
-
-
-def gather_blocks(own):
+MESH = pl.DeviceIdType.MESH
+
+
+def flip(index, mask):
+    bit = 1
+    out = index
+    while bit <= mask:
+        if mask & bit:
+            out = out + bit * (1 - 2 * lax.rem(lax.div(index, bit), 2))
+        bit *= 2
+    return out
+
+
+class Wire:
+    def __init__(self, send_sem, recv_sem):
+        self.send_sem, self.recv_sem = send_sem, recv_sem
+        self.started = []
+        self.landed = set()
+
+    def copy(self, src, dst, peer):
+        place = len(self.started)
+        item = pltpu.make_async_remote_copy(
+            src_ref=src,
+            dst_ref=dst,
+            send_sem=self.send_sem.at[place],
+            recv_sem=self.recv_sem.at[place],
+            device_id=peer,
+            device_id_type=MESH,
+        )
+        item.start()
+        self.started.append(item)
+        return place
+
+    def arrived(self, place):
+        if place not in self.landed:
+            self.landed.add(place)
+            self.started[place].wait_recv()
+
+    def finish(self):
+        for place in range(len(self.started)):
+            self.arrived(place)
+        for item in self.started:
+            item.wait_send()
+
+
+def greet(peers):
+    barrier = pltpu.get_barrier_semaphore()
+    for peer in peers:
+        pl.semaphore_signal(barrier, inc=1, device_id=peer, device_id_type=MESH)
+    pl.semaphore_wait(barrier, len(peers))
+
+
+def seq_peers(index, count):
+    return [{"seq": flip(index, 2 * d)} for d in range(1, count // 2)] + [
+        {"seq": flip(index, 1)}
+    ]
+
+
+def weights_kernel(count, tensor, *refs):
+    small_in, kv_in, q_in, o_in, fc_in, pj_in = refs[:6]
+    small_out, kv_out, q_out, o_out, fc_out, pj_out = refs[6:12]
+    send_sem, recv_sem, local_sem = refs[12:]
+    index = lax.axis_index("seq")
+    place = lax.axis_index("tensor")
+    half = lax.rem(lax.div(index, 2), 2)
+    over = [{"tensor": flip(place, d)} for d in range(1, tensor)]
+    along = seq_peers(index, count)
+    far, near = along[:-1], along[-1]
+    greet(over + along)
+    wire = Wire(send_sem, recv_sem)
+    own = []
+
+    def keep(src, dst):
+        item = pltpu.make_async_copy(src, dst, local_sem.at[len(own)])
+        item.start()
+        own.append(item)
+
+    first = [wire.copy(kv_in, kv_out.at[index, place], peer) for peer in over]
+    first += [wire.copy(small_in, small_out.at[index, place], peer) for peer in over]
+    keep(kv_in, kv_out.at[index, place])
+    keep(small_in, small_out.at[index, place])
+    hops = []
+
+    def spread(source, out):
+        handles = [wire.copy(source(d), out.at[index], far[d - 1]) for d in range(1, count // 2)]
+        wire.copy(source(0), out.at[index], near)
+        hops.append((out, handles))
+
+    spread(lambda d: q_in, q_out)
+    for item in first:
+        wire.arrived(item)
+    for item in own:
+        item.wait()
+    spread(lambda d: kv_out.at[index], kv_out)
+    spread(lambda d: small_out.at[index], small_out)
+    spread(lambda d: o_in, o_out)
+    spread(lambda d: fc_in.at[flip(half, d & 1)], fc_out)
+    spread(lambda d: pj_in.at[flip(half, d & 1)], pj_out)
+    held = len(own)
+    keep(q_in, q_out.at[index])
+    keep(o_in, o_out.at[index])
+    keep(fc_in.at[half], fc_out.at[index])
+    keep(pj_in.at[half], pj_out.at[index])
+    for out, handles in hops:
+        for d, handle in enumerate(handles, 1):
+            wire.arrived(handle)
+            block = out.at[flip(index, 2 * d)]
+            wire.copy(block, block, near)
+    for item in own[held:]:
+        item.wait()
+    wire.finish()
+
+
+def gather_weights(small, keyval, query, out, fc, proj):
+    count, tensor = lax.axis_size("seq"), lax.axis_size("tensor")
+    arrays = (small, keyval, query, out, fc, proj)
+    shapes = [
+        (count, tensor) + small.shape,
+        (count, tensor) + keyval.shape,
+        (count,) + query.shape,
+        (count,) + out.shape,
+        (count,) + fc.shape[1:],
+        (count,) + proj.shape[1:],
+    ]
+    copies = 2 * (tensor - 1) + 6 * (count - 1)
+    return pl.pallas_call(
+        partial(weights_kernel, count, tensor),
+        out_shape=[jax.ShapeDtypeStruct(shape, LOW) for shape in shapes],
+        in_specs=[pl.BlockSpec(memory_space=pl.ANY)] * 6,
+        out_specs=[pl.BlockSpec(memory_space=pl.ANY)] * 6,
+        scratch_shapes=[
+            pltpu.SemaphoreType.DMA((copies,)),
+            pltpu.SemaphoreType.DMA((copies,)),
+            pltpu.SemaphoreType.DMA((6,)),
+        ],
+        compiler_params=pltpu.CompilerParams(collective_id=0, has_side_effects=True),
+        name="gather_weights",
+    )(*arrays)
+
+
+def keyval_kernel(count, kv_in, kv_out, send_sem, recv_sem, local_sem):
+    index = lax.axis_index("seq")
+    place = lax.axis_index("tensor")
+    core = lax.rem(place, 2)
+    other = {"tensor": flip(place, 1)}
+    along = seq_peers(index, count)
+    far, near = along[:-1], along[-1]
+    greet([other] + along)
+    wire = Wire(send_sem, recv_sem)
+    handles = [
+        wire.copy(kv_in.at[core], kv_out.at[core, index], far[d - 1]) for d in range(1, count // 2)
+    ]
+    own_near = wire.copy(kv_in.at[core], kv_out.at[core, index], near)
+    own = []
+    for batch in range(2):
+        item = pltpu.make_async_copy(kv_in.at[batch], kv_out.at[batch, index], local_sem.at[batch])
+        item.start()
+        own.append(item)
+    relays = [(1, own_near)]
+    for d, handle in enumerate(handles, 1):
+        wire.arrived(handle)
+        block = kv_out.at[core, flip(index, 2 * d)]
+        relays.append((2 * d + 1, wire.copy(block, block, near)))
+        wire.copy(block, block, other)
+    for r, handle in relays:
+        wire.arrived(handle)
+        block = kv_out.at[core, flip(index, r)]
+        wire.copy(block, block, other)
+    for item in own:
+        item.wait()
+    wire.finish()
+
+
+def gather_keyval(keyval):
     count = lax.axis_size("seq")
-    blocks = {0: own}
-    for bit in reversed(range(bits_of(count))):
-        for r in list(blocks):
-            blocks[r | (1 << bit)] = swap(blocks[r], "seq", bit)
-    return blocks
+    copies = 2 * (count - 1)
+    batches, rows, two = keyval.shape
+    return pl.pallas_call(
+        partial(keyval_kernel, count),
+        out_shape=jax.ShapeDtypeStruct((batches, count, rows, two), LOW),
+        in_specs=[pl.BlockSpec(memory_space=pltpu.VMEM)],
+        out_specs=pl.BlockSpec(memory_space=pltpu.VMEM),
+        scratch_shapes=[
+            pltpu.SemaphoreType.DMA((copies,)),
+            pltpu.SemaphoreType.DMA((copies,)),
+            pltpu.SemaphoreType.DMA((2,)),
+        ],
+        compiler_params=pltpu.CompilerParams(collective_id=1, has_side_effects=True),
+        name="gather_keyval",
+    )(keyval)
+
+
+def scatter_kernel(count, split, arrays, *refs):
+    parts = refs[:arrays]
+    outs = refs[arrays : 2 * arrays]
+    from_near = refs[2 * arrays : 3 * arrays]
+    to_far = refs[3 * arrays : 4 * arrays]
+    from_far = refs[4 * arrays : 5 * arrays]
+    send_sem, recv_sem = refs[5 * arrays :]
+    index = lax.axis_index("seq")
+    half = lax.rem(lax.div(index, 2), 2)
+    along = seq_peers(index, count)
+    far, near = along[:-1], along[-1]
+    lines = count // 2
+    greet(along)
+    wire = Wire(send_sem, recv_sem)
+    turn = list(range(1, lines)) + [0]
+    near_handles, far_handles = {}, {}
+    for a in range(arrays):
+        for d in turn:
+            block = parts[a].at[flip(index, 2 * d + 1)]
+            near_handles[a, d] = wire.copy(block, from_near[a].at[d], near)
+    rows = parts[0].shape[1]
+    step = min(64, rows)
+
+    def by_rows(body):
+        def run(i, carry):
+            body(pl.ds(pl.multiple_of(i * step, step), step))
+            return carry
+
+        lax.fori_loop(0, rows // step, run, 0)
+
+    for a in range(arrays):
+        for d in range(1, lines):
+            wire.arrived(near_handles[a, d])
+
+            def join(at, a=a, d=d):
+                total = parts[a][flip(index, 2 * d), at].astype(F32)
+                total = total + from_near[a][d, at].astype(F32)
+                to_far[a][d - 1, at] = total.astype(LOW)
+
+            by_rows(join)
+            far_handles[a, d] = wire.copy(to_far[a].at[d - 1], from_far[a].at[d - 1], far[d - 1])
+    for a in range(arrays):
+        wire.arrived(near_handles[a, 0])
+        for d in range(1, lines):
+            wire.arrived(far_handles[a, d])
+        width = parts[a].shape[2]
+
+        def total(at, a=a, width=width):
+            same = parts[a][index, at].astype(F32) + from_near[a][0, at].astype(F32)
+            other = None
+            for d in range(1, lines):
+                got = from_far[a][d - 1, at].astype(F32)
+                if split and d % 2:
+                    other = got if other is None else other + got
+                else:
+                    same = same + got
+            if split:
+                outs[a][at, pl.ds(pl.multiple_of(half * width, width), width)] = same
+                outs[a][at, pl.ds(pl.multiple_of((1 - half) * width, width), width)] = other
+            else:
+                outs[a][at, :] = same
+
+        by_rows(total)
+    wire.finish()
+
+
+def scatter_grads(parts, split, collective_id):
+    count = lax.axis_size("seq")
+    lines = count // 2
+    arrays = len(parts)
+    copies = arrays * (count - 1)
+    scratch = []
+    for depth in (lines, lines - 1, lines - 1):
+        scratch += [pltpu.VMEM((depth,) + part.shape[1:], LOW) for part in parts]
+    return pl.pallas_call(
+        partial(scatter_kernel, count, split, arrays),
+        out_shape=[
+            jax.ShapeDtypeStruct((part.shape[1], part.shape[2] * (2 if split else 1)), F32)
+            for part in parts
+        ],
+        in_specs=[pl.BlockSpec(memory_space=pltpu.VMEM)] * arrays,
+        out_specs=[pl.BlockSpec(memory_space=pltpu.VMEM)] * arrays,
+        scratch_shapes=scratch
+        + [pltpu.SemaphoreType.DMA((copies,)), pltpu.SemaphoreType.DMA((copies,))],
+        compiler_params=pltpu.CompilerParams(
+            collective_id=collective_id, has_side_effects=True, vmem_limit_bytes=60 << 20
+        ),
+        name="scatter_grads",
+    )(*parts)
 
 
 def scatter_blocks(blocks):
@@ -308,32 +577,12 @@
     width_block = w_query.shape[0]
     group_width = w_query.shape[1]
     hidden_width = w_fc.shape[1]
+    unit_width = hidden_width // 2
+    unit_half = (seq_index >> 1) & 1
     hd = value_bias.shape[0]
     quarter = rows // tensor_size
-    order = offsets_in_order(seq_size)
     shard = vectors.shape[1]
     bias_shard = fc_bias.shape[0]
-
-    def to_order(array):
-        starts = [jnp.bitwise_xor(seq_index, r) * width_block for r in order]
-        last = array.ndim - 1
-        return jnp.concatenate(
-            [lax.dynamic_slice_in_dim(array, start, width_block, last) for start in starts], last
-        )
-
-    def from_order(array):
-        place = {r: p for p, r in enumerate(order)}
-        table = jnp.array([place[r] for r in range(seq_size)], jnp.int32)
-        last = array.ndim - 1
-        return jnp.concatenate(
-            [
-                lax.dynamic_slice_in_dim(
-                    array, table[jnp.bitwise_xor(seq_index, b)] * width_block, width_block, last
-                )
-                for b in range(seq_size)
-            ],
-            last,
-        )
 
     pieces = [
         vectors.reshape(-1).astype(LOW),
@@ -342,24 +591,37 @@
         (position // 128).reshape(-1).astype(LOW),
         (position % 128).reshape(-1).astype(LOW),
     ]
-    sizes = [piece.shape[0] for piece in pieces]
+    cuts = [0]
+    for piece in pieces:
+        cuts.append(cuts[-1] + piece.shape[0])
     packed = jnp.concatenate(pieces)
-    pad = -packed.shape[0] % 1024
-    packed = jnp.pad(packed, (0, pad)).reshape(-1, 128)
-    small = lax.all_gather(packed, ("seq", "tensor"), axis=0, tiled=False)
+    packed = jnp.pad(packed, (0, -packed.shape[0] % 2048)).reshape(-1, 128)
+
+    def halves(array):
+        return jnp.swapaxes(array.astype(LOW).reshape(width_block, 2, unit_width), 0, 1)
+
+    small, kv_mat, q_mat, out_t, fc_mat, proj_t = gather_weights(
+        packed,
+        w_keyval.astype(LOW),
+        w_query.astype(LOW),
+        w_out.T.astype(LOW),
+        halves(w_fc),
+        halves(w_proj.T),
+    )
+    kv_mat = kv_mat.reshape(full_width, 2 * hd)
+    q_mat = q_mat.reshape(full_width, group_width)
+    out_t = out_t.reshape(full_width, group_width)
+    fc_mat = fc_mat.reshape(full_width, unit_width)
+    proj_t = proj_t.reshape(full_width, unit_width)
+
     small = small.reshape(seq_size, tensor_size, -1).astype(F32)
-    cuts = [0]
-    for size in sizes:
-        cuts.append(cuts[-1] + size)
     vec_all = small[:, :, cuts[0] : cuts[1]].reshape(seq_size * tensor_size, 7, shard)
     vec_all = jnp.swapaxes(vec_all, 0, 1).reshape(7, full_width)
     fc_all = small[:, :, cuts[1] : cuts[2]].reshape(-1)
-    seg_all = small[:, 0, cuts[2] : cuts[3]].reshape(seq_size, batches, rows)
-    pos_all = 128.0 * small[:, 0, cuts[3] : cuts[4]] + small[:, 0, cuts[4] : cuts[5]]
-    pos_all = pos_all.reshape(seq_size, batches, rows)
-    offset_ids = jnp.bitwise_xor(seq_index, jnp.array(order, jnp.int32))
-    seg_keys = jnp.swapaxes(seg_all[offset_ids], 0, 1).astype(jnp.int32)
-    pos_keys = jnp.swapaxes(pos_all[offset_ids], 0, 1).astype(jnp.int32)
+    seg_keys = small[:, 0, cuts[2] : cuts[3]].reshape(seq_size, batches, rows)
+    pos_keys = 128.0 * small[:, 0, cuts[3] : cuts[4]] + small[:, 0, cuts[4] : cuts[5]]
+    seg_keys = jnp.swapaxes(seg_keys, 0, 1).astype(jnp.int32)
+    pos_keys = jnp.swapaxes(pos_keys.reshape(seq_size, batches, rows), 0, 1).astype(jnp.int32)
     meta_k = jnp.pad(jnp.stack([seg_keys, pos_keys], axis=2), ((0, 0), (0, 0), (0, 6), (0, 0)))
     meta_q = jnp.pad(jnp.stack([segment, position], axis=2), ((0, 0), (0, 0), (0, 126)))
     seg_lo, seg_hi = jnp.min(seg_keys, axis=2), jnp.max(seg_keys, axis=2)
@@ -370,63 +632,59 @@
         & (jnp.min(pos_keys, axis=2) <= jnp.max(position, axis=1, keepdims=True))
     ).astype(jnp.int32)
 
-    vec_rows = to_order(vec_all)
     gain_one, shift_one, _, out_bias, gain_two, shift_two, proj_bias = [
-        vec_rows[i] for i in range(7)
+        vec_all[i] for i in range(7)
     ]
     query_bias = lax.dynamic_slice_in_dim(vec_all[2], tensor_index * group_width, group_width, 0)
-    fc_local = lax.dynamic_slice_in_dim(fc_all, tensor_index * hidden_width, hidden_width, 0)
+    fc_local = lax.dynamic_slice_in_dim(
+        fc_all, tensor_index * hidden_width + unit_half * unit_width, unit_width, 0
+    )
     bias_value = value_bias.astype(LOW).astype(F32)
     kv_bias = jnp.concatenate([jnp.zeros((hd,), F32), bias_value])
 
-    kv_rows = tensor_gather(w_keyval.astype(LOW), 0).reshape(width_block, 2 * hd)
-    first_own = jnp.concatenate([w_query.astype(LOW), kv_rows], axis=1)
-    first_blocks = gather_blocks(first_own)
-    first_mat = jnp.concatenate([first_blocks[r] for r in order], axis=0)
-    out_blocks = gather_blocks(after(w_out.T.astype(LOW), first_blocks[seq_size - 1]))
-    out_t = jnp.concatenate([out_blocks[r] for r in order], axis=0)
-    fc_blocks = gather_blocks(after(w_fc.astype(LOW), out_blocks[seq_size // 2 - 1]))
-    fc_mat = jnp.concatenate([fc_blocks[r] for r in order], axis=0)
-    proj_blocks = gather_blocks(after(w_proj.T.astype(LOW), fc_blocks[seq_size // 2 - 1]))
-    proj_t = jnp.concatenate([proj_blocks[r] for r in order], axis=0)
-
-    hidden_in = to_order(inputs)
-    residual = hidden_in.astype(F32)
+    residual = inputs.astype(F32)
     centred, inverse = norm_parts(residual)
     normed = (centred * inverse * gain_one + shift_one).astype(LOW).reshape(-1, full_width)
-    first_out = dot(normed, first_mat)
-    queries = (first_out[:, :group_width] + query_bias).astype(LOW)
+    keyval = (dot(normed, kv_mat) + kv_bias).astype(LOW).reshape(batches, rows, 2 * hd)
+    kv_all = gather_keyval(keyval)
+    queries = (dot(normed, q_mat) + query_bias).astype(LOW)
     queries = queries.reshape(batches, rows, group_width)
-    keyval = (first_out[:, group_width:] + kv_bias).astype(LOW).reshape(batches, rows, 2 * hd)
-    kv_blocks = gather_blocks(keyval)
-    kv_all = jnp.stack([kv_blocks[r] for r in order], axis=1)
     mixed, lse = attend_forward(queries, kv_all, meta_q, meta_k, live)
     mixed_rows = mixed.reshape(-1, group_width)
 
     def quarters(array):
-        return array.reshape(batches, tensor_size, quarter, array.shape[-1])
+        return array.reshape(-1, batches, tensor_size, quarter, array.shape[-1])
 
     def my_quarter(array):
-        split = quarters(array)
+        split = array.reshape(batches, tensor_size, quarter, full_width)
         return lax.dynamic_index_in_dim(split, tensor_index, 1, keepdims=False)
 
-    attn_part = quarters(dot_nt(mixed_rows, out_t))
-    attn_sum = tensor_scatter(attn_part, 1)
-    middle = my_quarter(hidden_in).astype(F32) + attn_sum + out_bias
+    def pair_gather(own):
+        both = jnp.stack([own, swap(own, "seq", 1)])
+        return tensor_gather(both, 2).reshape(-1, full_width)
+
+    def pair_scatter(part):
+        split = quarters(part)
+        got = tensor_scatter(split, 2)
+        return got[0] + swap(got[1].astype(LOW), "seq", 1).astype(F32)
+
+    attn_sum = tensor_scatter(quarters(dot_nt(mixed_rows, out_t)), 2)[0]
+    middle = my_quarter(inputs).astype(F32) + attn_sum + out_bias
     centred, inverse = norm_parts(middle)
     normed_q = (centred * inverse * gain_two + shift_two).astype(LOW)
-    normed_two = tensor_gather(normed_q, 1).reshape(-1, full_width)
+    normed_two = pair_gather(normed_q)
     hidden = dot(normed_two, fc_mat) + fc_local
     active_f, slope = gelu_pair(hidden)
     active = active_f.astype(LOW)
 
-    grad_rows = to_order(grad_out)
-    grad_flat = grad_rows.reshape(-1, full_width)
+    grad_q_low = my_quarter(grad_out)
+    grad_flat = jnp.concatenate(
+        [grad_out.reshape(-1, full_width), swap(grad_out.reshape(-1, full_width), "seq", 1)]
+    )
     grad_hidden = (slope * dot(grad_flat, proj_t)).astype(LOW)
     fcbias_local = jnp.sum(grad_hidden.astype(F32), axis=0)
-    grad_normed_two = quarters(dot_nt(grad_hidden, fc_mat))
-    back_sum = tensor_scatter(grad_normed_two, 1)
-    grad_q = my_quarter(grad_rows).astype(F32)
+    back_sum = pair_scatter(dot_nt(grad_hidden, fc_mat))
+    grad_q = grad_q_low.astype(F32)
     norm_part, gain_part = norm_back(middle, gain_two, back_sum)
     grad_middle = grad_q + norm_part
     grad_gain_two = jnp.sum(gain_part, axis=(0, 1))
@@ -435,35 +693,46 @@
     grad_proj_bias = jnp.sum(grad_q, axis=(0, 1))
     grad_middle_low = tensor_gather(grad_middle.astype(LOW), 1).reshape(-1, full_width)
 
-    def grads_by_block(left, right):
-        return {
-            r: dot_tn(left[:, p * width_block : (p + 1) * width_block], right)
-            for p, r in enumerate(order)
-        }
-
-    proj_sum = scatter_blocks(grads_by_block(grad_flat, active))
-    fc_sum = scatter_blocks(grads_by_block(normed_two, grad_hidden))
-
-    ff_sum = tensor_scatter(quarters(dot_nt(active, proj_t)), 1)
+    def blocked(array):
+        return array.astype(LOW).reshape(seq_size, width_block, array.shape[-1])
+
+    proj_sum, fc_sum = scatter_grads(
+        [blocked(dot_tn(grad_flat, active)), blocked(dot_tn(normed_two, grad_hidden))], True, 2
+    )
+
+    ff_sum = pair_scatter(dot_nt(active, proj_t))
     result_q = (middle + ff_sum + proj_bias).astype(LOW)
-    result = from_order(tensor_gather(result_q, 1).reshape(batches, rows, full_width))
+    result = tensor_gather(result_q, 1).reshape(batches, rows, full_width)
 
     grad_mixed = dot(grad_middle_low, out_t).astype(LOW).reshape(batches, rows, group_width)
-    out_sum = scatter_blocks(grads_by_block(grad_middle_low, mixed_rows))
     grad_queries, grad_kv_all = attend_backward(
         queries, kv_all, meta_q, meta_k, live, mixed, lse, grad_mixed
     )
-    grad_keyval = scatter_blocks({r: grad_kv_all[:, p].astype(F32) for p, r in enumerate(order)})
+    grad_keyval = scatter_blocks(
+        {
+            r: lax.dynamic_index_in_dim(
+                grad_kv_all, jnp.bitwise_xor(seq_index, r), 1, keepdims=False
+            ).astype(F32)
+            for r in range(seq_size)
+        }
+    )
     grad_keyval = grad_keyval.astype(LOW).reshape(-1, 2 * hd)
     grad_queries = grad_queries.reshape(-1, group_width)
-    grad_first = jnp.concatenate([grad_queries, grad_keyval], axis=1)
-    first_sum = scatter_blocks(grads_by_block(normed, grad_first))
-    grad_normed = quarters(dot_nt(grad_first, first_mat))
-    in_sum = tensor_scatter(grad_normed, 1)
-    residual_q = my_quarter(hidden_in).astype(F32)
+    out_sum, query_sum, kv_sum = scatter_grads(
+        [
+            blocked(dot_tn(grad_middle_low, mixed_rows)),
+            blocked(dot_tn(normed, grad_queries)),
+            blocked(dot_tn(normed, grad_keyval)),
+        ],
+        False,
+        3,
+    )
+    grad_normed = dot_nt(grad_queries, q_mat) + dot_nt(grad_keyval, kv_mat)
+    in_sum = tensor_scatter(quarters(grad_normed), 2)[0]
+    residual_q = my_quarter(inputs).astype(F32)
     norm_part, gain_part = norm_back(residual_q, gain_one, in_sum)
     grad_in_q = (grad_middle + norm_part).astype(LOW)
-    input_grad = from_order(tensor_gather(grad_in_q, 1).reshape(batches, rows, full_width))
+    input_grad = tensor_gather(grad_in_q, 1).reshape(batches, rows, full_width)
     grad_gain_one = jnp.sum(gain_part, axis=(0, 1))
     grad_shift_one = jnp.sum(in_sum, axis=(0, 1))
     qbias_local = jnp.sum(grad_queries.astype(F32), axis=0)
@@ -474,13 +743,16 @@
     )
     full_hidden = bias_shard * seq_size * tensor_size
     fcbias_full = lax.dynamic_update_slice_in_dim(
-        jnp.zeros((full_hidden,), F32), fcbias_local, tensor_index * hidden_width, 0
-    )
-    grads_rel = jnp.stack(
+        jnp.zeros((full_hidden,), F32),
+        fcbias_local,
+        tensor_index * hidden_width + unit_half * unit_width,
+        0,
+    )
+    vec_grads = jnp.stack(
         [
             grad_gain_one,
             grad_shift_one,
-            to_order(qbias_full),
+            qbias_full,
             grad_out_bias,
             grad_gain_two,
             grad_shift_two,
@@ -488,24 +760,27 @@
         ]
     )
     chunk = full_hidden // seq_size
-    small_rows = {}
-    for p, r in enumerate(order):
-        part = lax.dynamic_slice_in_dim(
-            fcbias_full, jnp.bitwise_xor(seq_index, r) * chunk, chunk, 0
-        )
-        vec_part = grads_rel[:, p * width_block : (p + 1) * width_block].reshape(-1)
-        row = jnp.concatenate([vec_part, part, vbias_local])
-        small_rows[r] = jnp.pad(row, (0, -row.shape[0] % 1024)).reshape(-1, 128)
-    for bit in range(bits_of(seq_size)):
-        for r in sorted(small_rows):
-            if r & (1 << bit):
-                got = swap(small_rows.pop(r), "seq", bit)
-                small_rows[r ^ (1 << bit)] = small_rows[r ^ (1 << bit)] + got
-    small_sum = small_rows[0]
+    vec_cut = 7 * width_block
+    rows_all = jnp.concatenate(
+        [
+            jnp.swapaxes(vec_grads.reshape(7, seq_size, width_block), 0, 1).reshape(seq_size, -1),
+            fcbias_full.reshape(seq_size, chunk),
+            jnp.broadcast_to(vbias_local, (seq_size, hd)),
+        ],
+        axis=1,
+    )
+    rows_all = jnp.pad(rows_all, ((0, 0), (0, -rows_all.shape[1] % 1024)))
+    rows_all = rows_all.reshape(seq_size, -1, 128)
+    for bit in reversed(range(bits_of(seq_size))):
+        size = rows_all.shape[0] // 2
+        mine = (seq_index >> bit) & 1
+        keep = lax.dynamic_slice_in_dim(rows_all, mine * size, size, 0)
+        give = lax.dynamic_slice_in_dim(rows_all, (1 - mine) * size, size, 0)
+        rows_all = keep + swap(give, "seq", bit)
+    small_sum = rows_all[0]
     for bit in range(bits_of(tensor_size)):
         small_sum = small_sum + swap(small_sum, "tensor", bit)
     small_sum = small_sum.reshape(-1)
-    vec_cut = 7 * width_block
     vec_grad = lax.dynamic_slice_in_dim(
         small_sum[:vec_cut].reshape(7, width_block), tensor_index * shard, shard, 1
     )
@@ -513,14 +788,11 @@
         small_sum[vec_cut : vec_cut + chunk], tensor_index * bias_shard, bias_shard, 0
     )
     vbias_grad = small_sum[vec_cut + chunk : vec_cut + chunk + hd]
-
-    query_grad = first_sum[:, :group_width]
-    kv_part = first_sum[:, group_width:].reshape(tensor_size, -1, 2 * hd)
-    keyval_grad = tensor_scatter(kv_part, 0)
+    keyval_grad = tensor_scatter(kv_sum.reshape(tensor_size, -1, 2 * hd), 0)
     return (
         result,
         input_grad,
-        query_grad,
+        query_sum,
         keyval_grad,
         out_sum.T,
         fc_sum,

time: 881 us -> 821 us (0.932)
  Pallas kernels: 32.8 us -> 434 us
  waiting for transfers between devices: 437 us -> 169 us
  starting transfers between devices: 130 us -> 49.5 us
  blocking collectives: 41.3 us -> 0 us
  local copies, waits for them, and re-layouts: 82 us -> 49 us
  matrix products: 90.2 us -> 60.3 us
    pallas_call x0 -> x4, Pallas kernels: none -> 394 us  [the longest x2 192 us: scatter_grads(): pl.pallas_call(partial(scatter_kernel, count, split, arrays), out_shape=[...]
    ppermute x99 -> x34, waiting for transfers between devices: 437 us -> 169 us  [swap(): return lax.ppermute(value, axis, [(i, i ^ 1 << bit) for i in range(count)])]
    ppermute x99 -> x34, starting transfers between devices: 130 us -> 49.5 us  [swap(): return lax.ppermute(value, axis, [(i, i ^ 1 << bit) for i in range(count)])]
    all_gather x1 -> x0, blocking collectives: 41.3 us -> none  [local(): small = lax.all_gather(packed, ('seq', 'tensor'), axis=0, tiled=False)]
    unnamed x250 -> x107, local copies, waits for them, and re-layouts: 59.2 us -> 27.4 us
    dot_general x32 -> x5, matrix products: 45.7 us -> 21.9 us  [dot_tn(): lax.dot_general(left, right, (((0,), (0,)), ((), ())), preferred_element_...]
    dot_general x4 -> x5, matrix products: 27.9 us -> 22.1 us  [dot(): return jnp.dot(left, right, preferred_element_type=F32)]
  transfers between devices with their start and end apart: 99 -> 34, of which waited for: 44 -> 20; matrix products, arithmetic and copies ran while one was open for 23% -> 9% of each run, Pallas kernels for 4% -> 26%
where the time goes in v2:
time: 821 us; the launch traced here: 814 us
  Pallas kernels  434 us (53%)
  waiting for transfers between devices  169 us (21%)
  matrix products  60.3 us (7%)
  other arithmetic  49.7 us (6%)
  starting transfers between devices  49.5 us (6%)
  local copies, waits for them, and re-layouts  49 us (6%)
    pallas_call x2, Pallas kernels, scatter_grads(): pl.pallas_call(partial(scatter_kernel, count, split, arrays), out_shape=[...  192 us
    pallas_call x1, Pallas kernels, gather_weights(): pl.pallas_call(partial(weights_kernel, count, tensor), out_shape=[jax.Sha...  181 us
    ppermute x34, waiting for transfers between devices, swap(): return lax.ppermute(value, axis, [(i, i ^ 1 << bit) for i in range(count)])  169 us
    ppermute x34, starting transfers between devices, swap(): return lax.ppermute(value, axis, [(i, i ^ 1 << bit) for i in range(count)])  49.5 us
    unnamed x107, local copies, waits for them, and re-layouts  27.4 us
    pallas_call x1, Pallas kernels, attend_forward(): pl.pallas_call(forward_kernel, grid_spec=pltpu.PrefetchScalarGridSpec(num...  22.4 us
    dot_general x5, matrix products, dot(): return jnp.dot(left, right, preferred_element_type=F32)  22.1 us
    dot_general x5, matrix products, dot_tn(): lax.dot_general(left, right, (((0,), (0,)), ((), ())), preferred_element_...  21.9 us
  transfers between devices with their start and end apart: 34, of which 20 were waited for; matrix products, arithmetic and copies ran while one was open for 9% of the time, Pallas kernels for 26%

profile of v2, /device:TPU:0, one launch (start us, length us, event | category | flops | bytes accessed | tf_op | source)
XLA Modules:
  0.0 813.7 jit_solution(11794349419006594672)
XLA Ops:
  15.0 181.4 %gather_weights.1 = (bf16[8,4,32,128]{3,2,1,0:T(8,128)(2,1)}, bf16[8,4,64,256]{3,2,1,0:T(8,128)(2,1)}, bf16[8,256,512]{2,1,0:T(8,128)(2,1)}, bf16[8,256,512]{2,1...) custom-call(bf16[32,128]{1,0:T(8,128)(2,1)} %pad_bitcast_fusion.1.refs_0_, ...), custom_call_target="tpu_custom_call" | custom-call | tf_op jit(solution)/shard_map/gather_weights/pallas_call | solution.py:166
  203.4 20.3 %gather_keyval.1.kv_ref = bf16[2,8,256,256]{3,2,1,0:T(8,128)(2,1)} custom-call(bf16[2,256,256]{2,1,0:T(8,128)(2,1)} %bitcast.417), custom_call_target="tpu_custom_call" | custom-call | tf_op jit(solution)/shard_map/gather_keyval/pallas_call | solution.py:218
  225.6 4.3 fusion.21
  230.5 22.4 %attend_forward.1 = (bf16[2,256,512]{2,1,0:T(8,128)(2,1)}, f32[2,4,256,1]{3,2,1,0:T(8,128)}) custom-call(s32[2,8]{1,0:T(2,128)} %and_convert_fusion.live_ref, bf16[2,256,512]{2,1,0:T(8,128)(2,1)} %bitcast.439, bf16[2,8,256,256]{3,2,1,0:T(8,128)(2,1)} %gather_keyval.1.kv_ref, s32[2,256,128]{2,1,0:T(8,128)} %pad.19.mq_ref, s32[2,8,8,256]{3,2,1,0:T(8,128)} %pad.20.mk_ref), custom_call_target="tpu_custom_call" | custom-call | flops 2147483648 | bytes 2097152 | tf_op jit(solution)/shard_map/attend_forward/pallas_call | solution.py:414
  252.9 5.0 fusion.82
  260.1 2.4 collective-permute-done
  262.6 2.2 bitcast_add_fusion.3
  268.1 12.4 %collective-permute-done.1 = bf16[1,2,1,64,2048]{4,3,2,1,0:T(8,128)(2,1)} collective-permute-done((bf16[1,2,1,64,2048]{4,3,2,1,0:T(8,128)(2,1)S(1)}, bf16[1,2,1,64,2048]{4,3,2,1,0:T(8,128)(2,1)}, u32[]{:S(2)}, u32[]{:S(2)}) %collective-permute-start.1) | collective-permute-done | bytes 524320 | tf_op jit(solution)/shard_map/ppermute | solution.py:22
  282.9 2.6 collective-permute-start.2
  287.0 10.1 %collective-permute-done.2 = bf16[2,64,2048]{2,1,0:T(8,128)(2,1)S(1)} collective-permute-done((bf16[2,64,2048]{2,1,0:T(8,128)(2,1)S(1)}, bf16[2,64,2048]{2,1,0:T(8,128)(2,1)S(1)}, u32[]{:S(2)}, u32[]{:S(2)}) %collective-permute-start.2) | collective-permute-done | bytes 524320 | tf_op jit(solution)/shard_map/ppermute | solution.py:22
  299.8 22.8 %collective-permute-done.3 = bf16[2,2,1,64,2048]{4,3,1,0,2:T(8,128)(2,1)} collective-permute-done((bf16[2,2,1,64,2048]{4,3,1,0,2:T(8,128)(2,1)}, bf16[2,2,1,64,2048]{4,3,1,0,2:T(8,128)(2,1)}, u32[]{:S(2)}, u32[]{:S(2)}) %collective-permute-start.3) | collective-permute-done | bytes 1048608 | tf_op jit(solution)/shard_map/ppermute | solution.py:22
  328.7 2.1 collective-permute-done.4
  330.8 2.4 select_bitcast_fusion.1
  334.2 3.1 copy-done.38
  337.3 5.4 multiply_convert_fusion
  342.7 31.9 %collective-permute-done.10 = bf16[512,2048]{1,0:T(8,128)(2,1)} collective-permute-done((bf16[512,2048]{1,0:T(8,128)(2,1)}, bf16[512,2048]{1,0:T(8,128)(2,1)}, u32[]{:S(2)}, u32[]{:S(2)}) %collective-permute-start.10) | collective-permute-done | bytes 2097184 | tf_op jit(solution)/shard_map/ppermute | solution.py:22
  374.6 9.0 %convert_reduce_fusion.1 = (f32[1024]{0:T(1024)S(1)}, bf16[1024,1024]{1,0:T(8,128)(2,1)S(1)}) fusion(bf16[2048,1024]{1,0:T(8,128)(2,1)S(1)} %bitcast.433, bf16[512,2048]{1,0:T(8,128)(2,1)} %collective-permute-done.10, bf16[512,2048]{1,0:T(8,128)(2,1)} %bitcast.56, f32[1024,1024]{1,0:T(8,128)S(1)} %get-tuple-element.140, f32[1024]{0:T(1024)S(1)} %dynamic_slice.107), kind=kOutput, calls=%fused_computation.26 | convolution fusion | flops 4325374976 | bytes 14688256 | tf_op jit(solution)/shard_map/dot_general | solution.py:30
  384.9 4.6 fusion.84
  391.7 4.6 fusion.83
  405.8 19.4 %collective-permute-done.12 = bf16[2,2,1,64,2048]{4,3,1,2,0:T(8,128)(2,1)} collective-permute-done((bf16[2,2,1,64,2048]{4,3,1,2,0:T(8,128)(2,1)}, bf16[2,2,1,64,2048]{4,3,1,2,0:T(8,128)(2,1)}, u32[]{:S(2)}, u32[]{:S(2)}) %collective-permute-start.12) | collective-permute-done | bytes 1048608 | tf_op jit(solution)/shard_map/ppermute | solution.py:22
  425.2 2.2 convert_add_fusion
  429.0 18.2 %collective-permute-done.6 = bf16[2,2,1,64,2048]{4,3,1,2,0:T(8,128)(2,1)} collective-permute-done((bf16[2,2,1,64,2048]{4,3,1,2,0:T(8,128)(2,1)}, bf16[2,2,1,64,2048]{4,3,1,2,0:T(8,128)(2,1)}, u32[]{:S(2)}, u32[]{:S(2)}) %collective-permute-start.6) | collective-permute-done | bytes 1048608 | tf_op jit(solution)/shard_map/ppermute | solution.py:22
  450.8 11.5 %collective-permute-done.7 = bf16[2,64,2048]{2,1,0:T(8,128)(2,1)S(1)} collective-permute-done((bf16[2,64,2048]{2,1,0:T(8,128)(2,1)S(1)}, bf16[2,64,2048]{2,1,0:T(8,128)(2,1)S(1)}, u32[]{:S(2)}, u32[]{:S(2)}) %collective-permute-start.7) | collective-permute-done | bytes 524320 | tf_op jit(solution)/shard_map/ppermute | solution.py:22
  462.3 2.6 fusion.76
  468.8 10.0 %collective-permute-done.14 = bf16[2,1,64,2048]{3,2,0,1:T(8,128)(2,1)} collective-permute-done((bf16[2,1,64,2048]{3,2,0,1:T(8,128)(2,1)S(1)}, bf16[2,1,64,2048]{3,2,0,1:T(8,128)(2,1)}, u32[]{:S(2)}, u32[]{:S(2)}) %collective-permute-start.14) | collective-permute-done | bytes 524320 | tf_op jit(solution)/shard_map/ppermute | solution.py:22
  481.3 8.7 %convolution_convert_fusion.1 = bf16[2048,1024]{1,0:T(8,128)(2,1)} fusion(bf16[1024,1024]{1,0:T(8,128)(2,1)S(1)} %copy-done.41, bf16[512,2048]{1,0:T(8,128)(2,1)} %collective-permute-done.10, bf16[512,2048]{1,0:T(8,128)(2,1)} %bitcast.56), kind=kOutput, calls=%fused_computation.30 | convolution fusion | flops 4305453056 | bytes 10485760 | tf_op jit(solution)/shard_map/dot_general | solution.py:34
  490.0 6.2 convolution_convert_fusion
  496.2 115.9 %scatter_grads.3 = (f32[256,2048]{1,0:T(8,128)}, f32[256,2048]{1,0:T(8,128)}) custom-call(bf16[8,256,1024]{2,1,0:T(8,128)(2,1)} %bitcast.385, bf16[8,256,1024]{2,1,0:T(8,128)(2,1)} %bitcast.386), custom_call_target="tpu_custom_call" | custom-call | tf_op jit(solution)/shard_map/scatter_grads/pallas_call | solution.py:307
  612.1 2.9 copy.124
  617.7 2.1 copy-done.22
  619.8 2.1 convolution_convert_fusion.3
  621.9 17.8 %attend_backward.1 = (bf16[2,256,512]{2,1,0:T(8,128)(2,1)}, bf16[2,8,256,256]{3,2,1,0:T(8,128)(2,1)}) custom-call(s32[2,8]{1,0:T(2,128)} %and_convert_fusion.live_ref, bf16[2,256,512]{2,1,0:T(8,128)(2,1)} %bitcast.440, bf16[2,8,256,256]{3,2,1,0:T(8,128)(2,1)} %gather_keyval.1.kv_ref, s32[2,256,128]{2,1,0:T(8,128)} %pad.19.mq_ref, ...), custom_call_target="tpu_custom_call" | custom-call | flops 5368709120 | bytes 4194304 | tf_op jit(solution)/shard_map/attend_backward/pallas_call | solution.py:501
  642.6 1.9 collective-permute-start.17
  646.6 3.7 collective-permute-done.20
  650.4 13.2 %collective-permute-start.21 = (bf16[2,256,256]{2,1,0:T(8,128)(2,1)S(1)}, bf16[2,256,256]{2,1,0:T(8,128)(2,1)S(1)}, u32[]{:S(2)}, u32[]{:S(2)}) collective-permute-start(bf16[2,256,256]{2,1,0:T(8,128)(2,1)S(1)} %fusion.56), channel_id=1, source_target_pairs={{0,8},{4,12},{8,0},{12,4},{16,24},{20,28},{24,16},{28,20},{1,9},{5... | collective-permute-start | bytes 786440 | tf_op jit(solution)/shard_map/ppermute | solution.py:22
  664.9 3.0 collective-permute-done.21
  668.1 3.4 collective-permute-start.22
  671.5 3.5 collective-permute-start.18
  675.1 2.7 bitcast_convert_fusion
  678.8 2.7 collective-permute-done.18
  684.1 2.6 convolution_convert_fusion.2
  692.6 76.6 %scatter_grads.2 = (f32[256,512]{1,0:T(8,128)}, f32[256,512]{1,0:T(8,128)}, f32[256,256]{1,0:T(8,128)}) custom-call(bf16[8,256,512]{2,1,0:T(8,128)(2,1)} %bitcast.398, bf16[8,256,512]{2,1,0:T(8,128)(2,1)} %bitcast.397, bf16[8,256,256]{2,1,0:T(8,128)(2,1)} %bitcast.409), custom_call_target="tpu_custom_call" | custom-call | tf_op jit(solution)/shard_map/scatter_grads/pallas_call | solution.py:307
  775.6 2.1 collective-permute-start.29
  777.8 2.9 collective-permute-done.29
  780.7 2.0 collective-permute-start.30
  788.8 8.6 %collective-permute-done.25 = bf16[2,1,64,2048]{3,2,0,1:T(8,128)(2,1)S(1)} collective-permute-done((bf16[2,1,64,2048]{3,2,0,1:T(8,128)(2,1)S(1)}, bf16[2,1,64,2048]{3,2,0,1:T(8,128)(2,1)S(1)}, u32[]{:S(2)}, u32[]{:S(2)}) %collective-permute-start.25) | collective-permute-done | bytes 524320 | tf_op jit(solution)/shard_map/ppermute | solution.py:22
  800.4 2.0 copy.123
  803.5 2.6 collective-permute-done.33
  (287 shorter events, 109.4 us)
Async XLA Ops:
  15.0 183.7 %copy-start = (bf16[2,256,2048]{2,1,0:T(8,128)(2,1)S(1)}, bf16[2,256,2048]{2,1,0:T(8,128)(2,1)}, u32[]{:S(2)}) copy-start(bf16[2,256,2048]{2,1,0:T(8,128)(2,1)} %param.12) | copy-start | bytes 6291460
  203.4 20.3 %copy-start.33 = (s32[2,256]{1,0:T(2,128)S(1)}, s32[2,256]{1,0:T(2,128)}, u32[]{:S(2)}) copy-start(s32[2,256]{1,0:T(2,128)} %param.14) | copy-start | bytes 6148
  203.4 20.4 %copy-start.34 = (s32[2,256]{1,0:T(2,128)S(1)}, s32[2,256]{1,0:T(2,128)}, u32[]{:S(2)}) copy-start(s32[2,256]{1,0:T(2,128)} %param.13) | copy-start | bytes 6148
  259.7 2.9 collective-permute-start
  266.1 14.4 %collective-permute-start.1 = (bf16[1,2,1,64,2048]{4,3,2,1,0:T(8,128)(2,1)S(1)}, bf16[1,2,1,64,2048]{4,3,2,1,0:T(8,128)(2,1)}, u32[]{:S(2)}, u32[]{:S(2)}) collective-permute-start(bf16[1,2,1,64,2048]{4,3,2,1,0:T(8,128)(2,1)S(1)} %dynamic-slice_convert_fusion.4), channel_id=1, source_target_pairs={{0,2},{1,3},{2,0},{3,1},{4,6},{5,7},{6,4},{7,5},{8,10},{9,11},{10,... | collective-permute-start | bytes 1572872 | tf_op jit(solution)/shard_map/ppermute | solution.py:22
  282.9 14.2 %collective-permute-start.2 = (bf16[2,64,2048]{2,1,0:T(8,128)(2,1)S(1)}, bf16[2,64,2048]{2,1,0:T(8,128)(2,1)S(1)}, u32[]{:S(2)}, u32[]{:S(2)}) collective-permute-start(bf16[2,64,2048]{2,1,0:T(8,128)(2,1)S(1)} %add_convert_fusion), channel_id=1, source_target_pairs={{0,8},{4,12},{8,0},{12,4},{16,24},{20,28},{24,16},{28,20},{1,9},{5... | collective-permute-start | bytes 1572872 | tf_op jit(solution)/shard_map/ppermute | solution.py:22
  287.0 10.1 %copy-start.12 = (bf16[1,2,64,2048]{3,2,1,0:T(8,128)(2,1)}, bf16[1,2,64,2048]{3,2,1,0:T(8,128)(2,1)S(1)}, u32[]{:S(2)}) copy-start(bf16[1,2,64,2048]{3,2,1,0:T(8,128)(2,1)S(1)} %fusion.43) | copy-start | bytes 1572868
  298.3 24.3 %collective-permute-start.3 = (bf16[2,2,1,64,2048]{4,3,1,0,2:T(8,128)(2,1)}, bf16[2,2,1,64,2048]{4,3,1,0,2:T(8,128)(2,1)}, u32[]{:S(2)}, u32[]{:S(2)}) collective-permute-start(bf16[2,2,1,64,2048]{4,3,1,0,2:T(8,128)(2,1)} %maximum_bitcast_fusion.5), channel_id=1, source_target_pairs={{0,2},{1,3},{2,0},{3,1},{4,6},{5,7},{6,4},{7,5},{8,10},{9,11},{10,... | collective-permute-start | bytes 3145736 | tf_op jit(solution)/shard_map/ppermute | solution.py:22
  326.3 4.5 collective-permute-start.4
  326.3 48.4 %collective-permute-start.10 = (bf16[512,2048]{1,0:T(8,128)(2,1)}, bf16[512,2048]{1,0:T(8,128)(2,1)}, u32[]{:S(2)}, u32[]{:S(2)}) collective-permute-start(bf16[512,2048]{1,0:T(8,128)(2,1)} %bitcast.56), channel_id=1, source_target_pairs={{0,8},{4,12},{8,0},{12,4},{16,24},{20,28},{24,16},{28,20},{1,9},{5... | collective-permute-start | bytes 6291464 | tf_op jit(solution)/shard_map/ppermute | solution.py:22
  337.3 37.3 %copy-start.36 = (bf16[8,256,1024]{2,1,0:T(8,128)(2,1)S(1)}, bf16[8,256,1024]{2,1,0:T(8,128)(2,1)}, u32[]{:S(2)}) copy-start(bf16[8,256,1024]{2,1,0:T(8,128)(2,1)} %get-tuple-element.32) | copy-start | bytes 12582916
  342.7 47.2 %copy-start.40 = (bf16[1024,1024]{1,0:T(8,128)(2,1)}, bf16[1024,1024]{1,0:T(8,128)(2,1)S(1)}, u32[]{:S(2)}) copy-start(bf16[1024,1024]{1,0:T(8,128)(2,1)S(1)} %get-tuple-element.139) | copy-start | bytes 6291460
  389.8 6.9 collective-permute-start.11
  396.6 4.2 collective-permute-start.5
  398.8 26.3 %collective-permute-start.12 = (bf16[2,2,1,64,2048]{4,3,1,2,0:T(8,128)(2,1)}, bf16[2,2,1,64,2048]{4,3,1,2,0:T(8,128)(2,1)}, u32[]{:S(2)}, u32[]{:S(2)}) collective-permute-start(bf16[2,2,1,64,2048]{4,3,1,2,0:T(8,128)(2,1)} %dynamic-slice_convert_fusion), channel_id=1, source_target_pairs={{0,2},{1,3},{2,0},{3,1},{4,6},{5,7},{6,4},{7,5},{8,10},{9,11},{10,... | collective-permute-start | bytes 3145736 | tf_op jit(solution)/shard_map/ppermute | solution.py:22
  404.0 43.2 %collective-permute-start.6 = (bf16[2,2,1,64,2048]{4,3,1,2,0:T(8,128)(2,1)}, bf16[2,2,1,64,2048]{4,3,1,2,0:T(8,128)(2,1)}, u32[]{:S(2)}, u32[]{:S(2)}) collective-permute-start(bf16[2,2,1,64,2048]{4,3,1,2,0:T(8,128)(2,1)} %dynamic-slice_convert_fusion.1), channel_id=1, source_target_pairs={{0,2},{1,3},{2,0},{3,1},{4,6},{5,7},{6,4},{7,5},{8,10},{9,11},{10,... | collective-permute-start | bytes 3145736 | tf_op jit(solution)/shard_map/ppermute | solution.py:22
  405.8 41.4 %copy-start.5 = (f32[2,2,2,64,2048]{4,3,1,2,0:T(8,128)S(1)}, f32[2,2,2,64,2048]{4,3,1,2,0:T(8,128)}, u32[]{:S(2)}) copy-start(f32[2,2,2,64,2048]{4,3,1,2,0:T(8,128)} %copy-done.4) | copy-start | bytes 12582916
  427.4 22.9 %collective-permute-start.13 = (bf16[2,64,2048]{2,1,0:T(8,128)(2,1)S(1)}, bf16[2,64,2048]{2,1,0:T(8,128)(2,1)S(1)}, u32[]{:S(2)}, u32[]{:S(2)}) collective-permute-start(bf16[2,64,2048]{2,1,0:T(8,128)(2,1)S(1)} %fusion.54), channel_id=1, source_target_pairs={{0,8},{4,12},{8,0},{12,4},{16,24},{20,28},{24,16},{28,20},{1,9},{5... | collective-permute-start | bytes 1572872 | tf_op jit(solution)/shard_map/ppermute | solution.py:22
  448.8 13.5 %collective-permute-start.7 = (bf16[2,64,2048]{2,1,0:T(8,128)(2,1)S(1)}, bf16[2,64,2048]{2,1,0:T(8,128)(2,1)S(1)}, u32[]{:S(2)}, u32[]{:S(2)}) collective-permute-start(bf16[2,64,2048]{2,1,0:T(8,128)(2,1)S(1)} %fusion.53), channel_id=1, source_target_pairs={{0,8},{4,12},{8,0},{12,4},{16,24},{20,28},{24,16},{28,20},{1,9},{5... | collective-permute-start | bytes 1572872 | tf_op jit(solution)/shard_map/ppermute | solution.py:22
  466.0 12.8 %collective-permute-start.14 = (bf16[2,1,64,2048]{3,2,0,1:T(8,128)(2,1)S(1)}, bf16[2,1,64,2048]{3,2,0,1:T(8,128)(2,1)}, u32[]{:S(2)}, u32[]{:S(2)}) collective-permute-start(bf16[2,1,64,2048]{3,2,0,1:T(8,128)(2,1)S(1)} %convert_bitcast_fusion.3), channel_id=1, source_target_pairs={{0,2},{1,3},{2,0},{3,1},{4,6},{5,7},{6,4},{7,5},{8,10},{9,11},{10,... | collective-permute-start | bytes 1572872 | tf_op jit(solution)/shard_map/ppermute | solution.py:22
  468.8 12.5 %copy-start.41 = (bf16[1024,1024]{1,0:T(8,128)(2,1)S(1)}, bf16[1024,1024]{1,0:T(8,128)(2,1)}, u32[]{:S(2)}) copy-start(bf16[1024,1024]{1,0:T(8,128)(2,1)} %copy-done.40) | copy-start | bytes 6291460
  481.3 134.6 %collective-permute-start.15 = (bf16[2,2,64,2048]{3,2,0,1:T(8,128)(2,1)}, bf16[2,2,64,2048]{3,2,0,1:T(8,128)(2,1)}, u32[]{:S(2)}, u32[]{:S(2)}) collective-permute-start(bf16[2,2,64,2048]{3,2,0,1:T(8,128)(2,1)} %maximum_bitcast_fusion.7), channel_id=1, source_target_pairs={{0,1},{1,0},{2,3},{3,2},{4,5},{5,4},{6,7},{7,6},{8,9},{9,8},{10,11... | collective-permute-start | bytes 3145736 | tf_op jit(solution)/shard_map/ppermute | solution.py:22
  615.3 25.9 %collective-permute-start.8 = (bf16[2,1,64,2048]{3,2,0,1:T(8,128)(2,1)}, bf16[2,1,64,2048]{3,2,0,1:T(8,128)(2,1)}, u32[]{:S(2)}, u32[]{:S(2)}) collective-permute-start(bf16[2,1,64,2048]{3,2,0,1:T(8,128)(2,1)} %get-tuple-element.132), channel_id=1, source_target_pairs={{0,2},{1,3},{2,0},{3,1},{4,6},{5,7},{6,4},{7,5},{8,10},{9,11},{10,... | collective-permute-start | bytes 1572872 | tf_op jit(solution)/shard_map/ppermute | solution.py:22
  641.0 22.6 %copy-start.17 = (bf16[2,256,512]{2,1,0:T(8,128)(2,1)S(1)}, bf16[2,256,512]{2,1,0:T(8,128)(2,1)}, u32[]{:S(2)}) copy-start(bf16[2,256,512]{2,1,0:T(8,128)(2,1)} %get-tuple-element.34) | copy-start | bytes 1572868
  641.1 22.6 %copy-start.27 = (bf16[8,256,512]{2,1,0:T(8,128)(2,1)S(1)}, bf16[8,256,512]{2,1,0:T(8,128)(2,1)}, u32[]{:S(2)}) copy-start(bf16[8,256,512]{2,1,0:T(8,128)(2,1)} %get-tuple-element.27) | copy-start | bytes 6291460
  641.1 9.2 %collective-permute-start.20 = (bf16[2,256,256]{2,1,0:T(8,128)(2,1)S(1)}, bf16[2,256,256]{2,1,0:T(8,128)(2,1)S(1)}, u32[]{:S(2)}, u32[]{:S(2)}) collective-permute-start(bf16[2,256,256]{2,1,0:T(8,128)(2,1)S(1)} %get-tuple-element.119), channel_id=1, source_target_pairs={{0,4},{4,0},{8,12},{12,8},{16,20},{20,16},{24,28},{28,24},{1,5},{5... | collective-permute-start | bytes 786440 | tf_op jit(solution)/shard_map/ppermute | solution.py:22
  642.5 44.2 %collective-permute-start.9 = (bf16[2,2,64,2048]{3,2,0,1:T(8,128)(2,1)S(1)}, bf16[2,2,64,2048]{3,2,0,1:T(8,128)(2,1)S(1)}, u32[]{:S(2)}, u32[]{:S(2)}) collective-permute-start(bf16[2,2,64,2048]{3,2,0,1:T(8,128)(2,1)S(1)} %maximum_bitcast_fusion.6), channel_id=1, source_target_pairs={{0,1},{1,0},{2,3},{3,2},{4,5},{5,4},{6,7},{7,6},{8,9},{9,8},{10,11... | collective-permute-start | bytes 3145736 | tf_op jit(solution)/shard_map/ppermute | solution.py:22
  642.6 22.3 %collective-permute-start.17 = (bf16[2,256,256]{2,1,0:T(8,128)(2,1)S(1)}, bf16[2,256,256]{2,1,0:T(8,128)(2,1)S(1)}, u32[]{:S(2)}, u32[]{:S(2)}) collective-permute-start(bf16[2,256,256]{2,1,0:T(8,128)(2,1)S(1)} %get-tuple-element.118), channel_id=1, source_target_pairs={{0,4},{4,0},{8,12},{12,8},{16,20},{20,16},{24,28},{28,24},{1,5},{5... | collective-permute-start | bytes 786440 | tf_op jit(solution)/shard_map/ppermute | solution.py:22
  644.5 20.4 %collective-permute-start.19 = (bf16[2,256,256]{2,1,0:T(8,128)(2,1)S(1)}, bf16[2,256,256]{2,1,0:T(8,128)(2,1)S(1)}, u32[]{:S(2)}, u32[]{:S(2)}) collective-permute-start(bf16[2,256,256]{2,1,0:T(8,128)(2,1)S(1)} %get-tuple-element.117), channel_id=1, source_target_pairs={{0,4},{4,0},{8,12},{12,8},{16,20},{20,16},{24,28},{28,24},{1,5},{5... | collective-permute-start | bytes 786440 | tf_op jit(solution)/shard_map/ppermute | solution.py:22
  644.7 33.0 %collective-permute-start.16 = (bf16[2,256,256]{2,1,0:T(8,128)(2,1)S(1)}, bf16[2,256,256]{2,1,0:T(8,128)(2,1)S(1)}, u32[]{:S(2)}, u32[]{:S(2)}) collective-permute-start(bf16[2,256,256]{2,1,0:T(8,128)(2,1)S(1)} %get-tuple-element.116), channel_id=1, source_target_pairs={{0,4},{4,0},{8,12},{12,8},{16,20},{20,16},{24,28},{28,24},{1,5},{5... | collective-permute-start | bytes 786440 | tf_op jit(solution)/shard_map/ppermute | solution.py:22
  650.4 17.6 %collective-permute-start.21 = (bf16[2,256,256]{2,1,0:T(8,128)(2,1)S(1)}, bf16[2,256,256]{2,1,0:T(8,128)(2,1)S(1)}, u32[]{:S(2)}, u32[]{:S(2)}) collective-permute-start(bf16[2,256,256]{2,1,0:T(8,128)(2,1)S(1)} %fusion.56), channel_id=1, source_target_pairs={{0,8},{4,12},{8,0},{12,4},{16,24},{20,28},{24,16},{28,20},{1,9},{5... | collective-permute-start | bytes 786440 | tf_op jit(solution)/shard_map/ppermute | solution.py:22
  663.6 11.4 %copy-start.20 = (bf16[2,256,2048]{2,1,0:T(8,128)(2,1)S(1)}, bf16[2,256,2048]{2,1,0:T(8,128)(2,1)}, u32[]{:S(2)}) copy-start(bf16[2,256,2048]{2,1,0:T(8,128)(2,1)} %copy-done.19) | copy-start | bytes 6291460
  668.1 10.7 %collective-permute-start.22 = (bf16[2,256,256]{2,1,0:T(8,128)(2,1)S(1)}, bf16[2,256,256]{2,1,0:T(8,128)(2,1)S(1)}, u32[]{:S(2)}, u32[]{:S(2)}) collective-permute-start(bf16[2,256,256]{2,1,0:T(8,128)(2,1)S(1)} %get-tuple-element.121), channel_id=1, source_target_pairs={{0,16},{4,20},{8,24},{12,28},{16,0},{20,4},{24,8},{28,12},{1,17},{... | collective-permute-start | bytes 786440 | tf_op jit(solution)/shard_map/ppermute | solution.py:22
  671.5 10.1 %copy-start.29 = (bf16[8,4,64,256]{3,2,1,0:T(8,128)(2,1)S(1)}, bf16[8,4,64,256]{3,2,1,0:T(8,128)(2,1)}, u32[]{:S(2)}) copy-start(bf16[8,4,64,256]{3,2,1,0:T(8,128)(2,1)} %get-tuple-element.28) | copy-start | bytes 3145732
  671.5 10.0 %collective-permute-start.18 = (bf16[2,256,256]{2,1,0:T(8,128)(2,1)S(1)}, bf16[2,256,256]{2,1,0:T(8,128)(2,1)S(1)}, u32[]{:S(2)}, u32[]{:S(2)}) collective-permute-start(bf16[2,256,256]{2,1,0:T(8,128)(2,1)S(1)} %get-tuple-element.120), channel_id=1, source_target_pairs={{0,8},{4,12},{8,0},{12,4},{16,24},{20,28},{24,16},{28,20},{1,9},{5... | collective-permute-start | bytes 786440 | tf_op jit(solution)/shard_map/ppermute | solution.py:22
  682.6 5.6 collective-permute-start.23
  689.4 83.0 %collective-permute-start.24 = (bf16[1,2,1,64,2048]{4,3,1,2,0:T(8,128)(2,1)}, bf16[1,2,1,64,2048]{4,3,1,2,0:T(8,128)(2,1)}, u32[]{:S(2)}, u32[]{:S(2)}) collective-permute-start(bf16[1,2,1,64,2048]{4,3,1,2,0:T(8,128)(2,1)} %dynamic-slice_convert_fusion.3), channel_id=1, source_target_pairs={{0,2},{1,3},{2,0},{3,1},{4,6},{5,7},{6,4},{7,5},{8,10},{9,11},{10,... | collective-permute-start | bytes 1572872 | tf_op jit(solution)/shard_map/ppermute | solution.py:22
  770.1 1.3 collective-permute-start.27
  772.4 10.4 %copy-start.2 = (f32[2,64,2048]{2,1,0:T(8,128)S(1)}, f32[2,64,2048]{2,1,0:T(8,128)}, u32[]{:S(2)}) copy-start(f32[2,64,2048]{2,1,0:T(8,128)} %copy-done.1) | copy-start | bytes 3145732
  775.6 5.1 collective-permute-start.29
  780.7 4.2 collective-permute-start.30
  784.4 13.0 %collective-permute-start.25 = (bf16[2,1,64,2048]{3,2,0,1:T(8,128)(2,1)S(1)}, bf16[2,1,64,2048]{3,2,0,1:T(8,128)(2,1)S(1)}, u32[]{:S(2)}, u32[]{:S(2)}) collective-permute-start(bf16[2,1,64,2048]{3,2,0,1:T(8,128)(2,1)S(1)} %fusion.55), channel_id=1, source_target_pairs={{0,2},{1,3},{2,0},{3,1},{4,6},{5,7},{6,4},{7,5},{8,10},{9,11},{10,... | collective-permute-start | bytes 1572872 | tf_op jit(solution)/shard_map/ppermute | solution.py:22
  785.0 3.8 collective-permute-start.31
  785.6 17.3 %collective-permute-start.28 = (bf16[1,64,256]{2,1,0:T(8,128)(2,1)S(1)}, bf16[1,64,256]{2,1,0:T(8,128)(2,1)S(1)}, u32[]{:S(2)}, u32[]{:S(2)}) collective-permute-start(bf16[1,64,256]{2,1,0:T(8,128)(2,1)S(1)} %dynamic-slice_convert_fusion.5), channel_id=1, source_target_pairs={{0,2},{1,3},{2,0},{3,1},{4,6},{5,7},{6,4},{7,5},{8,10},{9,11},{10,... | collective-permute-start | bytes 98312 | tf_op jit(solution)/shard_map/ppermute | solution.py:22
  788.7 9.9 %copy-start.16 = (bf16[2,1,2,64,2048]{4,3,0,2,1:T(8,128)(2,1)S(1)}, bf16[2,1,2,64,2048]{4,3,0,2,1:T(8,128)(2,1)}, u32[]{:S(2)}) copy-start(bf16[2,1,2,64,2048]{4,3,0,2,1:T(8,128)(2,1)} %get-tuple-element.125) | copy-start | bytes 3145732
  788.7 13.7 %collective-permute-start.32 = (f32[24,128]{1,0:T(8,128)S(1)}, f32[24,128]{1,0:T(8,128)S(1)}, u32[]{:S(2)}, u32[]{:S(2)}) collective-permute-start(f32[24,128]{1,0:T(8,128)S(1)} %add_bitcast_fusion.1), channel_id=1, source_target_pairs={{0,1},{1,0},{2,3},{3,2},{4,5},{5,4},{6,7},{7,6},{8,9},{9,8},{10,11... | collective-permute-start | bytes 36872 | tf_op jit(solution)/shard_map/ppermute | solution.py:22
  798.6 9.3 %collective-permute-start.26 = (bf16[2,2,64,2048]{3,2,0,1:T(8,128)(2,1)}, bf16[2,2,64,2048]{3,2,0,1:T(8,128)(2,1)}, u32[]{:S(2)}, u32[]{:S(2)}) collective-permute-start(bf16[2,2,64,2048]{3,2,0,1:T(8,128)(2,1)} %maximum_bitcast_fusion.8), channel_id=1, source_target_pairs={{0,1},{1,0},{2,3},{3,2},{4,5},{5,4},{6,7},{7,6},{8,9},{9,8},{10,11... | collective-permute-start | bytes 3145736 | tf_op jit(solution)/shard_map/ppermute | solution.py:22
  802.4 3.7 collective-permute-start.33
  (30 other events, 98.6 us)

commit v3 on v2

--- a/solution.py
+++ b/solution.py
@@ -9,6 +9,7 @@
 
 EPS = 1e-05
 NEG = -1e30
+LOG2E = 1.4426950408889634
 LOW = jnp.bfloat16
 F32 = jnp.float32
 
@@ -96,17 +97,106 @@
     ]
 
 
-def weights_kernel(count, tensor, *refs):
-    small_in, kv_in, q_in, o_in, fc_in, pj_in = refs[:6]
-    small_out, kv_out, q_out, o_out, fc_out, pj_out = refs[6:12]
-    send_sem, recv_sem, local_sem = refs[12:]
+def first_kernel(count, tensor, *refs):
+    ins, outs = refs[:3], refs[3:6]
+    send_sem, recv_sem, local_sem = refs[6:]
     index = lax.axis_index("seq")
     place = lax.axis_index("tensor")
-    half = lax.rem(lax.div(index, 2), 2)
-    over = [{"tensor": flip(place, d)} for d in range(1, tensor)]
+    across = [{"tensor": flip(place, tensor >> (i + 1))} for i in range(bits_of(tensor))]
     along = seq_peers(index, count)
     far, near = along[:-1], along[-1]
-    greet(over + along)
+    greet(across + along)
+    wire = Wire(send_sem, recv_sem)
+    own = []
+    targets = [(lambda at, out=out: out.at[at, place]) for out in outs[:2]]
+    targets.append(lambda at: outs[2].at[at])
+    handles = []
+    for source, target in zip(ins, targets):
+        handles.append([wire.copy(source, target(index), peer) for peer in far])
+        handles[-1].append(wire.copy(source, target(index), near))
+        item = pltpu.make_async_copy(source, target(index), local_sem.at[len(own)])
+        item.start()
+        own.append(item)
+    relays = []
+    for a, target in enumerate(targets):
+        for d in range(1, count // 2):
+            wire.arrived(handles[a][d - 1])
+            block = target(flip(index, 2 * d))
+            relays.append(wire.copy(block, block, near))
+        if a == 1:
+            for handle in [handles[0][-1], handles[1][-1]] + relays:
+                wire.arrived(handle)
+            own[0].wait()
+            own[1].wait()
+            masks = [0]
+            for i, peer in enumerate(across):
+                step = tensor >> (i + 1)
+                sent = [
+                    wire.copy(out.at[:, flip(place, mask)], out.at[:, flip(place, mask)], peer)
+                    for mask in masks
+                    for out in outs[:2]
+                ]
+                masks = masks + [mask | step for mask in masks]
+                if i + 1 < len(across):
+                    for handle in sent:
+                        wire.arrived(handle)
+    own[2].wait()
+    wire.finish()
+
+
+def gather_first(small, keyval, query):
+    count, tensor = lax.axis_size("seq"), lax.axis_size("tensor")
+    arrays = (small, keyval, query)
+    shapes = [
+        (count, tensor) + small.shape,
+        (count, tensor) + keyval.shape,
+        (count,) + query.shape,
+    ]
+    copies = 3 * (count - 1) + 2 * (tensor - 1)
+    return pl.pallas_call(
+        partial(first_kernel, count, tensor),
+        out_shape=[jax.ShapeDtypeStruct(shape, LOW) for shape in shapes],
+        in_specs=[pl.BlockSpec(memory_space=pltpu.VMEM)] * 3,
+        out_specs=[pl.BlockSpec(memory_space=pltpu.VMEM)] * 3,
+        scratch_shapes=[
+            pltpu.SemaphoreType.DMA((copies,)),
+            pltpu.SemaphoreType.DMA((copies,)),
+            pltpu.SemaphoreType.DMA((3,)),
+        ],
+        compiler_params=pltpu.CompilerParams(collective_id=0, has_side_effects=True),
+        name="gather_first",
+    )(*arrays)
+
+
+def front_kernel(count, *refs):
+    q_in, kv_in, mq_in, mk_in, x_in, vec_in, o_in, fc_in, pj_in, dy_in = refs[:10]
+    mixed, lse, kv_all, out_t, middle, rows_two, fc_out, pj_out, dy_out = refs[10:19]
+    (
+        top,
+        total,
+        acc,
+        core_keep,
+        core_send,
+        core_got,
+        y_send,
+        y_got,
+        send_sem,
+        recv_sem,
+        local_sem,
+    ) = refs[19:]
+    index = lax.axis_index("seq")
+    place = lax.axis_index("tensor")
+    core = lax.rem(place, 2)
+    side = lax.div(place, 2)
+    half = lax.rem(lax.div(index, 2), 2)
+    other_core = {"tensor": flip(place, 1)}
+    other_side = {"tensor": flip(place, 2)}
+    across = {"tensor": flip(place, 3)}
+    along = seq_peers(index, count)
+    far, near = along[:-1], along[-1]
+    pair = far[0]
+    lines = count // 2
+    greet(along + [other_core, other_side, across])
     wire = Wire(send_sem, recv_sem)
     own = []
 
@@ -115,119 +205,216 @@
         item.start()
         own.append(item)
 
-    first = [wire.copy(kv_in, kv_out.at[index, place], peer) for peer in over]
-    first += [wire.copy(small_in, small_out.at[index, place], peer) for peer in over]
-    keep(kv_in, kv_out.at[index, place])
-    keep(small_in, small_out.at[index, place])
-    hops = []
-
-    def spread(source, out):
-        handles = [wire.copy(source(d), out.at[index], far[d - 1]) for d in range(1, count // 2)]
-        wire.copy(source(0), out.at[index], near)
-        hops.append((out, handles))
-
-    spread(lambda d: q_in, q_out)
-    for item in first:
-        wire.arrived(item)
-    for item in own:
-        item.wait()
-    spread(lambda d: kv_out.at[index], kv_out)
-    spread(lambda d: small_out.at[index], small_out)
-    spread(lambda d: o_in, o_out)
-    spread(lambda d: fc_in.at[flip(half, d & 1)], fc_out)
-    spread(lambda d: pj_in.at[flip(half, d & 1)], pj_out)
-    held = len(own)
-    keep(q_in, q_out.at[index])
-    keep(o_in, o_out.at[index])
+    kv_far = [wire.copy(kv_in.at[core], kv_all.at[core, index], peer) for peer in far]
+    kv_near = wire.copy(kv_in.at[core], kv_all.at[core, index], near)
+    for batch in range(2):
+        keep(kv_in.at[batch], kv_all.at[batch, index])
+    o_far = [wire.copy(o_in, out_t.at[index], peer) for peer in far]
+    o_near = [wire.copy(o_in, out_t.at[index], near)]
+    keep(o_in, out_t.at[index])
+    dy_pair = wire.copy(dy_in.at[place], dy_out.at[place], pair)
+
+    def send_far(source, out):
+        return [
+            wire.copy(source.at[flip(half, d & 1)], out.at[index], far[d - 1])
+            for d in range(1, lines)
+        ]
+
+    fc_far = send_far(fc_in, fc_out)
+    kv_near = [(1, kv_near)]
+    kv_core = []
+    for d in range(1, lines):
+        wire.arrived(kv_far[d - 1])
+        block = kv_all.at[core, flip(index, 2 * d)]
+        kv_near.append((2 * d + 1, wire.copy(block, block, near)))
+        kv_core.append(wire.copy(block, block, other_core))
+    wire.copy(fc_in.at[half], fc_out.at[index], near)
+    wire.copy(pj_in.at[half], pj_out.at[index], near)
     keep(fc_in.at[half], fc_out.at[index])
     keep(pj_in.at[half], pj_out.at[index])
-    for out, handles in hops:
-        for d, handle in enumerate(handles, 1):
-            wire.arrived(handle)
+    for r, handle in kv_near:
+        wire.arrived(handle)
+        block = kv_all.at[core, flip(index, r)]
+        kv_core.append(wire.copy(block, block, other_core))
+    own[0].wait()
+    own[1].wait()
+
+    jobs = [(o_far, out_t, d) for d in range(1, lines)]
+    jobs += [(fc_far, fc_out, d) for d in range(1, lines)]
+
+    def tick(number):
+        for _ in range(min(number, len(jobs))):
+            handles, out, d = jobs.pop(0)
+            wire.arrived(handles[d - 1])
             block = out.at[flip(index, 2 * d)]
-            wire.copy(block, block, near)
-    for item in own[held:]:
+            handle = wire.copy(block, block, near)
+            if out is out_t:
+                o_near.append(handle)
+
+    hd = kv_in.shape[-1] // 2
+    heads = q_in.shape[-1] // hd
+    scale = float(hd) ** (-0.5) * LOG2E
+
+    def attend(batch, block):
+        mask = visible(mq_in[batch], mk_in[batch, block])
+        keys = kv_all[batch, block, :, :hd]
+        values = kv_all[batch, block, :, hd:]
+        for head in range(heads):
+            cols = slice(head * hd, (head + 1) * hd)
+            scores = jnp.where(mask, dot_nt(q_in[batch, :, cols], keys) * scale, NEG)
+            before = top[head]
+            now = jnp.maximum(before, jnp.max(scores, axis=-1, keepdims=True))
+            shrink = jnp.exp2(before - now)
+            probs = jnp.exp2(scores - now)
+            total[head] = total[head] * shrink + jnp.sum(probs, axis=-1, keepdims=True)
+            acc[:, cols] = acc[:, cols] * shrink + dot(probs.astype(LOW), values)
+            top[head] = now
+
+    def attend_batch(batch, ticks):
+        top[...] = jnp.full_like(top, NEG)
+        total[...] = jnp.zeros_like(total)
+        acc[...] = jnp.zeros_like(acc)
+
+        def block_body(block, carry):
+            attend(batch, block)
+            return carry
+
+        parts = len(ticks)
+        for i in range(parts):
+            lax.fori_loop(i * count // parts, (i + 1) * count // parts, block_body, 0)
+            tick(ticks[i])
+        for head in range(heads):
+            cols = slice(head * hd, (head + 1) * hd)
+            mixed[batch, :, cols] = (acc[:, cols] / total[head]).astype(LOW)
+            lse[batch, head] = top[head] + jnp.log2(total[head])
+
+    spread = lines - 1
+    attend_batch(core, [spread // 3, spread - spread // 3])
+    for handle in kv_core:
+        wire.arrived(handle)
+    attend_batch(1 - core, [0, spread // 3])
+    wire.arrived(dy_pair)
+    for peer in (other_core, other_side, across):
+        wire.copy(dy_out.at[place], dy_out.at[place], peer)
+
+    quarter = x_in.shape[0] // 2
+    for handle in o_near:
+        wire.arrived(handle)
+    own[2].wait()
+    width = out_t.shape[1]
+    group = max(1, 256 // width)
+    for which, target in ((1 - core, core_send), (core, core_keep)):
+        rows = [
+            mixed[batch, pl.ds(pl.multiple_of((2 * s + which) * quarter, quarter), quarter), :]
+            for s in range(2)
+            for batch in range(2)
+        ]
+        rows = jnp.concatenate(rows, axis=0)
+
+        def project(i, carry, rows=rows, target=target):
+            cols = pl.ds(pl.multiple_of(i * group * width, group * width), group * width)
+            block = out_t[pl.ds(i * group, group)].reshape(group * width, -1)
+            target[:, cols] = dot_nt(rows, block).astype(target.dtype)
+            return carry
+
+        lax.fori_loop(0, count // group, project, 0)
+        if target is core_send:
+            core_handle = wire.copy(core_send, core_got, other_core)
+    wire.arrived(core_handle)
+    part = 2 * quarter
+    step = 16
+
+    def to_side(i, carry):
+        at = pl.ds(pl.multiple_of((1 - side) * part + i * step, step), step)
+        y_send[pl.ds(pl.multiple_of(i * step, step), step), :] = (
+            core_keep[at, :] + core_got[at, :].astype(F32)
+        ).astype(LOW)
+        return carry
+
+    lax.fori_loop(0, part // step, to_side, 0)
+    y_handle = wire.copy(y_send, y_got, other_side)
+    tick(spread - spread // 3 - 1)
+    wire.arrived(y_handle)
+    out_bias, gain_two, shift_two = vec_in[0:1, :], vec_in[1:2, :], vec_in[2:3, :]
+
+    def norm(i, carry):
+        at = pl.ds(pl.multiple_of(i * step, step), step)
+        far_at = pl.ds(pl.multiple_of(side * part + i * step, step), step)
+        value = core_keep[far_at, :] + core_got[far_at, :].astype(F32)
+        value = value + y_got[at, :].astype(F32)
+        value = x_in[at, :].astype(F32) + value + out_bias
+        middle[at, :] = value
+        centred, inverse = norm_parts(value)
+        rows_two[0, place, at, :] = (centred * inverse * gain_two + shift_two).astype(LOW)
+        return carry
+
+    lax.fori_loop(0, part // step, norm, 0)
+    mine = rows_two.at[0, place]
+    pair_handle = wire.copy(mine, rows_two.at[1, place], pair)
+    side_handle = wire.copy(mine, mine, other_side)
+    wire.copy(mine, mine, other_core)
+    pj_far = send_far(pj_in, pj_out)
+    tick(len(jobs))
+    jobs.extend((pj_far, pj_out, d) for d in range(1, lines))
+    wire.arrived(pair_handle)
+    theirs = rows_two.at[1, place]
+    side_two = wire.copy(theirs, theirs, other_side)
+    wire.copy(theirs, theirs, other_core)
+    wire.arrived(side_handle)
+    block = rows_two.at[0, flip(place, 2)]
+    wire.copy(block, block, other_core)
+    wire.arrived(side_two)
+    block = rows_two.at[1, flip(place, 2)]
+    wire.copy(block, block, other_core)
+    tick(len(jobs))
+    for item in own[3:]:
         item.wait()
     wire.finish()
 
 
-def gather_weights(small, keyval, query, out, fc, proj):
-    count, tensor = lax.axis_size("seq"), lax.axis_size("tensor")
-    arrays = (small, keyval, query, out, fc, proj)
+def front(queries, keyval, meta_q, meta_k, own_rows, vecs, out, fc, proj, grad_rows):
+    count = lax.axis_size("seq")
+    tensor = lax.axis_size("tensor")
+    batches, rows, width = queries.shape
+    two = keyval.shape[2]
+    heads = 2 * width // two
+    part, full = own_rows.shape
     shapes = [
-        (count, tensor) + small.shape,
-        (count, tensor) + keyval.shape,
-        (count,) + query.shape,
-        (count,) + out.shape,
-        (count,) + fc.shape[1:],
-        (count,) + proj.shape[1:],
+        ((batches, rows, width), LOW),
+        ((batches, heads, rows, 1), F32),
+        ((batches, count, rows, two), LOW),
+        ((count,) + out.shape, LOW),
+        ((part, full), F32),
+        ((2, tensor, part, full), LOW),
+        ((count,) + fc.shape[1:], LOW),
+        ((count,) + proj.shape[1:], LOW),
+        ((tensor, part, full), LOW),
     ]
-    copies = 2 * (tensor - 1) + 6 * (count - 1)
+    copies = 2 * (count - 1) + 3 * (count - 1) + 4 + 2 + 7
+    vmem, hbm = pl.BlockSpec(memory_space=pltpu.VMEM), pl.BlockSpec(memory_space=pl.ANY)
     return pl.pallas_call(
-        partial(weights_kernel, count, tensor),
-        out_shape=[jax.ShapeDtypeStruct(shape, LOW) for shape in shapes],
-        in_specs=[pl.BlockSpec(memory_space=pl.ANY)] * 6,
-        out_specs=[pl.BlockSpec(memory_space=pl.ANY)] * 6,
+        partial(front_kernel, count),
+        out_shape=[jax.ShapeDtypeStruct(shape, dtype) for shape, dtype in shapes],
+        in_specs=[vmem] * 6 + [hbm] * 4,
+        out_specs=[vmem] * 6 + [hbm] * 3,
         scratch_shapes=[
+            pltpu.VMEM((heads, rows, 1), F32),
+            pltpu.VMEM((heads, rows, 1), F32),
+            pltpu.VMEM((rows, width), F32),
+            pltpu.VMEM((2 * part, full), F32),
+            pltpu.VMEM((2 * part, full), LOW),
+            pltpu.VMEM((2 * part, full), LOW),
+            pltpu.VMEM((part, full), LOW),
+            pltpu.VMEM((part, full), LOW),
             pltpu.SemaphoreType.DMA((copies,)),
             pltpu.SemaphoreType.DMA((copies,)),
-            pltpu.SemaphoreType.DMA((6,)),
+            pltpu.SemaphoreType.DMA((5,)),
         ],
-        compiler_params=pltpu.CompilerParams(collective_id=0, has_side_effects=True),
-        name="gather_weights",
-    )(*arrays)
-
-
-def keyval_kernel(count, kv_in, kv_out, send_sem, recv_sem, local_sem):
-    index = lax.axis_index("seq")
-    place = lax.axis_index("tensor")
-    core = lax.rem(place, 2)
-    other = {"tensor": flip(place, 1)}
-    along = seq_peers(index, count)
-    far, near = along[:-1], along[-1]
-    greet([other] + along)
-    wire = Wire(send_sem, recv_sem)
-    handles = [
-        wire.copy(kv_in.at[core], kv_out.at[core, index], far[d - 1]) for d in range(1, count // 2)
-    ]
-    own_near = wire.copy(kv_in.at[core], kv_out.at[core, index], near)
-    own = []
-    for batch in range(2):
-        item = pltpu.make_async_copy(kv_in.at[batch], kv_out.at[batch, index], local_sem.at[batch])
-        item.start()
-        own.append(item)
-    relays = [(1, own_near)]
-    for d, handle in enumerate(handles, 1):
-        wire.arrived(handle)
-        block = kv_out.at[core, flip(index, 2 * d)]
-        relays.append((2 * d + 1, wire.copy(block, block, near)))
-        wire.copy(block, block, other)
-    for r, handle in relays:
-        wire.arrived(handle)
-        block = kv_out.at[core, flip(index, r)]
-        wire.copy(block, block, other)
-    for item in own:
-        item.wait()
-    wire.finish()
-
-
-def gather_keyval(keyval):
-    count = lax.axis_size("seq")
-    copies = 2 * (count - 1)
-    batches, rows, two = keyval.shape
-    return pl.pallas_call(
-        partial(keyval_kernel, count),
-        out_shape=jax.ShapeDtypeStruct((batches, count, rows, two), LOW),
-        in_specs=[pl.BlockSpec(memory_space=pltpu.VMEM)],
-        out_specs=pl.BlockSpec(memory_space=pltpu.VMEM),
-        scratch_shapes=[
-            pltpu.SemaphoreType.DMA((copies,)),
-            pltpu.SemaphoreType.DMA((copies,)),
-            pltpu.SemaphoreType.DMA((2,)),
-        ],
-        compiler_params=pltpu.CompilerParams(collective_id=1, has_side_effects=True),
-        name="gather_keyval",
-    )(keyval)
+        compiler_params=pltpu.CompilerParams(
+            collective_id=1, has_side_effects=True, vmem_limit_bytes=56 << 20
+        ),
+        name="front",
+    )(queries, keyval, meta_q, meta_k, own_rows, vecs, out, fc, proj, grad_rows)
 
 
 def scatter_kernel(count, split, arrays, *refs):
@@ -369,80 +556,6 @@
     return ((seg_k == 0) | (seg_k == seg_q)) & (pos_k <= pos_q)
 
 
-def forward_kernel(live_ref, q_ref, kv_ref, mq_ref, mk_ref, o_ref, lse_ref, top, total, acc):
-    batch = pl.program_id(0)
-    hd = kv_ref.shape[-1] // 2
-    heads = q_ref.shape[-1] // hd
-    blocks = kv_ref.shape[1]
-    scale = float(hd) ** (-0.5)
-    top[...] = jnp.full_like(top, NEG)
-    total[...] = jnp.zeros_like(total)
-    acc[...] = jnp.zeros_like(acc)
-
-    def step(index, carry):
-        @pl.when(live_ref[batch, index] > 0)
-        def _():
-            mask = visible(mq_ref[0], mk_ref[0, index])
-            keys = kv_ref[0, index, :, :hd]
-            values = kv_ref[0, index, :, hd:]
-            for head in range(heads):
-                cols = slice(head * hd, (head + 1) * hd)
-                scores = jnp.where(mask, dot_nt(q_ref[0, :, cols], keys) * scale, NEG)
-                before = top[head]
-                now = jnp.maximum(before, jnp.max(scores, axis=-1, keepdims=True))
-                shrink = jnp.exp(before - now)
-                probs = jnp.exp(scores - now)
-                total[head] = total[head] * shrink + jnp.sum(probs, axis=-1, keepdims=True)
-                acc[:, cols] = acc[:, cols] * shrink + dot(probs.astype(LOW), values)
-                top[head] = now
-
-        return carry
-
-    lax.fori_loop(0, blocks, step, 0)
-    for head in range(heads):
-        cols = slice(head * hd, (head + 1) * hd)
-        o_ref[0, :, cols] = (acc[:, cols] / total[head]).astype(LOW)
-        lse_ref[0, head] = top[head] + jnp.log(total[head])
-
-
-def attend_forward(queries, keyval, meta_q, meta_k, live):
-    batches, rows, width = queries.shape
-    _, blocks, keys, two = keyval.shape
-    hd = two // 2
-    heads = width // hd
-    flops = 4 * batches * rows * width * blocks * keys
-    return pl.pallas_call(
-        forward_kernel,
-        grid_spec=pltpu.PrefetchScalarGridSpec(
-            num_scalar_prefetch=1,
-            grid=(batches,),
-            in_specs=[
-                pl.BlockSpec((1, rows, width), lambda b, live: (b, 0, 0)),
-                pl.BlockSpec((1, blocks, keys, two), lambda b, live: (b, 0, 0, 0)),
-                pl.BlockSpec((1, rows, 128), lambda b, live: (b, 0, 0)),
-                pl.BlockSpec((1, blocks, 8, keys), lambda b, live: (b, 0, 0, 0)),
-            ],
-            out_specs=[
-                pl.BlockSpec((1, rows, width), lambda b, live: (b, 0, 0)),
-                pl.BlockSpec((1, heads, rows, 1), lambda b, live: (b, 0, 0, 0)),
-            ],
-            scratch_shapes=[
-                pltpu.VMEM((heads, rows, 1), F32),
-                pltpu.VMEM((heads, rows, 1), F32),
-                pltpu.VMEM((rows, width), F32),
-            ],
-        ),
-        out_shape=[
-            jax.ShapeDtypeStruct((batches, rows, width), LOW),
-            jax.ShapeDtypeStruct((batches, heads, rows, 1), F32),
-        ],
-        name="attend_forward",
-        cost_estimate=pl.CostEstimate(
-            flops=flops, transcendentals=0, bytes_accessed=2 * keyval.size
-        ),
-    )(live, queries, keyval, meta_q, meta_k)
-
-
 def backward_kernel(
     live_ref, q_ref, kv_ref, mq_ref, mk_ref, o_ref, lse_ref, do_ref, dq_ref, dkv_ref, delta, acc
 ):
@@ -451,6 +564,7 @@
     heads = q_ref.shape[-1] // hd
     blocks = kv_ref.shape[1]
     scale = float(hd) ** (-0.5)
+    scale_two = scale * LOG2E
     acc[...] = jnp.zeros_like(acc)
     for head in range(heads):
         cols = slice(head * hd, (head + 1) * hd)
@@ -470,8 +584,8 @@
                 cols = slice(head * hd, (head + 1) * hd)
                 query = q_ref[0, :, cols]
                 grad_o = do_ref[0, :, cols]
-                scores = dot_nt(query, keys) * scale
-                probs = jnp.where(mask, jnp.exp(scores - lse_ref[0, head]), 0.0)
+                scores = dot_nt(query, keys) * scale_two
+                probs = jnp.where(mask, jnp.exp2(scores - lse_ref[0, head]), 0.0)
                 grad_p = dot_nt(grad_o, values)
                 grad_s = (probs * (grad_p - delta[head])).astype(LOW)
                 acc[:, cols] += dot(grad_s, keys)
@@ -600,19 +714,9 @@
     def halves(array):
         return jnp.swapaxes(array.astype(LOW).reshape(width_block, 2, unit_width), 0, 1)
 
-    small, kv_mat, q_mat, out_t, fc_mat, proj_t = gather_weights(
-        packed,
-        w_keyval.astype(LOW),
-        w_query.astype(LOW),
-        w_out.T.astype(LOW),
-        halves(w_fc),
-        halves(w_proj.T),
-    )
+    small, kv_mat, q_mat = gather_first(packed, w_keyval.astype(LOW), w_query.astype(LOW))
     kv_mat = kv_mat.reshape(full_width, 2 * hd)
     q_mat = q_mat.reshape(full_width, group_width)
-    out_t = out_t.reshape(full_width, group_width)
-    fc_mat = fc_mat.reshape(full_width, unit_width)
-    proj_t = proj_t.reshape(full_width, unit_width)
 
     small = small.reshape(seq_size, tensor_size, -1).astype(F32)
     vec_all = small[:, :, cuts[0] : cuts[1]].reshape(seq_size * tensor_size, 7, shard)
@@ -646,52 +750,62 @@
     centred, inverse = norm_parts(residual)
     normed = (centred * inverse * gain_one + shift_one).astype(LOW).reshape(-1, full_width)
     keyval = (dot(normed, kv_mat) + kv_bias).astype(LOW).reshape(batches, rows, 2 * hd)
-    kv_all = gather_keyval(keyval)
     queries = (dot(normed, q_mat) + query_bias).astype(LOW)
     queries = queries.reshape(batches, rows, group_width)
-    mixed, lse = attend_forward(queries, kv_all, meta_q, meta_k, live)
-    mixed_rows = mixed.reshape(-1, group_width)
-
-    def quarters(array):
-        return array.reshape(-1, batches, tensor_size, quarter, array.shape[-1])
+
+    def by_quarter(array):
+        split = array.reshape(batches, tensor_size, quarter, array.shape[-1])
+        return jnp.swapaxes(split, 0, 1).reshape(tensor_size, batches * quarter, -1)
+
+    def by_batch(array):
+        split = array.reshape(tensor_size, batches, quarter, array.shape[-1])
+        return jnp.swapaxes(split, 0, 1).reshape(batches, rows, -1)
 
     def my_quarter(array):
         split = array.reshape(batches, tensor_size, quarter, full_width)
-        return lax.dynamic_index_in_dim(split, tensor_index, 1, keepdims=False)
-
-    def pair_gather(own):
-        both = jnp.stack([own, swap(own, "seq", 1)])
-        return tensor_gather(both, 2).reshape(-1, full_width)
+        own = lax.dynamic_index_in_dim(split, tensor_index, 1, keepdims=False)
+        return own.reshape(batches * quarter, full_width)
 
     def pair_scatter(part):
-        split = quarters(part)
-        got = tensor_scatter(split, 2)
+        got = tensor_scatter(part.reshape(2, tensor_size, batches * quarter, full_width), 1)
         return got[0] + swap(got[1].astype(LOW), "seq", 1).astype(F32)
 
-    attn_sum = tensor_scatter(quarters(dot_nt(mixed_rows, out_t)), 2)[0]
-    middle = my_quarter(inputs).astype(F32) + attn_sum + out_bias
-    centred, inverse = norm_parts(middle)
-    normed_q = (centred * inverse * gain_two + shift_two).astype(LOW)
-    normed_two = pair_gather(normed_q)
+    vecs = jnp.pad(jnp.stack([out_bias, gain_two, shift_two]), ((0, 5), (0, 0)))
+    grad_split = by_quarter(grad_out)
+    mixed, lse, kv_all, out_t, middle, rows_two, fc_mat, proj_t, grad_other = front(
+        queries,
+        keyval,
+        meta_q,
+        meta_k,
+        my_quarter(inputs),
+        vecs,
+        w_out.T.astype(LOW),
+        halves(w_fc),
+        halves(w_proj.T),
+        grad_split,
+    )
+    out_t = out_t.reshape(full_width, group_width)
+    fc_mat = fc_mat.reshape(full_width, unit_width)
+    proj_t = proj_t.reshape(full_width, unit_width)
+    mixed_rows = by_quarter(mixed).reshape(-1, group_width)
+    normed_two = rows_two.reshape(-1, full_width)
     hidden = dot(normed_two, fc_mat) + fc_local
     active_f, slope = gelu_pair(hidden)
     active = active_f.astype(LOW)
 
     grad_q_low = my_quarter(grad_out)
-    grad_flat = jnp.concatenate(
-        [grad_out.reshape(-1, full_width), swap(grad_out.reshape(-1, full_width), "seq", 1)]
-    )
+    grad_flat = jnp.concatenate([grad_split, grad_other]).reshape(-1, full_width)
     grad_hidden = (slope * dot(grad_flat, proj_t)).astype(LOW)
     fcbias_local = jnp.sum(grad_hidden.astype(F32), axis=0)
     back_sum = pair_scatter(dot_nt(grad_hidden, fc_mat))
     grad_q = grad_q_low.astype(F32)
     norm_part, gain_part = norm_back(middle, gain_two, back_sum)
     grad_middle = grad_q + norm_part
-    grad_gain_two = jnp.sum(gain_part, axis=(0, 1))
-    grad_shift_two = jnp.sum(back_sum, axis=(0, 1))
-    grad_out_bias = jnp.sum(grad_middle, axis=(0, 1))
-    grad_proj_bias = jnp.sum(grad_q, axis=(0, 1))
-    grad_middle_low = tensor_gather(grad_middle.astype(LOW), 1).reshape(-1, full_width)
+    grad_gain_two = jnp.sum(gain_part, axis=0)
+    grad_shift_two = jnp.sum(back_sum, axis=0)
+    grad_out_bias = jnp.sum(grad_middle, axis=0)
+    grad_proj_bias = jnp.sum(grad_q, axis=0)
+    grad_middle_low = tensor_gather(grad_middle.astype(LOW), 0).reshape(-1, full_width)
 
     def blocked(array):
         return array.astype(LOW).reshape(seq_size, width_block, array.shape[-1])
@@ -702,9 +816,9 @@
 
     ff_sum = pair_scatter(dot_nt(active, proj_t))
     result_q = (middle + ff_sum + proj_bias).astype(LOW)
-    result = tensor_gather(result_q, 1).reshape(batches, rows, full_width)
-
-    grad_mixed = dot(grad_middle_low, out_t).astype(LOW).reshape(batches, rows, group_width)
+    result = by_batch(tensor_gather(result_q, 0))
+
+    grad_mixed = by_batch(dot(grad_middle_low, out_t).astype(LOW))
     grad_queries, grad_kv_all = attend_backward(
         queries, kv_all, meta_q, meta_k, live, mixed, lse, grad_mixed
     )
@@ -728,13 +842,13 @@
         3,
     )
     grad_normed = dot_nt(grad_queries, q_mat) + dot_nt(grad_keyval, kv_mat)
-    in_sum = tensor_scatter(quarters(grad_normed), 2)[0]
+    in_sum = tensor_scatter(by_quarter(grad_normed), 0)
     residual_q = my_quarter(inputs).astype(F32)
     norm_part, gain_part = norm_back(residual_q, gain_one, in_sum)
     grad_in_q = (grad_middle + norm_part).astype(LOW)
-    input_grad = tensor_gather(grad_in_q, 1).reshape(batches, rows, full_width)
-    grad_gain_one = jnp.sum(gain_part, axis=(0, 1))
-    grad_shift_one = jnp.sum(in_sum, axis=(0, 1))
+    input_grad = by_batch(tensor_gather(grad_in_q, 0))
+    grad_gain_one = jnp.sum(gain_part, axis=0)
+    grad_shift_one = jnp.sum(in_sum, axis=0)
     qbias_local = jnp.sum(grad_queries.astype(F32), axis=0)
     vbias_local = jnp.sum(grad_keyval[:, hd:].astype(F32), axis=0)
 

time: 821 us -> 704 us (0.86)
  waiting for transfers between devices: 169 us -> 86.9 us
  Pallas kernels: 434 us -> 415 us
  matrix products: 60.3 us -> 51 us
    ppermute x34 -> x28, waiting for transfers between devices: 169 us -> 86.9 us  [swap(): return lax.ppermute(value, axis, [(i, i ^ 1 << bit) for i in range(count)])]
    pallas_call x3 -> x2, Pallas kernels: 224 us -> 212 us  [the longest x1 167 us: front(): pl.pallas_call(partial(front_kernel, count), out_shape=[jax.ShapeDtypeStr...]
    unnamed x107 -> x109, local copies, waits for them, and re-layouts: 27.4 us -> 21.9 us
    ppermute x34 -> x28, starting transfers between devices: 49.5 us -> 47.1 us  [swap(): return lax.ppermute(value, axis, [(i, i ^ 1 << bit) for i in range(count)])]
  transfers between devices with their start and end apart: 34 -> 28, of which waited for: 20 -> 14; matrix products, arithmetic and copies ran while one was open for 9% -> 9% of each run, Pallas kernels for 26% -> 29%
where the time goes in v3:
time: 704 us; the launch traced here: 695 us
  Pallas kernels  415 us (59%)
  waiting for transfers between devices  86.9 us (12%)
  matrix products  51 us (7%)
  local copies, waits for them, and re-layouts  50 us (7%)
  starting transfers between devices  47.1 us (7%)
  other arithmetic  43 us (6%)
    pallas_call x2, Pallas kernels, scatter_grads(): pl.pallas_call(partial(scatter_kernel, count, split, arrays), out_shape=[...  190 us
    pallas_call x1, Pallas kernels, front(): pl.pallas_call(partial(front_kernel, count), out_shape=[jax.ShapeDtypeStr...  167 us
    ppermute x28, waiting for transfers between devices, swap(): return lax.ppermute(value, axis, [(i, i ^ 1 << bit) for i in range(count)])  86.9 us
    ppermute x28, starting transfers between devices, swap(): return lax.ppermute(value, axis, [(i, i ^ 1 << bit) for i in range(count)])  47.1 us
    pallas_call x1, Pallas kernels, gather_first(): pl.pallas_call(partial(first_kernel, count, tensor), out_shape=[jax.Shape...  44.5 us
    unnamed x109, local copies, waits for them, and re-layouts  21.9 us
    dot_general x5, matrix products, dot(): return jnp.dot(left, right, preferred_element_type=F32)  20.4 us
    dot_general x5, matrix products, dot_tn(): lax.dot_general(left, right, (((0,), (0,)), ((), ())), preferred_element_...  19.5 us
  transfers between devices with their start and end apart: 28, of which 14 were waited for; matrix products, arithmetic and copies ran while one was open for 9% of the time, Pallas kernels for 29%

profile of v3, /device:TPU:0, one launch (start us, length us, event | category | flops | bytes accessed | tf_op | source)
XLA Modules:
  0.0 695.1 jit_solution(17656991009918433210)
XLA Ops:
  7.2 44.5 %gather_first.1 = (bf16[8,4,32,128]{3,2,1,0:T(8,128)(2,1)}, bf16[8,4,64,256]{3,2,1,0:T(8,128)(2,1)}, bf16[8,256,512]{2,1,0:T(8,128)(2,1)}) custom-call(bf16[32,128]{1,0:T(8,128)(2,1)} %pad_bitcast_fusion.1.refs_0_, bf16[64,256]{1,0:T(8,128)(2,1)} %convert_element_type.312.refs_1_, bf16[256,512]{1,0:T(8,128)(2,1)} %convert_element_type.313.refs_2_), custom_call_target="tpu_custom_call" | custom-call | tf_op jit(solution)/shard_map/gather_first/pallas_call | solution.py:156
  56.2 2.5 copy.149
  58.8 2.3 copy.150
  61.0 2.7 convert_element_type.329
  63.7 2.3 copy.151
  66.0 3.2 copy.152
  70.9 1.9 convert_reduce_fusion.2
  76.2 2.0 fusion.18
  78.9 167.3 %front.1 = (bf16[2,256,512]{2,1,0:T(8,128)(2,1)}, f32[2,4,256,1]{3,2,1,0:T(8,128)}, bf16[2,8,256,256]{3,2,1,0:T(8,128)(2,1)}, bf16[8,256,512]{2,1,0:T(8,128)(2,1...) custom-call(bf16[2,256,512]{2,1,0:T(8,128)(2,1)} %bitcast.354, ...), custom_call_target="tpu_custom_call" | custom-call | tf_op jit(solution)/shard_map/front/pallas_call | solution.py:395
  246.3 3.9 pad_maximum_fusion
  250.2 8.6 %multiply_convert_fusion = (bf16[1024,1024]{1,0:T(8,128)(2,1)S(1)}, f32[1024,1024]{1,0:T(8,128)S(1)}) fusion(f32[1024]{0:T(1024)S(1)} %dynamic_slice.103, bf16[1024,2048]{1,0:T(8,128)(2,1)} %bitcast.381, bf16[2048,1024]{1,0:T(8,128)(2,1)} %bitcast.385), kind=kOutput, calls=%fused_computation.26 | convolution fusion | flops 4305453056 | bytes 14684160 | tf_op jit(solution)/shard_map/dot_general | solution.py:31
  258.9 7.0 %convert_reduce_fusion.1 = (f32[1024]{0:T(1024)S(1)}, bf16[1024,1024]{1,0:T(8,128)(2,1)S(1)}) fusion(bf16[1024,2048]{1,0:T(8,128)(2,1)S(1)} %bitcast.330, bf16[2048,1024]{1,0:T(8,128)(2,1)S(1)} %bitcast.383, f32[1024,1024]{1,0:T(8,128)S(1)} %get-tuple-element.156, f32[1024]{0:T(1024)S(1)} %dynamic_slice.103), kind=kOutput, calls=%fused_computation.25 | convolution fusion | flops 4316986368 | bytes 14688256 | tf_op jit(solution)/shard_map/dot_general | solution.py:31
  265.9 4.6 fusion.56
  270.5 1.9 fusion.16
  272.4 1.9 copy-done.9
  274.3 4.6 fusion.55
  278.9 3.2 copy-done.8
  284.5 2.3 dynamic-slice_convert_fusion.3
  286.8 3.6 bitcast_add_fusion
  290.5 2.2 collective-permute-start.6
  292.7 2.5 bitcast_add_fusion.1
  300.4 16.4 %collective-permute-done.6 = bf16[2,1,128,2048]{3,2,1,0:T(8,128)(2,1)} collective-permute-done((bf16[2,1,128,2048]{3,2,1,0:T(8,128)(2,1)S(1)}, bf16[2,1,128,2048]{3,2,1,0:T(8,128)(2,1)}, u32[]{:S(2)}, u32[]{:S(2)}) %collective-permute-start.6) | collective-permute-done | bytes 1048608 | tf_op jit(solution)/shard_map/ppermute | solution.py:23
  316.8 2.2 convert_add_fusion
  319.2 20.0 %collective-permute-done.1 = bf16[2,1,128,2048]{3,2,1,0:T(8,128)(2,1)} collective-permute-done((bf16[2,1,128,2048]{3,2,1,0:T(8,128)(2,1)}, bf16[2,1,128,2048]{3,2,1,0:T(8,128)(2,1)}, u32[]{:S(2)}, u32[]{:S(2)}) %collective-permute-start.1) | collective-permute-done | bytes 1048608 | tf_op jit(solution)/shard_map/ppermute | solution.py:23
  341.4 13.2 %collective-permute-done.2 = bf16[128,2048]{1,0:T(8,128)(2,1)S(1)} collective-permute-done((bf16[128,2048]{1,0:T(8,128)(2,1)S(1)}, bf16[128,2048]{1,0:T(8,128)(2,1)S(1)}, u32[]{:S(2)}, u32[]{:S(2)}) %collective-permute-start.2) | collective-permute-done | bytes 524320 | tf_op jit(solution)/shard_map/ppermute | solution.py:23
  357.0 6.2 convolution_convert_fusion
  363.2 5.2 collective-permute-done.8
  369.6 6.3 convolution_convert_fusion.1
  375.9 115.3 %scatter_grads.3 = (f32[256,2048]{1,0:T(8,128)}, f32[256,2048]{1,0:T(8,128)}) custom-call(bf16[8,256,1024]{2,1,0:T(8,128)(2,1)} %bitcast.333, bf16[8,256,1024]{2,1,0:T(8,128)(2,1)} %bitcast.332), custom_call_target="tpu_custom_call" | custom-call | tf_op jit(solution)/shard_map/scatter_grads/pallas_call | solution.py:494
  491.1 2.9 copy.173
  497.9 2.1 copy-done.37
  502.1 13.4 %attend_backward.1 = (bf16[2,256,512]{2,1,0:T(8,128)(2,1)}, bf16[2,8,256,256]{3,2,1,0:T(8,128)(2,1)}) custom-call(s32[2,8]{1,0:T(2,128)} %and_convert_fusion.live_ref, bf16[2,256,512]{2,1,0:T(8,128)(2,1)} %bitcast.355, bf16[2,8,256,256]{3,2,1,0:T(8,128)(2,1)} %get-tuple-element.38.kv_ref, s32[2,256,128]{2,1,0:T(8,128)} %pad.23.refs_2_.mq_ref, ...), custom_call_target="tpu_custom_call" | custom-call | flops 5368709120 | bytes 4194304 | tf_op jit(solution)/shard_map/attend_backward/pallas_call | solution.py:615
  518.5 1.8 collective-permute-start.10
  522.3 2.6 collective-permute-done.14
  525.0 17.8 %collective-permute-start.15 = (bf16[2,256,256]{2,1,0:T(8,128)(2,1)S(1)}, bf16[2,256,256]{2,1,0:T(8,128)(2,1)S(1)}, u32[]{:S(2)}, u32[]{:S(2)}) collective-permute-start(bf16[2,256,256]{2,1,0:T(8,128)(2,1)S(1)} %fusion.34), channel_id=1, source_target_pairs={{0,8},{4,12},{8,0},{12,4},{16,24},{20,28},{24,16},{28,20},{1,9},{5... | collective-permute-start | bytes 786440 | tf_op jit(solution)/shard_map/ppermute | solution.py:23
  544.1 3.0 collective-permute-done.15
  547.3 10.3 %collective-permute-start.12 = (bf16[2,256,256]{2,1,0:T(8,128)(2,1)S(1)}, bf16[2,256,256]{2,1,0:T(8,128)(2,1)S(1)}, u32[]{:S(2)}, u32[]{:S(2)}) collective-permute-start(bf16[2,256,256]{2,1,0:T(8,128)(2,1)S(1)} %get-tuple-element.134), channel_id=1, source_target_pairs={{0,8},{4,12},{8,0},{12,4},{16,24},{20,28},{24,16},{28,20},{1,9},{5... | collective-permute-start | bytes 786440 | tf_op jit(solution)/shard_map/ppermute | solution.py:23
  557.6 2.6 bitcast_convert_fusion.2
  560.3 3.9 collective-permute-done.12
  564.2 5.8 collective-permute-done.16
  573.1 2.6 convolution_convert_fusion.2
  580.3 74.3 %scatter_grads.2 = (f32[256,512]{1,0:T(8,128)}, f32[256,512]{1,0:T(8,128)}, f32[256,256]{1,0:T(8,128)}) custom-call(bf16[8,256,512]{2,1,0:T(8,128)(2,1)} %bitcast.343, bf16[8,256,512]{2,1,0:T(8,128)(2,1)} %bitcast.342, bf16[8,256,256]{2,1,0:T(8,128)(2,1)} %bitcast.352), custom_call_target="tpu_custom_call" | custom-call | tf_op jit(solution)/shard_map/scatter_grads/pallas_call | solution.py:494
  661.5 3.3 collective-permute-done.23
  664.8 2.0 collective-permute-start.24
  670.0 2.5 collective-permute-done.25
  672.6 7.7 %collective-permute-done.19 = bf16[1,128,2048]{2,1,0:T(8,128)(2,1)S(1)} collective-permute-done((bf16[1,128,2048]{2,1,0:T(8,128)(2,1)S(1)}, bf16[1,128,2048]{2,1,0:T(8,128)(2,1)S(1)}, u32[]{:S(2)}, u32[]{:S(2)}) %collective-permute-start.19) | collective-permute-done | bytes 524320 | tf_op jit(solution)/shard_map/ppermute | solution.py:23
  682.5 2.0 copy.172
  686.4 1.9 collective-permute-done.27
  (280 shorter events, 70.6 us)
Async XLA Ops:
  0.6 52.4 %copy-start.38 = (f32[128]{0:T(128)S(1)}, f32[128]{0:T(128)}, u32[]{:S(2)}) copy-start(f32[128]{0:T(128)} %param.22) | copy-start | bytes 1540
  0.7 52.4 %copy-start = (bf16[2,256,2048]{2,1,0:T(8,128)(2,1)S(1)}, bf16[2,256,2048]{2,1,0:T(8,128)(2,1)}, u32[]{:S(2)}) copy-start(bf16[2,256,2048]{2,1,0:T(8,128)(2,1)} %param.12) | copy-start | bytes 6291460
  78.9 167.3 %copy-start.1 = (bf16[2,4,64,2048]{3,2,0,1:T(8,128)(2,1)S(1)}, bf16[2,4,64,2048]{3,2,0,1:T(8,128)(2,1)}, u32[]{:S(2)}) copy-start(bf16[2,4,64,2048]{3,2,0,1:T(8,128)(2,1)} %copy.152) | copy-start | bytes 6291460
  250.2 8.6 %copy-start.11 = (bf16[8,128,2048]{2,1,0:T(8,128)(2,1)S(1)}, bf16[8,128,2048]{2,1,0:T(8,128)(2,1)}, u32[]{:S(2)}) copy-start(bf16[8,128,2048]{2,1,0:T(8,128)(2,1)} %pad_maximum_fusion) | copy-start | bytes 12582916
  250.2 8.7 %copy-start.35 = (bf16[8,256,1024]{2,1,0:T(8,128)(2,1)S(1)}, bf16[8,256,1024]{2,1,0:T(8,128)(2,1)}, u32[]{:S(2)}) copy-start(bf16[8,256,1024]{2,1,0:T(8,128)(2,1)} %get-tuple-element.36) | copy-start | bytes 12582916
  258.8 15.5 %copy-start.39 = (bf16[1024,1024]{1,0:T(8,128)(2,1)}, bf16[1024,1024]{1,0:T(8,128)(2,1)S(1)}, u32[]{:S(2)}) copy-start(bf16[1024,1024]{1,0:T(8,128)(2,1)S(1)} %get-tuple-element.155) | copy-start | bytes 6291460
  258.9 7.1 %copy-start.36 = (bf16[8,256,1024]{2,1,0:T(8,128)(2,1)S(1)}, bf16[8,256,1024]{2,1,0:T(8,128)(2,1)}, u32[]{:S(2)}) copy-start(bf16[8,256,1024]{2,1,0:T(8,128)(2,1)} %get-tuple-element.35) | copy-start | bytes 12582916
  272.4 14.4 %collective-permute-start.5 = (bf16[2,2,128,2048]{3,2,1,0:T(8,128)(2,1)}, bf16[2,2,128,2048]{3,2,1,0:T(8,128)(2,1)}, u32[]{:S(2)}, u32[]{:S(2)}) collective-permute-start(bf16[2,2,128,2048]{3,2,1,0:T(8,128)(2,1)} %fusion.16), channel_id=1, source_target_pairs={{0,1},{1,0},{2,3},{3,2},{4,5},{5,4},{6,7},{7,6},{8,9},{9,8},{10,11... | collective-permute-start | bytes 6291464 | tf_op jit(solution)/shard_map/ppermute | solution.py:23
  283.8 9.0 %collective-permute-start = (bf16[2,2,128,2048]{3,2,1,0:T(8,128)(2,1)}, bf16[2,2,128,2048]{3,2,1,0:T(8,128)(2,1)}, u32[]{:S(2)}, u32[]{:S(2)}) collective-permute-start(bf16[2,2,128,2048]{3,2,1,0:T(8,128)(2,1)} %fusion.17), channel_id=1, source_target_pairs={{0,1},{1,0},{2,3},{3,2},{4,5},{5,4},{6,7},{7,6},{8,9},{9,8},{10,11... | collective-permute-start | bytes 6291464 | tf_op jit(solution)/shard_map/ppermute | solution.py:23
  284.5 8.2 %slice-start = ((s8[8388608]{0:T(1024)(128)(4,1)}), s8[4194304]{0:T(1024)(128)(4,1)S(1)}, s32[]{:S(2)}) async-start(s8[8388608]{0:T(1024)(128)(4,1)} %bitcast.326), calls=%async_computation | async-start | bytes 8388608
  290.5 26.3 %collective-permute-start.6 = (bf16[2,1,128,2048]{3,2,1,0:T(8,128)(2,1)S(1)}, bf16[2,1,128,2048]{3,2,1,0:T(8,128)(2,1)}, u32[]{:S(2)}, u32[]{:S(2)}) collective-permute-start(bf16[2,1,128,2048]{3,2,1,0:T(8,128)(2,1)S(1)} %dynamic-slice_convert_fusion), channel_id=1, source_target_pairs={{0,2},{1,3},{2,0},{3,1},{4,6},{5,7},{6,4},{7,5},{8,10},{9,11},{10,... | collective-permute-start | bytes 3145736 | tf_op jit(solution)/shard_map/ppermute | solution.py:23
  297.5 41.6 %collective-permute-start.1 = (bf16[2,1,128,2048]{3,2,1,0:T(8,128)(2,1)}, bf16[2,1,128,2048]{3,2,1,0:T(8,128)(2,1)}, u32[]{:S(2)}, u32[]{:S(2)}) collective-permute-start(bf16[2,1,128,2048]{3,2,1,0:T(8,128)(2,1)} %dynamic-slice_convert_fusion.1), channel_id=1, source_target_pairs={{0,2},{1,3},{2,0},{3,1},{4,6},{5,7},{6,4},{7,5},{8,10},{9,11},{10,... | collective-permute-start | bytes 3145736 | tf_op jit(solution)/shard_map/ppermute | solution.py:23
  300.4 38.7 %copy-start.6 = (f32[2,2,128,2048]{3,2,1,0:T(8,128)S(1)}, f32[2,2,128,2048]{3,2,1,0:T(8,128)}, u32[]{:S(2)}) copy-start(f32[2,2,128,2048]{3,2,1,0:T(8,128)} %copy-done.5) | copy-start | bytes 12582916
  319.1 21.8 %collective-permute-start.7 = (bf16[128,2048]{1,0:T(8,128)(2,1)S(1)}, bf16[128,2048]{1,0:T(8,128)(2,1)S(1)}, u32[]{:S(2)}, u32[]{:S(2)}) collective-permute-start(bf16[128,2048]{1,0:T(8,128)(2,1)S(1)} %fusion.33), channel_id=1, source_target_pairs={{0,8},{4,12},{8,0},{12,4},{16,24},{20,28},{24,16},{28,20},{1,9},{5... | collective-permute-start | bytes 1572872 | tf_op jit(solution)/shard_map/ppermute | solution.py:23
  340.7 13.9 %copy-start.10 = (f32[2,1,64,2048]{3,2,0,1:T(8,128)S(1)}, f32[2,1,64,2048]{3,2,0,1:T(8,128)}, u32[]{:S(2)}) copy-start(f32[2,1,64,2048]{3,2,0,1:T(8,128)} %dynamic-slice_convert_fusion.3) | copy-start | bytes 3145732
  340.8 13.8 %collective-permute-start.2 = (bf16[128,2048]{1,0:T(8,128)(2,1)S(1)}, bf16[128,2048]{1,0:T(8,128)(2,1)S(1)}, u32[]{:S(2)}, u32[]{:S(2)}) collective-permute-start(bf16[128,2048]{1,0:T(8,128)(2,1)S(1)} %fusion.32), channel_id=1, source_target_pairs={{0,8},{4,12},{8,0},{12,4},{16,24},{20,28},{24,16},{28,20},{1,9},{5... | collective-permute-start | bytes 1572872 | tf_op jit(solution)/shard_map/ppermute | solution.py:23
  341.4 15.5 %copy-start.34 = (bf16[2,4,128,2048]{3,2,1,0:T(8,128)(2,1)S(1)}, bf16[2,4,128,2048]{3,2,1,0:T(8,128)(2,1)}, u32[]{:S(2)}) copy-start(bf16[2,4,128,2048]{3,2,1,0:T(8,128)(2,1)} %get-tuple-element.34) | copy-start | bytes 12582916
  341.4 15.5 %copy-start.42 = (bf16[1024,1024]{1,0:T(8,128)(2,1)S(1)}, bf16[1024,1024]{1,0:T(8,128)(2,1)}, u32[]{:S(2)}) copy-start(bf16[1024,1024]{1,0:T(8,128)(2,1)} %copy-done.41) | copy-start | bytes 6291460
  355.4 13.0 %collective-permute-start.8 = (bf16[1,128,2048]{2,1,0:T(8,128)(2,1)S(1)}, bf16[1,128,2048]{2,1,0:T(8,128)(2,1)S(1)}, u32[]{:S(2)}, u32[]{:S(2)}) collective-permute-start(bf16[1,128,2048]{2,1,0:T(8,128)(2,1)S(1)} %convert_bitcast_fusion), channel_id=1, source_target_pairs={{0,2},{1,3},{2,0},{3,1},{4,6},{5,7},{6,4},{7,5},{8,10},{9,11},{10,... | collective-permute-start | bytes 1572872 | tf_op jit(solution)/shard_map/ppermute | solution.py:23
  357.0 12.6 %copy-start.40 = (bf16[1024,1024]{1,0:T(8,128)(2,1)S(1)}, bf16[1024,1024]{1,0:T(8,128)(2,1)}, u32[]{:S(2)}) copy-start(bf16[1024,1024]{1,0:T(8,128)(2,1)} %copy-done.39) | copy-start | bytes 6291460
  369.6 126.5 %collective-permute-start.9 = (bf16[2,128,2048]{2,1,0:T(8,128)(2,1)}, bf16[2,128,2048]{2,1,0:T(8,128)(2,1)}, u32[]{:S(2)}, u32[]{:S(2)}) collective-permute-start(bf16[2,128,2048]{2,1,0:T(8,128)(2,1)} %maximum_bitcast_fusion.4), channel_id=1, source_target_pairs={{0,1},{1,0},{2,3},{3,2},{4,5},{5,4},{6,7},{7,6},{8,9},{9,8},{10,11... | collective-permute-start | bytes 3145736 | tf_op jit(solution)/shard_map/ppermute | solution.py:23
  494.8 22.2 %collective-permute-start.3 = (bf16[1,128,2048]{2,1,0:T(8,128)(2,1)S(1)}, bf16[1,128,2048]{2,1,0:T(8,128)(2,1)}, u32[]{:S(2)}, u32[]{:S(2)}) collective-permute-start(bf16[1,128,2048]{2,1,0:T(8,128)(2,1)S(1)} %get-tuple-element.144), channel_id=1, source_target_pairs={{0,2},{1,3},{2,0},{3,1},{4,6},{5,7},{6,4},{7,5},{8,10},{9,11},{10,... | collective-permute-start | bytes 1572872 | tf_op jit(solution)/shard_map/ppermute | solution.py:23
  516.8 8.1 %copy-start.18 = (bf16[2,8,256,256]{3,2,1,0:T(8,128)(2,1)S(1)}, bf16[2,8,256,256]{3,2,1,0:T(8,128)(2,1)}, u32[]{:S(2)}) copy-start(bf16[2,8,256,256]{3,2,1,0:T(8,128)(2,1)} %get-tuple-element.43) | copy-start | bytes 6291460
  516.8 26.0 %copy-start.15 = (bf16[2,256,512]{2,1,0:T(8,128)(2,1)S(1)}, bf16[2,256,512]{2,1,0:T(8,128)(2,1)}, u32[]{:S(2)}) copy-start(bf16[2,256,512]{2,1,0:T(8,128)(2,1)} %get-tuple-element.42) | copy-start | bytes 1572868
  516.8 26.0 %copy-start.23 = (bf16[8,256,512]{2,1,0:T(8,128)(2,1)S(1)}, bf16[8,256,512]{2,1,0:T(8,128)(2,1)}, u32[]{:S(2)}) copy-start(bf16[8,256,512]{2,1,0:T(8,128)(2,1)} %get-tuple-element.31) | copy-start | bytes 6291460
  516.8 8.1 %collective-permute-start.14 = (bf16[2,256,256]{2,1,0:T(8,128)(2,1)S(1)}, bf16[2,256,256]{2,1,0:T(8,128)(2,1)S(1)}, u32[]{:S(2)}, u32[]{:S(2)}) collective-permute-start(bf16[2,256,256]{2,1,0:T(8,128)(2,1)S(1)} %get-tuple-element.133), channel_id=1, source_target_pairs={{0,4},{4,0},{8,12},{12,8},{16,20},{20,16},{24,28},{28,24},{1,5},{5... | collective-permute-start | bytes 786440 | tf_op jit(solution)/shard_map/ppermute | solution.py:23
  518.4 57.3 %collective-permute-start.4 = (bf16[2,128,2048]{2,1,0:T(8,128)(2,1)S(1)}, bf16[2,128,2048]{2,1,0:T(8,128)(2,1)S(1)}, u32[]{:S(2)}, u32[]{:S(2)}) collective-permute-start(bf16[2,128,2048]{2,1,0:T(8,128)(2,1)S(1)} %maximum_bitcast_fusion.3), channel_id=1, source_target_pairs={{0,1},{1,0},{2,3},{3,2},{4,5},{5,4},{6,7},{7,6},{8,9},{9,8},{10,11... | collective-permute-start | bytes 3145736 | tf_op jit(solution)/shard_map/ppermute | solution.py:23
  518.5 41.8 %collective-permute-start.10 = (bf16[2,256,256]{2,1,0:T(8,128)(2,1)S(1)}, bf16[2,256,256]{2,1,0:T(8,128)(2,1)S(1)}, u32[]{:S(2)}, u32[]{:S(2)}) collective-permute-start(bf16[2,256,256]{2,1,0:T(8,128)(2,1)S(1)} %get-tuple-element.130), channel_id=1, source_target_pairs={{0,4},{4,0},{8,12},{12,8},{16,20},{20,16},{24,28},{28,24},{1,5},{5... | collective-permute-start | bytes 786440 | tf_op jit(solution)/shard_map/ppermute | solution.py:23
  520.3 23.8 %collective-permute-start.13 = (bf16[2,256,256]{2,1,0:T(8,128)(2,1)S(1)}, bf16[2,256,256]{2,1,0:T(8,128)(2,1)S(1)}, u32[]{:S(2)}, u32[]{:S(2)}) collective-permute-start(bf16[2,256,256]{2,1,0:T(8,128)(2,1)S(1)} %get-tuple-element.131), channel_id=1, source_target_pairs={{0,4},{4,0},{8,12},{12,8},{16,20},{20,16},{24,28},{28,24},{1,5},{5... | collective-permute-start | bytes 786440 | tf_op jit(solution)/shard_map/ppermute | solution.py:23
  520.6 23.5 %collective-permute-start.11 = (bf16[2,256,256]{2,1,0:T(8,128)(2,1)S(1)}, bf16[2,256,256]{2,1,0:T(8,128)(2,1)S(1)}, u32[]{:S(2)}, u32[]{:S(2)}) collective-permute-start(bf16[2,256,256]{2,1,0:T(8,128)(2,1)S(1)} %get-tuple-element.132), channel_id=1, source_target_pairs={{0,4},{4,0},{8,12},{12,8},{16,20},{20,16},{24,28},{28,24},{1,5},{5... | collective-permute-start | bytes 786440 | tf_op jit(solution)/shard_map/ppermute | solution.py:23
  525.0 22.2 %collective-permute-start.15 = (bf16[2,256,256]{2,1,0:T(8,128)(2,1)S(1)}, bf16[2,256,256]{2,1,0:T(8,128)(2,1)S(1)}, u32[]{:S(2)}, u32[]{:S(2)}) collective-permute-start(bf16[2,256,256]{2,1,0:T(8,128)(2,1)S(1)} %fusion.34), channel_id=1, source_target_pairs={{0,8},{4,12},{8,0},{12,4},{16,24},{20,28},{24,16},{28,20},{1,9},{5... | collective-permute-start | bytes 786440 | tf_op jit(solution)/shard_map/ppermute | solution.py:23
  542.8 14.8 %copy-start.17 = (bf16[2,256,2048]{2,1,0:T(8,128)(2,1)S(1)}, bf16[2,256,2048]{2,1,0:T(8,128)(2,1)}, u32[]{:S(2)}) copy-start(bf16[2,256,2048]{2,1,0:T(8,128)(2,1)} %copy-done.16) | copy-start | bytes 6291460
  547.3 16.8 %collective-permute-start.12 = (bf16[2,256,256]{2,1,0:T(8,128)(2,1)S(1)}, bf16[2,256,256]{2,1,0:T(8,128)(2,1)S(1)}, u32[]{:S(2)}, u32[]{:S(2)}) collective-permute-start(bf16[2,256,256]{2,1,0:T(8,128)(2,1)S(1)} %get-tuple-element.134), channel_id=1, source_target_pairs={{0,8},{4,12},{8,0},{12,4},{16,24},{20,28},{24,16},{28,20},{1,9},{5... | collective-permute-start | bytes 786440 | tf_op jit(solution)/shard_map/ppermute | solution.py:23
  557.6 12.5 %copy-start.25 = (bf16[8,4,64,256]{3,2,1,0:T(8,128)(2,1)S(1)}, bf16[8,4,64,256]{3,2,1,0:T(8,128)(2,1)}, u32[]{:S(2)}) copy-start(bf16[8,4,64,256]{3,2,1,0:T(8,128)(2,1)} %get-tuple-element.32) | copy-start | bytes 3145732
  557.6 12.3 %collective-permute-start.16 = (bf16[2,256,256]{2,1,0:T(8,128)(2,1)S(1)}, bf16[2,256,256]{2,1,0:T(8,128)(2,1)S(1)}, u32[]{:S(2)}, u32[]{:S(2)}) collective-permute-start(bf16[2,256,256]{2,1,0:T(8,128)(2,1)S(1)} %get-tuple-element.135), channel_id=1, source_target_pairs={{0,16},{4,20},{8,24},{12,28},{16,0},{20,4},{24,8},{28,12},{1,17},{... | collective-permute-start | bytes 786440 | tf_op jit(solution)/shard_map/ppermute | solution.py:23
  571.6 5.6 collective-permute-start.17
  577.6 80.1 %collective-permute-start.18 = (bf16[1,128,2048]{2,1,0:T(8,128)(2,1)S(1)}, bf16[1,128,2048]{2,1,0:T(8,128)(2,1)S(1)}, u32[]{:S(2)}, u32[]{:S(2)}) collective-permute-start(bf16[1,128,2048]{2,1,0:T(8,128)(2,1)S(1)} %dynamic-slice_convert_fusion.2), channel_id=1, source_target_pairs={{0,2},{1,3},{2,0},{3,1},{4,6},{5,7},{6,4},{7,5},{8,10},{9,11},{10,... | collective-permute-start | bytes 1572872 | tf_op jit(solution)/shard_map/ppermute | solution.py:23
  655.5 1.3 collective-permute-start.21
  659.7 5.1 collective-permute-start.23
  664.8 3.9 collective-permute-start.24
  667.3 13.0 %collective-permute-start.19 = (bf16[1,128,2048]{2,1,0:T(8,128)(2,1)S(1)}, bf16[1,128,2048]{2,1,0:T(8,128)(2,1)S(1)}, u32[]{:S(2)}, u32[]{:S(2)}) collective-permute-start(bf16[1,128,2048]{2,1,0:T(8,128)(2,1)S(1)} %fusion.30), channel_id=1, source_target_pairs={{0,2},{1,3},{2,0},{3,1},{4,6},{5,7},{6,4},{7,5},{8,10},{9,11},{10,... | collective-permute-start | bytes 1572872 | tf_op jit(solution)/shard_map/ppermute | solution.py:23
  668.7 3.8 collective-permute-start.25
  668.8 16.9 %collective-permute-start.22 = (bf16[1,64,256]{2,1,0:T(8,128)(2,1)S(1)}, bf16[1,64,256]{2,1,0:T(8,128)(2,1)S(1)}, u32[]{:S(2)}, u32[]{:S(2)}) collective-permute-start(bf16[1,64,256]{2,1,0:T(8,128)(2,1)S(1)} %dynamic-slice_convert_fusion.4), channel_id=1, source_target_pairs={{0,2},{1,3},{2,0},{3,1},{4,6},{5,7},{6,4},{7,5},{8,10},{9,11},{10,... | collective-permute-start | bytes 98312 | tf_op jit(solution)/shard_map/ppermute | solution.py:23
  672.5 8.1 %copy-start.13 = (bf16[1,2,128,2048]{3,2,1,0:T(8,128)(2,1)S(1)}, bf16[1,2,128,2048]{3,2,1,0:T(8,128)(2,1)}, u32[]{:S(2)}) copy-start(bf16[1,2,128,2048]{3,2,1,0:T(8,128)(2,1)} %get-tuple-element.138) | copy-start | bytes 3145732
  672.5 8.1 %copy-start.14 = (bf16[1,2,128,2048]{3,2,1,0:T(8,128)(2,1)S(1)}, bf16[1,2,128,2048]{3,2,1,0:T(8,128)(2,1)}, u32[]{:S(2)}) copy-start(bf16[1,2,128,2048]{3,2,1,0:T(8,128)(2,1)} %get-tuple-element.139) | copy-start | bytes 3145732
  672.5 12.1 %collective-permute-start.26 = (f32[24,128]{1,0:T(8,128)S(1)}, f32[24,128]{1,0:T(8,128)S(1)}, u32[]{:S(2)}, u32[]{:S(2)}) collective-permute-start(f32[24,128]{1,0:T(8,128)S(1)} %add_bitcast_fusion.1), channel_id=1, source_target_pairs={{0,1},{1,0},{2,3},{3,2},{4,5},{5,4},{6,7},{7,6},{8,9},{9,8},{10,11... | collective-permute-start | bytes 36872 | tf_op jit(solution)/shard_map/ppermute | solution.py:23
  680.5 9.5 %collective-permute-start.20 = (bf16[2,128,2048]{2,1,0:T(8,128)(2,1)S(1)}, bf16[2,128,2048]{2,1,0:T(8,128)(2,1)S(1)}, u32[]{:S(2)}, u32[]{:S(2)}) collective-permute-start(bf16[2,128,2048]{2,1,0:T(8,128)(2,1)S(1)} %maximum_bitcast_fusion.5), channel_id=1, source_target_pairs={{0,1},{1,0},{2,3},{3,2},{4,5},{5,4},{6,7},{7,6},{8,9},{9,8},{10,11... | collective-permute-start | bytes 3145736 | tf_op jit(solution)/shard_map/ppermute | solution.py:23
  684.6 3.7 collective-permute-start.27
  (26 other events, 73.3 us)

commit v4 on v3

--- a/solution.py
+++ b/solution.py
@@ -417,6 +417,230 @@
     )(queries, keyval, meta_q, meta_k, own_rows, vecs, out, fc, proj, grad_rows)
 
 
+def by_rows(rows, step, body):
+    def run(i, carry):
+        body(pl.ds(pl.multiple_of(i * step, step), step))
+        return carry
+
+    lax.fori_loop(0, rows // step, run, 0)
+
+
+class SeqSum:
+    def __init__(self, wire, index, peers, part, from_near, to_far, from_far, out, split):
+        self.wire, self.index = wire, index
+        self.far, self.near = peers[:-1], peers[-1]
+        self.lines = len(peers)
+        self.part, self.out, self.split = part, out, split
+        self.from_near, self.to_far, self.from_far = from_near, to_far, from_far
+        self.rows = part.shape[1]
+        self.step = min(64, self.rows)
+        self.near_handles, self.far_handles = {}, {}
+        self.next = 1
+
+    def start(self):
+        for d in list(range(1, self.lines)) + [0]:
+            block = self.part.at[flip(self.index, 2 * d + 1)]
+            self.near_handles[d] = self.wire.copy(block, self.from_near.at[d], self.near)
+
+    def relay(self, number):
+        for _ in range(number):
+            d = self.next
+            self.next += 1
+            self.wire.arrived(self.near_handles[d])
+
+            def join(at, d=d):
+                total = self.part[flip(self.index, 2 * d), at].astype(F32)
+                total = total + self.from_near[d, at].astype(F32)
+                self.to_far[d - 1, at] = total.astype(LOW)
+
+            by_rows(self.rows, self.step, join)
+            self.far_handles[d] = self.wire.copy(
+                self.to_far.at[d - 1], self.from_far.at[d - 1], self.far[d - 1]
+            )
+
+    def close(self):
+        self.wire.arrived(self.near_handles[0])
+        for d in range(1, self.lines):
+            self.wire.arrived(self.far_handles[d])
+        width = self.part.shape[2]
+        half = lax.rem(lax.div(self.index, 2), 2)
+
+        def total(at):
+            same = self.part[self.index, at].astype(F32) + self.from_near[0, at].astype(F32)
+            other = None
+            for d in range(1, self.lines):
+                got = self.from_far[d - 1, at].astype(F32)
+                if self.split and d % 2:
+                    other = got if other is None else other + got
+                else:
+                    same = same + got
+            if self.split:
+                out = self.out
+                out[at, pl.ds(pl.multiple_of(half * width, width), width)] = same
+                out[at, pl.ds(pl.multiple_of((1 - half) * width, width), width)] = other
+            else:
+                self.out[at, :] = same
+
+        by_rows(self.rows, self.step, total)
+
+
+def seq_sum_scratch(part):
+    lines = part.shape[0] // 2
+    return [
+        pltpu.VMEM((depth,) + part.shape[1:], LOW) for depth in (lines, lines - 1, lines - 1)
+    ]
+
+
+class RowSum:
+    def __init__(self, wire, place, pair, part, core_got, y_send, y_got, pair_send, pair_got):
+        self.wire, self.place, self.pair = wire, place, pair
+        self.core, self.side = lax.rem(place, 2), lax.div(place, 2)
+        self.part, self.core_got, self.y_send, self.y_got = part, core_got, y_send, y_got
+        self.pair_send, self.pair_got = pair_send, pair_got
+        self.sides = (1 - self.side, self.side)
+        self.rows = part.shape[2]
+        self.core_handles, self.y_handles = {}, {}
+
+    def start(self):
+        peer = {"tensor": flip(self.place, 1)}
+        for which in range(2):
+            for p in reversed(range(self.part.shape[0])):
+                at = self.sides[which]
+                block = self.part.at[p, 2 * at + 1 - self.core]
+                self.core_handles[p, which] = self.wire.copy(block, self.core_got.at[p, at], peer)
+
+    def both(self, p, which, at):
+        side = self.sides[which]
+        mine = self.part[p, 2 * side + self.core, at, :].astype(F32)
+        return mine + self.core_got[p, side, at, :].astype(F32)
+
+    def to_side(self, p):
+        self.wire.arrived(self.core_handles[p, 0])
+
+        def body(at):
+            self.y_send[p, at, :] = self.both(p, 0, at).astype(LOW)
+
+        by_rows(self.rows, 16, body)
+        peer = {"tensor": flip(self.place, 2)}
+        self.y_handles[p] = self.wire.copy(self.y_send.at[p], self.y_got.at[p], peer)
+
+    def to_pair(self):
+        self.wire.arrived(self.core_handles[1, 1])
+        self.wire.arrived(self.y_handles[1])
+
+        def body(at):
+            total = self.both(1, 1, at) + self.y_got[1, at, :].astype(F32)
+            self.pair_send[at, :] = total.astype(LOW)
+
+        by_rows(self.rows, 16, body)
+        self.pair_handle = self.wire.copy(self.pair_send, self.pair_got, self.pair)
+
+    def ready(self):
+        self.wire.arrived(self.core_handles[0, 1])
+        self.wire.arrived(self.y_handles[0])
+        if self.pair is not None:
+            self.wire.arrived(self.pair_handle)
+
+    def total(self, at):
+        total = self.both(0, 1, at) + self.y_got[0, at, :].astype(F32)
+        if self.pair is not None:
+            total = total + self.pair_got[at, :].astype(F32)
+        return total
+
+
+def row_sum_scratch(part):
+    pairs, _, rows, width = part.shape
+    scratch = [pltpu.VMEM((pairs, 2, rows, width), LOW)]
+    scratch += [pltpu.VMEM((pairs, rows, width), LOW)] * 2
+    if pairs == 2:
+        scratch += [pltpu.VMEM((rows, width), LOW)] * 2
+    return scratch
+
+
+class RowGather:
+    def __init__(self, wire, place, rows):
+        self.wire, self.place, self.rows = wire, place, rows
+
+    def start(self):
+        mine = self.rows.at[self.place]
+        self.side_handle = self.wire.copy(mine, mine, {"tensor": flip(self.place, 2)})
+        self.wire.copy(mine, mine, {"tensor": flip(self.place, 1)})
+
+    def forward(self):
+        self.wire.arrived(self.side_handle)
+        block = self.rows.at[flip(self.place, 2)]
+        self.wire.copy(block, block, {"tensor": flip(self.place, 1)})
+
+
+def sem_scratch(copies):
+    return [pltpu.SemaphoreType.DMA((copies,)), pltpu.SemaphoreType.DMA((copies,))]
+
+
+def middle_kernel(count, *refs):
+    back, proj, centre, dy, vec = refs[:5]
+    proj_sum, grad, rows, sums = refs[5:9]
+    row_refs, seq_refs, (send_sem, recv_sem) = refs[9:14], refs[14:17], refs[17:]
+    index, place = lax.axis_index("seq"), lax.axis_index("tensor")
+    along = seq_peers(index, count)
+    greet(along + [{"tensor": flip(place, 1)}, {"tensor": flip(place, 2)}])
+    wire = Wire(send_sem, recv_sem)
+    reduce = RowSum(wire, place, along[0], back, *row_refs)
+    bulk = SeqSum(wire, index, along, proj, *seq_refs, proj_sum, True)
+    gather = RowGather(wire, place, rows)
+    lines = count // 2
+    reduce.start()
+    bulk.start()
+    reduce.to_side(1)
+    reduce.to_side(0)
+    bulk.relay(1)
+    reduce.to_pair()
+    bulk.relay((lines - 1) // 3)
+    reduce.ready()
+    sums[...] = jnp.zeros_like(sums)
+    gain = vec[0:1, :]
+
+    def body(at):
+        over = reduce.total(at)
+        inner, product = norm_back(centre[at, :], gain, over)
+        value = dy[at, :].astype(F32) + inner
+        grad[at, :] = value
+        rows[place, at, :] = value.astype(LOW)
+        sums[0] += product
+        sums[1] += over
+        sums[2] += value
+
+    by_rows(centre.shape[0], 16, body)
+    gather.start()
+    bulk.relay(lines - 1 - 1 - (lines - 1) // 3)
+    gather.forward()
+    bulk.close()
+    wire.finish()
+
+
+def middle_stage(back, proj, centre, dy, vec):
+    count = lax.axis_size("seq")
+    tensor = lax.axis_size("tensor")
+    part, full = centre.shape
+    vmem = pl.BlockSpec(memory_space=pltpu.VMEM)
+    copies = 2 * count + 12
+    return pl.pallas_call(
+        partial(middle_kernel, count),
+        out_shape=[
+            jax.ShapeDtypeStruct((proj.shape[1], 2 * proj.shape[2]), F32),
+            jax.ShapeDtypeStruct((part, full), F32),
+            jax.ShapeDtypeStruct((tensor, part, full), LOW),
+            jax.ShapeDtypeStruct((3, 16, full), F32),
+        ],
+        in_specs=[vmem] * 5,
+        out_specs=[vmem] * 4,
+        scratch_shapes=row_sum_scratch(back) + seq_sum_scratch(proj) + sem_scratch(copies),
+        compiler_params=pltpu.CompilerParams(
+            collective_id=2, has_side_effects=True, vmem_limit_bytes=60 << 20
+        ),
+        name="middle",
+    )(back, proj, centre, dy, vec)
+
+
 def scatter_kernel(count, split, arrays, *refs):
     parts = refs[:arrays]
     outs = refs[arrays : 2 * arrays]
@@ -797,22 +1021,23 @@
     grad_flat = jnp.concatenate([grad_split, grad_other]).reshape(-1, full_width)
     grad_hidden = (slope * dot(grad_flat, proj_t)).astype(LOW)
     fcbias_local = jnp.sum(grad_hidden.astype(F32), axis=0)
-    back_sum = pair_scatter(dot_nt(grad_hidden, fc_mat))
-    grad_q = grad_q_low.astype(F32)
-    norm_part, gain_part = norm_back(middle, gain_two, back_sum)
-    grad_middle = grad_q + norm_part
-    grad_gain_two = jnp.sum(gain_part, axis=0)
-    grad_shift_two = jnp.sum(back_sum, axis=0)
-    grad_out_bias = jnp.sum(grad_middle, axis=0)
-    grad_proj_bias = jnp.sum(grad_q, axis=0)
-    grad_middle_low = tensor_gather(grad_middle.astype(LOW), 0).reshape(-1, full_width)
+    back_part = dot_nt(grad_hidden, fc_mat).astype(LOW)
+    back_part = back_part.reshape(2, tensor_size, batches * quarter, full_width)
 
     def blocked(array):
         return array.astype(LOW).reshape(seq_size, width_block, array.shape[-1])
 
-    proj_sum, fc_sum = scatter_grads(
-        [blocked(dot_tn(grad_flat, active)), blocked(dot_tn(normed_two, grad_hidden))], True, 2
-    )
+    proj_sum, grad_middle, rows_middle, sums = middle_stage(
+        back_part,
+        blocked(dot_tn(grad_flat, active)),
+        middle,
+        grad_q_low,
+        jnp.pad(gain_two[None], ((0, 7), (0, 0))),
+    )
+    grad_gain_two, grad_shift_two, grad_out_bias = jnp.sum(sums, axis=1)
+    grad_proj_bias = jnp.sum(grad_q_low.astype(F32), axis=0)
+    grad_middle_low = rows_middle.reshape(-1, full_width)
+    (fc_sum,) = scatter_grads([blocked(dot_tn(normed_two, grad_hidden))], True, 4)
 
     ff_sum = pair_scatter(dot_nt(active, proj_t))
     result_q = (middle + ff_sum + proj_bias).astype(LOW)

time: 704 us -> 704 us (level)
  Pallas kernels: 415 us -> 453 us
  waiting for transfers between devices: 86.9 us -> 55.9 us
  matrix products: 51 us -> 63.7 us
  starting transfers between devices: 47.1 us -> 35.6 us
    pallas_call x0 -> x1, Pallas kernels: none -> 69.4 us  [middle_stage(): pl.pallas_call(partial(middle_kernel, count), out_shape=[jax.ShapeDtypeSt...]
    pallas_call x2, Pallas kernels: 190 us -> 156 us  [scatter_grads(): pl.pallas_call(partial(scatter_kernel, count, split, arrays), out_shape=[...]
    ppermute x28 -> x23, waiting for transfers between devices: 86.9 us -> 55.9 us  [swap(): return lax.ppermute(value, axis, [(i, i ^ 1 << bit) for i in range(count)])]
    ppermute x28 -> x23, starting transfers between devices: 47.1 us -> 35.6 us  [swap(): return lax.ppermute(value, axis, [(i, i ^ 1 << bit) for i in range(count)])]
    dot_general x4, matrix products: 11.2 us -> 19 us  [dot_nt(): lax.dot_general(left, right, (((1,), (1,)), ((), ())), preferred_element_...]
    unnamed x109 -> x96, local copies, waits for them, and re-layouts: 21.9 us -> 15.9 us
  transfers between devices with their start and end apart: 28 -> 23, of which waited for: 14 -> 9; matrix products, arithmetic and copies ran while one was open for 9% -> 10% of each run, Pallas kernels for 29% -> 22%
where the time goes in v4:
time: 704 us; the launch traced here: 694 us
  Pallas kernels  453 us (64%)
  matrix products  63.7 us (9%)
  waiting for transfers between devices  55.9 us (8%)
  local copies, waits for them, and re-layouts  43.3 us (6%)
  other arithmetic  41.2 us (6%)
  starting transfers between devices  35.6 us (5%)
    pallas_call x1, Pallas kernels, front(): pl.pallas_call(partial(front_kernel, count), out_shape=[jax.ShapeDtypeStr...  167 us
    pallas_call x2, Pallas kernels, scatter_grads(): pl.pallas_call(partial(scatter_kernel, count, split, arrays), out_shape=[...  156 us
    pallas_call x1, Pallas kernels, middle_stage(): pl.pallas_call(partial(middle_kernel, count), out_shape=[jax.ShapeDtypeSt...  69.4 us
    ppermute x23, waiting for transfers between devices, swap(): return lax.ppermute(value, axis, [(i, i ^ 1 << bit) for i in range(count)])  55.9 us
    pallas_call x1, Pallas kernels, gather_first(): pl.pallas_call(partial(first_kernel, count, tensor), out_shape=[jax.Shape...  44.4 us
    ppermute x23, starting transfers between devices, swap(): return lax.ppermute(value, axis, [(i, i ^ 1 << bit) for i in range(count)])  35.6 us
    dot_general x5, matrix products, dot(): return jnp.dot(left, right, preferred_element_type=F32)  22.4 us
    dot_general x5, matrix products, dot_tn(): lax.dot_general(left, right, (((0,), (0,)), ((), ())), preferred_element_...  22.3 us
  transfers between devices with their start and end apart: 23, of which 9 were waited for; matrix products, arithmetic and copies ran while one was open for 10% of the time, Pallas kernels for 22%

profile of v4, /device:TPU:0, one launch (start us, length us, event | category | flops | bytes accessed | tf_op | source)
XLA Modules:
  0.0 694.4 jit_solution(17642383905960314248)
XLA Ops:
  5.4 1.8 convert_element_type.286.refs_2_
  7.2 44.4 %gather_first.1 = (bf16[8,4,32,128]{3,2,1,0:T(8,128)(2,1)}, bf16[8,4,64,256]{3,2,1,0:T(8,128)(2,1)}, bf16[8,256,512]{2,1,0:T(8,128)(2,1)}) custom-call(bf16[32,128]{1,0:T(8,128)(2,1)} %pad_bitcast_fusion.1.refs_0_, bf16[64,256]{1,0:T(8,128)(2,1)} %convert_element_type.285.refs_1_, bf16[256,512]{1,0:T(8,128)(2,1)} %convert_element_type.286.refs_2_), custom_call_target="tpu_custom_call" | custom-call | tf_op jit(solution)/shard_map/gather_first/pallas_call | solution.py:156
  53.9 1.9 convert_reduce_fusion
  58.6 1.8 copy.142
  64.7 3.2 copy.145
  70.1 2.1 convert_reduce_fusion.2
  74.6 2.0 fusion.17
  77.3 166.9 %front.1 = (bf16[2,256,512]{2,1,0:T(8,128)(2,1)}, f32[2,4,256,1]{3,2,1,0:T(8,128)}, bf16[2,8,256,256]{3,2,1,0:T(8,128)(2,1)}, bf16[8,256,512]{2,1,0:T(8,128)(2,1...) custom-call(bf16[2,256,512]{2,1,0:T(8,128)(2,1)} %bitcast.300, ...), custom_call_target="tpu_custom_call" | custom-call | tf_op jit(solution)/shard_map/front/pallas_call | solution.py:395
  244.2 3.9 pad_maximum_fusion
  248.1 8.6 %multiply_convert_fusion = (bf16[1024,1024]{1,0:T(8,128)(2,1)S(1)}, f32[1024,1024]{1,0:T(8,128)S(1)}) fusion(f32[1024]{0:T(1024)S(1)} %dynamic_slice.95, bf16[1024,2048]{1,0:T(8,128)(2,1)} %bitcast.327, bf16[2048,1024]{1,0:T(8,128)(2,1)} %bitcast.331), kind=kOutput, calls=%fused_computation.24 | convolution fusion | flops 4305453056 | bytes 14684160 | tf_op jit(solution)/shard_map/dot_general | solution.py:31
  256.8 7.4 %convert_reduce_fusion.1 = (f32[1024]{0:T(1024)}, bf16[1024,1024]{1,0:T(8,128)(2,1)S(1)}) fusion(bf16[1024,2048]{1,0:T(8,128)(2,1)S(1)} %bitcast.275, bf16[2048,1024]{1,0:T(8,128)(2,1)S(1)} %bitcast.330, f32[1024,1024]{1,0:T(8,128)S(1)} %get-tuple-element.152, f32[1024]{0:T(1024)S(1)} %dynamic_slice.95), kind=kOutput, calls=%fused_computation.23 | convolution fusion | flops 4316986368 | bytes 14688256 | tf_op jit(solution)/shard_map/dot_general | solution.py:31
  264.2 6.1 convolution_convert_fusion.2
  270.3 6.6 convolution_convert_fusion.1
  276.9 69.4 %middle.1 = (f32[256,2048]{1,0:T(8,128)}, f32[128,2048]{1,0:T(8,128)}, bf16[4,128,2048]{2,1,0:T(8,128)(2,1)}, f32[3,16,2048]{2,1,0:T(8,128)}) custom-call(bf16[2,4,128,2048]{3,2,1,0:T(8,128)(2,1)} %bitcast.277, bf16[8,256,1024]{2,1,0:T(8,128)(2,1)} %bitcast.278, f32[128,2048]{1,0:T(8,128)} %get-tuple-element.35.refs_2_, bf16[128,2048]{1,0:T(8,128)(2,1)} %bitcast.291, ...), custom_call_target="tpu_custom_call" | custom-call | tf_op jit(solution)/shard_map/middle/pallas_call | solution.py:626
  346.4 2.8 convolution_convert_fusion.4
  350.7 16.2 %attend_backward.1 = (bf16[2,256,512]{2,1,0:T(8,128)(2,1)}, bf16[2,8,256,256]{3,2,1,0:T(8,128)(2,1)}) custom-call(s32[2,8]{1,0:T(2,128)} %and_convert_fusion.live_ref, bf16[2,256,512]{2,1,0:T(8,128)(2,1)} %bitcast.301, bf16[2,8,256,256]{3,2,1,0:T(8,128)(2,1)} %get-tuple-element.41.kv_ref, s32[2,256,128]{2,1,0:T(8,128)} %pad.27.refs_2_.mq_ref, ...), custom_call_target="tpu_custom_call" | custom-call | flops 5368709120 | bytes 4194304 | tf_op jit(solution)/shard_map/attend_backward/pallas_call | solution.py:839
  366.9 2.1 dynamic-slice_bitcast_fusion.3
  369.0 5.4 collective-permute-start.5
  374.5 2.0 collective-permute-start.6
  376.5 6.4 fusion.50
  382.9 3.2 copy-done.6
  388.4 8.7 %convolution_convert_fusion = bf16[2048,1024]{1,0:T(8,128)(2,1)} fusion(bf16[1024,2048]{1,0:T(8,128)(2,1)} %bitcast.328, bf16[1024,1024]{1,0:T(8,128)(2,1)S(1)} %copy-done.38), kind=kOutput, calls=%fused_computation.26 | convolution fusion | flops 4297064448 | bytes 10485760 | tf_op jit(solution)/shard_map/dot_general | solution.py:35
  398.8 3.3 fusion.51
  402.1 2.6 bitcast_convert_fusion.1
  405.9 6.0 collective-permute-start.10
  411.9 2.6 convolution_convert_fusion.3
  414.5 3.6 collective-permute-done.10
  418.2 2.1 fusion.34
  420.3 1.7 collective-permute-start.7
  422.1 7.5 %collective-permute-start.11 = (bf16[2,256,256]{2,1,0:T(8,128)(2,1)}, bf16[2,256,256]{2,1,0:T(8,128)(2,1)}, u32[]{:S(2)}, u32[]{:S(2)}) collective-permute-start(bf16[2,256,256]{2,1,0:T(8,128)(2,1)} %get-tuple-element.135), channel_id=1, source_target_pairs={{0,16},{4,20},{8,24},{12,28},{16,0},{20,4},{24,8},{28,12},{1,17},{... | collective-permute-start | bytes 786440 | tf_op jit(solution)/shard_map/ppermute | solution.py:23
  431.0 5.4 collective-permute-done.11
  437.8 3.3 convolution_add_fusion
  441.6 2.0 copy-done.3
  445.3 72.3 %scatter_grads.3 = f32[256,2048]{1,0:T(8,128)} custom-call(bf16[8,256,1024]{2,1,0:T(8,128)(2,1)} %bitcast.274), custom_call_target="tpu_custom_call" | custom-call | tf_op jit(solution)/shard_map/scatter_grads/pallas_call | solution.py:718
  517.5 2.9 copy.164
  520.5 1.8 fusion.15
  522.2 83.7 %scatter_grads.2 = (f32[256,512]{1,0:T(8,128)}, f32[256,512]{1,0:T(8,128)}, f32[256,256]{1,0:T(8,128)}) custom-call(bf16[8,256,512]{2,1,0:T(8,128)(2,1)} %bitcast.288, bf16[8,256,512]{2,1,0:T(8,128)(2,1)} %bitcast.287, bf16[8,256,256]{2,1,0:T(8,128)(2,1)} %bitcast.298), custom_call_target="tpu_custom_call" | custom-call | tf_op jit(solution)/shard_map/scatter_grads/pallas_call | solution.py:718
  606.9 2.0 copy.163
  610.0 2.0 collective-permute-start.17
  612.0 2.2 bitcast_add_fusion.1
  614.4 5.7 bitcast_add_fusion
  620.1 8.2 %collective-permute-done.13 = bf16[1,128,2048]{2,1,0:T(8,128)(2,1)S(1)} collective-permute-done((bf16[1,128,2048]{2,1,0:T(8,128)(2,1)S(1)}, bf16[1,128,2048]{2,1,0:T(8,128)(2,1)S(1)}, u32[]{:S(2)}, u32[]{:S(2)}) %collective-permute-start.13) | collective-permute-done | bytes 524320 | tf_op jit(solution)/shard_map/ppermute | solution.py:23
  629.1 3.4 collective-permute-start.18
  638.6 2.2 collective-permute-start.20
  645.2 13.4 %collective-permute-done.1 = bf16[2,1,128,2048]{3,2,1,0:T(8,128)(2,1)S(1)} collective-permute-done((bf16[2,1,128,2048]{3,2,1,0:T(8,128)(2,1)S(1)}, bf16[2,1,128,2048]{3,2,1,0:T(8,128)(2,1)S(1)}, u32[]{:S(2)}, u32[]{:S(2)}) %collective-permute-start.1) | collective-permute-done | bytes 1048608 | tf_op jit(solution)/shard_map/ppermute | solution.py:23
  658.6 1.9 convert_add_fusion
  663.0 10.6 %collective-permute-done.2 = bf16[128,2048]{1,0:T(8,128)(2,1)} collective-permute-done((bf16[128,2048]{1,0:T(8,128)(2,1)}, bf16[128,2048]{1,0:T(8,128)(2,1)}, u32[]{:S(2)}, u32[]{:S(2)}) %collective-permute-start.2) | collective-permute-done | bytes 524320 | tf_op jit(solution)/shard_map/ppermute | solution.py:23
  676.2 10.1 %collective-permute-done.3 = bf16[1,128,2048]{2,1,0:T(8,128)(2,1)S(1)} collective-permute-done((bf16[1,128,2048]{2,1,0:T(8,128)(2,1)S(1)}, bf16[1,128,2048]{2,1,0:T(8,128)(2,1)S(1)}, u32[]{:S(2)}, u32[]{:S(2)}) %collective-permute-start.3) | collective-permute-done | bytes 524320 | tf_op jit(solution)/shard_map/ppermute | solution.py:23
  (239 shorter events, 57.1 us)
Async XLA Ops:
  0.6 56.7 %copy-start.24 = (s32[2,256]{1,0:T(2,128)S(1)}, s32[2,256]{1,0:T(2,128)}, u32[]{:S(2)}) copy-start(s32[2,256]{1,0:T(2,128)} %param.14) | copy-start | bytes 6148
  0.7 56.9 %copy-start.25 = (s32[2,256]{1,0:T(2,128)S(1)}, s32[2,256]{1,0:T(2,128)}, u32[]{:S(2)}) copy-start(s32[2,256]{1,0:T(2,128)} %param.13) | copy-start | bytes 6148
  0.7 55.2 %copy-start = (bf16[2,256,2048]{2,1,0:T(8,128)(2,1)S(1)}, bf16[2,256,2048]{2,1,0:T(8,128)(2,1)}, u32[]{:S(2)}) copy-start(bf16[2,256,2048]{2,1,0:T(8,128)(2,1)} %param.12) | copy-start | bytes 6291460
  0.7 55.9 %copy-start.17 = (f32[512,256]{1,0:T(8,128)S(1)}, f32[512,256]{1,0:T(8,128)}, u32[]{:S(2)}) copy-start(f32[512,256]{1,0:T(8,128)} %param.17) | copy-start | bytes 1572868
  61.7 6.4 slice-start
  76.6 167.5 %copy-start.1 = (bf16[2,4,64,2048]{3,2,0,1:T(8,128)(2,1)S(1)}, bf16[2,4,64,2048]{3,2,0,1:T(8,128)(2,1)}, u32[]{:S(2)}) copy-start(bf16[2,4,64,2048]{3,2,0,1:T(8,128)(2,1)} %copy.145) | copy-start | bytes 6291460
  248.1 8.6 %copy-start.8 = (bf16[8,128,2048]{2,1,0:T(8,128)(2,1)S(1)}, bf16[8,128,2048]{2,1,0:T(8,128)(2,1)}, u32[]{:S(2)}) copy-start(bf16[8,128,2048]{2,1,0:T(8,128)(2,1)} %pad_maximum_fusion) | copy-start | bytes 12582916
  248.1 8.6 %copy-start.31 = (bf16[8,256,1024]{2,1,0:T(8,128)(2,1)S(1)}, bf16[8,256,1024]{2,1,0:T(8,128)(2,1)}, u32[]{:S(2)}) copy-start(bf16[8,256,1024]{2,1,0:T(8,128)(2,1)} %get-tuple-element.38) | copy-start | bytes 12582916
  256.7 13.6 %copy-start.35 = (bf16[1024,1024]{1,0:T(8,128)(2,1)}, bf16[1024,1024]{1,0:T(8,128)(2,1)S(1)}, u32[]{:S(2)}) copy-start(bf16[1024,1024]{1,0:T(8,128)(2,1)S(1)} %get-tuple-element.151) | copy-start | bytes 6291460
  256.7 7.4 %copy-start.32 = (bf16[8,256,1024]{2,1,0:T(8,128)(2,1)S(1)}, bf16[8,256,1024]{2,1,0:T(8,128)(2,1)}, u32[]{:S(2)}) copy-start(bf16[8,256,1024]{2,1,0:T(8,128)(2,1)} %get-tuple-element.37) | copy-start | bytes 12582916
  264.2 6.1 copy-start.37
  276.9 69.4 %copy-start.34 = (bf16[8,256,512]{2,1,0:T(8,128)(2,1)S(1)}, bf16[8,256,512]{2,1,0:T(8,128)(2,1)}, u32[]{:S(2)}) copy-start(bf16[8,256,512]{2,1,0:T(8,128)(2,1)} %get-tuple-element.45) | copy-start | bytes 6291460
  350.7 25.8 %copy-start.36 = (bf16[1024,1024]{1,0:T(8,128)(2,1)S(1)}, bf16[1024,1024]{1,0:T(8,128)(2,1)}, u32[]{:S(2)}) copy-start(bf16[1024,1024]{1,0:T(8,128)(2,1)} %copy-done.35) | copy-start | bytes 6291460
  369.0 62.0 %collective-permute-start.5 = (bf16[2,256,256]{2,1,0:T(8,128)(2,1)}, bf16[2,256,256]{2,1,0:T(8,128)(2,1)}, u32[]{:S(2)}, u32[]{:S(2)}) collective-permute-start(bf16[2,256,256]{2,1,0:T(8,128)(2,1)} %get-tuple-element.130), channel_id=1, source_target_pairs={{0,4},{4,0},{8,12},{12,8},{16,20},{20,16},{24,28},{28,24},{1,5},{5... | collective-permute-start | bytes 786440 | tf_op jit(solution)/shard_map/ppermute | solution.py:23
  374.4 40.1 %collective-permute-start.8 = (bf16[2,256,256]{2,1,0:T(8,128)(2,1)}, bf16[2,256,256]{2,1,0:T(8,128)(2,1)}, u32[]{:S(2)}, u32[]{:S(2)}) collective-permute-start(bf16[2,256,256]{2,1,0:T(8,128)(2,1)} %get-tuple-element.131), channel_id=1, source_target_pairs={{0,4},{4,0},{8,12},{12,8},{16,20},{20,16},{24,28},{28,24},{1,5},{5... | collective-permute-start | bytes 786440 | tf_op jit(solution)/shard_map/ppermute | solution.py:23
  374.5 40.1 %collective-permute-start.6 = (bf16[2,256,256]{2,1,0:T(8,128)(2,1)}, bf16[2,256,256]{2,1,0:T(8,128)(2,1)}, u32[]{:S(2)}, u32[]{:S(2)}) collective-permute-start(bf16[2,256,256]{2,1,0:T(8,128)(2,1)} %get-tuple-element.132), channel_id=1, source_target_pairs={{0,4},{4,0},{8,12},{12,8},{16,20},{20,16},{24,28},{28,24},{1,5},{5... | collective-permute-start | bytes 786440 | tf_op jit(solution)/shard_map/ppermute | solution.py:23
  376.5 28.3 %collective-permute-start.9 = (bf16[2,256,256]{2,1,0:T(8,128)(2,1)S(1)}, bf16[2,256,256]{2,1,0:T(8,128)(2,1)}, u32[]{:S(2)}, u32[]{:S(2)}) collective-permute-start(bf16[2,256,256]{2,1,0:T(8,128)(2,1)S(1)} %get-tuple-element.133), channel_id=1, source_target_pairs={{0,4},{4,0},{8,12},{12,8},{16,20},{20,16},{24,28},{28,24},{1,5},{5... | collective-permute-start | bytes 786440 | tf_op jit(solution)/shard_map/ppermute | solution.py:23
  387.7 226.7 %collective-permute-start = (bf16[2,2,128,2048]{3,2,1,0:T(8,128)(2,1)}, bf16[2,2,128,2048]{3,2,1,0:T(8,128)(2,1)}, u32[]{:S(2)}, u32[]{:S(2)}) collective-permute-start(bf16[2,2,128,2048]{3,2,1,0:T(8,128)(2,1)} %fusion.16), channel_id=1, source_target_pairs={{0,1},{1,0},{2,3},{3,2},{4,5},{5,4},{6,7},{7,6},{8,9},{9,8},{10,11... | collective-permute-start | bytes 6291464 | tf_op jit(solution)/shard_map/ppermute | solution.py:23
  388.4 8.7 %copy-start.2 = (bf16[2,1,64,2048]{3,2,1,0:T(8,128)(2,1)S(1)}, bf16[2,1,64,2048]{3,2,1,0:T(8,128)(2,1)}, u32[]{:S(2)}) copy-start(bf16[2,1,64,2048]{3,2,1,0:T(8,128)(2,1)} %get-tuple-element.127) | copy-start | bytes 1572868
  388.4 9.6 %copy-start.19 = (bf16[2,256,512]{2,1,0:T(8,128)(2,1)S(1)}, bf16[2,256,512]{2,1,0:T(8,128)(2,1)}, u32[]{:S(2)}) copy-start(bf16[2,256,512]{2,1,0:T(8,128)(2,1)} %get-tuple-element.42.o_ref) | copy-start | bytes 1572868
  388.4 10.4 %copy-start.9 = (bf16[2,256,512]{2,1,0:T(8,128)(2,1)S(1)}, bf16[2,256,512]{2,1,0:T(8,128)(2,1)}, u32[]{:S(2)}) copy-start(bf16[2,256,512]{2,1,0:T(8,128)(2,1)} %get-tuple-element.46) | copy-start | bytes 1572868
  388.4 10.4 %copy-start.13 = (bf16[8,256,512]{2,1,0:T(8,128)(2,1)S(1)}, bf16[8,256,512]{2,1,0:T(8,128)(2,1)}, u32[]{:S(2)}) copy-start(bf16[8,256,512]{2,1,0:T(8,128)(2,1)} %get-tuple-element.33) | copy-start | bytes 6291460
  402.1 9.8 %copy-start.20 = (bf16[2,4,64,512]{3,2,0,1:T(8,128)(2,1)S(1)}, bf16[2,4,64,512]{3,2,0,1:T(8,128)(2,1)}, u32[]{:S(2)}) copy-start(bf16[2,4,64,512]{3,2,0,1:T(8,128)(2,1)} %copy.159) | copy-start | bytes 1572868
  402.1 9.8 %copy-start.33 = (bf16[4,128,2048]{2,1,0:T(8,128)(2,1)S(1)}, bf16[4,128,2048]{2,1,0:T(8,128)(2,1)}, u32[]{:S(2)}) copy-start(bf16[4,128,2048]{2,1,0:T(8,128)(2,1)} %get-tuple-element.44) | copy-start | bytes 6291460
  405.9 12.3 %collective-permute-start.10 = (bf16[2,256,256]{2,1,0:T(8,128)(2,1)S(1)}, bf16[2,256,256]{2,1,0:T(8,128)(2,1)S(1)}, u32[]{:S(2)}, u32[]{:S(2)}) collective-permute-start(bf16[2,256,256]{2,1,0:T(8,128)(2,1)S(1)} %fusion.31), channel_id=1, source_target_pairs={{0,8},{4,12},{8,0},{12,4},{16,24},{20,28},{24,16},{28,20},{1,9},{5... | collective-permute-start | bytes 786440 | tf_op jit(solution)/shard_map/ppermute | solution.py:23
  411.9 18.3 %copy-start.21 = (f32[3,16,2048]{2,1,0:T(8,128)S(1)}, f32[3,16,2048]{2,1,0:T(8,128)}, u32[]{:S(2)}) copy-start(f32[3,16,2048]{2,1,0:T(8,128)} %get-tuple-element.52) | copy-start | bytes 1179652
  420.3 10.7 %collective-permute-start.7 = (bf16[2,256,256]{2,1,0:T(8,128)(2,1)}, bf16[2,256,256]{2,1,0:T(8,128)(2,1)}, u32[]{:S(2)}, u32[]{:S(2)}) collective-permute-start(bf16[2,256,256]{2,1,0:T(8,128)(2,1)} %get-tuple-element.134), channel_id=1, source_target_pairs={{0,8},{4,12},{8,0},{12,4},{16,24},{20,28},{24,16},{28,20},{1,9},{5... | collective-permute-start | bytes 786440 | tf_op jit(solution)/shard_map/ppermute | solution.py:23
  422.1 14.4 %collective-permute-start.11 = (bf16[2,256,256]{2,1,0:T(8,128)(2,1)}, bf16[2,256,256]{2,1,0:T(8,128)(2,1)}, u32[]{:S(2)}, u32[]{:S(2)}) collective-permute-start(bf16[2,256,256]{2,1,0:T(8,128)(2,1)} %get-tuple-element.135), channel_id=1, source_target_pairs={{0,16},{4,20},{8,24},{12,28},{16,0},{20,4},{24,8},{28,12},{1,17},{... | collective-permute-start | bytes 786440 | tf_op jit(solution)/shard_map/ppermute | solution.py:23
  430.3 14.5 %copy-start.22 = (f32[3,2048]{1,0:T(4,128)}, f32[3,2048]{1,0:T(4,128)S(1)}, u32[]{:S(2)}) copy-start(f32[3,2048]{1,0:T(4,128)S(1)} %reduce_sum.126) | copy-start | bytes 73732
  444.6 167.3 %collective-permute-start.12 = (bf16[2,128,2048]{2,1,0:T(8,128)(2,1)}, bf16[2,128,2048]{2,1,0:T(8,128)(2,1)}, u32[]{:S(2)}, u32[]{:S(2)}) collective-permute-start(bf16[2,128,2048]{2,1,0:T(8,128)(2,1)} %fusion.21), channel_id=1, source_target_pairs={{0,1},{1,0},{2,3},{3,2},{4,5},{5,4},{6,7},{7,6},{8,9},{9,8},{10,11... | collective-permute-start | bytes 3145736 | tf_op jit(solution)/shard_map/ppermute | solution.py:23
  445.2 75.2 %copy-start.26 = (f32[512]{0:T(512)S(1)}, f32[512]{0:T(512)}, u32[]{:S(2)}) copy-start(f32[512]{0:T(512)} %convert_reduce_fusion.4) | copy-start | bytes 6148
  606.8 2.2 collective-permute-start.16
  610.0 26.3 %collective-permute-start.17 = (bf16[1,64,256]{2,1,0:T(8,128)(2,1)S(1)}, bf16[1,64,256]{2,1,0:T(8,128)(2,1)S(1)}, u32[]{:S(2)}, u32[]{:S(2)}) collective-permute-start(bf16[1,64,256]{2,1,0:T(8,128)(2,1)S(1)} %dynamic-slice_convert_fusion.2), channel_id=1, source_target_pairs={{0,2},{1,3},{2,0},{3,1},{4,6},{5,7},{6,4},{7,5},{8,10},{9,11},{10,... | collective-permute-start | bytes 98312 | tf_op jit(solution)/shard_map/ppermute | solution.py:23
  614.2 14.1 %collective-permute-start.13 = (bf16[1,128,2048]{2,1,0:T(8,128)(2,1)S(1)}, bf16[1,128,2048]{2,1,0:T(8,128)(2,1)S(1)}, u32[]{:S(2)}, u32[]{:S(2)}) collective-permute-start(bf16[1,128,2048]{2,1,0:T(8,128)(2,1)S(1)} %dynamic-slice_convert_fusion.1), channel_id=1, source_target_pairs={{0,2},{1,3},{2,0},{3,1},{4,6},{5,7},{6,4},{7,5},{8,10},{9,11},{10,... | collective-permute-start | bytes 1572872 | tf_op jit(solution)/shard_map/ppermute | solution.py:23
  620.1 8.9 %slice-start.1 = ((f32[3,2048]{1,0:T(4,128)}), f32[2,2048]{1,0:T(2,128)S(1)}, s32[]{:S(2)}) async-start(f32[3,2048]{1,0:T(4,128)} %copy-done.22), calls=%async_computation.1 | async-start | bytes 32768 | tf_op jit(solution)/shard_map/unstack | solution.py:1037
  629.1 32.3 %copy-start.15 = (f32[128,2048]{1,0:T(8,128)S(1)}, f32[128,2048]{1,0:T(8,128)}, u32[]{:S(2)}) copy-start(f32[128,2048]{1,0:T(8,128)} %get-tuple-element.40) | copy-start | bytes 3145732
  629.1 5.5 collective-permute-start.18
  634.3 24.3 %collective-permute-start.1 = (bf16[2,1,128,2048]{3,2,1,0:T(8,128)(2,1)S(1)}, bf16[2,1,128,2048]{3,2,1,0:T(8,128)(2,1)S(1)}, u32[]{:S(2)}, u32[]{:S(2)}) collective-permute-start(bf16[2,1,128,2048]{3,2,1,0:T(8,128)(2,1)S(1)} %dynamic-slice_convert_fusion), channel_id=1, source_target_pairs={{0,2},{1,3},{2,0},{3,1},{4,6},{5,7},{6,4},{7,5},{8,10},{9,11},{10,... | collective-permute-start | bytes 3145736 | tf_op jit(solution)/shard_map/ppermute | solution.py:23
  634.7 3.9 collective-permute-start.19
  638.6 3.9 collective-permute-start.20
  642.4 1.2 collective-permute-start.21
  643.6 30.0 %copy-start.7 = (f32[128,2048]{1,0:T(8,128)S(1)}, f32[128,2048]{1,0:T(8,128)}, u32[]{:S(2)}) copy-start(f32[128,2048]{1,0:T(8,128)} %get-tuple-element.35.refs_2_) | copy-start | bytes 3145732
  643.6 18.8 %collective-permute-start.22 = (f32[24,128]{1,0:T(8,128)S(1)}, f32[24,128]{1,0:T(8,128)S(1)}, u32[]{:S(2)}, u32[]{:S(2)}) collective-permute-start(f32[24,128]{1,0:T(8,128)S(1)} %add.331), channel_id=1, source_target_pairs={{0,2},{1,3},{2,0},{3,1},{4,6},{5,7},{6,4},{7,5},{8,10},{9,11},{10,... | collective-permute-start | bytes 36872 | tf_op jit(solution)/shard_map/ppermute | solution.py:23
  661.4 12.2 %collective-permute-start.2 = (bf16[128,2048]{1,0:T(8,128)(2,1)}, bf16[128,2048]{1,0:T(8,128)(2,1)}, u32[]{:S(2)}, u32[]{:S(2)}) collective-permute-start(bf16[128,2048]{1,0:T(8,128)(2,1)} %fusion.30), channel_id=1, source_target_pairs={{0,8},{4,12},{8,0},{12,4},{16,24},{20,28},{24,16},{28,20},{1,9},{5... | collective-permute-start | bytes 1572872 | tf_op jit(solution)/shard_map/ppermute | solution.py:23
  662.0 14.0 %collective-permute-start.14 = (bf16[1,128,2048]{2,1,0:T(8,128)(2,1)S(1)}, bf16[1,128,2048]{2,1,0:T(8,128)(2,1)S(1)}, u32[]{:S(2)}, u32[]{:S(2)}) collective-permute-start(bf16[1,128,2048]{2,1,0:T(8,128)(2,1)S(1)} %fusion.28), channel_id=1, source_target_pairs={{0,2},{1,3},{2,0},{3,1},{4,6},{5,7},{6,4},{7,5},{8,10},{9,11},{10,... | collective-permute-start | bytes 1572872 | tf_op jit(solution)/shard_map/ppermute | solution.py:23
  675.2 11.1 %collective-permute-start.3 = (bf16[1,128,2048]{2,1,0:T(8,128)(2,1)S(1)}, bf16[1,128,2048]{2,1,0:T(8,128)(2,1)S(1)}, u32[]{:S(2)}, u32[]{:S(2)}) collective-permute-start(bf16[1,128,2048]{2,1,0:T(8,128)(2,1)S(1)} %fusion.29), channel_id=1, source_target_pairs={{0,2},{1,3},{2,0},{3,1},{4,6},{5,7},{6,4},{7,5},{8,10},{9,11},{10,... | collective-permute-start | bytes 1572872 | tf_op jit(solution)/shard_map/ppermute | solution.py:23
  676.1 11.8 %collective-permute-start.15 = (bf16[2,128,2048]{2,1,0:T(8,128)(2,1)S(1)}, bf16[2,128,2048]{2,1,0:T(8,128)(2,1)S(1)}, u32[]{:S(2)}, u32[]{:S(2)}) collective-permute-start(bf16[2,128,2048]{2,1,0:T(8,128)(2,1)S(1)} %maximum_bitcast_fusion.3), channel_id=1, source_target_pairs={{0,1},{1,0},{2,3},{3,2},{4,5},{5,4},{6,7},{7,6},{8,9},{9,8},{10,11... | collective-permute-start | bytes 3145736 | tf_op jit(solution)/shard_map/ppermute | solution.py:23
  686.6 3.4 collective-permute-start.4
  (16 other events, 50.4 us)

commit v5 on v4

--- a/solution.py
+++ b/solution.py
@@ -437,8 +437,8 @@
         self.near_handles, self.far_handles = {}, {}
         self.next = 1
 
-    def start(self):
-        for d in list(range(1, self.lines)) + [0]:
+    def start(self, order=None):
+        for d in order or list(range(1, self.lines)) + [0]:
             block = self.part.at[flip(self.index, 2 * d + 1)]
             self.near_handles[d] = self.wire.copy(block, self.from_near.at[d], self.near)
 
@@ -641,124 +641,228 @@
     )(back, proj, centre, dy, vec)
 
 
-def scatter_kernel(count, split, arrays, *refs):
-    parts = refs[:arrays]
-    outs = refs[arrays : 2 * arrays]
-    from_near = refs[2 * arrays : 3 * arrays]
-    to_far = refs[3 * arrays : 4 * arrays]
-    from_far = refs[4 * arrays : 5 * arrays]
-    send_sem, recv_sem = refs[5 * arrays :]
-    index = lax.axis_index("seq")
-    half = lax.rem(lax.div(index, 2), 2)
+def back_kernel(count, *refs):
+    feed, fc, q_in, kv_in, mq_in, mk_in, mixed, lse, grad_o_in, centre, vec = refs[:11]
+    fc_sum, dq, dkv, result = refs[11:15]
+    row_refs, seq_refs, kv_refs = refs[15:20], refs[20:23], refs[23:26]
+    kv_send, kv_got, kv_part, kv_total, delta, acc, send_sem, recv_sem = refs[26:]
+    index, place = lax.axis_index("seq"), lax.axis_index("tensor")
+    core = lax.rem(place, 2)
+    other_core = {"tensor": flip(place, 1)}
     along = seq_peers(index, count)
-    far, near = along[:-1], along[-1]
     lines = count // 2
-    greet(along)
+    spread = lines - 1
+    greet(along + [other_core, {"tensor": flip(place, 2)}])
     wire = Wire(send_sem, recv_sem)
-    turn = list(range(1, lines)) + [0]
-    near_handles, far_handles = {}, {}
-    for a in range(arrays):
-        for d in turn:
-            block = parts[a].at[flip(index, 2 * d + 1)]
-            near_handles[a, d] = wire.copy(block, from_near[a].at[d], near)
-    rows = parts[0].shape[1]
-    step = min(64, rows)
-
-    def by_rows(body):
-        def run(i, carry):
-            body(pl.ds(pl.multiple_of(i * step, step), step))
+    reduce = RowSum(wire, place, along[0], feed, *row_refs)
+    bulk = SeqSum(wire, index, along, fc, *seq_refs, fc_sum, True)
+    keys_sum = SeqSum(wire, index, along, kv_part, *kv_refs, kv_total, False)
+    gather = RowGather(wire, place, result)
+    hd = kv_in.shape[-1] // 2
+    heads = q_in.shape[-1] // hd
+    scale = float(hd) ** (-0.5)
+    scale_two = scale * LOG2E
+    near_x = 1 - lax.rem(index, 2)
+
+    def open_batch(batch):
+        acc[...] = jnp.zeros_like(acc)
+        for head in range(heads):
+            cols = slice(head * hd, (head + 1) * hd)
+            product = grad_o_in[batch, :, cols].astype(F32) * mixed[batch, :, cols].astype(F32)
+            delta[head] = jnp.sum(product, axis=-1, keepdims=True)
+
+    def blocks_of(batch, which, target, extra):
+        def body(line, carry):
+            block = 2 * line + which
+            mask = visible(mq_in[batch], mk_in[batch, block])
+            keys = kv_in[batch, block, :, :hd]
+            values = kv_in[batch, block, :, hd:]
+            grad_k = jnp.zeros((keys.shape[0], hd), F32)
+            grad_v = jnp.zeros((keys.shape[0], hd), F32)
+            for head in range(heads):
+                cols = slice(head * hd, (head + 1) * hd)
+                query = q_in[batch, :, cols]
+                grad_o = grad_o_in[batch, :, cols]
+                scores = dot_nt(query, keys) * scale_two
+                probs = jnp.where(mask, jnp.exp2(scores - lse[batch, head]), 0.0)
+                grad_p = dot_nt(grad_o, values)
+                grad_s = (probs * (grad_p - delta[head])).astype(LOW)
+                acc[:, cols] += dot(grad_s, keys)
+                grad_k = grad_k + dot_tn(grad_s, query)
+                grad_v = grad_v + dot_tn(probs.astype(LOW), grad_o)
+            grad_k = grad_k * scale
+            if extra is not None:
+                grad_k = grad_k + extra[block, :, :hd].astype(F32)
+                grad_v = grad_v + extra[block, :, hd:].astype(F32)
+            target[block, :, :hd] = grad_k.astype(LOW)
+            target[block, :, hd:] = grad_v.astype(LOW)
             return carry
 
-        lax.fori_loop(0, rows // step, run, 0)
-
-    for a in range(arrays):
-        for d in range(1, lines):
-            wire.arrived(near_handles[a, d])
-
-            def join(at, a=a, d=d):
-                total = parts[a][flip(index, 2 * d), at].astype(F32)
-                total = total + from_near[a][d, at].astype(F32)
-                to_far[a][d - 1, at] = total.astype(LOW)
-
-            by_rows(join)
-            far_handles[a, d] = wire.copy(to_far[a].at[d - 1], from_far[a].at[d - 1], far[d - 1])
-    for a in range(arrays):
-        wire.arrived(near_handles[a, 0])
-        for d in range(1, lines):
-            wire.arrived(far_handles[a, d])
-        width = parts[a].shape[2]
-
-        def total(at, a=a, width=width):
-            same = parts[a][index, at].astype(F32) + from_near[a][0, at].astype(F32)
-            other = None
-            for d in range(1, lines):
-                got = from_far[a][d - 1, at].astype(F32)
-                if split and d % 2:
-                    other = got if other is None else other + got
-                else:
-                    same = same + got
-            if split:
-                outs[a][at, pl.ds(pl.multiple_of(half * width, width), width)] = same
-                outs[a][at, pl.ds(pl.multiple_of((1 - half) * width, width), width)] = other
-            else:
-                outs[a][at, :] = same
-
-        by_rows(total)
+        lax.fori_loop(0, lines, body, 0)
+
+    def close_batch(batch):
+        dq[batch] = (acc[...] * scale).astype(LOW)
+
+    def to_core(which):
+        return [
+            wire.copy(kv_send.at[2 * line + which], kv_got.at[2 * line + which], other_core)
+            for line in range(lines)
+        ]
+
+    reduce.start()
+    bulk.start(list(range(1, lines)))
+    open_batch(1 - core)
+    blocks_of(1 - core, near_x, kv_send, None)
+    near_handles = to_core(near_x)
+    reduce.to_side(1)
+    reduce.to_side(0)
+    blocks_of(1 - core, 1 - near_x, kv_send, None)
+    own_handles = to_core(1 - near_x)
+    close_batch(1 - core)
+    bulk.relay(spread // 3)
+    for handle in near_handles:
+        wire.arrived(handle)
+    open_batch(core)
+    blocks_of(core, near_x, kv_part, kv_got)
+    keys_sum.start()
+    bulk.start([0])
+    reduce.to_pair()
+    bulk.relay(spread // 3)
+    for handle in own_handles:
+        wire.arrived(handle)
+    blocks_of(core, 1 - near_x, kv_part, kv_got)
+    close_batch(core)
+    reduce.ready()
+    bias = vec[0:1, :]
+
+    def body(at):
+        total = centre[at, :] + reduce.total(at) + bias
+        result[place, at, :] = total.astype(LOW)
+
+    by_rows(centre.shape[0], 16, body)
+    gather.start()
+    keys_sum.relay(spread)
+    bulk.relay(spread - 2 * (spread // 3))
+    gather.forward()
+    keys_sum.close()
+    dkv[1 - core] = jnp.zeros(dkv.shape[1:], LOW)
+    dkv[core] = kv_total[...].astype(LOW)
+    bulk.close()
     wire.finish()
 
 
-def scatter_grads(parts, split, collective_id):
+def back_stage(feed, fc, queries, keyval, meta_q, meta_k, mixed, lse, grad_mixed, centre, vec):
     count = lax.axis_size("seq")
-    lines = count // 2
-    arrays = len(parts)
-    copies = arrays * (count - 1)
-    scratch = []
-    for depth in (lines, lines - 1, lines - 1):
-        scratch += [pltpu.VMEM((depth,) + part.shape[1:], LOW) for part in parts]
+    tensor = lax.axis_size("tensor")
+    part, full = centre.shape
+    batches, rows, width = queries.shape
+    blocks, two = keyval.shape[1], keyval.shape[3]
+    heads = 2 * width // two
+    vmem = pl.BlockSpec(memory_space=pltpu.VMEM)
+    kv_part = jax.ShapeDtypeStruct((blocks, rows, two), LOW)
+    copies = 3 * count + 14
     return pl.pallas_call(
-        partial(scatter_kernel, count, split, arrays),
+        partial(back_kernel, count),
         out_shape=[
-            jax.ShapeDtypeStruct((part.shape[1], part.shape[2] * (2 if split else 1)), F32)
-            for part in parts
+            jax.ShapeDtypeStruct((fc.shape[1], 2 * fc.shape[2]), F32),
+            jax.ShapeDtypeStruct((batches, rows, width), LOW),
+            jax.ShapeDtypeStruct((batches, rows, two), LOW),
+            jax.ShapeDtypeStruct((tensor, part, full), LOW),
         ],
-        in_specs=[pl.BlockSpec(memory_space=pltpu.VMEM)] * arrays,
-        out_specs=[pl.BlockSpec(memory_space=pltpu.VMEM)] * arrays,
-        scratch_shapes=scratch
-        + [pltpu.SemaphoreType.DMA((copies,)), pltpu.SemaphoreType.DMA((copies,))],
+        in_specs=[vmem] * 11,
+        out_specs=[vmem] * 4,
+        scratch_shapes=row_sum_scratch(feed)
+        + seq_sum_scratch(fc)
+        + seq_sum_scratch(kv_part)
+        + [pltpu.VMEM(kv_part.shape, LOW)] * 3
+        + [
+            pltpu.VMEM((rows, two), F32),
+            pltpu.VMEM((heads, rows, 1), F32),
+            pltpu.VMEM((rows, width), F32),
+        ]
+        + sem_scratch(copies),
         compiler_params=pltpu.CompilerParams(
-            collective_id=collective_id, has_side_effects=True, vmem_limit_bytes=60 << 20
+            collective_id=3, has_side_effects=True, vmem_limit_bytes=60 << 20
         ),
-        name="scatter_grads",
-    )(*parts)
-
-
-def scatter_blocks(blocks):
+        name="back",
+    )(feed, fc, queries, keyval, meta_q, meta_k, mixed, lse, grad_mixed, centre, vec)
+
+
+def last_kernel(count, *refs):
+    back, out, query, keyval, own, dy, vec = refs[:7]
+    out_sum, query_sum, keyval_sum, rows, sums = refs[7:12]
+    row_refs = list(refs[12:15]) + [None, None]
+    out_refs, query_refs, keyval_refs = refs[15:18], refs[18:21], refs[21:24]
+    send_sem, recv_sem = refs[24:]
+    index, place = lax.axis_index("seq"), lax.axis_index("tensor")
+    along = seq_peers(index, count)
+    greet(along + [{"tensor": flip(place, 1)}, {"tensor": flip(place, 2)}])
+    wire = Wire(send_sem, recv_sem)
+    reduce = RowSum(wire, place, None, back, *row_refs)
+    out_bulk = SeqSum(wire, index, along, out, *out_refs, out_sum, False)
+    query_bulk = SeqSum(wire, index, along, query, *query_refs, query_sum, False)
+    keyval_bulk = SeqSum(wire, index, along, keyval, *keyval_refs, keyval_sum, False)
+    gather = RowGather(wire, place, rows)
+    spread = count // 2 - 1
+    first = 2 * spread // 3
+    reduce.start()
+    for bulk in (out_bulk, query_bulk, keyval_bulk):
+        bulk.start()
+    reduce.to_side(0)
+    out_bulk.relay(first)
+    reduce.ready()
+    sums[...] = jnp.zeros_like(sums)
+    gain = vec[0:1, :]
+
+    def body(at):
+        over = reduce.total(at)
+        inner, product = norm_back(own[at, :].astype(F32), gain, over)
+        rows[place, at, :] = (dy[at, :] + inner).astype(LOW)
+        sums[0] += product
+        sums[1] += over
+
+    by_rows(own.shape[0], 16, body)
+    gather.start()
+    out_bulk.relay(spread - first)
+    gather.forward()
+    query_bulk.relay(spread)
+    keyval_bulk.relay(spread)
+    for bulk in (out_bulk, query_bulk, keyval_bulk):
+        bulk.close()
+    wire.finish()
+
+
+def last_stage(back, out, query, keyval, own, dy, vec):
     count = lax.axis_size("seq")
-    blocks = dict(blocks)
-    for bit in range(bits_of(count)):
-        for r in sorted(blocks):
-            if r & (1 << bit):
-                arrived = swap(blocks.pop(r).astype(LOW), "seq", bit)
-                blocks[r ^ (1 << bit)] = blocks[r ^ (1 << bit)] + arrived.astype(F32)
-    return blocks[0]
-
-
-def tensor_gather(own, axis):
-    count = lax.axis_size("tensor")
-    out = jnp.expand_dims(own, axis)
-    for bit in reversed(range(bits_of(count))):
-        out_other = swap(out, "tensor", bit)
-        mine = (lax.axis_index("tensor") >> bit) & 1
-        low_part = jnp.where(mine == 0, out, out_other)
-        high_part = jnp.where(mine == 0, out_other, out)
-        size = out.shape[axis]
-        shape = out.shape
-        low_part = jnp.expand_dims(low_part, axis)
-        high_part = jnp.expand_dims(high_part, axis)
-        out = jnp.concatenate([low_part, high_part], axis=axis)
-        out = jnp.swapaxes(out, axis, axis + 1) if size > 1 else out
-        out = out.reshape(shape[:axis] + (2 * size,) + shape[axis + 1 :])
-    return out
+    tensor = lax.axis_size("tensor")
+    part, full = own.shape
+    vmem = pl.BlockSpec(memory_space=pltpu.VMEM)
+    bulk = (out, query, keyval)
+    copies = 3 * count + 8
+    scratch = row_sum_scratch(back)
+    for array in bulk:
+        scratch += seq_sum_scratch(array)
+    return pl.pallas_call(
+        partial(last_kernel, count),
+        out_shape=[jax.ShapeDtypeStruct(array.shape[1:], F32) for array in bulk]
+        + [
+            jax.ShapeDtypeStruct((tensor, part, full), LOW),
+            jax.ShapeDtypeStruct((2, 16, full), F32),
+        ],
+        in_specs=[vmem] * 7,
+        out_specs=[vmem] * 5,
+        scratch_shapes=scratch + sem_scratch(copies),
+        compiler_params=pltpu.CompilerParams(
+            collective_id=4, has_side_effects=True, vmem_limit_bytes=60 << 20
+        ),
+        name="last",
+    )(back, out, query, keyval, own, dy, vec)
+
+
+def visible(meta_q, meta_k):
+    seg_q, pos_q = meta_q[:, 0:1], meta_q[:, 1:2]
+    seg_k, pos_k = meta_k[0:1, :], meta_k[1:2, :]
+    return ((seg_k == 0) | (seg_k == seg_q)) & (pos_k <= pos_q)
 
 
 def tensor_scatter(parts, axis):
@@ -772,99 +876,6 @@
         give = lax.dynamic_index_in_dim(split, 1 - mine, axis + 1, keepdims=False)
         parts = keep.astype(F32) + swap(give.astype(LOW), "tensor", bit).astype(F32)
     return lax.squeeze(parts, (axis,))
-
-
-def visible(meta_q, meta_k):
-    seg_q, pos_q = meta_q[:, 0:1], meta_q[:, 1:2]
-    seg_k, pos_k = meta_k[0:1, :], meta_k[1:2, :]
-    return ((seg_k == 0) | (seg_k == seg_q)) & (pos_k <= pos_q)
-
-
-def backward_kernel(
-    live_ref, q_ref, kv_ref, mq_ref, mk_ref, o_ref, lse_ref, do_ref, dq_ref, dkv_ref, delta, acc
-):
-    batch = pl.program_id(0)
-    hd = kv_ref.shape[-1] // 2
-    heads = q_ref.shape[-1] // hd
-    blocks = kv_ref.shape[1]
-    scale = float(hd) ** (-0.5)
-    scale_two = scale * LOG2E
-    acc[...] = jnp.zeros_like(acc)
-    for head in range(heads):
-        cols = slice(head * hd, (head + 1) * hd)
-        delta[head] = jnp.sum(
-            do_ref[0, :, cols].astype(F32) * o_ref[0, :, cols].astype(F32), axis=-1, keepdims=True
-        )
-
-    def step(index, carry):
-        @pl.when(live_ref[batch, index] > 0)
-        def _():
-            mask = visible(mq_ref[0], mk_ref[0, index])
-            keys = kv_ref[0, index, :, :hd]
-            values = kv_ref[0, index, :, hd:]
-            grad_k = jnp.zeros((keys.shape[0], hd), F32)
-            grad_v = jnp.zeros((keys.shape[0], hd), F32)
-            for head in range(heads):
-                cols = slice(head * hd, (head + 1) * hd)
-                query = q_ref[0, :, cols]
-                grad_o = do_ref[0, :, cols]
-                scores = dot_nt(query, keys) * scale_two
-                probs = jnp.where(mask, jnp.exp2(scores - lse_ref[0, head]), 0.0)
-                grad_p = dot_nt(grad_o, values)
-                grad_s = (probs * (grad_p - delta[head])).astype(LOW)
-                acc[:, cols] += dot(grad_s, keys)
-                grad_k = grad_k + dot_tn(grad_s, query)
-                grad_v = grad_v + dot_tn(probs.astype(LOW), grad_o)
-            dkv_ref[0, index, :, :hd] = (grad_k * scale).astype(LOW)
-            dkv_ref[0, index, :, hd:] = grad_v.astype(LOW)
-
-        @pl.when(live_ref[batch, index] == 0)
-        def _():
-            dkv_ref[0, index] = jnp.zeros(dkv_ref.shape[2:], LOW)
-
-        return carry
-
-    lax.fori_loop(0, blocks, step, 0)
-    dq_ref[0] = (acc[...] * scale).astype(LOW)
-
-
-def attend_backward(queries, keyval, meta_q, meta_k, live, mixed, lse, grad_mixed):
-    batches, rows, width = queries.shape
-    _, blocks, keys, two = keyval.shape
-    hd = two // 2
-    heads = width // hd
-    flops = 10 * batches * rows * width * blocks * keys
-    row_spec = pl.BlockSpec((1, rows, width), lambda b, live: (b, 0, 0))
-    kv_spec = pl.BlockSpec((1, blocks, keys, two), lambda b, live: (b, 0, 0, 0))
-    return pl.pallas_call(
-        backward_kernel,
-        grid_spec=pltpu.PrefetchScalarGridSpec(
-            num_scalar_prefetch=1,
-            grid=(batches,),
-            in_specs=[
-                row_spec,
-                kv_spec,
-                pl.BlockSpec((1, rows, 128), lambda b, live: (b, 0, 0)),
-                pl.BlockSpec((1, blocks, 8, keys), lambda b, live: (b, 0, 0, 0)),
-                row_spec,
-                pl.BlockSpec((1, heads, rows, 1), lambda b, live: (b, 0, 0, 0)),
-                row_spec,
-            ],
-            out_specs=[row_spec, kv_spec],
-            scratch_shapes=[
-                pltpu.VMEM((heads, rows, 1), F32),
-                pltpu.VMEM((rows, width), F32),
-            ],
-        ),
-        out_shape=[
-            jax.ShapeDtypeStruct((batches, rows, width), LOW),
-            jax.ShapeDtypeStruct((batches, blocks, keys, two), LOW),
-        ],
-        name="attend_backward",
-        cost_estimate=pl.CostEstimate(
-            flops=flops, transcendentals=0, bytes_accessed=4 * keyval.size
-        ),
-    )(live, queries, keyval, meta_q, meta_k, mixed, lse, grad_mixed)
 
 
 def norm_parts(values):
@@ -952,13 +963,6 @@
     pos_keys = jnp.swapaxes(pos_keys.reshape(seq_size, batches, rows), 0, 1).astype(jnp.int32)
     meta_k = jnp.pad(jnp.stack([seg_keys, pos_keys], axis=2), ((0, 0), (0, 0), (0, 6), (0, 0)))
     meta_q = jnp.pad(jnp.stack([segment, position], axis=2), ((0, 0), (0, 0), (0, 126)))
-    seg_lo, seg_hi = jnp.min(seg_keys, axis=2), jnp.max(seg_keys, axis=2)
-    own_lo = jnp.min(segment, axis=1, keepdims=True)
-    own_hi = jnp.max(segment, axis=1, keepdims=True)
-    live = (
-        ((seg_lo == 0) | ((seg_lo <= own_hi) & (own_lo <= seg_hi)))
-        & (jnp.min(pos_keys, axis=2) <= jnp.max(position, axis=1, keepdims=True))
-    ).astype(jnp.int32)
 
     gain_one, shift_one, _, out_bias, gain_two, shift_two, proj_bias = [
         vec_all[i] for i in range(7)
@@ -989,10 +993,6 @@
         split = array.reshape(batches, tensor_size, quarter, full_width)
         own = lax.dynamic_index_in_dim(split, tensor_index, 1, keepdims=False)
         return own.reshape(batches * quarter, full_width)
-
-    def pair_scatter(part):
-        got = tensor_scatter(part.reshape(2, tensor_size, batches * quarter, full_width), 1)
-        return got[0] + swap(got[1].astype(LOW), "seq", 1).astype(F32)
 
     vecs = jnp.pad(jnp.stack([out_bias, gain_two, shift_two]), ((0, 5), (0, 0)))
     grad_split = by_quarter(grad_out)
@@ -1037,43 +1037,39 @@
     grad_gain_two, grad_shift_two, grad_out_bias = jnp.sum(sums, axis=1)
     grad_proj_bias = jnp.sum(grad_q_low.astype(F32), axis=0)
     grad_middle_low = rows_middle.reshape(-1, full_width)
-    (fc_sum,) = scatter_grads([blocked(dot_tn(normed_two, grad_hidden))], True, 4)
-
-    ff_sum = pair_scatter(dot_nt(active, proj_t))
-    result_q = (middle + ff_sum + proj_bias).astype(LOW)
-    result = by_batch(tensor_gather(result_q, 0))
+    def one_row(row):
+        return jnp.pad(row[None], ((0, 7), (0, 0)))
 
     grad_mixed = by_batch(dot(grad_middle_low, out_t).astype(LOW))
-    grad_queries, grad_kv_all = attend_backward(
-        queries, kv_all, meta_q, meta_k, live, mixed, lse, grad_mixed
-    )
-    grad_keyval = scatter_blocks(
-        {
-            r: lax.dynamic_index_in_dim(
-                grad_kv_all, jnp.bitwise_xor(seq_index, r), 1, keepdims=False
-            ).astype(F32)
-            for r in range(seq_size)
-        }
-    )
-    grad_keyval = grad_keyval.astype(LOW).reshape(-1, 2 * hd)
+    feed_part = dot_nt(active, proj_t).astype(LOW)
+    fc_sum, grad_queries, grad_keyval, result_rows = back_stage(
+        feed_part.reshape(2, tensor_size, batches * quarter, full_width),
+        blocked(dot_tn(normed_two, grad_hidden)),
+        queries,
+        kv_all,
+        meta_q,
+        meta_k,
+        mixed,
+        lse,
+        grad_mixed,
+        middle,
+        one_row(proj_bias),
+    )
+    result = by_batch(result_rows)
+    grad_keyval = grad_keyval.reshape(-1, 2 * hd)
     grad_queries = grad_queries.reshape(-1, group_width)
-    out_sum, query_sum, kv_sum = scatter_grads(
-        [
-            blocked(dot_tn(grad_middle_low, mixed_rows)),
-            blocked(dot_tn(normed, grad_queries)),
-            blocked(dot_tn(normed, grad_keyval)),
-        ],
-        False,
-        3,
-    )
     grad_normed = dot_nt(grad_queries, q_mat) + dot_nt(grad_keyval, kv_mat)
-    in_sum = tensor_scatter(by_quarter(grad_normed), 0)
-    residual_q = my_quarter(inputs).astype(F32)
-    norm_part, gain_part = norm_back(residual_q, gain_one, in_sum)
-    grad_in_q = (grad_middle + norm_part).astype(LOW)
-    input_grad = by_batch(tensor_gather(grad_in_q, 0))
-    grad_gain_one = jnp.sum(gain_part, axis=0)
-    grad_shift_one = jnp.sum(in_sum, axis=0)
+    out_sum, query_sum, kv_sum, input_rows, sums_one = last_stage(
+        by_quarter(grad_normed.astype(LOW))[None],
+        blocked(dot_tn(grad_middle_low, mixed_rows)),
+        blocked(dot_tn(normed, grad_queries)),
+        blocked(dot_tn(normed, grad_keyval)),
+        my_quarter(inputs),
+        grad_middle,
+        one_row(gain_one),
+    )
+    input_grad = by_batch(input_rows)
+    grad_gain_one, grad_shift_one = jnp.sum(sums_one, axis=1)
     qbias_local = jnp.sum(grad_queries.astype(F32), axis=0)
     vbias_local = jnp.sum(grad_keyval[:, hd:].astype(F32), axis=0)
 

time: 704 us -> 605 us (0.86)
  waiting for transfers between devices: 55.9 us -> 5.3 us
  starting transfers between devices: 35.6 us -> 10.5 us
  other arithmetic: 41.2 us -> 23.7 us
  local copies, waits for them, and re-layouts: 43.3 us -> 32.5 us
    ppermute x23 -> x7, waiting for transfers between devices: 55.9 us -> 5.3 us  [swap(): return lax.ppermute(value, axis, [(i, i ^ 1 << bit) for i in range(count)])]
    ppermute x23 -> x7, starting transfers between devices: 35.6 us -> 10.5 us  [swap(): return lax.ppermute(value, axis, [(i, i ^ 1 << bit) for i in range(count)])]
    add x4 -> x1, other arithmetic: 10.7 us -> 0.92 us  [tensor_scatter(): parts = keep.astype(F32) + swap(give.astype(LOW), 'tensor', bit).astype(F32)]
    unnamed x96 -> x67, local copies, waits for them, and re-layouts: 15.9 us -> 7.79 us
    pallas_call x3 -> x2, Pallas kernels: 172 us -> 178 us  [the longest x1 90 us: back_stage(): pl.pallas_call(partial(back_kernel, count), out_shape=[jax.ShapeDtypeStru...]
  transfers between devices with their start and end apart: 23 -> 7, of which waited for: 9 -> 4; matrix products, arithmetic and copies ran while one was open for 10% -> 2% of each run, Pallas kernels for 22% -> 0%
where the time goes in v5:
time: 605 us; the launch traced here: 596 us
  Pallas kernels  459 us (76%)
  matrix products  62.8 us (10%)
  local copies, waits for them, and re-layouts  32.5 us (5%)
  other arithmetic  23.7 us (4%)
  starting transfers between devices  10.5 us (2%)
    pallas_call x1, Pallas kernels, front(): pl.pallas_call(partial(front_kernel, count), out_shape=[jax.ShapeDtypeStr...  167 us
    pallas_call x1, Pallas kernels, back_stage(): pl.pallas_call(partial(back_kernel, count), out_shape=[jax.ShapeDtypeStru...  90 us
    pallas_call x1, Pallas kernels, last_stage(): pl.pallas_call(partial(last_kernel, count), out_shape=[jax.ShapeDtypeStru...  88.4 us
    pallas_call x1, Pallas kernels, middle_stage(): pl.pallas_call(partial(middle_kernel, count), out_shape=[jax.ShapeDtypeSt...  69.6 us
    pallas_call x1, Pallas kernels, gather_first(): pl.pallas_call(partial(first_kernel, count, tensor), out_shape=[jax.Shape...  44.5 us
    dot_general x5, matrix products, dot_tn(): lax.dot_general(left, right, (((0,), (0,)), ((), ())), preferred_element_...  22.4 us
    dot_general x5, matrix products, dot(): return jnp.dot(left, right, preferred_element_type=F32)  20.8 us
    dot_general x4, matrix products, dot_nt(): lax.dot_general(left, right, (((1,), (1,)), ((), ())), preferred_element_...  19.5 us
  transfers between devices with their start and end apart: 7, of which 4 were waited for; matrix products, arithmetic and copies ran while one was open for 2% of the time, Pallas kernels for 0%

profile of v5, /device:TPU:0, one launch (start us, length us, event | category | flops | bytes accessed | tf_op | source)
XLA Modules:
  0.0 595.8 jit_solution(5109312862341605890)
XLA Ops:
  4.4 1.5 convert_element_type.171.refs_1_
  5.9 1.8 convert_element_type.172.refs_2_
  7.6 44.5 %gather_first.1 = (bf16[8,4,32,128]{3,2,1,0:T(8,128)(2,1)}, bf16[8,4,64,256]{3,2,1,0:T(8,128)(2,1)}, bf16[8,256,512]{2,1,0:T(8,128)(2,1)}) custom-call(bf16[32,128]{1,0:T(8,128)(2,1)} %pad_bitcast_fusion.1.refs_0_, bf16[64,256]{1,0:T(8,128)(2,1)} %convert_element_type.171.refs_1_, bf16[256,512]{1,0:T(8,128)(2,1)} %convert_element_type.172.refs_2_), custom_call_target="tpu_custom_call" | custom-call | tf_op jit(solution)/shard_map/gather_first/pallas_call | solution.py:156
  52.1 1.1 reshape.264
  54.2 1.9 convert_reduce_fusion
  58.9 3.2 copy.97
  62.1 1.9 convert_reduce_fusion.2
  64.8 1.8 copy.94
  66.6 1.3 copy.95
  67.9 1.7 convert_element_type.188
  69.6 1.3 copy.96
  73.6 1.4 fusion.17
  75.0 2.1 fusion.16
  77.7 166.8 %front.1 = (bf16[2,256,512]{2,1,0:T(8,128)(2,1)}, f32[2,4,256,1]{3,2,1,0:T(8,128)}, bf16[2,8,256,256]{3,2,1,0:T(8,128)(2,1)}, bf16[8,256,512]{2,1,0:T(8,128)(2,1...) custom-call(bf16[2,256,512]{2,1,0:T(8,128)(2,1)} %bitcast.178, ...), custom_call_target="tpu_custom_call" | custom-call | tf_op jit(solution)/shard_map/front/pallas_call | solution.py:395
  244.6 3.9 pad_maximum_fusion
  248.5 7.7 %fusion.26 = f32[1024,1024]{1,0:T(8,128)S(1)} fusion(bf16[1024,2048]{1,0:T(8,128)(2,1)} %bitcast.222, bf16[2048,1024]{1,0:T(8,128)(2,1)} %bitcast.224), kind=kOutput, calls=%fused_computation.103 | convolution fusion | flops 4294967296 | bytes 12582912 | tf_op jit(solution)/shard_map/dot_general | solution.py:31
  256.2 6.8 %convert_reduce_fusion.1 = (f32[1024]{0:T(1024)S(1)}, bf16[1024,1024]{1,0:T(8,128)(2,1)S(1)}) fusion(bf16[1024,2048]{1,0:T(8,128)(2,1)S(1)} %bitcast.166, bf16[2048,1024]{1,0:T(8,128)(2,1)S(1)} %bitcast.220, f32[1024,1024]{1,0:T(8,128)S(1)} %fusion.26, f32[1024]{0:T(1024)S(1)} %dynamic_slice.50), kind=kOutput, calls=%fused_computation.21 | convolution fusion | flops 4316986368 | bytes 14688256 | tf_op jit(solution)/shard_map/dot_general | solution.py:31
  263.0 6.2 %convolution_convert_fusion.1 = bf16[1024,2048]{1,0:T(8,128)(2,1)} fusion(bf16[1024,1024]{1,0:T(8,128)(2,1)S(1)} %get-tuple-element.123, bf16[2048,1024]{1,0:T(8,128)(2,1)S(1)} %bitcast.225), kind=kOutput, calls=%fused_computation.26 | convolution fusion | flops 4297064448 | bytes 10485760 | tf_op jit(solution)/shard_map/dot_general | solution.py:39
  269.3 6.2 %convolution_convert_fusion.2 = bf16[2048,1024]{1,0:T(8,128)(2,1)} fusion(bf16[1024,2048]{1,0:T(8,128)(2,1)S(1)} %bitcast.223, bf16[1024,1024]{1,0:T(8,128)(2,1)S(1)} %get-tuple-element.123), kind=kOutput, calls=%fused_computation.27 | convolution fusion | flops 4297064448 | bytes 10485760 | tf_op jit(solution)/shard_map/dot_general | solution.py:35
  275.4 7.2 %convolution_convert_fusion.3 = bf16[1024,2048]{1,0:T(8,128)(2,1)} fusion(bf16[2048,1024]{1,0:T(8,128)(2,1)S(1)} %bitcast.221, f32[1024,1024]{1,0:T(8,128)S(1)} %fusion.26, f32[1024]{0:T(1024)S(1)} %dynamic_slice.50), kind=kOutput, calls=%fused_computation.28 | convolution fusion | flops 4307550208 | bytes 12587008 | tf_op jit(solution)/shard_map/dot_general | solution.py:39
  282.6 6.5 %convolution_convert_fusion = bf16[2048,1024]{1,0:T(8,128)(2,1)} fusion(bf16[1024,2048]{1,0:T(8,128)(2,1)S(1)} %bitcast.167, f32[1024,1024]{1,0:T(8,128)S(1)} %fusion.26, f32[1024]{0:T(1024)S(1)} %dynamic_slice.50), kind=kOutput, calls=%fused_computation.25 | convolution fusion | flops 4307550208 | bytes 12587008 | tf_op jit(solution)/shard_map/dot_general | solution.py:35
  289.0 69.6 %middle.1 = (f32[256,2048]{1,0:T(8,128)}, f32[128,2048]{1,0:T(8,128)}, bf16[4,128,2048]{2,1,0:T(8,128)(2,1)}, f32[3,16,2048]{2,1,0:T(8,128)}) custom-call(bf16[2,4,128,2048]{3,2,1,0:T(8,128)(2,1)} %bitcast.168, bf16[8,256,1024]{2,1,0:T(8,128)(2,1)} %bitcast.169, f32[128,2048]{1,0:T(8,128)} %get-tuple-element.46.refs_2_.refs_9_, bf16[128,2048]{1,0:T(8,128)(2,1)} %bitcast.185, ...), custom_call_target="tpu_custom_call" | custom-call | tf_op jit(solution)/shard_map/middle/pallas_call | solution.py:626
  358.6 1.1 reduce_sum.76
  360.4 2.8 convolution_convert_fusion.5
  364.1 90.0 %back.1 = (f32[256,2048]{1,0:T(8,128)}, bf16[2,256,512]{2,1,0:T(8,128)(2,1)}, bf16[2,256,256]{2,1,0:T(8,128)(2,1)}, bf16[4,128,2048]{2,1,0:T(8,128)(2,1)}) custom-call(bf16[2,4,128,2048]{3,2,1,0:T(8,128)(2,1)} %bitcast.163, bf16[8,256,1024]{2,1,0:T(8,128)(2,1)} %bitcast.162, bf16[2,256,512]{2,1,0:T(8,128)(2,1)} %bitcast.179, ...), custom_call_target="tpu_custom_call" | custom-call | tf_op jit(solution)/shard_map/back/pallas_call | solution.py:764
  454.2 1.2 convert_reduce_fusion.3
  455.3 3.7 bitcast_convert_fusion
  459.0 1.7 fusion.15
  460.9 2.7 fusion.27
  464.7 4.4 convolution_convert_fusion.4
  469.0 3.5 add_convert_fusion
  472.5 1.5 copy.101
  474.0 88.4 %last.1 = (f32[256,512]{1,0:T(8,128)}, f32[256,512]{1,0:T(8,128)}, f32[256,256]{1,0:T(8,128)}, bf16[4,128,2048]{2,1,0:T(8,128)(2,1)}, f32[2,16,2048]{2,1,0:T(8,128)}) custom-call(bf16[1,4,128,2048]{3,2,1,0:T(8,128)(2,1)} %bitcast.158, bf16[8,256,512]{2,1,0:T(8,128)(2,1)} %bitcast.177, bf16[8,256,512]{2,1,0:T(8,128)(2,1)} %bitcast.176, ...), custom_call_target="tpu_custom_call" | custom-call | tf_op jit(solution)/shard_map/last/pallas_call | solution.py:845
  562.4 1.2 reduce_sum.74
  563.7 4.4 collective-permute-start.2
  569.2 1.6 collective-permute-done.2
  570.8 1.3 collective-permute-start.3
  572.0 0.9 bitcast_add_fusion
  573.0 1.7 collective-permute-done.3
  574.8 2.7 collective-permute-start.1
  577.5 0.9 collective-permute-done.4
  578.4 3.2 copy.100
  581.6 1.8 copy.108
  583.4 3.3 copy.105
  586.7 1.0 copy.107
  587.7 2.0 collective-permute-start.6
  590.4 1.1 collective-permute-done.6
  594.0 1.3 copy.147
  (144 shorter events, 18.6 us)
Async XLA Ops:
  0.6 57.2 %copy-start.19 = (s32[2,256]{1,0:T(2,128)S(1)}, s32[2,256]{1,0:T(2,128)}, u32[]{:S(2)}) copy-start(s32[2,256]{1,0:T(2,128)} %param.13) | copy-start | bytes 6148
  0.7 57.1 %copy-start.18 = (s32[2,256]{1,0:T(2,128)S(1)}, s32[2,256]{1,0:T(2,128)}, u32[]{:S(2)}) copy-start(s32[2,256]{1,0:T(2,128)} %param.14) | copy-start | bytes 6148
  0.7 55.5 %copy-start = (bf16[2,256,2048]{2,1,0:T(8,128)(2,1)S(1)}, bf16[2,256,2048]{2,1,0:T(8,128)(2,1)}, u32[]{:S(2)}) copy-start(bf16[2,256,2048]{2,1,0:T(8,128)(2,1)} %param.12) | copy-start | bytes 6291460
  0.7 56.2 %copy-start.14 = (f32[512,256]{1,0:T(8,128)S(1)}, f32[512,256]{1,0:T(8,128)}, u32[]{:S(2)}) copy-start(f32[512,256]{1,0:T(8,128)} %param.17) | copy-start | bytes 1572868
  53.3 4.5 copy-start.12
  66.6 4.4 slice-start
  70.9 2.6 copy-start.11
  72.6 2.4 copy-start.3
  73.5 3.5 copy-start.5
  77.1 167.5 %copy-start.1 = (bf16[2,4,64,2048]{3,2,0,1:T(8,128)(2,1)S(1)}, bf16[2,4,64,2048]{3,2,0,1:T(8,128)(2,1)}, u32[]{:S(2)}) copy-start(bf16[2,4,64,2048]{3,2,0,1:T(8,128)(2,1)} %copy.97) | copy-start | bytes 6291460
  248.5 7.7 %copy-start.2 = (bf16[8,128,2048]{2,1,0:T(8,128)(2,1)S(1)}, bf16[8,128,2048]{2,1,0:T(8,128)(2,1)}, u32[]{:S(2)}) copy-start(bf16[8,128,2048]{2,1,0:T(8,128)(2,1)} %pad_maximum_fusion) | copy-start | bytes 12582916
  248.5 7.7 %copy-start.21 = (bf16[8,256,1024]{2,1,0:T(8,128)(2,1)S(1)}, bf16[8,256,1024]{2,1,0:T(8,128)(2,1)}, u32[]{:S(2)}) copy-start(bf16[8,256,1024]{2,1,0:T(8,128)(2,1)} %get-tuple-element.41) | copy-start | bytes 12582916
  256.1 6.8 %copy-start.23 = (bf16[8,256,1024]{2,1,0:T(8,128)(2,1)S(1)}, bf16[8,256,1024]{2,1,0:T(8,128)(2,1)}, u32[]{:S(2)}) copy-start(bf16[8,256,1024]{2,1,0:T(8,128)(2,1)} %get-tuple-element.40) | copy-start | bytes 12582916
  263.0 6.3 %copy-start.22 = (bf16[2,4,128,2048]{3,2,1,0:T(8,128)(2,1)S(1)}, bf16[2,4,128,2048]{3,2,1,0:T(8,128)(2,1)}, u32[]{:S(2)}) copy-start(bf16[2,4,128,2048]{3,2,1,0:T(8,128)(2,1)} %get-tuple-element.39) | copy-start | bytes 12582916
  289.0 71.4 %copy-start.24 = (bf16[8,256,512]{2,1,0:T(8,128)(2,1)S(1)}, bf16[8,256,512]{2,1,0:T(8,128)(2,1)}, u32[]{:S(2)}) copy-start(bf16[8,256,512]{2,1,0:T(8,128)(2,1)} %get-tuple-element.48) | copy-start | bytes 6291460
  359.7 4.4 copy-start.17
  364.1 91.2 %copy-start.6 = (bf16[2,256,2048]{2,1,0:T(8,128)(2,1)S(1)}, bf16[2,256,2048]{2,1,0:T(8,128)(2,1)}, u32[]{:S(2)}) copy-start(bf16[2,256,2048]{2,1,0:T(8,128)(2,1)} %copy-done.5) | copy-start | bytes 6291460
  455.3 3.7 copy-start.13
  460.8 3.5 copy-start.7
  464.6 4.4 copy-start.4
  464.6 4.4 copy-start.8
  474.0 89.7 %slice-start.1 = ((f32[3,2048]{1,0:T(4,128)}), f32[2,2048]{1,0:T(2,128)S(1)}, s32[]{:S(2)}) async-start(f32[3,2048]{1,0:T(4,128)} %copy-done.17), calls=%async_computation.1 | async-start | bytes 32768 | tf_op jit(solution)/shard_map/unstack | solution.py:1037
  562.4 19.2 %copy-start.10 = (f32[256,2048]{1,0:T(8,128)S(1)}, f32[256,2048]{1,0:T(8,128)}, u32[]{:S(2)}) copy-start(f32[256,2048]{1,0:T(8,128)} %get-tuple-element.58) | copy-start | bytes 6291460
  563.7 7.0 %collective-permute-start.2 = (f32[4,24,128]{2,1,0:T(8,128)S(1)}, f32[4,24,128]{2,1,0:T(8,128)S(1)}, u32[]{:S(2)}, u32[]{:S(2)}) collective-permute-start(f32[4,24,128]{2,1,0:T(8,128)S(1)} %constant_dynamic-slice_fusion.3), channel_id=1, source_target_pairs={{0,16},{4,20},{8,24},{12,28},{16,0},{20,4},{24,8},{28,12},{1,17},{... | collective-permute-start | bytes 147464 | tf_op jit(solution)/shard_map/ppermute | solution.py:23
  569.1 3.0 collective-permute-start
  570.8 3.9 collective-permute-start.3
  574.7 3.8 collective-permute-start.4
  574.8 14.9 %collective-permute-start.1 = (bf16[1,64,256]{2,1,0:T(8,128)(2,1)S(1)}, bf16[1,64,256]{2,1,0:T(8,128)(2,1)S(1)}, u32[]{:S(2)}, u32[]{:S(2)}) collective-permute-start(bf16[1,64,256]{2,1,0:T(8,128)(2,1)S(1)} %dynamic-slice_convert_fusion), channel_id=1, source_target_pairs={{0,2},{1,3},{2,0},{3,1},{4,6},{5,7},{6,4},{7,5},{8,10},{9,11},{10,... | collective-permute-start | bytes 98312 | tf_op jit(solution)/shard_map/ppermute | solution.py:23
  578.4 9.3 %collective-permute-start.5 = (f32[24,128]{1,0:T(8,128)S(1)}, f32[24,128]{1,0:T(8,128)S(1)}, u32[]{:S(2)}, u32[]{:S(2)}) collective-permute-start(f32[24,128]{1,0:T(8,128)S(1)} %add_bitcast_fusion.1), channel_id=1, source_target_pairs={{0,1},{1,0},{2,3},{3,2},{4,5},{5,4},{6,7},{7,6},{8,9},{9,8},{10,11... | collective-permute-start | bytes 36872 | tf_op jit(solution)/shard_map/ppermute | solution.py:23
  581.6 5.1 copy-start.16
  581.6 11.6 %copy-start.15 = (f32[256,512]{1,0:T(8,128)S(1)}, f32[256,512]{1,0:T(8,128)}, u32[]{:S(2)}) copy-start(f32[256,512]{1,0:T(8,128)} %get-tuple-element.139) | copy-start | bytes 1572868
  583.4 10.6 %copy-start.9 = (f32[256,2048]{1,0:T(8,128)S(1)}, f32[256,2048]{1,0:T(8,128)}, u32[]{:S(2)}) copy-start(f32[256,2048]{1,0:T(8,128)} %get-tuple-element.142) | copy-start | bytes 6291460
  587.7 3.7 collective-permute-start.6
  592.0 3.3 copy-start.20

commit v6 on v5

--- a/solution.py
+++ b/solution.py
@@ -451,7 +451,7 @@
             def join(at, d=d):
                 total = self.part[flip(self.index, 2 * d), at].astype(F32)
                 total = total + self.from_near[d, at].astype(F32)
-                self.to_far[d - 1, at] = total.astype(LOW)
+                self.to_far[d - 1, at] = total.astype(self.to_far.dtype)
 
             by_rows(self.rows, self.step, join)
             self.far_handles[d] = self.wire.copy(
@@ -484,10 +484,10 @@
         by_rows(self.rows, self.step, total)
 
 
-def seq_sum_scratch(part):
+def seq_sum_scratch(part, dtype=LOW):
     lines = part.shape[0] // 2
     return [
-        pltpu.VMEM((depth,) + part.shape[1:], LOW) for depth in (lines, lines - 1, lines - 1)
+        pltpu.VMEM((depth,) + part.shape[1:], dtype) for depth in (lines, lines - 1, lines - 1)
     ]
 
 
@@ -642,10 +642,10 @@
 
 
 def back_kernel(count, *refs):
-    feed, fc, q_in, kv_in, mq_in, mk_in, mixed, lse, grad_o_in, centre, vec = refs[:11]
-    fc_sum, dq, dkv, result = refs[11:15]
-    row_refs, seq_refs, kv_refs = refs[15:20], refs[20:23], refs[23:26]
-    kv_send, kv_got, kv_part, kv_total, delta, acc, send_sem, recv_sem = refs[26:]
+    feed, fc, out, q_in, kv_in, mq_in, mk_in, mixed, lse, grad_o_in, centre, vec = refs[:12]
+    fc_sum, out_sum, dq, dkv, result = refs[12:17]
+    row_refs, seq_refs, out_refs, kv_refs = refs[17:22], refs[22:25], refs[25:28], refs[28:31]
+    kv_send, kv_got, kv_part, kv_total, delta, acc, send_sem, recv_sem = refs[31:]
     index, place = lax.axis_index("seq"), lax.axis_index("tensor")
     core = lax.rem(place, 2)
     other_core = {"tensor": flip(place, 1)}
@@ -656,6 +656,7 @@
     wire = Wire(send_sem, recv_sem)
     reduce = RowSum(wire, place, along[0], feed, *row_refs)
     bulk = SeqSum(wire, index, along, fc, *seq_refs, fc_sum, True)
+    out_bulk = SeqSum(wire, index, along, out, *out_refs, out_sum, False)
     keys_sum = SeqSum(wire, index, along, kv_part, *kv_refs, kv_total, False)
     gather = RowGather(wire, place, result)
     hd = kv_in.shape[-1] // 2
@@ -726,6 +727,7 @@
     blocks_of(core, near_x, kv_part, kv_got)
     keys_sum.start()
     bulk.start([0])
+    out_bulk.start()
     reduce.to_pair()
     bulk.relay(spread // 3)
     for handle in own_handles:
@@ -744,14 +746,16 @@
     keys_sum.relay(spread)
     bulk.relay(spread - 2 * (spread // 3))
     gather.forward()
+    out_bulk.relay(spread)
     keys_sum.close()
     dkv[1 - core] = jnp.zeros(dkv.shape[1:], LOW)
     dkv[core] = kv_total[...].astype(LOW)
     bulk.close()
+    out_bulk.close()
     wire.finish()
 
 
-def back_stage(feed, fc, queries, keyval, meta_q, meta_k, mixed, lse, grad_mixed, centre, vec):
+def back_stage(feed, fc, out, queries, keyval, meta_q, meta_k, mixed, lse, grad_mixed, centre, vec):
     count = lax.axis_size("seq")
     tensor = lax.axis_size("tensor")
     part, full = centre.shape
@@ -760,19 +764,21 @@
     heads = 2 * width // two
     vmem = pl.BlockSpec(memory_space=pltpu.VMEM)
     kv_part = jax.ShapeDtypeStruct((blocks, rows, two), LOW)
-    copies = 3 * count + 14
+    copies = 4 * count + 14
     return pl.pallas_call(
         partial(back_kernel, count),
         out_shape=[
             jax.ShapeDtypeStruct((fc.shape[1], 2 * fc.shape[2]), F32),
+            jax.ShapeDtypeStruct(out.shape[1:], F32),
             jax.ShapeDtypeStruct((batches, rows, width), LOW),
             jax.ShapeDtypeStruct((batches, rows, two), LOW),
             jax.ShapeDtypeStruct((tensor, part, full), LOW),
         ],
-        in_specs=[vmem] * 11,
-        out_specs=[vmem] * 4,
+        in_specs=[vmem] * 12,
+        out_specs=[vmem] * 5,
         scratch_shapes=row_sum_scratch(feed)
         + seq_sum_scratch(fc)
+        + seq_sum_scratch(out)
         + seq_sum_scratch(kv_part)
         + [pltpu.VMEM(kv_part.shape, LOW)] * 3
         + [
@@ -785,31 +791,33 @@
             collective_id=3, has_side_effects=True, vmem_limit_bytes=60 << 20
         ),
         name="back",
-    )(feed, fc, queries, keyval, meta_q, meta_k, mixed, lse, grad_mixed, centre, vec)
+    )(feed, fc, out, queries, keyval, meta_q, meta_k, mixed, lse, grad_mixed, centre, vec)
 
 
 def last_kernel(count, *refs):
-    back, out, query, keyval, own, dy, vec = refs[:7]
-    out_sum, query_sum, keyval_sum, rows, sums = refs[7:12]
-    row_refs = list(refs[12:15]) + [None, None]
-    out_refs, query_refs, keyval_refs = refs[15:18], refs[18:21], refs[21:24]
-    send_sem, recv_sem = refs[24:]
+    back, query, keyval, small, own, dy, vec = refs[:7]
+    query_sum, keyval_sum, rows, small_sum = refs[7:11]
+    row_refs, key_row_refs = refs[11:14], refs[14:17]
+    query_refs, key_refs, small_refs = refs[17:20], refs[20:23], refs[23:26]
+    key_part, small_part, small_own, small_got, sums, send_sem, recv_sem = refs[26:]
     index, place = lax.axis_index("seq"), lax.axis_index("tensor")
     along = seq_peers(index, count)
-    greet(along + [{"tensor": flip(place, 1)}, {"tensor": flip(place, 2)}])
+    other_core, other_side = {"tensor": flip(place, 1)}, {"tensor": flip(place, 2)}
+    greet(along + [other_core, other_side])
     wire = Wire(send_sem, recv_sem)
-    reduce = RowSum(wire, place, None, back, *row_refs)
-    out_bulk = SeqSum(wire, index, along, out, *out_refs, out_sum, False)
+    reduce = RowSum(wire, place, None, back, *row_refs, None, None)
+    key_reduce = RowSum(wire, place, None, keyval, *key_row_refs, None, None)
     query_bulk = SeqSum(wire, index, along, query, *query_refs, query_sum, False)
-    keyval_bulk = SeqSum(wire, index, along, keyval, *keyval_refs, keyval_sum, False)
+    key_bulk = SeqSum(wire, index, along, key_part, *key_refs, keyval_sum, False)
+    small_bulk = SeqSum(wire, index, along, small_part, *small_refs, small_own.at[0], False)
     gather = RowGather(wire, place, rows)
     spread = count // 2 - 1
-    first = 2 * spread // 3
     reduce.start()
-    for bulk in (out_bulk, query_bulk, keyval_bulk):
-        bulk.start()
+    query_bulk.start()
+    key_reduce.start()
     reduce.to_side(0)
-    out_bulk.relay(first)
+    key_reduce.to_side(0)
+    query_bulk.relay(spread // 3)
     reduce.ready()
     sums[...] = jnp.zeros_like(sums)
     gain = vec[0:1, :]
@@ -823,59 +831,79 @@
 
     by_rows(own.shape[0], 16, body)
     gather.start()
-    out_bulk.relay(spread - first)
+    small_part[...] = small[...]
+    width = own.shape[1] // count
+    for row in range(2):
+        line = jnp.sum(sums[row], axis=0, keepdims=True)
+        for block in range(count):
+            part = line[:, block * width : (block + 1) * width]
+            small_part[block, row : row + 1, 0:width] = part
+    small_bulk.start()
+    key_reduce.ready()
+    step = key_part.shape[1]
+    for block in range(count):
+        key_part[block] = key_reduce.total(slice(block * step, (block + 1) * step)).astype(LOW)
+    key_bulk.start()
+    query_bulk.relay(spread // 3)
     gather.forward()
-    query_bulk.relay(spread)
-    keyval_bulk.relay(spread)
-    for bulk in (out_bulk, query_bulk, keyval_bulk):
-        bulk.close()
+    small_bulk.relay(spread)
+    query_bulk.relay(spread - 2 * (spread // 3))
+    key_bulk.relay(spread)
+    small_bulk.close()
+    for turn, peer in enumerate((other_core, other_side)):
+        handle = wire.copy(small_own.at[turn], small_got.at[turn], peer)
+        wire.arrived(handle)
+        total = small_own[turn] + small_got[turn]
+        if turn:
+            small_sum[...] = total
+        else:
+            small_own[1] = total
+    query_bulk.close()
+    key_bulk.close()
     wire.finish()
 
 
-def last_stage(back, out, query, keyval, own, dy, vec):
+def last_stage(back, query, keyval, small, own, dy, vec):
     count = lax.axis_size("seq")
     tensor = lax.axis_size("tensor")
     part, full = own.shape
     vmem = pl.BlockSpec(memory_space=pltpu.VMEM)
-    bulk = (out, query, keyval)
-    copies = 3 * count + 8
-    scratch = row_sum_scratch(back)
-    for array in bulk:
-        scratch += seq_sum_scratch(array)
+    key_part = jax.ShapeDtypeStruct((count, keyval.shape[2] // count, keyval.shape[3]), LOW)
+    copies = 3 * count + 12
     return pl.pallas_call(
         partial(last_kernel, count),
-        out_shape=[jax.ShapeDtypeStruct(array.shape[1:], F32) for array in bulk]
-        + [
+        out_shape=[
+            jax.ShapeDtypeStruct(query.shape[1:], F32),
+            jax.ShapeDtypeStruct(key_part.shape[1:], F32),
             jax.ShapeDtypeStruct((tensor, part, full), LOW),
-            jax.ShapeDtypeStruct((2, 16, full), F32),
+            jax.ShapeDtypeStruct(small.shape[1:], F32),
         ],
         in_specs=[vmem] * 7,
-        out_specs=[vmem] * 5,
-        scratch_shapes=scratch + sem_scratch(copies),
+        out_specs=[vmem] * 4,
+        scratch_shapes=row_sum_scratch(back)
+        + row_sum_scratch(keyval)
+        + seq_sum_scratch(query)
+        + seq_sum_scratch(key_part)
+        + seq_sum_scratch(small, F32)
+        + [
+            pltpu.VMEM(key_part.shape, LOW),
+            pltpu.VMEM(small.shape, F32),
+            pltpu.VMEM((2,) + small.shape[1:], F32),
+            pltpu.VMEM((2,) + small.shape[1:], F32),
+            pltpu.VMEM((2, 16, full), F32),
+        ]
+        + sem_scratch(copies),
         compiler_params=pltpu.CompilerParams(
             collective_id=4, has_side_effects=True, vmem_limit_bytes=60 << 20
         ),
         name="last",
-    )(back, out, query, keyval, own, dy, vec)
+    )(back, query, keyval, small, own, dy, vec)
 
 
 def visible(meta_q, meta_k):
     seg_q, pos_q = meta_q[:, 0:1], meta_q[:, 1:2]
     seg_k, pos_k = meta_k[0:1, :], meta_k[1:2, :]
     return ((seg_k == 0) | (seg_k == seg_q)) & (pos_k <= pos_q)
-
-
-def tensor_scatter(parts, axis):
-    count = lax.axis_size("tensor")
-    index = lax.axis_index("tensor")
-    for bit in range(bits_of(count)):
-        shape = parts.shape
-        split = parts.reshape(shape[:axis] + (shape[axis] // 2, 2) + shape[axis + 1 :])
-        mine = (index >> bit) & 1
-        keep = lax.dynamic_index_in_dim(split, mine, axis + 1, keepdims=False)
-        give = lax.dynamic_index_in_dim(split, 1 - mine, axis + 1, keepdims=False)
-        parts = keep.astype(F32) + swap(give.astype(LOW), "tensor", bit).astype(F32)
-    return lax.squeeze(parts, (axis,))
 
 
 def norm_parts(values):
@@ -1042,9 +1070,10 @@
 
     grad_mixed = by_batch(dot(grad_middle_low, out_t).astype(LOW))
     feed_part = dot_nt(active, proj_t).astype(LOW)
-    fc_sum, grad_queries, grad_keyval, result_rows = back_stage(
+    fc_sum, out_sum, grad_queries, grad_keyval, result_rows = back_stage(
         feed_part.reshape(2, tensor_size, batches * quarter, full_width),
         blocked(dot_tn(normed_two, grad_hidden)),
+        blocked(dot_tn(grad_middle_low, mixed_rows)),
         queries,
         kv_all,
         meta_q,
@@ -1059,17 +1088,6 @@
     grad_keyval = grad_keyval.reshape(-1, 2 * hd)
     grad_queries = grad_queries.reshape(-1, group_width)
     grad_normed = dot_nt(grad_queries, q_mat) + dot_nt(grad_keyval, kv_mat)
-    out_sum, query_sum, kv_sum, input_rows, sums_one = last_stage(
-        by_quarter(grad_normed.astype(LOW))[None],
-        blocked(dot_tn(grad_middle_low, mixed_rows)),
-        blocked(dot_tn(normed, grad_queries)),
-        blocked(dot_tn(normed, grad_keyval)),
-        my_quarter(inputs),
-        grad_middle,
-        one_row(gain_one),
-    )
-    input_grad = by_batch(input_rows)
-    grad_gain_one, grad_shift_one = jnp.sum(sums_one, axis=1)
     qbias_local = jnp.sum(grad_queries.astype(F32), axis=0)
     vbias_local = jnp.sum(grad_keyval[:, hd:].astype(F32), axis=0)
 
@@ -1083,47 +1101,52 @@
         tensor_index * hidden_width + unit_half * unit_width,
         0,
     )
+    chunk = full_hidden // seq_size
+    blank = jnp.zeros((full_width,), F32)
     vec_grads = jnp.stack(
+        [blank, blank, qbias_full, grad_out_bias, grad_gain_two, grad_shift_two, grad_proj_bias]
+    )
+
+    def in_rows(array):
+        array = jnp.pad(array, ((0, 0), (0, -array.shape[1] % width_block)))
+        return array.reshape(seq_size, -1, width_block)
+
+    vec_rows = 7
+    bias_rows = chunk // width_block
+    small_rows = jnp.concatenate(
         [
-            grad_gain_one,
-            grad_shift_one,
-            qbias_full,
-            grad_out_bias,
-            grad_gain_two,
-            grad_shift_two,
-            grad_proj_bias,
-        ]
-    )
-    chunk = full_hidden // seq_size
-    vec_cut = 7 * width_block
-    rows_all = jnp.concatenate(
-        [
-            jnp.swapaxes(vec_grads.reshape(7, seq_size, width_block), 0, 1).reshape(seq_size, -1),
-            fcbias_full.reshape(seq_size, chunk),
-            jnp.broadcast_to(vbias_local, (seq_size, hd)),
+            jnp.swapaxes(vec_grads.reshape(7, seq_size, width_block), 0, 1),
+            in_rows(fcbias_full.reshape(seq_size, chunk)),
+            in_rows(jnp.broadcast_to(vbias_local, (seq_size, hd))),
         ],
         axis=1,
     )
-    rows_all = jnp.pad(rows_all, ((0, 0), (0, -rows_all.shape[1] % 1024)))
-    rows_all = rows_all.reshape(seq_size, -1, 128)
-    for bit in reversed(range(bits_of(seq_size))):
-        size = rows_all.shape[0] // 2
-        mine = (seq_index >> bit) & 1
-        keep = lax.dynamic_slice_in_dim(rows_all, mine * size, size, 0)
-        give = lax.dynamic_slice_in_dim(rows_all, (1 - mine) * size, size, 0)
-        rows_all = keep + swap(give, "seq", bit)
-    small_sum = rows_all[0]
-    for bit in range(bits_of(tensor_size)):
-        small_sum = small_sum + swap(small_sum, "tensor", bit)
-    small_sum = small_sum.reshape(-1)
-    vec_grad = lax.dynamic_slice_in_dim(
-        small_sum[:vec_cut].reshape(7, width_block), tensor_index * shard, shard, 1
-    )
+    small_rows = jnp.pad(
+        small_rows,
+        ((0, 0), (0, -small_rows.shape[1] % 8), (0, -width_block % 128)),
+    )
+    key_grad = dot_tn(normed, grad_keyval).astype(LOW)
+    key_grad = key_grad.reshape(seq_size, tensor_size, -1, 2 * hd)
+    key_grad = jnp.swapaxes(key_grad, 0, 1).reshape(1, tensor_size, -1, 2 * hd)
+    query_sum, keyval_grad, input_rows, small_sum = last_stage(
+        by_quarter(grad_normed.astype(LOW))[None],
+        blocked(dot_tn(normed, grad_queries)),
+        key_grad,
+        small_rows,
+        my_quarter(inputs),
+        grad_middle,
+        one_row(gain_one),
+    )
+    input_grad = by_batch(input_rows)
+    small_sum = small_sum[:, :width_block]
+    vec_grad = lax.dynamic_slice_in_dim(small_sum[:vec_rows], tensor_index * shard, shard, 1)
     fcbias_grad = lax.dynamic_slice_in_dim(
-        small_sum[vec_cut : vec_cut + chunk], tensor_index * bias_shard, bias_shard, 0
-    )
-    vbias_grad = small_sum[vec_cut + chunk : vec_cut + chunk + hd]
-    keyval_grad = tensor_scatter(kv_sum.reshape(tensor_size, -1, 2 * hd), 0)
+        small_sum[vec_rows : vec_rows + bias_rows].reshape(-1),
+        tensor_index * bias_shard,
+        bias_shard,
+        0,
+    )
+    vbias_grad = small_sum[vec_rows + bias_rows :].reshape(-1)[:hd]
     return (
         result,
         input_grad,

time: 605 us -> 592 us (0.979)
  starting transfers between devices: 10.5 us -> 0 us
  local copies, waits for them, and re-layouts: 32.5 us -> 42.7 us
  matrix products: 62.8 us -> 55.4 us
    pallas_call x1, Pallas kernels: 90 us -> 121 us  [back_stage(): pl.pallas_call(partial(back_kernel, count), out_shape=[jax.ShapeDtypeStru...]
    pallas_call x1, Pallas kernels: 88.4 us -> 62.5 us  [last_stage(): pl.pallas_call(partial(last_kernel, count), out_shape=[jax.ShapeDtypeStru...]
    ppermute x7 -> x0, starting transfers between devices: 10.5 us -> none  [swap(): return lax.ppermute(value, axis, [(i, i ^ 1 << bit) for i in range(count)])]
    unnamed x67 -> x76, local copies, waits for them, and re-layouts: 7.79 us -> 13.9 us
  transfers between devices with their start and end apart: 7 -> 0, of which waited for: 4 -> 0; matrix products, arithmetic and copies ran while one was open for 2% -> 0% of each run, Pallas kernels for 0% -> 0%
where the time goes in v6:
time: 592 us; the launch traced here: 582 us
  Pallas kernels  465 us (79%)
  matrix products  55.4 us (9%)
  local copies, waits for them, and re-layouts  42.7 us (7%)
  other arithmetic  17.9 us (3%)
    pallas_call x1, Pallas kernels, front(): pl.pallas_call(partial(front_kernel, count), out_shape=[jax.ShapeDtypeStr...  167 us
    pallas_call x1, Pallas kernels, back_stage(): pl.pallas_call(partial(back_kernel, count), out_shape=[jax.ShapeDtypeStru...  121 us
    pallas_call x1, Pallas kernels, middle_stage(): pl.pallas_call(partial(middle_kernel, count), out_shape=[jax.ShapeDtypeSt...  69.4 us
    pallas_call x1, Pallas kernels, last_stage(): pl.pallas_call(partial(last_kernel, count), out_shape=[jax.ShapeDtypeStru...  62.5 us
    pallas_call x1, Pallas kernels, gather_first(): pl.pallas_call(partial(first_kernel, count, tensor), out_shape=[jax.Shape...  44.5 us
    dot_general x4, matrix products, dot_nt(): lax.dot_general(left, right, (((1,), (1,)), ((), ())), preferred_element_...  18.9 us
    dot_general x5, matrix products, dot_tn(): lax.dot_general(left, right, (((0,), (0,)), ((), ())), preferred_element_...  18.7 us
    dot_general x5, matrix products, dot(): return jnp.dot(left, right, preferred_element_type=F32)  17.8 us

profile of v6, /device:TPU:0, one launch (start us, length us, event | category | flops | bytes accessed | tf_op | source)
XLA Modules:
  0.0 582.0 jit_solution(14334844331183663089)
XLA Ops:
  0.7 0.8 convert_element_type.149
  3.7 1.9 convert_reduce_fusion
  5.7 2.3 fusion.2
  10.1 0.9 copy.93
  12.1 0.8 constant_dynamic-slice_fusion.2
  12.9 1.9 convert_reduce_fusion.2
  14.9 1.8 copy.94
  16.6 1.3 copy.95
  18.0 1.7 convert_element_type.173
  19.6 1.3 copy.96
  21.0 3.2 copy.97
  24.1 44.5 %gather_first.1 = (bf16[8,4,32,128]{3,2,1,0:T(8,128)(2,1)}, bf16[8,4,64,256]{3,2,1,0:T(8,128)(2,1)}, bf16[8,256,512]{2,1,0:T(8,128)(2,1)}) custom-call(bf16[32,128]{1,0:T(8,128)(2,1)} %pad_bitcast_fusion.refs_0_, bf16[64,256]{1,0:T(8,128)(2,1)} %convert_element_type.156.refs_1_, bf16[256,512]{1,0:T(8,128)(2,1)} %convert_element_type.157.refs_2_), custom_call_target="tpu_custom_call" | custom-call | tf_op jit(solution)/shard_map/gather_first/pallas_call | solution.py:156
  68.6 2.0 reshape.257
  70.6 0.9 slice_bitcast_fusion
  71.5 1.1 fusion.23
  72.7 0.8 slice.95
  77.3 0.8 fusion.5
  78.2 1.4 fusion.17
  79.6 2.1 fusion.16
  81.7 166.8 %front.1 = (bf16[2,256,512]{2,1,0:T(8,128)(2,1)}, f32[2,4,256,1]{3,2,1,0:T(8,128)}, bf16[2,8,256,256]{3,2,1,0:T(8,128)(2,1)}, bf16[8,256,512]{2,1,0:T(8,128)(2,1...) custom-call(bf16[2,256,512]{2,1,0:T(8,128)(2,1)} %bitcast.154, ...), custom_call_target="tpu_custom_call" | custom-call | tf_op jit(solution)/shard_map/front/pallas_call | solution.py:395
  248.6 1.1 copy.99
  249.7 2.1 pad_maximum_fusion
  252.5 2.8 copy-done.26
  255.3 4.5 fusion.25
  259.8 6.8 %convert_reduce_fusion.1 = (f32[1024]{0:T(1024)S(1)}, bf16[1024,1024]{1,0:T(8,128)(2,1)S(1)}) fusion(bf16[1024,2048]{1,0:T(8,128)(2,1)S(1)} %bitcast.141, bf16[2048,1024]{1,0:T(8,128)(2,1)S(1)} %bitcast.196, f32[1024,1024]{1,0:T(8,128)S(1)} %fusion.25, f32[1024]{0:T(1024)S(1)} %dynamic_slice.22), kind=kOutput, calls=%fused_computation.21 | convolution fusion | flops 4316986368 | bytes 14688256 | tf_op jit(solution)/shard_map/dot_general | solution.py:31
  267.0 8.4 %convolution_convert_fusion.1 = bf16[1024,2048]{1,0:T(8,128)(2,1)} fusion(bf16[1024,1024]{1,0:T(8,128)(2,1)S(1)} %get-tuple-element.123, bf16[2048,1024]{1,0:T(8,128)(2,1)} %bitcast.200), kind=kOutput, calls=%fused_computation.26 | convolution fusion | flops 4297064448 | bytes 10485760 | tf_op jit(solution)/shard_map/dot_general | solution.py:39
  275.5 6.2 %convolution_convert_fusion.2 = bf16[2048,1024]{1,0:T(8,128)(2,1)} fusion(bf16[1024,2048]{1,0:T(8,128)(2,1)S(1)} %bitcast.199, bf16[1024,1024]{1,0:T(8,128)(2,1)S(1)} %get-tuple-element.123), kind=kOutput, calls=%fused_computation.27 | convolution fusion | flops 4297064448 | bytes 10485760 | tf_op jit(solution)/shard_map/dot_general | solution.py:35
  281.7 7.2 %convolution_convert_fusion.3 = bf16[1024,2048]{1,0:T(8,128)(2,1)} fusion(bf16[2048,1024]{1,0:T(8,128)(2,1)S(1)} %bitcast.197, f32[1024,1024]{1,0:T(8,128)S(1)} %copy-done.30, f32[1024]{0:T(1024)S(1)} %dynamic_slice.22), kind=kOutput, calls=%fused_computation.28 | convolution fusion | flops 4307550208 | bytes 12587008 | tf_op jit(solution)/shard_map/dot_general | solution.py:39
  288.9 6.5 %convolution_convert_fusion = bf16[2048,1024]{1,0:T(8,128)(2,1)} fusion(bf16[1024,2048]{1,0:T(8,128)(2,1)S(1)} %bitcast.142, f32[1024,1024]{1,0:T(8,128)S(1)} %copy-done.30, f32[1024]{0:T(1024)S(1)} %dynamic_slice.22), kind=kOutput, calls=%fused_computation.25 | convolution fusion | flops 4307550208 | bytes 12587008 | tf_op jit(solution)/shard_map/dot_general | solution.py:35
  295.4 69.4 %middle.1 = (f32[256,2048]{1,0:T(8,128)}, f32[128,2048]{1,0:T(8,128)}, bf16[4,128,2048]{2,1,0:T(8,128)(2,1)}, f32[3,16,2048]{2,1,0:T(8,128)}) custom-call(bf16[2,4,128,2048]{3,2,1,0:T(8,128)(2,1)} %bitcast.143, bf16[8,256,1024]{2,1,0:T(8,128)(2,1)} %bitcast.144, f32[128,2048]{1,0:T(8,128)} %get-tuple-element.43.refs_2_.refs_10_, ...), custom_call_target="tpu_custom_call" | custom-call | tf_op jit(solution)/shard_map/middle/pallas_call | solution.py:626
  364.8 3.0 convolution_convert_fusion.5
  367.8 2.6 convolution_convert_fusion.4
  370.4 0.8 copy.100
  371.3 121.4 %back.1 = (f32[256,2048]{1,0:T(8,128)}, f32[256,512]{1,0:T(8,128)}, bf16[2,256,512]{2,1,0:T(8,128)(2,1)}, bf16[2,256,256]{2,1,0:T(8,128)(2,1)}, bf16[4,128,2048]{2,1,0:T(8,128)(2,1)}) custom-call(bf16[2,4,128,2048]{3,2,1,0:T(8,128)(2,1)} %bitcast.149, bf16[8,256,1024]{2,1,0:T(8,128)(2,1)} %bitcast.148, bf16[8,256,512]{2,1,0:T(8,128)(2,1)} %bitcast.168, ...), custom_call_target="tpu_custom_call" | custom-call | tf_op jit(solution)/shard_map/back/pallas_call | solution.py:768
  492.8 3.3 copy.101
  496.1 1.0 copy.107
  497.2 1.1 reduce_sum.66
  499.2 0.8 fusion.15
  500.0 2.6 bitcast_convert_fusion
  502.6 1.1 copy.105
  503.6 3.0 copy.108
  506.7 2.0 fusion.26
  508.7 1.3 add_convert_fusion
  509.9 1.5 copy.102
  511.4 62.5 %last.1 = (f32[256,512]{1,0:T(8,128)}, f32[64,256]{1,0:T(8,128)}, bf16[4,128,2048]{2,1,0:T(8,128)(2,1)}, f32[16,256]{1,0:T(8,128)}) custom-call(bf16[1,4,128,2048]{3,2,1,0:T(8,128)(2,1)} %bitcast.136, bf16[8,256,512]{2,1,0:T(8,128)(2,1)} %bitcast.165, bf16[1,4,512,256]{3,2,1,0:T(8,128)(2,1)} %bitcast.147, f32[8,16,256]{2,1,0:T(8,128)} %select_maximum_fusion.refs_3_, ...), custom_call_target="tpu_custom_call" | custom-call | tf_op jit(solution)/shard_map/last/pallas_call | solution.py:873
  574.0 3.3 copy.106
  579.1 0.8 copy.134
  580.5 1.3 copy.136
  (125 shorter events, 13.8 us)
Async XLA Ops:
  0.6 11.5 %copy-start = (bf16[2,256,2048]{2,1,0:T(8,128)(2,1)S(1)}, bf16[2,256,2048]{2,1,0:T(8,128)(2,1)}, u32[]{:S(2)}) copy-start(bf16[2,256,2048]{2,1,0:T(8,128)(2,1)} %param.12) | copy-start | bytes 6291460
  0.7 7.3 %copy-start.19 = (s32[2,256]{1,0:T(2,128)S(1)}, s32[2,256]{1,0:T(2,128)}, u32[]{:S(2)}) copy-start(s32[2,256]{1,0:T(2,128)} %param.14) | copy-start | bytes 6148
  0.7 10.4 %copy-start.20 = (s32[2,256]{1,0:T(2,128)S(1)}, s32[2,256]{1,0:T(2,128)}, u32[]{:S(2)}) copy-start(s32[2,256]{1,0:T(2,128)} %param.13) | copy-start | bytes 6148
  0.7 9.4 %copy-start.13 = (f32[512,256]{1,0:T(8,128)S(1)}, f32[512,256]{1,0:T(8,128)}, u32[]{:S(2)}) copy-start(f32[512,256]{1,0:T(8,128)} %param.17) | copy-start | bytes 1572868
  0.7 8.0 %copy-start.16 = (f32[64,256]{1,0:T(8,128)S(1)}, f32[64,256]{1,0:T(8,128)}, u32[]{:S(2)}) copy-start(f32[64,256]{1,0:T(8,128)} %param.16) | copy-start | bytes 196612
  0.7 8.6 %copy-start.12 = (f32[256,512]{1,0:T(8,128)S(1)}, f32[256,512]{1,0:T(8,128)}, u32[]{:S(2)}) copy-start(f32[256,512]{1,0:T(8,128)} %param.15) | copy-start | bytes 1572868
  68.6 9.6 %copy-start.10 = (bf16[8,4,64,256]{3,2,1,0:T(8,128)(2,1)S(1)}, bf16[8,4,64,256]{3,2,1,0:T(8,128)(2,1)}, u32[]{:S(2)}) copy-start(bf16[8,4,64,256]{3,2,1,0:T(8,128)(2,1)} %get-tuple-element.38) | copy-start | bytes 3145732
  76.7 3.0 copy-start.4
  78.2 3.5 copy-start.6
  81.7 167.9 %copy-start.1 = (bf16[2,4,64,2048]{3,2,0,1:T(8,128)(2,1)S(1)}, bf16[2,4,64,2048]{3,2,0,1:T(8,128)(2,1)}, u32[]{:S(2)}) copy-start(bf16[2,4,64,2048]{3,2,0,1:T(8,128)(2,1)} %copy.97) | copy-start | bytes 6291460
  249.7 2.8 copy-start.24
  249.7 5.6 copy-start.26
  251.8 8.0 %copy-start.2 = (bf16[8,128,2048]{2,1,0:T(8,128)(2,1)}, bf16[8,128,2048]{2,1,0:T(8,128)(2,1)S(1)}, u32[]{:S(2)}) copy-start(bf16[8,128,2048]{2,1,0:T(8,128)(2,1)S(1)} %pad_maximum_fusion) | copy-start | bytes 12582916
  255.3 4.5 copy-start.22
  259.8 6.9 %copy-start.29 = (f32[1024,1024]{1,0:T(8,128)}, f32[1024,1024]{1,0:T(8,128)S(1)}, u32[]{:S(2)}) copy-start(f32[1024,1024]{1,0:T(8,128)S(1)} %fusion.25) | copy-start | bytes 12582916
  267.0 8.4 %copy-start.25 = (bf16[2,4,128,2048]{3,2,1,0:T(8,128)(2,1)S(1)}, bf16[2,4,128,2048]{3,2,1,0:T(8,128)(2,1)}, u32[]{:S(2)}) copy-start(bf16[2,4,128,2048]{3,2,1,0:T(8,128)(2,1)} %get-tuple-element.39) | copy-start | bytes 12582916
  275.5 6.2 %copy-start.23 = (bf16[8,256,1024]{2,1,0:T(8,128)(2,1)S(1)}, bf16[8,256,1024]{2,1,0:T(8,128)(2,1)}, u32[]{:S(2)}) copy-start(bf16[8,256,1024]{2,1,0:T(8,128)(2,1)} %get-tuple-element.41) | copy-start | bytes 12582916
  275.5 6.2 %copy-start.30 = (f32[1024,1024]{1,0:T(8,128)S(1)}, f32[1024,1024]{1,0:T(8,128)}, u32[]{:S(2)}) copy-start(f32[1024,1024]{1,0:T(8,128)} %copy-done.29) | copy-start | bytes 12582916
  281.7 7.2 %copy-start.3 = (bf16[8,128,2048]{2,1,0:T(8,128)(2,1)S(1)}, bf16[8,128,2048]{2,1,0:T(8,128)(2,1)}, u32[]{:S(2)}) copy-start(bf16[8,128,2048]{2,1,0:T(8,128)(2,1)} %copy-done.2) | copy-start | bytes 12582916
  295.4 69.5 %copy-start.27 = (bf16[8,256,512]{2,1,0:T(8,128)(2,1)S(1)}, bf16[8,256,512]{2,1,0:T(8,128)(2,1)}, u32[]{:S(2)}) copy-start(bf16[8,256,512]{2,1,0:T(8,128)(2,1)} %get-tuple-element.48) | copy-start | bytes 6291460
  364.8 3.0 copy-start.28
  492.7 3.4 copy-start.15
  492.7 4.3 copy-start.11
  492.7 5.5 copy-start.8
  492.7 6.4 %copy-start.7 = (bf16[2,256,2048]{2,1,0:T(8,128)(2,1)S(1)}, bf16[2,256,2048]{2,1,0:T(8,128)(2,1)}, u32[]{:S(2)}) copy-start(bf16[2,256,2048]{2,1,0:T(8,128)(2,1)} %copy-done.6) | copy-start | bytes 6291460
  503.6 5.0 copy-start.5
  573.9 3.4 copy-start.18
  574.0 5.1 copy-start.14
  574.0 5.9 %copy-start.17 = (f32[64,256]{1,0:T(8,128)S(1)}, f32[64,256]{1,0:T(8,128)}, u32[]{:S(2)}) copy-start(f32[64,256]{1,0:T(8,128)} %get-tuple-element.140) | copy-start | bytes 196612
  574.0 6.5 %copy-start.9 = (f32[256,2048]{1,0:T(8,128)S(1)}, f32[256,2048]{1,0:T(8,128)}, u32[]{:S(2)}) copy-start(f32[256,2048]{1,0:T(8,128)} %get-tuple-element.142) | copy-start | bytes 6291460
  578.0 3.8 copy-start.21

commit v7 on v6

--- a/solution.py
+++ b/solution.py
@@ -95,6 +95,10 @@
     return [{"seq": flip(index, 2 * d)} for d in range(1, count // 2)] + [
         {"seq": flip(index, 1)}
     ]
+
+
+def turns(lines):
+    return list(range(lines // 2, lines)) + list(range(1, lines // 2))
 
 
 def first_kernel(count, tensor, *refs):
@@ -112,19 +116,19 @@
     targets.append(lambda at: outs[2].at[at])
     handles = []
     for source, target in zip(ins, targets):
-        handles.append([wire.copy(source, target(index), peer) for peer in far])
-        handles[-1].append(wire.copy(source, target(index), near))
+        handles.append({d: wire.copy(source, target(index), far[d - 1]) for d in range(1, count // 2)})
+        handles[-1][0] = wire.copy(source, target(index), near)
         item = pltpu.make_async_copy(source, target(index), local_sem.at[len(own)])
         item.start()
         own.append(item)
     relays = []
     for a, target in enumerate(targets):
         for d in range(1, count // 2):
-            wire.arrived(handles[a][d - 1])
+            wire.arrived(handles[a][d])
             block = target(flip(index, 2 * d))
             relays.append(wire.copy(block, block, near))
         if a == 1:
-            for handle in [handles[0][-1], handles[1][-1]] + relays:
+            for handle in [handles[0][0], handles[1][0]] + relays:
                 wire.arrived(handle)
             own[0].wait()
             own[1].wait()
@@ -205,26 +209,26 @@
         item.start()
         own.append(item)
 
-    kv_far = [wire.copy(kv_in.at[core], kv_all.at[core, index], peer) for peer in far]
+    order = range(1, lines)
+    kv_far = {d: wire.copy(kv_in.at[core], kv_all.at[core, index], far[d - 1]) for d in order}
     kv_near = wire.copy(kv_in.at[core], kv_all.at[core, index], near)
     for batch in range(2):
         keep(kv_in.at[batch], kv_all.at[batch, index])
-    o_far = [wire.copy(o_in, out_t.at[index], peer) for peer in far]
+    o_far = {d: wire.copy(o_in, out_t.at[index], far[d - 1]) for d in order}
     o_near = [wire.copy(o_in, out_t.at[index], near)]
     keep(o_in, out_t.at[index])
     dy_pair = wire.copy(dy_in.at[place], dy_out.at[place], pair)
 
     def send_far(source, out):
-        return [
-            wire.copy(source.at[flip(half, d & 1)], out.at[index], far[d - 1])
-            for d in range(1, lines)
-        ]
+        return {
+            d: wire.copy(source.at[flip(half, d & 1)], out.at[index], far[d - 1]) for d in order
+        }
 
     fc_far = send_far(fc_in, fc_out)
     kv_near = [(1, kv_near)]
     kv_core = []
-    for d in range(1, lines):
-        wire.arrived(kv_far[d - 1])
+    for d in order:
+        wire.arrived(kv_far[d])
         block = kv_all.at[core, flip(index, 2 * d)]
         kv_near.append((2 * d + 1, wire.copy(block, block, near)))
         kv_core.append(wire.copy(block, block, other_core))
@@ -239,13 +243,13 @@
     own[0].wait()
     own[1].wait()
 
-    jobs = [(o_far, out_t, d) for d in range(1, lines)]
-    jobs += [(fc_far, fc_out, d) for d in range(1, lines)]
+    jobs = [(o_far, out_t, d) for d in order]
+    jobs += [(fc_far, fc_out, d) for d in order]
 
     def tick(number):
         for _ in range(min(number, len(jobs))):
             handles, out, d = jobs.pop(0)
-            wire.arrived(handles[d - 1])
+            wire.arrived(handles[d])
             block = out.at[flip(index, 2 * d)]
             handle = wire.copy(block, block, near)
             if out is out_t:
@@ -355,7 +359,7 @@
     wire.copy(mine, mine, other_core)
     pj_far = send_far(pj_in, pj_out)
     tick(len(jobs))
-    jobs.extend((pj_far, pj_out, d) for d in range(1, lines))
+    jobs.extend((pj_far, pj_out, d) for d in order)
     wire.arrived(pair_handle)
     theirs = rows_two.at[1, place]
     side_two = wire.copy(theirs, theirs, other_side)
@@ -435,17 +439,16 @@
         self.rows = part.shape[1]
         self.step = min(64, self.rows)
         self.near_handles, self.far_handles = {}, {}
-        self.next = 1
+        self.order = turns(self.lines)
 
     def start(self, order=None):
-        for d in order or list(range(1, self.lines)) + [0]:
+        for d in order or turns(self.lines) + [0]:
             block = self.part.at[flip(self.index, 2 * d + 1)]
             self.near_handles[d] = self.wire.copy(block, self.from_near.at[d], self.near)
 
     def relay(self, number):
         for _ in range(number):
-            d = self.next
-            self.next += 1
+            d = self.order.pop(0)
             self.wire.arrived(self.near_handles[d])
 
             def join(at, d=d):
@@ -651,7 +654,6 @@
     other_core = {"tensor": flip(place, 1)}
     along = seq_peers(index, count)
     lines = count // 2
-    spread = lines - 1
     greet(along + [other_core, {"tensor": flip(place, 2)}])
     wire = Wire(send_sem, recv_sem)
     reduce = RowSum(wire, place, along[0], feed, *row_refs)
@@ -711,29 +713,36 @@
         ]
 
     reduce.start()
-    bulk.start(list(range(1, lines)))
+    middle, edge = turns(lines)[: lines // 2], turns(lines)[lines // 2 :]
+    bulk.start(middle)
+    out_bulk.start(middle)
+    bulk.start(edge)
+    out_bulk.start(edge)
     open_batch(1 - core)
     blocks_of(1 - core, near_x, kv_send, None)
     near_handles = to_core(near_x)
     reduce.to_side(1)
     reduce.to_side(0)
+    bulk.relay(lines // 4)
     blocks_of(1 - core, 1 - near_x, kv_send, None)
     own_handles = to_core(1 - near_x)
     close_batch(1 - core)
-    bulk.relay(spread // 3)
+    bulk.relay(lines // 2 - lines // 4)
     for handle in near_handles:
         wire.arrived(handle)
     open_batch(core)
     blocks_of(core, near_x, kv_part, kv_got)
     keys_sum.start()
     bulk.start([0])
-    out_bulk.start()
+    out_bulk.start([0])
     reduce.to_pair()
-    bulk.relay(spread // 3)
+    out_bulk.relay(lines // 2)
     for handle in own_handles:
         wire.arrived(handle)
     blocks_of(core, 1 - near_x, kv_part, kv_got)
     close_batch(core)
+    bulk.relay(len(edge))
+    out_bulk.relay(len(edge))
     reduce.ready()
     bias = vec[0:1, :]
 
@@ -743,10 +752,8 @@
 
     by_rows(centre.shape[0], 16, body)
     gather.start()
-    keys_sum.relay(spread)
-    bulk.relay(spread - 2 * (spread // 3))
+    keys_sum.relay(lines - 1)
     gather.forward()
-    out_bulk.relay(spread)
     keys_sum.close()
     dkv[1 - core] = jnp.zeros(dkv.shape[1:], LOW)
     dkv[core] = kv_total[...].astype(LOW)

time: 592 us -> 574 us (0.970)
  Pallas kernels: 465 us -> 446 us
    pallas_call x1, Pallas kernels: 121 us -> 110 us  [back_stage(): pl.pallas_call(partial(back_kernel, count), out_shape=[jax.ShapeDtypeStru...]
    pallas_call x1, Pallas kernels: 62.5 us -> 50.9 us  [last_stage(): pl.pallas_call(partial(last_kernel, count), out_shape=[jax.ShapeDtypeStru...]
where the time goes in v7:
time: 574 us; the launch traced here: 563 us
  Pallas kernels  446 us (78%)
  matrix products  55.4 us (10%)
  local copies, waits for them, and re-layouts  42.7 us (7%)
  other arithmetic  17.9 us (3%)
    pallas_call x1, Pallas kernels, front(): pl.pallas_call(partial(front_kernel, count), out_shape=[jax.ShapeDtypeStr...  167 us
    pallas_call x1, Pallas kernels, back_stage(): pl.pallas_call(partial(back_kernel, count), out_shape=[jax.ShapeDtypeStru...  110 us
    pallas_call x1, Pallas kernels, middle_stage(): pl.pallas_call(partial(middle_kernel, count), out_shape=[jax.ShapeDtypeSt...  74.1 us
    pallas_call x1, Pallas kernels, last_stage(): pl.pallas_call(partial(last_kernel, count), out_shape=[jax.ShapeDtypeStru...  50.9 us
    pallas_call x1, Pallas kernels, gather_first(): pl.pallas_call(partial(first_kernel, count, tensor), out_shape=[jax.Shape...  44.5 us
    dot_general x4, matrix products, dot_nt(): lax.dot_general(left, right, (((1,), (1,)), ((), ())), preferred_element_...  18.9 us
    dot_general x5, matrix products, dot_tn(): lax.dot_general(left, right, (((0,), (0,)), ((), ())), preferred_element_...  18.7 us
    dot_general x5, matrix products, dot(): return jnp.dot(left, right, preferred_element_type=F32)  17.8 us

profile of v7, /device:TPU:0, one launch (start us, length us, event | category | flops | bytes accessed | tf_op | source)
XLA Modules:
  0.0 563.3 jit_solution(1841597212283229139)
XLA Ops:
  0.7 0.8 convert_element_type.149
  3.7 1.9 convert_reduce_fusion
  5.7 2.3 fusion.2
  10.1 0.9 copy.93
  12.1 0.8 constant_dynamic-slice_fusion.2
  12.9 1.9 convert_reduce_fusion.2
  14.9 1.8 copy.94
  16.6 1.3 copy.95
  18.0 1.7 convert_element_type.173
  19.6 1.3 copy.96
  21.0 3.2 copy.97
  24.1 44.5 %gather_first.1 = (bf16[8,4,32,128]{3,2,1,0:T(8,128)(2,1)}, bf16[8,4,64,256]{3,2,1,0:T(8,128)(2,1)}, bf16[8,256,512]{2,1,0:T(8,128)(2,1)}) custom-call(bf16[32,128]{1,0:T(8,128)(2,1)} %pad_bitcast_fusion.refs_0_, bf16[64,256]{1,0:T(8,128)(2,1)} %convert_element_type.156.refs_1_, bf16[256,512]{1,0:T(8,128)(2,1)} %convert_element_type.157.refs_2_), custom_call_target="tpu_custom_call" | custom-call | tf_op jit(solution)/shard_map/gather_first/pallas_call | solution.py:160
  68.6 2.0 reshape.257
  70.6 0.9 slice_bitcast_fusion
  71.5 1.1 fusion.23
  72.7 0.8 slice.95
  77.3 0.8 fusion.5
  78.2 1.4 fusion.17
  79.6 2.1 fusion.16
  81.7 166.8 %front.1 = (bf16[2,256,512]{2,1,0:T(8,128)(2,1)}, f32[2,4,256,1]{3,2,1,0:T(8,128)}, bf16[2,8,256,256]{3,2,1,0:T(8,128)(2,1)}, bf16[8,256,512]{2,1,0:T(8,128)(2,1...) custom-call(bf16[2,256,512]{2,1,0:T(8,128)(2,1)} %bitcast.154, ...), custom_call_target="tpu_custom_call" | custom-call | tf_op jit(solution)/shard_map/front/pallas_call | solution.py:399
  248.6 1.1 copy.99
  249.7 2.1 pad_maximum_fusion
  252.5 2.8 copy-done.26
  255.3 4.5 fusion.25
  259.8 6.8 %convert_reduce_fusion.1 = (f32[1024]{0:T(1024)S(1)}, bf16[1024,1024]{1,0:T(8,128)(2,1)S(1)}) fusion(bf16[1024,2048]{1,0:T(8,128)(2,1)S(1)} %bitcast.141, bf16[2048,1024]{1,0:T(8,128)(2,1)S(1)} %bitcast.196, f32[1024,1024]{1,0:T(8,128)S(1)} %fusion.25, f32[1024]{0:T(1024)S(1)} %dynamic_slice.22), kind=kOutput, calls=%fused_computation.21 | convolution fusion | flops 4316986368 | bytes 14688256 | tf_op jit(solution)/shard_map/dot_general | solution.py:31
  267.0 8.4 %convolution_convert_fusion.1 = bf16[1024,2048]{1,0:T(8,128)(2,1)} fusion(bf16[1024,1024]{1,0:T(8,128)(2,1)S(1)} %get-tuple-element.123, bf16[2048,1024]{1,0:T(8,128)(2,1)} %bitcast.200), kind=kOutput, calls=%fused_computation.26 | convolution fusion | flops 4297064448 | bytes 10485760 | tf_op jit(solution)/shard_map/dot_general | solution.py:39
  275.5 6.2 %convolution_convert_fusion.2 = bf16[2048,1024]{1,0:T(8,128)(2,1)} fusion(bf16[1024,2048]{1,0:T(8,128)(2,1)S(1)} %bitcast.199, bf16[1024,1024]{1,0:T(8,128)(2,1)S(1)} %get-tuple-element.123), kind=kOutput, calls=%fused_computation.27 | convolution fusion | flops 4297064448 | bytes 10485760 | tf_op jit(solution)/shard_map/dot_general | solution.py:35
  281.7 7.2 %convolution_convert_fusion.3 = bf16[1024,2048]{1,0:T(8,128)(2,1)} fusion(bf16[2048,1024]{1,0:T(8,128)(2,1)S(1)} %bitcast.197, f32[1024,1024]{1,0:T(8,128)S(1)} %copy-done.30, f32[1024]{0:T(1024)S(1)} %dynamic_slice.22), kind=kOutput, calls=%fused_computation.28 | convolution fusion | flops 4307550208 | bytes 12587008 | tf_op jit(solution)/shard_map/dot_general | solution.py:39
  288.9 6.5 %convolution_convert_fusion = bf16[2048,1024]{1,0:T(8,128)(2,1)} fusion(bf16[1024,2048]{1,0:T(8,128)(2,1)S(1)} %bitcast.142, f32[1024,1024]{1,0:T(8,128)S(1)} %copy-done.30, f32[1024]{0:T(1024)S(1)} %dynamic_slice.22), kind=kOutput, calls=%fused_computation.25 | convolution fusion | flops 4307550208 | bytes 12587008 | tf_op jit(solution)/shard_map/dot_general | solution.py:35
  295.4 74.1 %middle.1 = (f32[256,2048]{1,0:T(8,128)}, f32[128,2048]{1,0:T(8,128)}, bf16[4,128,2048]{2,1,0:T(8,128)(2,1)}, f32[3,16,2048]{2,1,0:T(8,128)}) custom-call(bf16[2,4,128,2048]{3,2,1,0:T(8,128)(2,1)} %bitcast.143, bf16[8,256,1024]{2,1,0:T(8,128)(2,1)} %bitcast.144, f32[128,2048]{1,0:T(8,128)} %get-tuple-element.43.refs_2_.refs_10_, ...), custom_call_target="tpu_custom_call" | custom-call | tf_op jit(solution)/shard_map/middle/pallas_call | solution.py:629
  369.5 3.0 convolution_convert_fusion.5
  372.5 2.6 convolution_convert_fusion.4
  375.1 0.8 copy.100
  376.0 109.7 %back.1 = (f32[256,2048]{1,0:T(8,128)}, f32[256,512]{1,0:T(8,128)}, bf16[2,256,512]{2,1,0:T(8,128)(2,1)}, bf16[2,256,256]{2,1,0:T(8,128)(2,1)}, bf16[4,128,2048]{2,1,0:T(8,128)(2,1)}) custom-call(bf16[2,4,128,2048]{3,2,1,0:T(8,128)(2,1)} %bitcast.149, bf16[8,256,1024]{2,1,0:T(8,128)(2,1)} %bitcast.148, bf16[8,256,512]{2,1,0:T(8,128)(2,1)} %bitcast.168, ...), custom_call_target="tpu_custom_call" | custom-call | tf_op jit(solution)/shard_map/back/pallas_call | solution.py:775
  485.7 3.3 copy.101
  489.0 1.0 copy.107
  490.1 1.1 reduce_sum.66
  492.1 0.8 fusion.15
  492.9 2.6 bitcast_convert_fusion
  495.5 1.1 copy.105
  496.5 3.0 copy.108
  499.6 2.0 fusion.26
  501.6 1.3 add_convert_fusion
  502.8 1.5 copy.102
  504.3 50.9 %last.1 = (f32[256,512]{1,0:T(8,128)}, f32[64,256]{1,0:T(8,128)}, bf16[4,128,2048]{2,1,0:T(8,128)(2,1)}, f32[16,256]{1,0:T(8,128)}) custom-call(bf16[1,4,128,2048]{3,2,1,0:T(8,128)(2,1)} %bitcast.136, bf16[8,256,512]{2,1,0:T(8,128)(2,1)} %bitcast.165, bf16[1,4,512,256]{3,2,1,0:T(8,128)(2,1)} %bitcast.147, f32[8,16,256]{2,1,0:T(8,128)} %select_maximum_fusion.refs_3_, ...), custom_call_target="tpu_custom_call" | custom-call | tf_op jit(solution)/shard_map/last/pallas_call | solution.py:880
  555.3 3.3 copy.106
  560.3 0.8 copy.134
  561.8 1.3 copy.136
  (125 shorter events, 13.8 us)
Async XLA Ops:
  0.6 11.5 %copy-start = (bf16[2,256,2048]{2,1,0:T(8,128)(2,1)S(1)}, bf16[2,256,2048]{2,1,0:T(8,128)(2,1)}, u32[]{:S(2)}) copy-start(bf16[2,256,2048]{2,1,0:T(8,128)(2,1)} %param.12) | copy-start | bytes 6291460
  0.7 7.3 %copy-start.19 = (s32[2,256]{1,0:T(2,128)S(1)}, s32[2,256]{1,0:T(2,128)}, u32[]{:S(2)}) copy-start(s32[2,256]{1,0:T(2,128)} %param.14) | copy-start | bytes 6148
  0.7 10.4 %copy-start.20 = (s32[2,256]{1,0:T(2,128)S(1)}, s32[2,256]{1,0:T(2,128)}, u32[]{:S(2)}) copy-start(s32[2,256]{1,0:T(2,128)} %param.13) | copy-start | bytes 6148
  0.7 9.4 %copy-start.13 = (f32[512,256]{1,0:T(8,128)S(1)}, f32[512,256]{1,0:T(8,128)}, u32[]{:S(2)}) copy-start(f32[512,256]{1,0:T(8,128)} %param.17) | copy-start | bytes 1572868
  0.7 8.0 %copy-start.16 = (f32[64,256]{1,0:T(8,128)S(1)}, f32[64,256]{1,0:T(8,128)}, u32[]{:S(2)}) copy-start(f32[64,256]{1,0:T(8,128)} %param.16) | copy-start | bytes 196612
  0.7 8.6 %copy-start.12 = (f32[256,512]{1,0:T(8,128)S(1)}, f32[256,512]{1,0:T(8,128)}, u32[]{:S(2)}) copy-start(f32[256,512]{1,0:T(8,128)} %param.15) | copy-start | bytes 1572868
  68.6 9.6 %copy-start.10 = (bf16[8,4,64,256]{3,2,1,0:T(8,128)(2,1)S(1)}, bf16[8,4,64,256]{3,2,1,0:T(8,128)(2,1)}, u32[]{:S(2)}) copy-start(bf16[8,4,64,256]{3,2,1,0:T(8,128)(2,1)} %get-tuple-element.38) | copy-start | bytes 3145732
  76.7 3.0 copy-start.4
  78.2 3.5 copy-start.6
  81.7 167.9 %copy-start.1 = (bf16[2,4,64,2048]{3,2,0,1:T(8,128)(2,1)S(1)}, bf16[2,4,64,2048]{3,2,0,1:T(8,128)(2,1)}, u32[]{:S(2)}) copy-start(bf16[2,4,64,2048]{3,2,0,1:T(8,128)(2,1)} %copy.97) | copy-start | bytes 6291460
  249.7 2.8 copy-start.24
  249.7 5.6 copy-start.26
  251.8 8.0 %copy-start.2 = (bf16[8,128,2048]{2,1,0:T(8,128)(2,1)}, bf16[8,128,2048]{2,1,0:T(8,128)(2,1)S(1)}, u32[]{:S(2)}) copy-start(bf16[8,128,2048]{2,1,0:T(8,128)(2,1)S(1)} %pad_maximum_fusion) | copy-start | bytes 12582916
  255.3 4.5 copy-start.22
  259.8 6.9 %copy-start.29 = (f32[1024,1024]{1,0:T(8,128)}, f32[1024,1024]{1,0:T(8,128)S(1)}, u32[]{:S(2)}) copy-start(f32[1024,1024]{1,0:T(8,128)S(1)} %fusion.25) | copy-start | bytes 12582916
  267.0 8.4 %copy-start.25 = (bf16[2,4,128,2048]{3,2,1,0:T(8,128)(2,1)S(1)}, bf16[2,4,128,2048]{3,2,1,0:T(8,128)(2,1)}, u32[]{:S(2)}) copy-start(bf16[2,4,128,2048]{3,2,1,0:T(8,128)(2,1)} %get-tuple-element.39) | copy-start | bytes 12582916
  275.5 6.2 %copy-start.23 = (bf16[8,256,1024]{2,1,0:T(8,128)(2,1)S(1)}, bf16[8,256,1024]{2,1,0:T(8,128)(2,1)}, u32[]{:S(2)}) copy-start(bf16[8,256,1024]{2,1,0:T(8,128)(2,1)} %get-tuple-element.41) | copy-start | bytes 12582916
  275.5 6.2 %copy-start.30 = (f32[1024,1024]{1,0:T(8,128)S(1)}, f32[1024,1024]{1,0:T(8,128)}, u32[]{:S(2)}) copy-start(f32[1024,1024]{1,0:T(8,128)} %copy-done.29) | copy-start | bytes 12582916
  281.7 7.2 %copy-start.3 = (bf16[8,128,2048]{2,1,0:T(8,128)(2,1)S(1)}, bf16[8,128,2048]{2,1,0:T(8,128)(2,1)}, u32[]{:S(2)}) copy-start(bf16[8,128,2048]{2,1,0:T(8,128)(2,1)} %copy-done.2) | copy-start | bytes 12582916
  295.4 74.1 %copy-start.27 = (bf16[8,256,512]{2,1,0:T(8,128)(2,1)S(1)}, bf16[8,256,512]{2,1,0:T(8,128)(2,1)}, u32[]{:S(2)}) copy-start(bf16[8,256,512]{2,1,0:T(8,128)(2,1)} %get-tuple-element.48) | copy-start | bytes 6291460
  369.5 3.0 copy-start.28
  485.6 3.4 copy-start.15
  485.6 4.3 copy-start.11
  485.6 5.5 copy-start.8
  485.6 6.4 %copy-start.7 = (bf16[2,256,2048]{2,1,0:T(8,128)(2,1)S(1)}, bf16[2,256,2048]{2,1,0:T(8,128)(2,1)}, u32[]{:S(2)}) copy-start(bf16[2,256,2048]{2,1,0:T(8,128)(2,1)} %copy-done.6) | copy-start | bytes 6291460
  496.5 5.0 copy-start.5
  555.2 3.4 copy-start.18
  555.2 5.1 copy-start.14
  555.2 5.9 %copy-start.17 = (f32[64,256]{1,0:T(8,128)S(1)}, f32[64,256]{1,0:T(8,128)}, u32[]{:S(2)}) copy-start(f32[64,256]{1,0:T(8,128)} %get-tuple-element.140) | copy-start | bytes 196612
  555.2 6.5 %copy-start.9 = (f32[256,2048]{1,0:T(8,128)S(1)}, f32[256,2048]{1,0:T(8,128)}, u32[]{:S(2)}) copy-start(f32[256,2048]{1,0:T(8,128)} %get-tuple-element.142) | copy-start | bytes 6291460
  559.3 3.8 copy-start.21

commit v8 on v7

--- a/solution.py
+++ b/solution.py
@@ -195,12 +195,11 @@
     half = lax.rem(lax.div(index, 2), 2)
     other_core = {"tensor": flip(place, 1)}
     other_side = {"tensor": flip(place, 2)}
-    across = {"tensor": flip(place, 3)}
     along = seq_peers(index, count)
     far, near = along[:-1], along[-1]
     pair = far[0]
     lines = count // 2
-    greet(along + [other_core, other_side, across])
+    greet(along + [other_core, other_side])
     wire = Wire(send_sem, recv_sem)
     own = []
 
@@ -219,9 +218,9 @@
     keep(o_in, out_t.at[index])
     dy_pair = wire.copy(dy_in.at[place], dy_out.at[place], pair)
 
-    def send_far(source, out):
+    def send_far(source, out, which=order):
         return {
-            d: wire.copy(source.at[flip(half, d & 1)], out.at[index], far[d - 1]) for d in order
+            d: wire.copy(source.at[flip(half, d & 1)], out.at[index], far[d - 1]) for d in which
         }
 
     fc_far = send_far(fc_in, fc_out)
@@ -293,13 +292,17 @@
             lse[batch, head] = top[head] + jnp.log2(total[head])
 
     spread = lines - 1
-    attend_batch(core, [spread // 3, spread - spread // 3])
+    attend_batch(core, [spread])
+    pj_far = send_far(pj_in, pj_out, order[:1])
+    wire.arrived(dy_pair)
+    dy_side = wire.copy(dy_out.at[place], dy_out.at[place], other_side)
+    wire.copy(dy_out.at[place], dy_out.at[place], other_core)
     for handle in kv_core:
         wire.arrived(handle)
-    attend_batch(1 - core, [0, spread // 3])
-    wire.arrived(dy_pair)
-    for peer in (other_core, other_side, across):
-        wire.copy(dy_out.at[place], dy_out.at[place], peer)
+    attend_batch(1 - core, [spread // 3])
+    wire.arrived(dy_side)
+    block = dy_out.at[flip(place, 2)]
+    wire.copy(block, block, other_core)
 
     quarter = x_in.shape[0] // 2
     for handle in o_near:
@@ -357,7 +360,7 @@
     pair_handle = wire.copy(mine, rows_two.at[1, place], pair)
     side_handle = wire.copy(mine, mine, other_side)
     wire.copy(mine, mine, other_core)
-    pj_far = send_far(pj_in, pj_out)
+    pj_far.update(send_far(pj_in, pj_out, order[1:]))
     tick(len(jobs))
     jobs.extend((pj_far, pj_out, d) for d in order)
     wire.arrived(pair_handle)
@@ -581,8 +584,46 @@
 
 def middle_kernel(count, *refs):
     back, proj, centre, dy, vec = refs[:5]
-    proj_sum, grad, rows, sums = refs[5:9]
-    row_refs, seq_refs, (send_sem, recv_sem) = refs[9:14], refs[14:17], refs[17:]
+    sources, (feed_out, fc_out) = refs[5:9], refs[13:15]
+    proj_sum, grad, rows, sums = refs[9:13]
+    row_refs, seq_refs = refs[15:20], refs[20:23]
+    local = refs[23:27]
+    feed, fc_grad, send_sem, recv_sem, local_sem = refs[27:]
+    loads = [
+        pltpu.make_async_copy(source, target, local_sem.at[i])
+        for i, (source, target) in enumerate(zip(sources, local))
+    ]
+    for item in loads:
+        item.start()
+    active, proj_t, unit, slope = local
+    stores = [
+        pltpu.make_async_copy(feed, feed_out, local_sem.at[4]),
+        pltpu.make_async_copy(fc_grad, fc_out, local_sem.at[5]),
+    ]
+    tall, wide = active.shape[0] // 2, 256
+    steps = proj_t.shape[0] // wide
+
+    def feed_rows(which):
+        at = slice(which * tall, (which + 1) * tall)
+
+        def run(i, carry):
+            cols = pl.ds(pl.multiple_of(i * wide, wide), wide)
+            feed[at, cols] = dot_nt(active[at, :], proj_t[cols, :]).astype(LOW)
+            return carry
+
+        lax.fori_loop(0, steps, run, 0)
+
+    def fc_rows(which):
+        half_width = slope.shape[1] // 2
+        out = slice(which * half_width, (which + 1) * half_width)
+
+        def run(i, carry):
+            cols = pl.ds(pl.multiple_of(i * wide, wide), wide)
+            fc_grad[cols, out] = dot_tn(unit[:, cols], slope[:, out]).astype(LOW)
+            return carry
+
+        lax.fori_loop(0, steps, run, 0)
+
     index, place = lax.axis_index("seq"), lax.axis_index("tensor")
     along = seq_peers(index, count)
     greet(along + [{"tensor": flip(place, 1)}, {"tensor": flip(place, 2)}])
@@ -595,8 +636,13 @@
     bulk.start()
     reduce.to_side(1)
     reduce.to_side(0)
+    loads[0].wait()
+    loads[1].wait()
+    feed_rows(0)
     bulk.relay(1)
     reduce.to_pair()
+    feed_rows(1)
+    stores[0].start()
     bulk.relay((lines - 1) // 3)
     reduce.ready()
     sums[...] = jnp.zeros_like(sums)
@@ -614,17 +660,27 @@
 
     by_rows(centre.shape[0], 16, body)
     gather.start()
+    loads[2].wait()
+    loads[3].wait()
+    fc_rows(0)
     bulk.relay(lines - 1 - 1 - (lines - 1) // 3)
     gather.forward()
+    fc_rows(1)
+    stores[1].start()
     bulk.close()
+    for item in stores:
+        item.wait()
     wire.finish()
 
 
-def middle_stage(back, proj, centre, dy, vec):
+def middle_stage(back, proj, centre, dy, vec, active, proj_t, unit, slope):
     count = lax.axis_size("seq")
     tensor = lax.axis_size("tensor")
     part, full = centre.shape
     vmem = pl.BlockSpec(memory_space=pltpu.VMEM)
+    hbm = pl.BlockSpec(memory_space=pl.ANY)
+    feed = jax.ShapeDtypeStruct((active.shape[0], proj_t.shape[0]), LOW)
+    fc_grad = jax.ShapeDtypeStruct((unit.shape[1], slope.shape[1]), LOW)
     copies = 2 * count + 12
     return pl.pallas_call(
         partial(middle_kernel, count),
@@ -633,22 +689,28 @@
             jax.ShapeDtypeStruct((part, full), F32),
             jax.ShapeDtypeStruct((tensor, part, full), LOW),
             jax.ShapeDtypeStruct((3, 16, full), F32),
+            feed,
+            fc_grad,
         ],
-        in_specs=[vmem] * 5,
-        out_specs=[vmem] * 4,
-        scratch_shapes=row_sum_scratch(back) + seq_sum_scratch(proj) + sem_scratch(copies),
+        in_specs=[vmem] * 5 + [hbm] * 4,
+        out_specs=[vmem] * 4 + [hbm] * 2,
+        scratch_shapes=row_sum_scratch(back)
+        + seq_sum_scratch(proj)
+        + [pltpu.VMEM(array.shape, LOW) for array in (active, proj_t, unit, slope, feed, fc_grad)]
+        + sem_scratch(copies)
+        + [pltpu.SemaphoreType.DMA((6,))],
         compiler_params=pltpu.CompilerParams(
             collective_id=2, has_side_effects=True, vmem_limit_bytes=60 << 20
         ),
         name="middle",
-    )(back, proj, centre, dy, vec)
+    )(back, proj, centre, dy, vec, active, proj_t, unit, slope)
 
 
 def back_kernel(count, *refs):
     feed, fc, out, q_in, kv_in, mq_in, mk_in, mixed, lse, grad_o_in, centre, vec = refs[:12]
     fc_sum, out_sum, dq, dkv, result = refs[12:17]
     row_refs, seq_refs, out_refs, kv_refs = refs[17:22], refs[22:25], refs[25:28], refs[28:31]
-    kv_send, kv_got, kv_part, kv_total, delta, acc, send_sem, recv_sem = refs[31:]
+    kv_send, kv_got, kv_part, kv_total, kv_acc, delta, acc, send_sem, recv_sem = refs[31:]
     index, place = lax.axis_index("seq"), lax.axis_index("tensor")
     core = lax.rem(place, 2)
     other_core = {"tensor": flip(place, 1)}
@@ -680,10 +742,10 @@
             mask = visible(mq_in[batch], mk_in[batch, block])
             keys = kv_in[batch, block, :, :hd]
             values = kv_in[batch, block, :, hd:]
-            grad_k = jnp.zeros((keys.shape[0], hd), F32)
-            grad_v = jnp.zeros((keys.shape[0], hd), F32)
-            for head in range(heads):
-                cols = slice(head * hd, (head + 1) * hd)
+            kv_acc[...] = jnp.zeros_like(kv_acc)
+
+            def one_head(head, inner):
+                cols = pl.ds(pl.multiple_of(head * hd, hd), hd)
                 query = q_in[batch, :, cols]
                 grad_o = grad_o_in[batch, :, cols]
                 scores = dot_nt(query, keys) * scale_two
@@ -691,9 +753,13 @@
                 grad_p = dot_nt(grad_o, values)
                 grad_s = (probs * (grad_p - delta[head])).astype(LOW)
                 acc[:, cols] += dot(grad_s, keys)
-                grad_k = grad_k + dot_tn(grad_s, query)
-                grad_v = grad_v + dot_tn(probs.astype(LOW), grad_o)
-            grad_k = grad_k * scale
+                kv_acc[:, :hd] += dot_tn(grad_s, query)
+                kv_acc[:, hd:] += dot_tn(probs.astype(LOW), grad_o)
+                return inner
+
+            lax.fori_loop(0, heads, one_head, 0)
+            grad_k = kv_acc[:, :hd] * scale
+            grad_v = kv_acc[:, hd:]
             if extra is not None:
                 grad_k = grad_k + extra[block, :, :hd].astype(F32)
                 grad_v = grad_v + extra[block, :, hd:].astype(F32)
@@ -789,6 +855,7 @@
         + seq_sum_scratch(kv_part)
         + [pltpu.VMEM(kv_part.shape, LOW)] * 3
         + [
+            pltpu.VMEM((rows, two), F32),
             pltpu.VMEM((rows, two), F32),
             pltpu.VMEM((heads, rows, 1), F32),
             pltpu.VMEM((rows, width), F32),
@@ -1062,12 +1129,16 @@
     def blocked(array):
         return array.astype(LOW).reshape(seq_size, width_block, array.shape[-1])
 
-    proj_sum, grad_middle, rows_middle, sums = middle_stage(
+    proj_sum, grad_middle, rows_middle, sums, feed_part, fc_part = middle_stage(
         back_part,
         blocked(dot_tn(grad_flat, active)),
         middle,
         grad_q_low,
         jnp.pad(gain_two[None], ((0, 7), (0, 0))),
+        active,
+        proj_t,
+        normed_two,
+        grad_hidden,
     )
     grad_gain_two, grad_shift_two, grad_out_bias = jnp.sum(sums, axis=1)
     grad_proj_bias = jnp.sum(grad_q_low.astype(F32), axis=0)
@@ -1076,10 +1147,9 @@
         return jnp.pad(row[None], ((0, 7), (0, 0)))
 
     grad_mixed = by_batch(dot(grad_middle_low, out_t).astype(LOW))
-    feed_part = dot_nt(active, proj_t).astype(LOW)
     fc_sum, out_sum, grad_queries, grad_keyval, result_rows = back_stage(
         feed_part.reshape(2, tensor_size, batches * quarter, full_width),
-        blocked(dot_tn(normed_two, grad_hidden)),
+        blocked(fc_part),
         blocked(dot_tn(grad_middle_low, mixed_rows)),
         queries,
         kv_all,

time: 574 us -> 544 us (0.948); the launches traced: 563 us -> 543 us
  matrix products: 55.4 us -> 45.3 us
    dot_general x4 -> x3, matrix products: 18.9 us -> 9.5 us  [dot_nt(): lax.dot_general(left, right, (((1,), (1,)), ((), ())), preferred_element_...]
    dot_general x5 -> x4, matrix products: 18.7 us -> 12.1 us  [dot_tn(): lax.dot_general(left, right, (((0,), (0,)), ((), ())), preferred_element_...]
    pallas_call x1, Pallas kernels: 167 us -> 160 us  [front(): pl.pallas_call(partial(front_kernel, count), out_shape=[jax.ShapeDtypeStr...]
    dot_general x5, matrix products: 17.8 us -> 23.7 us  [dot(): return jnp.dot(left, right, preferred_element_type=F32)]
    unnamed x76 -> x74, local copies, waits for them, and re-layouts: 13.9 us -> 11.7 us
where the time goes in v8:
time: 544 us; the launch traced here: 543 us
  Pallas kernels  442 us (81%)
  matrix products  45.3 us (8%)
  local copies, waits for them, and re-layouts  37.7 us (7%)
  other arithmetic  17.7 us (3%)
    pallas_call x1, Pallas kernels, front(): pl.pallas_call(partial(front_kernel, count), out_shape=[jax.ShapeDtypeStr...  160 us
    pallas_call x1, Pallas kernels, back_stage(): pl.pallas_call(partial(back_kernel, count), out_shape=[jax.ShapeDtypeStru...  108 us
    pallas_call x1, Pallas kernels, middle_stage(): pl.pallas_call(partial(middle_kernel, count), out_shape=[jax.ShapeDtypeSt...  78.5 us
    pallas_call x1, Pallas kernels, last_stage(): pl.pallas_call(partial(last_kernel, count), out_shape=[jax.ShapeDtypeStru...  50.5 us
    pallas_call x1, Pallas kernels, gather_first(): pl.pallas_call(partial(first_kernel, count, tensor), out_shape=[jax.Shape...  44.5 us
    dot_general x5, matrix products, dot(): return jnp.dot(left, right, preferred_element_type=F32)  23.7 us
    dot_general x4, matrix products, dot_tn(): lax.dot_general(left, right, (((0,), (0,)), ((), ())), preferred_element_...  12.1 us
    unnamed x74, local copies, waits for them, and re-layouts  11.7 us

profile of v8, /device:TPU:0, one launch (start us, length us, event | category | flops | bytes accessed | tf_op | source)
XLA Modules:
  0.0 543.4 jit_solution(1354166329556906489)
XLA Ops:
  0.7 0.8 fusion.21
  1.5 0.7 convert_element_type.141
  4.4 1.8 convert_element_type.151.refs_2_
  6.2 1.5 convert_element_type.150.refs_1_
  7.6 44.5 %gather_first.1 = (bf16[8,4,32,128]{3,2,1,0:T(8,128)(2,1)}, bf16[8,4,64,256]{3,2,1,0:T(8,128)(2,1)}, bf16[8,256,512]{2,1,0:T(8,128)(2,1)}) custom-call(bf16[32,128]{1,0:T(8,128)(2,1)} %pad_bitcast_fusion.refs_0_, bf16[64,256]{1,0:T(8,128)(2,1)} %convert_element_type.150.refs_1_, bf16[256,512]{1,0:T(8,128)(2,1)} %convert_element_type.151.refs_2_), custom_call_target="tpu_custom_call" | custom-call | tf_op jit(solution)/shard_map/gather_first/pallas_call | solution.py:160
  52.1 1.1 reshape.257
  54.0 2.1 convert_reduce_fusion
  56.8 0.8 fusion.5
  57.7 2.0 fusion.16
  59.8 1.1 fusion.23
  62.6 3.0 fusion.17
  65.6 0.9 constant_dynamic-slice_fusion.2
  66.5 3.3 copy.97
  70.2 0.7 pad.37.refs_2_.refs_5_
  71.6 1.3 copy.95
  72.9 1.7 convert_element_type.167
  74.6 1.3 copy.96
  75.9 0.8 copy.93
  76.7 160.4 %front.1 = (bf16[2,256,512]{2,1,0:T(8,128)(2,1)}, f32[2,4,256,1]{3,2,1,0:T(8,128)}, bf16[2,8,256,256]{3,2,1,0:T(8,128)(2,1)}, bf16[8,256,512]{2,1,0:T(8,128)(2,1...) custom-call(bf16[2,256,512]{2,1,0:T(8,128)(2,1)} %bitcast.156, ...), custom_call_target="tpu_custom_call" | custom-call | tf_op jit(solution)/shard_map/front/pallas_call | solution.py:402
  237.1 0.9 slice_bitcast_fusion
  238.1 8.8 %multiply_convert_fusion = (bf16[1024,1024]{1,0:T(8,128)(2,1)S(1)}, f32[1024,1024]{1,0:T(8,128)S(1)}) fusion(f32[1024]{0:T(1024)S(1)} %dynamic_slice.22, bf16[1024,2048]{1,0:T(8,128)(2,1)} %bitcast.144, bf16[2048,1024]{1,0:T(8,128)(2,1)} %bitcast.198), kind=kOutput, calls=%fused_computation.23 | convolution fusion | flops 4305453056 | bytes 14684160 | tf_op jit(solution)/shard_map/dot_general | solution.py:31
  247.3 0.9 copy-done.12
  248.2 6.1 %convolution_convert_fusion = bf16[2048,1024]{1,0:T(8,128)(2,1)} fusion(bf16[1024,2048]{1,0:T(8,128)(2,1)S(1)} %bitcast.139, bf16[1024,1024]{1,0:T(8,128)(2,1)S(1)} %get-tuple-element.126.refs_5_), kind=kOutput, calls=%fused_computation.25 | convolution fusion | flops 4297064448 | bytes 10485760 | tf_op jit(solution)/shard_map/dot_general | solution.py:35
  254.3 6.8 %convert_reduce_fusion.1 = (f32[1024]{0:T(1024)S(1)}, bf16[1024,1024]{1,0:T(8,128)(2,1)S(1)}) fusion(bf16[1024,2048]{1,0:T(8,128)(2,1)S(1)} %bitcast.140, bf16[2048,1024]{1,0:T(8,128)(2,1)S(1)} %bitcast.147, f32[1024,1024]{1,0:T(8,128)S(1)} %get-tuple-element.127, f32[1024]{0:T(1024)S(1)} %dynamic_slice.22), kind=kOutput, calls=%fused_computation.21 | convolution fusion | flops 4316986368 | bytes 14688256 | tf_op jit(solution)/shard_map/dot_general | solution.py:31
  261.2 6.2 %convolution_convert_fusion.1 = bf16[1024,2048]{1,0:T(8,128)(2,1)} fusion(bf16[1024,1024]{1,0:T(8,128)(2,1)S(1)} %get-tuple-element.129.refs_8_, bf16[2048,1024]{1,0:T(8,128)(2,1)S(1)} %bitcast.199), kind=kOutput, calls=%fused_computation.26 | convolution fusion | flops 4297064448 | bytes 10485760 | tf_op jit(solution)/shard_map/dot_general | solution.py:39
  267.3 1.9 convert_reduce_fusion.2
  269.3 78.5 %middle.1 = (f32[256,2048]{1,0:T(8,128)}, f32[128,2048]{1,0:T(8,128)}, bf16[4,128,2048]{2,1,0:T(8,128)(2,1)}, f32[3,16,2048]{2,1,0:T(8,128)}, bf16[1024,2048]{1,0:T(8,128)(2,1)}, /*index=5*/bf16[2048,1024]{1,0:T(8,128)(2,1)}) custom-call(bf16[2,4,128,2048]{3,2,1,0:T(8,128)(2,1)} %bitcast.151, bf16[8,256,1024]{2,1,0:T(8,128)(2,1)} %bitcast.150, ...), custom_call_target="tpu_custom_call" | custom-call | tf_op jit(solution)/shard_map/middle/pallas_call | solution.py:685
  347.8 3.0 convolution_convert_fusion.3
  350.8 0.8 copy.100
  351.7 2.6 convolution_convert_fusion.2
  355.0 107.7 %back.1 = (f32[256,2048]{1,0:T(8,128)}, f32[256,512]{1,0:T(8,128)}, bf16[2,256,512]{2,1,0:T(8,128)(2,1)}, bf16[2,256,256]{2,1,0:T(8,128)(2,1)}, bf16[4,128,2048]{2,1,0:T(8,128)(2,1)}) custom-call(bf16[2,4,128,2048]{3,2,1,0:T(8,128)(2,1)} %bitcast.148, bf16[8,256,1024]{2,1,0:T(8,128)(2,1)} %bitcast.149, bf16[8,256,512]{2,1,0:T(8,128)(2,1)} %bitcast.170, ...), custom_call_target="tpu_custom_call" | custom-call | tf_op jit(solution)/shard_map/back/pallas_call | solution.py:841
  462.7 1.3 convert_reduce_fusion.3
  464.3 1.0 convert_reduce_fusion.4
  465.6 0.7 select_maximum_fusion.refs_3_
  466.3 2.1 fusion.25
  468.4 1.3 add_convert_fusion
  469.7 1.5 copy.102
  471.2 0.9 copy-done.6
  472.0 2.6 bitcast_convert_fusion
  474.7 0.8 fusion.15
  475.4 1.0 copy.105
  477.2 50.5 %last.1 = (f32[256,512]{1,0:T(8,128)}, f32[64,256]{1,0:T(8,128)}, bf16[4,128,2048]{2,1,0:T(8,128)(2,1)}, f32[16,256]{1,0:T(8,128)}) custom-call(bf16[1,4,128,2048]{3,2,1,0:T(8,128)(2,1)} %bitcast.134, bf16[8,256,512]{2,1,0:T(8,128)(2,1)} %bitcast.168, bf16[1,4,512,256]{3,2,1,0:T(8,128)(2,1)} %bitcast.142, f32[8,16,256]{2,1,0:T(8,128)} %select_maximum_fusion.refs_3_, ...), custom_call_target="tpu_custom_call" | custom-call | tf_op jit(solution)/shard_map/last/pallas_call | solution.py:947
  527.7 3.3 copy.106
  532.8 3.2 copy.101
  536.0 1.0 copy.107
  537.0 1.8 copy.108
  538.8 0.8 copy.134
  540.3 3.1 copy.136
  (121 shorter events, 11.2 us)
Async XLA Ops:
  0.6 55.5 %copy-start = (bf16[2,256,2048]{2,1,0:T(8,128)(2,1)S(1)}, bf16[2,256,2048]{2,1,0:T(8,128)(2,1)}, u32[]{:S(2)}) copy-start(bf16[2,256,2048]{2,1,0:T(8,128)(2,1)} %param.12) | copy-start | bytes 6291460
  53.2 4.4 copy-start.15
  54.0 3.7 copy-start.3
  57.7 4.0 copy-start.5
  57.7 4.9 copy-start.29
  57.7 4.9 copy-start.14
  62.6 7.2 %copy-start.23 = (s32[2,256]{1,0:T(2,128)S(1)}, s32[2,256]{1,0:T(2,128)}, u32[]{:S(2)}) copy-start(s32[2,256]{1,0:T(2,128)} %param.13) | copy-start | bytes 6148
  62.6 7.3 %copy-start.24 = (s32[2,256]{1,0:T(2,128)S(1)}, s32[2,256]{1,0:T(2,128)}, u32[]{:S(2)}) copy-start(s32[2,256]{1,0:T(2,128)} %param.14) | copy-start | bytes 6148
  66.5 4.5 copy-start.9
  71.5 4.3 copy-start.17
  238.0 8.8 %copy-start.1 = (bf16[2,4,64,2048]{3,2,0,1:T(8,128)(2,1)S(1)}, bf16[2,4,64,2048]{3,2,0,1:T(8,128)(2,1)}, u32[]{:S(2)}) copy-start(bf16[2,4,64,2048]{3,2,0,1:T(8,128)(2,1)} %copy.97) | copy-start | bytes 6291460
  238.1 8.8 %copy-start.11 = (bf16[4,128,2048]{2,1,0:T(8,128)(2,1)S(1)}, bf16[4,128,2048]{2,1,0:T(8,128)(2,1)}, u32[]{:S(2)}) copy-start(bf16[4,128,2048]{2,1,0:T(8,128)(2,1)} %get-tuple-element.43) | copy-start | bytes 6291460
  246.9 1.3 copy-start.12
  248.2 6.1 %copy-start.2 = (bf16[8,256,1024]{2,1,0:T(8,128)(2,1)S(1)}, bf16[8,256,1024]{2,1,0:T(8,128)(2,1)}, u32[]{:S(2)}) copy-start(bf16[8,256,1024]{2,1,0:T(8,128)(2,1)} %get-tuple-element.44) | copy-start | bytes 12582916
  254.3 6.9 %copy-start.26 = (bf16[8,256,1024]{2,1,0:T(8,128)(2,1)S(1)}, bf16[8,256,1024]{2,1,0:T(8,128)(2,1)}, u32[]{:S(2)}) copy-start(bf16[8,256,1024]{2,1,0:T(8,128)(2,1)} %get-tuple-element.42) | copy-start | bytes 12582916
  261.1 6.2 %copy-start.13 = (bf16[1024,1024]{1,0:T(8,128)(2,1)}, bf16[1024,1024]{1,0:T(8,128)(2,1)S(1)}, u32[]{:S(2)}) copy-start(bf16[1024,1024]{1,0:T(8,128)(2,1)S(1)} %get-tuple-element.129.refs_8_) | copy-start | bytes 6291460
  269.3 78.5 %copy-start.27 = (bf16[8,256,512]{2,1,0:T(8,128)(2,1)S(1)}, bf16[8,256,512]{2,1,0:T(8,128)(2,1)}, u32[]{:S(2)}) copy-start(bf16[8,256,512]{2,1,0:T(8,128)(2,1)} %get-tuple-element.52) | copy-start | bytes 6291460
  347.8 3.8 copy-start.7
  347.8 3.9 copy-start.28
  355.0 109.1 %copy-start.20 = (f32[3,16,2048]{2,1,0:T(8,128)S(1)}, f32[3,16,2048]{2,1,0:T(8,128)}, u32[]{:S(2)}) copy-start(f32[3,16,2048]{2,1,0:T(8,128)} %get-tuple-element.56) | copy-start | bytes 1179652
  462.7 5.7 %copy-start.4 = (bf16[8,256,512]{2,1,0:T(8,128)(2,1)S(1)}, bf16[8,256,512]{2,1,0:T(8,128)(2,1)}, u32[]{:S(2)}) copy-start(bf16[8,256,512]{2,1,0:T(8,128)(2,1)} %get-tuple-element.39) | copy-start | bytes 6291460
  462.7 5.7 %copy-start.8 = (bf16[2,256,512]{2,1,0:T(8,128)(2,1)S(1)}, bf16[2,256,512]{2,1,0:T(8,128)(2,1)}, u32[]{:S(2)}) copy-start(bf16[2,256,512]{2,1,0:T(8,128)(2,1)} %get-tuple-element.54) | copy-start | bytes 1572868
  469.7 2.4 copy-start.6
  472.0 2.6 copy-start.16
  527.7 3.3 copy-start.22
  527.7 8.3 %copy-start.18 = (f32[256,512]{1,0:T(8,128)S(1)}, f32[256,512]{1,0:T(8,128)}, u32[]{:S(2)}) copy-start(f32[256,512]{1,0:T(8,128)} %get-tuple-element.61) | copy-start | bytes 1572868
  527.7 9.3 %copy-start.10 = (f32[256,2048]{1,0:T(8,128)S(1)}, f32[256,2048]{1,0:T(8,128)}, u32[]{:S(2)}) copy-start(f32[256,2048]{1,0:T(8,128)} %get-tuple-element.63) | copy-start | bytes 6291460
  531.1 7.7 %copy-start.25 = (f32[7,64]{1,0:T(8,128)}, f32[7,64]{1,0:T(8,128)S(1)}, u32[]{:S(2)}) copy-start(f32[7,64]{1,0:T(8,128)S(1)} %constant_dynamic-slice_fusion) | copy-start | bytes 5380
  532.8 6.0 %copy-start.19 = (f32[256,512]{1,0:T(8,128)S(1)}, f32[256,512]{1,0:T(8,128)}, u32[]{:S(2)}) copy-start(f32[256,512]{1,0:T(8,128)} %get-tuple-element.145) | copy-start | bytes 1572868
  536.0 3.6 copy-start.21

commit v9 on v8

--- a/solution.py
+++ b/solution.py
@@ -53,8 +53,9 @@
 
 
 class Wire:
-    def __init__(self, send_sem, recv_sem):
-        self.send_sem, self.recv_sem = send_sem, recv_sem
+    def __init__(self, send_sem, recv_sem, local_sem=None):
+        self.send_sem, self.recv_sem, self.local_sem = send_sem, recv_sem, local_sem
+        self.loads = []
         self.started = []
         self.landed = set()
 
@@ -71,6 +72,12 @@
         item.start()
         self.started.append(item)
         return place
+
+    def load(self, src, dst):
+        item = pltpu.make_async_copy(src, dst, self.local_sem.at[len(self.loads)])
+        item.start()
+        self.loads.append(item)
+        return item
 
     def arrived(self, place):
         if place not in self.landed:
@@ -121,29 +128,38 @@
         item = pltpu.make_async_copy(source, target(index), local_sem.at[len(own)])
         item.start()
         own.append(item)
-    relays = []
-    for a, target in enumerate(targets):
-        for d in range(1, count // 2):
-            wire.arrived(handles[a][d])
-            block = target(flip(index, 2 * d))
-            relays.append(wire.copy(block, block, near))
-        if a == 1:
-            for handle in [handles[0][0], handles[1][0]] + relays:
+    relays = [[], [], []]
+    order = list(range(1, count // 2))
+
+    def relay(a, d):
+        wire.arrived(handles[a][d])
+        block = targets[a](flip(index, 2 * d))
+        relays[a].append(wire.copy(block, block, near))
+
+    for d in order:
+        relay(0, d)
+        relay(1, d)
+    cut = len(order) // 3
+    for d in order[:cut]:
+        relay(2, d)
+    for handle in [handles[0][0], handles[1][0]] + relays[0] + relays[1]:
+        wire.arrived(handle)
+    own[0].wait()
+    own[1].wait()
+    masks = [0]
+    for i, peer in enumerate(across):
+        step = tensor >> (i + 1)
+        sent = [
+            wire.copy(out.at[:, flip(place, mask)], out.at[:, flip(place, mask)], peer)
+            for mask in masks
+            for out in outs[:2]
+        ]
+        masks = masks + [mask | step for mask in masks]
+        for d in order[cut:] if i == 0 else []:
+            relay(2, d)
+        if i + 1 < len(across):
+            for handle in sent:
                 wire.arrived(handle)
-            own[0].wait()
-            own[1].wait()
-            masks = [0]
-            for i, peer in enumerate(across):
-                step = tensor >> (i + 1)
-                sent = [
-                    wire.copy(out.at[:, flip(place, mask)], out.at[:, flip(place, mask)], peer)
-                    for mask in masks
-                    for out in outs[:2]
-                ]
-                masks = masks + [mask | step for mask in masks]
-                if i + 1 < len(across):
-                    for handle in sent:
-                        wire.arrived(handle)
     own[2].wait()
     wire.finish()
 
@@ -433,7 +449,7 @@
 
 
 class SeqSum:
-    def __init__(self, wire, index, peers, part, from_near, to_far, from_far, out, split):
+    def __init__(self, wire, index, peers, part, from_near, to_far, from_far, held, out, split):
         self.wire, self.index = wire, index
         self.far, self.near = peers[:-1], peers[-1]
         self.lines = len(peers)
@@ -443,6 +459,17 @@
         self.step = min(64, self.rows)
         self.near_handles, self.far_handles = {}, {}
         self.order = turns(self.lines)
+        self.held, self.loads = held, {}
+
+    def load(self):
+        for d in self.order + [0]:
+            block = self.part.at[flip(self.index, 2 * d)]
+            self.loads[d] = self.wire.load(block, self.held.at[d])
+
+    def mine(self, d, at):
+        if self.held is None:
+            return self.part[flip(self.index, 2 * d), at].astype(F32)
+        return self.held[d, at].astype(F32)
 
     def start(self, order=None):
         for d in order or turns(self.lines) + [0]:
@@ -453,9 +480,11 @@
         for _ in range(number):
             d = self.order.pop(0)
             self.wire.arrived(self.near_handles[d])
+            if self.held is not None:
+                self.loads[d].wait()
 
             def join(at, d=d):
-                total = self.part[flip(self.index, 2 * d), at].astype(F32)
+                total = self.mine(d, at)
                 total = total + self.from_near[d, at].astype(F32)
                 self.to_far[d - 1, at] = total.astype(self.to_far.dtype)
 
@@ -466,13 +495,15 @@
 
     def close(self):
         self.wire.arrived(self.near_handles[0])
+        if self.held is not None:
+            self.loads[0].wait()
         for d in range(1, self.lines):
             self.wire.arrived(self.far_handles[d])
         width = self.part.shape[2]
         half = lax.rem(lax.div(self.index, 2), 2)
 
         def total(at):
-            same = self.part[self.index, at].astype(F32) + self.from_near[0, at].astype(F32)
+            same = self.mine(0, at) + self.from_near[0, at].astype(F32)
             other = None
             for d in range(1, self.lines):
                 got = self.from_far[d - 1, at].astype(F32)
@@ -490,15 +521,16 @@
         by_rows(self.rows, self.step, total)
 
 
-def seq_sum_scratch(part, dtype=LOW):
+def seq_sum_scratch(part, dtype=LOW, held=False):
     lines = part.shape[0] // 2
-    return [
-        pltpu.VMEM((depth,) + part.shape[1:], dtype) for depth in (lines, lines - 1, lines - 1)
-    ]
+    depths = [lines, lines - 1, lines - 1] + [lines] * held
+    return [pltpu.VMEM((depth,) + part.shape[1:], dtype) for depth in depths]
 
 
 class RowSum:
-    def __init__(self, wire, place, pair, part, core_got, y_send, y_got, pair_send, pair_got):
+    def __init__(
+        self, wire, place, pair, part, core_got, y_send, y_got, pair_send, pair_got, held
+    ):
         self.wire, self.place, self.pair = wire, place, pair
         self.core, self.side = lax.rem(place, 2), lax.div(place, 2)
         self.part, self.core_got, self.y_send, self.y_got = part, core_got, y_send, y_got
@@ -506,6 +538,7 @@
         self.sides = (1 - self.side, self.side)
         self.rows = part.shape[2]
         self.core_handles, self.y_handles = {}, {}
+        self.held, self.loads = held, {}
 
     def start(self):
         peer = {"tensor": flip(self.place, 1)}
@@ -514,14 +547,23 @@
                 at = self.sides[which]
                 block = self.part.at[p, 2 * at + 1 - self.core]
                 self.core_handles[p, which] = self.wire.copy(block, self.core_got.at[p, at], peer)
+        for which in range(2):
+            for p in reversed(range(self.part.shape[0])):
+                at = self.sides[which]
+                block = self.part.at[p, 2 * at + self.core]
+                self.loads[p, which] = self.wire.load(block, self.held.at[p, at])
+
+    def settle(self, p, which):
+        self.wire.arrived(self.core_handles[p, which])
+        self.loads[p, which].wait()
 
     def both(self, p, which, at):
         side = self.sides[which]
-        mine = self.part[p, 2 * side + self.core, at, :].astype(F32)
+        mine = self.held[p, side, at, :].astype(F32)
         return mine + self.core_got[p, side, at, :].astype(F32)
 
     def to_side(self, p):
-        self.wire.arrived(self.core_handles[p, 0])
+        self.settle(p, 0)
 
         def body(at):
             self.y_send[p, at, :] = self.both(p, 0, at).astype(LOW)
@@ -531,7 +573,7 @@
         self.y_handles[p] = self.wire.copy(self.y_send.at[p], self.y_got.at[p], peer)
 
     def to_pair(self):
-        self.wire.arrived(self.core_handles[1, 1])
+        self.settle(1, 1)
         self.wire.arrived(self.y_handles[1])
 
         def body(at):
@@ -542,7 +584,7 @@
         self.pair_handle = self.wire.copy(self.pair_send, self.pair_got, self.pair)
 
     def ready(self):
-        self.wire.arrived(self.core_handles[0, 1])
+        self.settle(0, 1)
         self.wire.arrived(self.y_handles[0])
         if self.pair is not None:
             self.wire.arrived(self.pair_handle)
@@ -560,7 +602,7 @@
     scratch += [pltpu.VMEM((pairs, rows, width), LOW)] * 2
     if pairs == 2:
         scratch += [pltpu.VMEM((rows, width), LOW)] * 2
-    return scratch
+    return scratch + [pltpu.VMEM((pairs, 2, rows, width), LOW)]
 
 
 class RowGather:
@@ -586,15 +628,13 @@
     back, proj, centre, dy, vec = refs[:5]
     sources, (feed_out, fc_out) = refs[5:9], refs[13:15]
     proj_sum, grad, rows, sums = refs[9:13]
-    row_refs, seq_refs = refs[15:20], refs[20:23]
-    local = refs[23:27]
-    feed, fc_grad, send_sem, recv_sem, local_sem = refs[27:]
+    row_refs, seq_refs = refs[15:21], refs[21:25]
+    local = refs[25:29]
+    feed, fc_grad, send_sem, recv_sem, local_sem, load_sem = refs[29:]
     loads = [
         pltpu.make_async_copy(source, target, local_sem.at[i])
         for i, (source, target) in enumerate(zip(sources, local))
     ]
-    for item in loads:
-        item.start()
     active, proj_t, unit, slope = local
     stores = [
         pltpu.make_async_copy(feed, feed_out, local_sem.at[4]),
@@ -627,23 +667,24 @@
     index, place = lax.axis_index("seq"), lax.axis_index("tensor")
     along = seq_peers(index, count)
     greet(along + [{"tensor": flip(place, 1)}, {"tensor": flip(place, 2)}])
-    wire = Wire(send_sem, recv_sem)
+    wire = Wire(send_sem, recv_sem, load_sem)
     reduce = RowSum(wire, place, along[0], back, *row_refs)
     bulk = SeqSum(wire, index, along, proj, *seq_refs, proj_sum, True)
     gather = RowGather(wire, place, rows)
     lines = count // 2
     reduce.start()
     bulk.start()
+    bulk.load()
+    for item in loads:
+        item.start()
     reduce.to_side(1)
     reduce.to_side(0)
+    bulk.relay(lines // 4)
+    reduce.to_pair()
+    bulk.relay(lines // 2 - lines // 4)
     loads[0].wait()
     loads[1].wait()
     feed_rows(0)
-    bulk.relay(1)
-    reduce.to_pair()
-    feed_rows(1)
-    stores[0].start()
-    bulk.relay((lines - 1) // 3)
     reduce.ready()
     sums[...] = jnp.zeros_like(sums)
     gain = vec[0:1, :]
@@ -660,10 +701,12 @@
 
     by_rows(centre.shape[0], 16, body)
     gather.start()
+    bulk.relay(lines - 1 - lines // 2)
+    feed_rows(1)
+    stores[0].start()
     loads[2].wait()
     loads[3].wait()
     fc_rows(0)
-    bulk.relay(lines - 1 - 1 - (lines - 1) // 3)
     gather.forward()
     fc_rows(1)
     stores[1].start()
@@ -692,13 +735,13 @@
             feed,
             fc_grad,
         ],
-        in_specs=[vmem] * 5 + [hbm] * 4,
+        in_specs=[hbm] * 2 + [vmem] * 3 + [hbm] * 4,
         out_specs=[vmem] * 4 + [hbm] * 2,
         scratch_shapes=row_sum_scratch(back)
-        + seq_sum_scratch(proj)
+        + seq_sum_scratch(proj, held=True)
         + [pltpu.VMEM(array.shape, LOW) for array in (active, proj_t, unit, slope, feed, fc_grad)]
         + sem_scratch(copies)
-        + [pltpu.SemaphoreType.DMA((6,))],
+        + [pltpu.SemaphoreType.DMA((6,)), pltpu.SemaphoreType.DMA((4 + count // 2,))],
         compiler_params=pltpu.CompilerParams(
             collective_id=2, has_side_effects=True, vmem_limit_bytes=60 << 20
         ),
@@ -709,19 +752,20 @@
 def back_kernel(count, *refs):
     feed, fc, out, q_in, kv_in, mq_in, mk_in, mixed, lse, grad_o_in, centre, vec = refs[:12]
     fc_sum, out_sum, dq, dkv, result = refs[12:17]
-    row_refs, seq_refs, out_refs, kv_refs = refs[17:22], refs[22:25], refs[25:28], refs[28:31]
-    kv_send, kv_got, kv_part, kv_total, kv_acc, delta, acc, send_sem, recv_sem = refs[31:]
+    row_refs, seq_refs, out_refs, kv_refs = refs[17:23], refs[23:27], refs[27:31], refs[31:34]
+    kv_send, kv_got, kv_part, kv_total, kv_acc, delta, acc = refs[34:41]
+    send_sem, recv_sem, load_sem = refs[41:]
     index, place = lax.axis_index("seq"), lax.axis_index("tensor")
     core = lax.rem(place, 2)
     other_core = {"tensor": flip(place, 1)}
     along = seq_peers(index, count)
     lines = count // 2
     greet(along + [other_core, {"tensor": flip(place, 2)}])
-    wire = Wire(send_sem, recv_sem)
+    wire = Wire(send_sem, recv_sem, load_sem)
     reduce = RowSum(wire, place, along[0], feed, *row_refs)
     bulk = SeqSum(wire, index, along, fc, *seq_refs, fc_sum, True)
     out_bulk = SeqSum(wire, index, along, out, *out_refs, out_sum, False)
-    keys_sum = SeqSum(wire, index, along, kv_part, *kv_refs, kv_total, False)
+    keys_sum = SeqSum(wire, index, along, kv_part, *kv_refs, None, kv_total, False)
     gather = RowGather(wire, place, result)
     hd = kv_in.shape[-1] // 2
     heads = q_in.shape[-1] // hd
@@ -784,16 +828,20 @@
     out_bulk.start(middle)
     bulk.start(edge)
     out_bulk.start(edge)
+    bulk.load()
+    out_bulk.load()
+    reduce.to_side(1)
+    reduce.to_side(0)
+    bulk.relay(lines // 4)
     open_batch(1 - core)
     blocks_of(1 - core, near_x, kv_send, None)
     near_handles = to_core(near_x)
-    reduce.to_side(1)
-    reduce.to_side(0)
-    bulk.relay(lines // 4)
+    bulk.relay(lines // 2 - lines // 4)
     blocks_of(1 - core, 1 - near_x, kv_send, None)
     own_handles = to_core(1 - near_x)
     close_batch(1 - core)
-    bulk.relay(lines // 2 - lines // 4)
+    reduce.to_pair()
+    out_bulk.relay(lines // 4)
     for handle in near_handles:
         wire.arrived(handle)
     open_batch(core)
@@ -801,23 +849,22 @@
     keys_sum.start()
     bulk.start([0])
     out_bulk.start([0])
-    reduce.to_pair()
-    out_bulk.relay(lines // 2)
+    out_bulk.relay(lines // 2 - lines // 4)
+    bulk.relay(len(edge))
+    out_bulk.relay(len(edge))
+    reduce.ready()
+    bias = vec[0:1, :]
+
+    def body(at):
+        total = centre[at, :] + reduce.total(at) + bias
+        result[place, at, :] = total.astype(LOW)
+
+    by_rows(centre.shape[0], 16, body)
+    gather.start()
     for handle in own_handles:
         wire.arrived(handle)
     blocks_of(core, 1 - near_x, kv_part, kv_got)
     close_batch(core)
-    bulk.relay(len(edge))
-    out_bulk.relay(len(edge))
-    reduce.ready()
-    bias = vec[0:1, :]
-
-    def body(at):
-        total = centre[at, :] + reduce.total(at) + bias
-        result[place, at, :] = total.astype(LOW)
-
-    by_rows(centre.shape[0], 16, body)
-    gather.start()
     keys_sum.relay(lines - 1)
     gather.forward()
     keys_sum.close()
@@ -835,7 +882,7 @@
     batches, rows, width = queries.shape
     blocks, two = keyval.shape[1], keyval.shape[3]
     heads = 2 * width // two
-    vmem = pl.BlockSpec(memory_space=pltpu.VMEM)
+    vmem, hbm = pl.BlockSpec(memory_space=pltpu.VMEM), pl.BlockSpec(memory_space=pl.ANY)
     kv_part = jax.ShapeDtypeStruct((blocks, rows, two), LOW)
     copies = 4 * count + 14
     return pl.pallas_call(
@@ -847,11 +894,11 @@
             jax.ShapeDtypeStruct((batches, rows, two), LOW),
             jax.ShapeDtypeStruct((tensor, part, full), LOW),
         ],
-        in_specs=[vmem] * 12,
+        in_specs=[hbm] * 3 + [vmem] * 9,
         out_specs=[vmem] * 5,
         scratch_shapes=row_sum_scratch(feed)
-        + seq_sum_scratch(fc)
-        + seq_sum_scratch(out)
+        + seq_sum_scratch(fc, held=True)
+        + seq_sum_scratch(out, held=True)
         + seq_sum_scratch(kv_part)
         + [pltpu.VMEM(kv_part.shape, LOW)] * 3
         + [
@@ -860,7 +907,8 @@
             pltpu.VMEM((heads, rows, 1), F32),
             pltpu.VMEM((rows, width), F32),
         ]
-        + sem_scratch(copies),
+        + sem_scratch(copies)
+        + [pltpu.SemaphoreType.DMA((4 + count,))],
         compiler_params=pltpu.CompilerParams(
             collective_id=3, has_side_effects=True, vmem_limit_bytes=60 << 20
         ),
@@ -871,23 +919,26 @@
 def last_kernel(count, *refs):
     back, query, keyval, small, own, dy, vec = refs[:7]
     query_sum, keyval_sum, rows, small_sum = refs[7:11]
-    row_refs, key_row_refs = refs[11:14], refs[14:17]
-    query_refs, key_refs, small_refs = refs[17:20], refs[20:23], refs[23:26]
-    key_part, small_part, small_own, small_got, sums, send_sem, recv_sem = refs[26:]
+    row_refs, key_row_refs = refs[11:15], refs[15:19]
+    query_refs, key_refs, small_refs = refs[19:23], refs[23:26], refs[26:29]
+    key_part, small_part, small_own, small_got, sums, send_sem, recv_sem, load_sem = refs[29:]
     index, place = lax.axis_index("seq"), lax.axis_index("tensor")
     along = seq_peers(index, count)
     other_core, other_side = {"tensor": flip(place, 1)}, {"tensor": flip(place, 2)}
     greet(along + [other_core, other_side])
-    wire = Wire(send_sem, recv_sem)
-    reduce = RowSum(wire, place, None, back, *row_refs, None, None)
-    key_reduce = RowSum(wire, place, None, keyval, *key_row_refs, None, None)
+    wire = Wire(send_sem, recv_sem, load_sem)
+    reduce = RowSum(wire, place, None, back, *row_refs[:3], None, None, row_refs[3])
+    key_reduce = RowSum(
+        wire, place, None, keyval, *key_row_refs[:3], None, None, key_row_refs[3]
+    )
     query_bulk = SeqSum(wire, index, along, query, *query_refs, query_sum, False)
-    key_bulk = SeqSum(wire, index, along, key_part, *key_refs, keyval_sum, False)
-    small_bulk = SeqSum(wire, index, along, small_part, *small_refs, small_own.at[0], False)
+    key_bulk = SeqSum(wire, index, along, key_part, *key_refs, None, keyval_sum, False)
+    small_bulk = SeqSum(wire, index, along, small_part, *small_refs, None, small_own.at[0], False)
     gather = RowGather(wire, place, rows)
     spread = count // 2 - 1
     reduce.start()
     query_bulk.start()
+    query_bulk.load()
     key_reduce.start()
     reduce.to_side(0)
     key_reduce.to_side(0)
@@ -941,7 +992,7 @@
     count = lax.axis_size("seq")
     tensor = lax.axis_size("tensor")
     part, full = own.shape
-    vmem = pl.BlockSpec(memory_space=pltpu.VMEM)
+    vmem, hbm = pl.BlockSpec(memory_space=pltpu.VMEM), pl.BlockSpec(memory_space=pl.ANY)
     key_part = jax.ShapeDtypeStruct((count, keyval.shape[2] // count, keyval.shape[3]), LOW)
     copies = 3 * count + 12
     return pl.pallas_call(
@@ -952,11 +1003,11 @@
             jax.ShapeDtypeStruct((tensor, part, full), LOW),
             jax.ShapeDtypeStruct(small.shape[1:], F32),
         ],
-        in_specs=[vmem] * 7,
+        in_specs=[hbm] * 3 + [vmem] * 4,
         out_specs=[vmem] * 4,
         scratch_shapes=row_sum_scratch(back)
         + row_sum_scratch(keyval)
-        + seq_sum_scratch(query)
+        + seq_sum_scratch(query, held=True)
         + seq_sum_scratch(key_part)
         + seq_sum_scratch(small, F32)
         + [
@@ -966,7 +1017,8 @@
             pltpu.VMEM((2,) + small.shape[1:], F32),
             pltpu.VMEM((2, 16, full), F32),
         ]
-        + sem_scratch(copies),
+        + sem_scratch(copies)
+        + [pltpu.SemaphoreType.DMA((4 + count // 2,))],
         compiler_params=pltpu.CompilerParams(
             collective_id=4, has_side_effects=True, vmem_limit_bytes=60 << 20
         ),

time: 544 us -> 536 us (0.985)
  Pallas kernels: 442 us -> 434 us
where the time goes in v9:
time: 536 us; the launch traced here: 535 us
  Pallas kernels  434 us (81%)
  matrix products  45.3 us (8%)
  local copies, waits for them, and re-layouts  37.7 us (7%)
  other arithmetic  17.7 us (3%)
    pallas_call x1, Pallas kernels, front(): pl.pallas_call(partial(front_kernel, count), out_shape=[jax.ShapeDtypeStr...  159 us
    pallas_call x1, Pallas kernels, back_stage(): pl.pallas_call(partial(back_kernel, count), out_shape=[jax.ShapeDtypeStru...  105 us
    pallas_call x1, Pallas kernels, middle_stage(): pl.pallas_call(partial(middle_kernel, count), out_shape=[jax.ShapeDtypeSt...  79.1 us
    pallas_call x1, Pallas kernels, last_stage(): pl.pallas_call(partial(last_kernel, count), out_shape=[jax.ShapeDtypeStru...  48.6 us
    pallas_call x1, Pallas kernels, gather_first(): pl.pallas_call(partial(first_kernel, count, tensor), out_shape=[jax.Shape...  41.7 us
    dot_general x5, matrix products, dot(): return jnp.dot(left, right, preferred_element_type=F32)  23.7 us
    dot_general x4, matrix products, dot_tn(): lax.dot_general(left, right, (((0,), (0,)), ((), ())), preferred_element_...  12.1 us
    unnamed x74, local copies, waits for them, and re-layouts  11.6 us

profile of v9, /device:TPU:0, one launch (start us, length us, event | category | flops | bytes accessed | tf_op | source)
XLA Modules:
  0.0 535.5 jit_solution(7302020300396297663)
XLA Ops:
  0.7 0.8 fusion.21
  1.5 0.7 convert_element_type.141
  4.4 1.8 convert_element_type.151.refs_2_
  6.2 1.5 convert_element_type.150.refs_1_
  7.6 41.7 %gather_first.1 = (bf16[8,4,32,128]{3,2,1,0:T(8,128)(2,1)}, bf16[8,4,64,256]{3,2,1,0:T(8,128)(2,1)}, bf16[8,256,512]{2,1,0:T(8,128)(2,1)}) custom-call(bf16[32,128]{1,0:T(8,128)(2,1)} %pad_bitcast_fusion.refs_0_, bf16[64,256]{1,0:T(8,128)(2,1)} %convert_element_type.150.refs_1_, bf16[256,512]{1,0:T(8,128)(2,1)} %convert_element_type.151.refs_2_), custom_call_target="tpu_custom_call" | custom-call | tf_op jit(solution)/shard_map/gather_first/pallas_call | solution.py:176
  49.3 1.1 reshape.257
  51.2 2.1 convert_reduce_fusion
  54.0 0.8 fusion.5
  54.9 2.0 fusion.16
  56.9 1.1 fusion.23
  59.8 3.0 fusion.17
  62.8 0.9 constant_dynamic-slice_fusion.2
  63.6 3.3 copy.97
  67.4 0.7 pad.37.refs_2_.refs_5_
  68.7 1.3 copy.95
  70.1 1.7 convert_element_type.167
  71.8 1.3 copy.96
  73.1 0.8 copy.93
  73.9 159.4 %front.1 = (bf16[2,256,512]{2,1,0:T(8,128)(2,1)}, f32[2,4,256,1]{3,2,1,0:T(8,128)}, bf16[2,8,256,256]{3,2,1,0:T(8,128)(2,1)}, bf16[8,256,512]{2,1,0:T(8,128)(2,1...) custom-call(bf16[2,256,512]{2,1,0:T(8,128)(2,1)} %bitcast.156, ...), custom_call_target="tpu_custom_call" | custom-call | tf_op jit(solution)/shard_map/front/pallas_call | solution.py:418
  233.3 0.9 slice_bitcast_fusion
  234.3 8.8 %multiply_convert_fusion = (bf16[1024,1024]{1,0:T(8,128)(2,1)S(1)}, f32[1024,1024]{1,0:T(8,128)S(1)}) fusion(f32[1024]{0:T(1024)S(1)} %dynamic_slice.22, bf16[1024,2048]{1,0:T(8,128)(2,1)} %bitcast.144, bf16[2048,1024]{1,0:T(8,128)(2,1)} %bitcast.198), kind=kOutput, calls=%fused_computation.23 | convolution fusion | flops 4305453056 | bytes 14684160 | tf_op jit(solution)/shard_map/dot_general | solution.py:31
  243.5 0.9 copy-done.12
  244.4 6.1 %convolution_convert_fusion = bf16[2048,1024]{1,0:T(8,128)(2,1)} fusion(bf16[1024,2048]{1,0:T(8,128)(2,1)S(1)} %bitcast.139, bf16[1024,1024]{1,0:T(8,128)(2,1)S(1)} %get-tuple-element.126.refs_5_), kind=kOutput, calls=%fused_computation.25 | convolution fusion | flops 4297064448 | bytes 10485760 | tf_op jit(solution)/shard_map/dot_general | solution.py:35
  250.5 6.8 %convert_reduce_fusion.1 = (f32[1024]{0:T(1024)S(1)}, bf16[1024,1024]{1,0:T(8,128)(2,1)S(1)}) fusion(bf16[1024,2048]{1,0:T(8,128)(2,1)S(1)} %bitcast.140, bf16[2048,1024]{1,0:T(8,128)(2,1)S(1)} %bitcast.147, f32[1024,1024]{1,0:T(8,128)S(1)} %get-tuple-element.127, f32[1024]{0:T(1024)S(1)} %dynamic_slice.22), kind=kOutput, calls=%fused_computation.21 | convolution fusion | flops 4316986368 | bytes 14688256 | tf_op jit(solution)/shard_map/dot_general | solution.py:31
  257.4 6.2 %convolution_convert_fusion.1 = bf16[1024,2048]{1,0:T(8,128)(2,1)} fusion(bf16[1024,1024]{1,0:T(8,128)(2,1)S(1)} %get-tuple-element.129.refs_8_, bf16[2048,1024]{1,0:T(8,128)(2,1)S(1)} %bitcast.199), kind=kOutput, calls=%fused_computation.26 | convolution fusion | flops 4297064448 | bytes 10485760 | tf_op jit(solution)/shard_map/dot_general | solution.py:39
  263.5 1.9 convert_reduce_fusion.2
  265.5 79.1 %middle.1 = (f32[256,2048]{1,0:T(8,128)}, f32[128,2048]{1,0:T(8,128)}, bf16[4,128,2048]{2,1,0:T(8,128)(2,1)}, f32[3,16,2048]{2,1,0:T(8,128)}, bf16[1024,2048]{1,0:T(8,128)(2,1)}, /*index=5*/bf16[2048,1024]{1,0:T(8,128)(2,1)}) custom-call(bf16[2,4,128,2048]{3,2,1,0:T(8,128)(2,1)} %bitcast.151, bf16[8,256,1024]{2,1,0:T(8,128)(2,1)} %bitcast.150, ...), custom_call_target="tpu_custom_call" | custom-call | tf_op jit(solution)/shard_map/middle/pallas_call | solution.py:728
  344.6 3.0 convolution_convert_fusion.3
  347.6 0.8 copy.100
  348.5 2.6 convolution_convert_fusion.2
  351.8 104.9 %back.1 = (f32[256,2048]{1,0:T(8,128)}, f32[256,512]{1,0:T(8,128)}, bf16[2,256,512]{2,1,0:T(8,128)(2,1)}, bf16[2,256,256]{2,1,0:T(8,128)(2,1)}, bf16[4,128,2048]{2,1,0:T(8,128)(2,1)}) custom-call(bf16[2,4,128,2048]{3,2,1,0:T(8,128)(2,1)} %bitcast.148, bf16[8,256,1024]{2,1,0:T(8,128)(2,1)} %bitcast.149, bf16[8,256,512]{2,1,0:T(8,128)(2,1)} %bitcast.170, ...), custom_call_target="tpu_custom_call" | custom-call | tf_op jit(solution)/shard_map/back/pallas_call | solution.py:888
  456.7 1.3 convert_reduce_fusion.3
  458.3 1.0 convert_reduce_fusion.4
  459.6 0.7 select_maximum_fusion.refs_3_
  460.3 2.1 fusion.25
  462.4 1.3 add_convert_fusion
  463.7 1.5 copy.102
  465.1 0.9 copy-done.6
  466.0 2.6 bitcast_convert_fusion
  468.6 0.8 fusion.15
  469.4 1.0 copy.105
  471.2 48.6 %last.1 = (f32[256,512]{1,0:T(8,128)}, f32[64,256]{1,0:T(8,128)}, bf16[4,128,2048]{2,1,0:T(8,128)(2,1)}, f32[16,256]{1,0:T(8,128)}) custom-call(bf16[1,4,128,2048]{3,2,1,0:T(8,128)(2,1)} %bitcast.134, bf16[8,256,512]{2,1,0:T(8,128)(2,1)} %bitcast.168, bf16[1,4,512,256]{3,2,1,0:T(8,128)(2,1)} %bitcast.142, f32[8,16,256]{2,1,0:T(8,128)} %select_maximum_fusion.refs_3_, ...), custom_call_target="tpu_custom_call" | custom-call | tf_op jit(solution)/shard_map/last/pallas_call | solution.py:998
  519.8 3.3 copy.106
  524.9 3.2 copy.101
  528.1 1.0 copy.107
  529.1 1.8 copy.108
  530.9 0.8 copy.134
  532.4 3.1 copy.136
  (121 shorter events, 11.2 us)
Async XLA Ops:
  0.6 52.6 %copy-start = (bf16[2,256,2048]{2,1,0:T(8,128)(2,1)S(1)}, bf16[2,256,2048]{2,1,0:T(8,128)(2,1)}, u32[]{:S(2)}) copy-start(bf16[2,256,2048]{2,1,0:T(8,128)(2,1)} %param.12) | copy-start | bytes 6291460
  50.4 4.4 copy-start.15
  51.2 3.7 copy-start.3
  54.9 4.0 copy-start.5
  54.9 4.9 copy-start.29
  54.9 4.9 copy-start.14
  59.8 7.2 %copy-start.23 = (s32[2,256]{1,0:T(2,128)S(1)}, s32[2,256]{1,0:T(2,128)}, u32[]{:S(2)}) copy-start(s32[2,256]{1,0:T(2,128)} %param.13) | copy-start | bytes 6148
  59.8 7.3 %copy-start.24 = (s32[2,256]{1,0:T(2,128)S(1)}, s32[2,256]{1,0:T(2,128)}, u32[]{:S(2)}) copy-start(s32[2,256]{1,0:T(2,128)} %param.14) | copy-start | bytes 6148
  63.6 4.5 copy-start.9
  68.7 4.3 copy-start.17
  234.3 8.9 %copy-start.1 = (bf16[2,4,64,2048]{3,2,0,1:T(8,128)(2,1)S(1)}, bf16[2,4,64,2048]{3,2,0,1:T(8,128)(2,1)}, u32[]{:S(2)}) copy-start(bf16[2,4,64,2048]{3,2,0,1:T(8,128)(2,1)} %copy.97) | copy-start | bytes 6291460
  234.3 8.9 %copy-start.11 = (bf16[4,128,2048]{2,1,0:T(8,128)(2,1)S(1)}, bf16[4,128,2048]{2,1,0:T(8,128)(2,1)}, u32[]{:S(2)}) copy-start(bf16[4,128,2048]{2,1,0:T(8,128)(2,1)} %get-tuple-element.43) | copy-start | bytes 6291460
  243.1 1.3 copy-start.12
  244.4 6.1 %copy-start.2 = (bf16[8,256,1024]{2,1,0:T(8,128)(2,1)S(1)}, bf16[8,256,1024]{2,1,0:T(8,128)(2,1)}, u32[]{:S(2)}) copy-start(bf16[8,256,1024]{2,1,0:T(8,128)(2,1)} %get-tuple-element.44) | copy-start | bytes 12582916
  250.5 6.9 %copy-start.26 = (bf16[8,256,1024]{2,1,0:T(8,128)(2,1)S(1)}, bf16[8,256,1024]{2,1,0:T(8,128)(2,1)}, u32[]{:S(2)}) copy-start(bf16[8,256,1024]{2,1,0:T(8,128)(2,1)} %get-tuple-element.42) | copy-start | bytes 12582916
  257.4 6.2 %copy-start.13 = (bf16[1024,1024]{1,0:T(8,128)(2,1)}, bf16[1024,1024]{1,0:T(8,128)(2,1)S(1)}, u32[]{:S(2)}) copy-start(bf16[1024,1024]{1,0:T(8,128)(2,1)S(1)} %get-tuple-element.129.refs_8_) | copy-start | bytes 6291460
  265.5 79.1 %copy-start.27 = (bf16[8,256,512]{2,1,0:T(8,128)(2,1)S(1)}, bf16[8,256,512]{2,1,0:T(8,128)(2,1)}, u32[]{:S(2)}) copy-start(bf16[8,256,512]{2,1,0:T(8,128)(2,1)} %get-tuple-element.52) | copy-start | bytes 6291460
  344.6 3.8 copy-start.7
  344.6 3.9 copy-start.28
  351.8 106.2 %copy-start.20 = (f32[3,16,2048]{2,1,0:T(8,128)S(1)}, f32[3,16,2048]{2,1,0:T(8,128)}, u32[]{:S(2)}) copy-start(f32[3,16,2048]{2,1,0:T(8,128)} %get-tuple-element.56) | copy-start | bytes 1179652
  456.7 5.7 %copy-start.4 = (bf16[8,256,512]{2,1,0:T(8,128)(2,1)S(1)}, bf16[8,256,512]{2,1,0:T(8,128)(2,1)}, u32[]{:S(2)}) copy-start(bf16[8,256,512]{2,1,0:T(8,128)(2,1)} %get-tuple-element.39) | copy-start | bytes 6291460
  456.7 5.7 %copy-start.8 = (bf16[2,256,512]{2,1,0:T(8,128)(2,1)S(1)}, bf16[2,256,512]{2,1,0:T(8,128)(2,1)}, u32[]{:S(2)}) copy-start(bf16[2,256,512]{2,1,0:T(8,128)(2,1)} %get-tuple-element.54) | copy-start | bytes 1572868
  463.7 2.4 copy-start.6
  466.0 2.6 copy-start.16
  519.8 3.3 copy-start.22
  519.8 8.3 %copy-start.18 = (f32[256,512]{1,0:T(8,128)S(1)}, f32[256,512]{1,0:T(8,128)}, u32[]{:S(2)}) copy-start(f32[256,512]{1,0:T(8,128)} %get-tuple-element.61) | copy-start | bytes 1572868
  519.8 9.3 %copy-start.10 = (f32[256,2048]{1,0:T(8,128)S(1)}, f32[256,2048]{1,0:T(8,128)}, u32[]{:S(2)}) copy-start(f32[256,2048]{1,0:T(8,128)} %get-tuple-element.63) | copy-start | bytes 6291460
  523.2 7.7 %copy-start.25 = (f32[7,64]{1,0:T(8,128)}, f32[7,64]{1,0:T(8,128)S(1)}, u32[]{:S(2)}) copy-start(f32[7,64]{1,0:T(8,128)S(1)} %constant_dynamic-slice_fusion) | copy-start | bytes 5380
  524.9 6.0 %copy-start.19 = (f32[256,512]{1,0:T(8,128)S(1)}, f32[256,512]{1,0:T(8,128)}, u32[]{:S(2)}) copy-start(f32[256,512]{1,0:T(8,128)} %get-tuple-element.145) | copy-start | bytes 1572868
  528.1 3.6 copy-start.21

commit v10 on v9

--- a/solution.py
+++ b/solution.py
@@ -316,6 +316,7 @@
     for handle in kv_core:
         wire.arrived(handle)
     attend_batch(1 - core, [spread // 3])
+    pj_far.update(send_far(pj_in, pj_out, order[1 : lines // 2]))
     wire.arrived(dy_side)
     block = dy_out.at[flip(place, 2)]
     wire.copy(block, block, other_core)
@@ -376,9 +377,10 @@
     pair_handle = wire.copy(mine, rows_two.at[1, place], pair)
     side_handle = wire.copy(mine, mine, other_side)
     wire.copy(mine, mine, other_core)
-    pj_far.update(send_far(pj_in, pj_out, order[1:]))
+    pj_far.update(send_far(pj_in, pj_out, order[lines // 2 :]))
     tick(len(jobs))
     jobs.extend((pj_far, pj_out, d) for d in order)
+    tick(lines // 2)
     wire.arrived(pair_handle)
     theirs = rows_two.at[1, place]
     side_two = wire.copy(theirs, theirs, other_side)

time: 536 us -> 522 us (0.974)
  Pallas kernels: 434 us -> 419 us
    pallas_call x1, Pallas kernels: 159 us -> 146 us  [front(): pl.pallas_call(partial(front_kernel, count), out_shape=[jax.ShapeDtypeStr...]
where the time goes in v10:
time: 522 us; the launch traced here: 521 us
  Pallas kernels  419 us (80%)
  matrix products  45.3 us (9%)
  local copies, waits for them, and re-layouts  37.7 us (7%)
  other arithmetic  17.7 us (3%)
    pallas_call x1, Pallas kernels, front(): pl.pallas_call(partial(front_kernel, count), out_shape=[jax.ShapeDtypeStr...  146 us
    pallas_call x1, Pallas kernels, back_stage(): pl.pallas_call(partial(back_kernel, count), out_shape=[jax.ShapeDtypeStru...  105 us
    pallas_call x1, Pallas kernels, middle_stage(): pl.pallas_call(partial(middle_kernel, count), out_shape=[jax.ShapeDtypeSt...  77.6 us
    pallas_call x1, Pallas kernels, last_stage(): pl.pallas_call(partial(last_kernel, count), out_shape=[jax.ShapeDtypeStru...  48.6 us
    pallas_call x1, Pallas kernels, gather_first(): pl.pallas_call(partial(first_kernel, count, tensor), out_shape=[jax.Shape...  41.7 us
    dot_general x5, matrix products, dot(): return jnp.dot(left, right, preferred_element_type=F32)  23.7 us
    dot_general x4, matrix products, dot_tn(): lax.dot_general(left, right, (((0,), (0,)), ((), ())), preferred_element_...  12.1 us
    unnamed x74, local copies, waits for them, and re-layouts  11.6 us

profile of v10, /device:TPU:0, one launch (start us, length us, event | category | flops | bytes accessed | tf_op | source)
XLA Modules:
  0.0 520.9 jit_solution(2157909512781959915)
XLA Ops:
  0.7 0.8 fusion.21
  1.5 0.7 convert_element_type.141
  4.4 1.8 convert_element_type.151.refs_2_
  6.2 1.5 convert_element_type.150.refs_1_
  7.6 41.7 %gather_first.1 = (bf16[8,4,32,128]{3,2,1,0:T(8,128)(2,1)}, bf16[8,4,64,256]{3,2,1,0:T(8,128)(2,1)}, bf16[8,256,512]{2,1,0:T(8,128)(2,1)}) custom-call(bf16[32,128]{1,0:T(8,128)(2,1)} %pad_bitcast_fusion.refs_0_, bf16[64,256]{1,0:T(8,128)(2,1)} %convert_element_type.150.refs_1_, bf16[256,512]{1,0:T(8,128)(2,1)} %convert_element_type.151.refs_2_), custom_call_target="tpu_custom_call" | custom-call | tf_op jit(solution)/shard_map/gather_first/pallas_call | solution.py:176
  49.3 1.1 reshape.257
  51.2 2.1 convert_reduce_fusion
  54.0 0.8 fusion.5
  54.9 2.0 fusion.16
  56.9 1.1 fusion.23
  59.8 3.0 fusion.17
  62.8 0.9 constant_dynamic-slice_fusion.2
  63.6 3.3 copy.97
  67.4 0.7 pad.37.refs_2_.refs_5_
  68.7 1.3 copy.95
  70.1 1.7 convert_element_type.167
  71.8 1.3 copy.96
  73.1 0.8 copy.93
  73.9 146.5 %front.1 = (bf16[2,256,512]{2,1,0:T(8,128)(2,1)}, f32[2,4,256,1]{3,2,1,0:T(8,128)}, bf16[2,8,256,256]{3,2,1,0:T(8,128)(2,1)}, bf16[8,256,512]{2,1,0:T(8,128)(2,1...) custom-call(bf16[2,256,512]{2,1,0:T(8,128)(2,1)} %bitcast.156, ...), custom_call_target="tpu_custom_call" | custom-call | tf_op jit(solution)/shard_map/front/pallas_call | solution.py:420
  220.4 0.9 slice_bitcast_fusion
  221.4 8.8 %multiply_convert_fusion = (bf16[1024,1024]{1,0:T(8,128)(2,1)S(1)}, f32[1024,1024]{1,0:T(8,128)S(1)}) fusion(f32[1024]{0:T(1024)S(1)} %dynamic_slice.22, bf16[1024,2048]{1,0:T(8,128)(2,1)} %bitcast.144, bf16[2048,1024]{1,0:T(8,128)(2,1)} %bitcast.198), kind=kOutput, calls=%fused_computation.23 | convolution fusion | flops 4305453056 | bytes 14684160 | tf_op jit(solution)/shard_map/dot_general | solution.py:31
  230.6 0.9 copy-done.12
  231.5 6.1 %convolution_convert_fusion = bf16[2048,1024]{1,0:T(8,128)(2,1)} fusion(bf16[1024,2048]{1,0:T(8,128)(2,1)S(1)} %bitcast.139, bf16[1024,1024]{1,0:T(8,128)(2,1)S(1)} %get-tuple-element.126.refs_5_), kind=kOutput, calls=%fused_computation.25 | convolution fusion | flops 4297064448 | bytes 10485760 | tf_op jit(solution)/shard_map/dot_general | solution.py:35
  237.6 6.8 %convert_reduce_fusion.1 = (f32[1024]{0:T(1024)S(1)}, bf16[1024,1024]{1,0:T(8,128)(2,1)S(1)}) fusion(bf16[1024,2048]{1,0:T(8,128)(2,1)S(1)} %bitcast.140, bf16[2048,1024]{1,0:T(8,128)(2,1)S(1)} %bitcast.147, f32[1024,1024]{1,0:T(8,128)S(1)} %get-tuple-element.127, f32[1024]{0:T(1024)S(1)} %dynamic_slice.22), kind=kOutput, calls=%fused_computation.21 | convolution fusion | flops 4316986368 | bytes 14688256 | tf_op jit(solution)/shard_map/dot_general | solution.py:31
  244.5 6.2 %convolution_convert_fusion.1 = bf16[1024,2048]{1,0:T(8,128)(2,1)} fusion(bf16[1024,1024]{1,0:T(8,128)(2,1)S(1)} %get-tuple-element.129.refs_8_, bf16[2048,1024]{1,0:T(8,128)(2,1)S(1)} %bitcast.199), kind=kOutput, calls=%fused_computation.26 | convolution fusion | flops 4297064448 | bytes 10485760 | tf_op jit(solution)/shard_map/dot_general | solution.py:39
  250.6 1.9 convert_reduce_fusion.2
  252.6 77.6 %middle.1 = (f32[256,2048]{1,0:T(8,128)}, f32[128,2048]{1,0:T(8,128)}, bf16[4,128,2048]{2,1,0:T(8,128)(2,1)}, f32[3,16,2048]{2,1,0:T(8,128)}, bf16[1024,2048]{1,0:T(8,128)(2,1)}, /*index=5*/bf16[2048,1024]{1,0:T(8,128)(2,1)}) custom-call(bf16[2,4,128,2048]{3,2,1,0:T(8,128)(2,1)} %bitcast.151, bf16[8,256,1024]{2,1,0:T(8,128)(2,1)} %bitcast.150, ...), custom_call_target="tpu_custom_call" | custom-call | tf_op jit(solution)/shard_map/middle/pallas_call | solution.py:730
  330.2 3.0 convolution_convert_fusion.3
  333.2 0.8 copy.100
  334.1 2.6 convolution_convert_fusion.2
  337.4 104.7 %back.1 = (f32[256,2048]{1,0:T(8,128)}, f32[256,512]{1,0:T(8,128)}, bf16[2,256,512]{2,1,0:T(8,128)(2,1)}, bf16[2,256,256]{2,1,0:T(8,128)(2,1)}, bf16[4,128,2048]{2,1,0:T(8,128)(2,1)}) custom-call(bf16[2,4,128,2048]{3,2,1,0:T(8,128)(2,1)} %bitcast.148, bf16[8,256,1024]{2,1,0:T(8,128)(2,1)} %bitcast.149, bf16[8,256,512]{2,1,0:T(8,128)(2,1)} %bitcast.170, ...), custom_call_target="tpu_custom_call" | custom-call | tf_op jit(solution)/shard_map/back/pallas_call | solution.py:890
  442.2 1.3 convert_reduce_fusion.3
  443.7 1.0 convert_reduce_fusion.4
  445.0 0.7 select_maximum_fusion.refs_3_
  445.7 2.0 fusion.25
  447.8 1.3 add_convert_fusion
  449.1 1.5 copy.102
  450.6 0.9 copy-done.6
  451.5 2.6 bitcast_convert_fusion
  454.1 0.8 fusion.15
  454.8 1.0 copy.105
  456.6 48.6 %last.1 = (f32[256,512]{1,0:T(8,128)}, f32[64,256]{1,0:T(8,128)}, bf16[4,128,2048]{2,1,0:T(8,128)(2,1)}, f32[16,256]{1,0:T(8,128)}) custom-call(bf16[1,4,128,2048]{3,2,1,0:T(8,128)(2,1)} %bitcast.134, bf16[8,256,512]{2,1,0:T(8,128)(2,1)} %bitcast.168, bf16[1,4,512,256]{3,2,1,0:T(8,128)(2,1)} %bitcast.142, f32[8,16,256]{2,1,0:T(8,128)} %select_maximum_fusion.refs_3_, ...), custom_call_target="tpu_custom_call" | custom-call | tf_op jit(solution)/shard_map/last/pallas_call | solution.py:1000
  505.3 3.3 copy.106
  510.3 3.2 copy.101
  513.6 1.0 copy.107
  514.6 1.8 copy.108
  516.4 0.8 copy.134
  517.8 3.1 copy.136
  (121 shorter events, 11.2 us)
Async XLA Ops:
  0.6 52.6 %copy-start = (bf16[2,256,2048]{2,1,0:T(8,128)(2,1)S(1)}, bf16[2,256,2048]{2,1,0:T(8,128)(2,1)}, u32[]{:S(2)}) copy-start(bf16[2,256,2048]{2,1,0:T(8,128)(2,1)} %param.12) | copy-start | bytes 6291460
  50.4 4.4 copy-start.15
  51.2 3.7 copy-start.3
  54.9 4.0 copy-start.5
  54.9 4.9 copy-start.29
  54.9 4.9 copy-start.14
  59.8 7.2 %copy-start.23 = (s32[2,256]{1,0:T(2,128)S(1)}, s32[2,256]{1,0:T(2,128)}, u32[]{:S(2)}) copy-start(s32[2,256]{1,0:T(2,128)} %param.13) | copy-start | bytes 6148
  59.8 7.3 %copy-start.24 = (s32[2,256]{1,0:T(2,128)S(1)}, s32[2,256]{1,0:T(2,128)}, u32[]{:S(2)}) copy-start(s32[2,256]{1,0:T(2,128)} %param.14) | copy-start | bytes 6148
  63.6 4.5 copy-start.9
  68.7 4.3 copy-start.17
  221.4 8.8 %copy-start.1 = (bf16[2,4,64,2048]{3,2,0,1:T(8,128)(2,1)S(1)}, bf16[2,4,64,2048]{3,2,0,1:T(8,128)(2,1)}, u32[]{:S(2)}) copy-start(bf16[2,4,64,2048]{3,2,0,1:T(8,128)(2,1)} %copy.97) | copy-start | bytes 6291460
  221.4 8.8 %copy-start.11 = (bf16[4,128,2048]{2,1,0:T(8,128)(2,1)S(1)}, bf16[4,128,2048]{2,1,0:T(8,128)(2,1)}, u32[]{:S(2)}) copy-start(bf16[4,128,2048]{2,1,0:T(8,128)(2,1)} %get-tuple-element.43) | copy-start | bytes 6291460
  230.2 1.3 copy-start.12
  231.5 6.1 %copy-start.2 = (bf16[8,256,1024]{2,1,0:T(8,128)(2,1)S(1)}, bf16[8,256,1024]{2,1,0:T(8,128)(2,1)}, u32[]{:S(2)}) copy-start(bf16[8,256,1024]{2,1,0:T(8,128)(2,1)} %get-tuple-element.44) | copy-start | bytes 12582916
  237.6 6.9 %copy-start.26 = (bf16[8,256,1024]{2,1,0:T(8,128)(2,1)S(1)}, bf16[8,256,1024]{2,1,0:T(8,128)(2,1)}, u32[]{:S(2)}) copy-start(bf16[8,256,1024]{2,1,0:T(8,128)(2,1)} %get-tuple-element.42) | copy-start | bytes 12582916
  244.4 6.2 %copy-start.13 = (bf16[1024,1024]{1,0:T(8,128)(2,1)}, bf16[1024,1024]{1,0:T(8,128)(2,1)S(1)}, u32[]{:S(2)}) copy-start(bf16[1024,1024]{1,0:T(8,128)(2,1)S(1)} %get-tuple-element.129.refs_8_) | copy-start | bytes 6291460
  252.6 77.6 %copy-start.27 = (bf16[8,256,512]{2,1,0:T(8,128)(2,1)S(1)}, bf16[8,256,512]{2,1,0:T(8,128)(2,1)}, u32[]{:S(2)}) copy-start(bf16[8,256,512]{2,1,0:T(8,128)(2,1)} %get-tuple-element.52) | copy-start | bytes 6291460
  330.2 3.8 copy-start.7
  330.2 3.9 copy-start.28
  337.4 106.1 %copy-start.20 = (f32[3,16,2048]{2,1,0:T(8,128)S(1)}, f32[3,16,2048]{2,1,0:T(8,128)}, u32[]{:S(2)}) copy-start(f32[3,16,2048]{2,1,0:T(8,128)} %get-tuple-element.56) | copy-start | bytes 1179652
  442.1 5.6 %copy-start.4 = (bf16[8,256,512]{2,1,0:T(8,128)(2,1)S(1)}, bf16[8,256,512]{2,1,0:T(8,128)(2,1)}, u32[]{:S(2)}) copy-start(bf16[8,256,512]{2,1,0:T(8,128)(2,1)} %get-tuple-element.39) | copy-start | bytes 6291460
  442.2 5.6 %copy-start.8 = (bf16[2,256,512]{2,1,0:T(8,128)(2,1)S(1)}, bf16[2,256,512]{2,1,0:T(8,128)(2,1)}, u32[]{:S(2)}) copy-start(bf16[2,256,512]{2,1,0:T(8,128)(2,1)} %get-tuple-element.54) | copy-start | bytes 1572868
  449.1 2.4 copy-start.6
  451.5 2.6 copy-start.16
  505.2 3.3 copy-start.22
  505.2 8.3 %copy-start.18 = (f32[256,512]{1,0:T(8,128)S(1)}, f32[256,512]{1,0:T(8,128)}, u32[]{:S(2)}) copy-start(f32[256,512]{1,0:T(8,128)} %get-tuple-element.61) | copy-start | bytes 1572868
  505.2 9.3 %copy-start.10 = (f32[256,2048]{1,0:T(8,128)S(1)}, f32[256,2048]{1,0:T(8,128)}, u32[]{:S(2)}) copy-start(f32[256,2048]{1,0:T(8,128)} %get-tuple-element.63) | copy-start | bytes 6291460
  508.6 7.7 %copy-start.25 = (f32[7,64]{1,0:T(8,128)}, f32[7,64]{1,0:T(8,128)S(1)}, u32[]{:S(2)}) copy-start(f32[7,64]{1,0:T(8,128)S(1)} %constant_dynamic-slice_fusion) | copy-start | bytes 5380
  510.3 6.0 %copy-start.19 = (f32[256,512]{1,0:T(8,128)S(1)}, f32[256,512]{1,0:T(8,128)}, u32[]{:S(2)}) copy-start(f32[256,512]{1,0:T(8,128)} %get-tuple-element.145) | copy-start | bytes 1572868
  513.6 3.6 copy-start.21
